TPU v7x, 128 devices: a whole 4x4x4 slice. The times are simulated.
128 devices in a mesh: view: 4 (over x_lo, core), vol: 32 (over x_hi, z, y).
Axes of the slice: x: 4 (x_hi: 2, x_lo: 2; x = x_hi * 2 + x_lo), y: 4, z: 4, core: 2. Of those that a mesh axis runs over, the one named last changes fastest.
Arguments:
- raw_views: bfloat16 [12, 256, 256, 128], P('view', 'vol'), may hold values from 0.18 to 5.41, as said below
- weights: float32 [12, 256, 8], P('view'), may hold values from 0.05 to 1
- offsets: int32 [12, 256], P('view'), may hold values from 0 to 248, as said below
- psf_taps: float32 [12, 3, 9], P('view'), may hold values from 0.01 to 1
Outputs:
- joined_volume: float32 [256, 256, 128], P(None, 'vol')
Inputs may be any that keep to these rules, and one draw needn't show every extreme that they name: offsets[v, x] - x + 4 lies in -3 to 4 except where clipped to 0 or 248. `raw_views`: positive intensities.
All inputs are finite; a program needn't handle non-finite values.
Results may differ from a plain program's by a relative error of at most 0.0003.
The roundings to bfloat16 on the way count: a program that leaves them out, or rounds other values in their place, can miss the bound.
Values may be sent and summed in bfloat16 or wider, within the bound.
A program may use at most 64 MiB of HBM per device.

v0:
```python
import jax
import jax.numpy as jnp
from jax import lax
from jax.sharding import PartitionSpec as P

ITERS = 2


def extended_2(shard, sides, width):
    for axis, dim in sides:
        devices, length = (lax.axis_size(axis), shard.shape[dim])
        up = [(i, (i + 1) % devices) for i in range(devices - 1)]
        down = [(j, i) for i, j in up]
        last = lax.slice_in_dim(shard, length - width, length, axis=dim)
        first = lax.slice_in_dim(shard, 0, width, axis=dim)
        before = lax.ppermute(last, axis, up)
        after = lax.ppermute(first, axis, down)
        shard = jnp.concatenate([before, shard, after], axis=dim)
    return shard


def pad_axis(field, axis, width):
    widths = [(0, 0)] * field.ndim
    widths[axis] = (width, width)
    return jnp.pad(field, widths)


def correlate(extended, taps, axis, length):
    result = taps[0] * lax.slice_in_dim(extended, 0, length, axis=axis)
    for offset in range(1, taps.shape[0]):
        result = result + taps[offset] * lax.slice_in_dim(
            extended, offset, offset + length, axis=axis
        )
    return result


def blur_forward(extended, taps, length):
    rim_width = (taps.shape[1] - 1) // 2
    along_x = correlate(extended, taps[1], 1, length)
    along_z = correlate(pad_axis(along_x, 0, rim_width), taps[0], 0, along_x.shape[0])
    return correlate(pad_axis(along_z, 2, rim_width), taps[2], 2, along_z.shape[2])


def blur_back_yz(field, taps):
    rim_width = (taps.shape[1] - 1) // 2
    along_y = correlate(pad_axis(field, 2, rim_width), taps[2][::-1], 2, field.shape[2])
    return correlate(pad_axis(along_y, 0, rim_width), taps[0][::-1], 0, field.shape[0])


def resample_view(planes, weight_rows, first_rows):
    result = jnp.zeros((planes.shape[0], first_rows.shape[0], planes.shape[2]), jnp.float32)
    for offset in range(weight_rows.shape[1]):
        gathered = jnp.take(planes, first_rows + offset, axis=1).astype(jnp.float32)
        result = result + weight_rows[None, :, offset, None] * gathered
    return result.astype(jnp.bfloat16)


def update_estimate(joined_volume, logs, total_views):
    summed = lax.psum(logs, "view")
    return joined_volume * jnp.exp(summed / total_views)


def per_device(raw_views, weights, offsets, psf_taps):
    count = raw_views.shape[0]
    total_views = count * lax.axis_size("view")
    rim_width = (psf_taps.shape[2] - 1) // 2
    weight_norm = weights / jnp.sum(weights, axis=-1, keepdims=True)
    taps_norm = psf_taps / jnp.sum(psf_taps, axis=-1, keepdims=True)
    local_views = jnp.stack(
        [
            resample_view(raw_views[index], weight_norm[index], offsets[index])
            for index in range(count)
        ]
    )
    bricks = lax.all_to_all(local_views, "vol", split_axis=2, concat_axis=1, tiled=True)
    width = bricks.shape[2]
    local_sum = bricks[0].astype(jnp.float32)
    for index in range(1, count):
        local_sum = local_sum + bricks[index].astype(jnp.float32)
    joined_volume = lax.psum(local_sum, "view") / total_views
    for turn in range(ITERS):
        extended = extended_2(joined_volume, (("vol", 1),), rim_width)
        partials = []
        for index in range(count):
            blurred = blur_forward(extended, taps_norm[index], width)
            ratio = bricks[index].astype(jnp.float32) / blurred
            partials.append(blur_back_yz(ratio, taps_norm[index]))
        ratio_wide = extended_2(jnp.stack(partials), (("vol", 2),), rim_width)
        logs = jnp.zeros(joined_volume.shape, jnp.float32)
        for index in range(count):
            back = correlate(ratio_wide[index], taps_norm[index, 1][::-1], 1, width)
            logs = logs + jnp.log(back)
        joined_volume = update_estimate(joined_volume, logs, total_views)
    return joined_volume


def solution(mesh):
    placed = (
        P("view", "vol", None, None),
        P("view", None, None),
        P("view", None),
        P("view", None, None),
    )
    return jax.shard_map(
        per_device, mesh=mesh, in_specs=placed, out_specs=P(None, "vol", None), check_vma=False
    )
```

profile of v0, /device:TPU:5, one launch (start us, length us, event | category | flops | bytes accessed | tf_op | source)
XLA Modules:
  0.0 674.6 jit_solution(16217242641233608025)
XLA Ops:
  47.6 7.2 %fusion.328 = bf16[1,8,256,128]{3,1,2,0:T(8,128)(2,1)S(1)} fusion(bf16[256,8,128]{2,1,0:T(8,128)(2,1)S(1)} %gather_fusion.7, pred[256]{0:T(512)(128)(4,1)S(1)} %get-tuple-element.138, f32[256]{0:T(256)S(1)} %bitcast.296, bf16[256,8,128]{2,1,0:T(8,128)(2,1)S(1)} %gather_fusion.6, pred[256]{0:T(512)(128)(4,1)S(1)} %get-tuple-element.139, ...), kind=kLoop, calls=%fused_computation.609 | loop fusion | flops 8388608 | bytes 4728832 | tf_op jit(solution)/shard_map/stack | solution.py:69
  55.0 5.2 fusion.330
  60.3 5.2 fusion.329
  65.9 31.9 %all_to_all.15 = bf16[3,8,256,128]{3,1,0,2:T(8,128)(2,1)S(1)} all-to-all(bf16[3,8,256,128]{3,1,0,2:T(8,128)(2,1)S(1)} %copy.15), channel_id=1, replica_groups=mesh['view'=4,'vol'=32] {'vol'}, dimensions={2} | all-to-all | bytes 3145728 | tf_op jit(solution)/shard_map/all_to_all | solution.py:75
  101.8 40.4 %all-reduce.28.cloned.1.call-done = f32[256,8,128]{2,1,0:T(8,128)} async-done(((f32[256,8,128]{2,1,0:T(8,128)}), f32[256,8,128]{2,1,0:T(8,128)}) %all-reduce.28.cloned.1.call-update) | async-done | bytes 1048592 | tf_op jit(solution)/shard_map/psum | solution.py:80
  144.7 7.0 %collective-permute-start.1 = (f32[256,4,128]{2,1,0:T(4,128)}, f32[256,4,128]{2,1,0:T(4,128)}, u32[]{:S(2)}, u32[]{:S(2)}) collective-permute-start(f32[256,4,128]{2,1,0:T(4,128)} %get-tuple-element.24), channel_id=1, source_target_pairs={{1,0},{2,1},{3,2},{4,3},{5,4},{6,5},{7,6},{8,7},{9,8},{10,9},{11,1... | collective-permute-start | bytes 1572872 | tf_op jit(solution)/shard_map/ppermute | solution.py:17
  163.0 9.5 %collective-permute-done = f32[256,4,128]{2,1,0:T(4,128)} collective-permute-done((f32[256,4,128]{2,1,0:T(4,128)}, f32[256,4,128]{2,1,0:T(4,128)}, u32[]{:S(2)}, u32[]{:S(2)}) %collective-permute-start) | collective-permute-done | bytes 524320 | tf_op jit(solution)/shard_map/ppermute | solution.py:16
  172.6 9.6 %multiply_add_fusion.11 = f32[256,8,128]{2,1,0:T(8,128)S(1)} fusion(f32[256,8,128]{2,1,0:T(8,128)S(1)} %copy-done.1, f32[]{:T(128)} %bitcast.78, f32[]{:T(128)} %bitcast.77, f32[]{:T(128)} %bitcast.76, f32[]{:T(128)S(6)} %mul.1801, f32[]{:T(128)} %bitcast.74, f32[]{:T(128)} %bitcast.73, f32[]{:T(128)} %bitcast.72, f32[]{:T(128)} %bitcast.71, f32[]{:T(128)} %bitcast.66, ...), kind=kLoop, calls=%fused_computation.598 | loop fusion | flops 6553600 | bytes 4194340 | tf_op jit(solution)/shard_map/add | solution.py:31
  182.2 6.3 multiply_add_fusion.10
  188.5 7.6 %fusion.21 = f32[256,8,128]{2,1,0:T(8,128)S(1)} fusion(f32[256,8,128]{2,1,0:T(8,128)S(1)} %multiply_add_fusion.10, f32[1,32,8,8,128]{4,3,2,1,0:T(8,128)S(1)} %copy-done.8, f32[]{:T(128)} %bitcast.92, f32[]{:T(128)} %bitcast.91, f32[]{:T(128)} %bitcast.90, f32[]{:T(128)} %bitcast.89, f32[]{:T(128)} %bitcast.88, f32[]{:T(128)} %bitcast.87, f32[]{:T(128)} %bitcast.86, ...), kind=kLoop, calls=%fused_computation.176 | loop fusion | flops 4718592 | bytes 3145764 | tf_op jit(solution)/shard_map/div | solution.py:86
  196.1 7.6 %fusion.37 = f32[256,8,128]{2,1,0:T(8,128)S(1)} fusion(f32[256,8,128]{2,1,0:T(8,128)S(1)} %fusion.21, f32[]{:T(128)} %bitcast.92, f32[]{:T(128)} %bitcast.91, f32[]{:T(128)} %bitcast.90, f32[]{:T(128)} %bitcast.89, f32[]{:T(128)} %bitcast.88, f32[]{:T(128)} %bitcast.87, f32[]{:T(128)} %bitcast.86, f32[]{:T(128)} %bitcast.69, f32[]{:T(128)} %bitcast.68), kind=kLoop, calls=%fused_computation.192 | loop fusion | flops 4456448 | bytes 2097188 | tf_op jit(solution)/shard_map/add | solution.py:31
  203.7 6.2 add_bitcast_fusion.5
  210.0 9.7 %multiply_add_fusion.9 = f32[256,8,128]{2,1,0:T(8,128)S(1)} fusion(f32[256,8,128]{2,1,0:T(8,128)S(1)} %copy-done.1, f32[]{:T(128)} %bitcast.106, f32[]{:T(128)} %bitcast.105, f32[]{:T(128)} %bitcast.104, f32[]{:T(128)} %bitcast.103, f32[]{:T(128)S(6)} %mul.1873, f32[]{:T(128)} %bitcast.101, f32[]{:T(128)} %bitcast.100, f32[]{:T(128)} %bitcast.99, ...), kind=kLoop, calls=%fused_computation.579 | loop fusion | flops 6553600 | bytes 4194340 | tf_op jit(solution)/shard_map/add | solution.py:31
  219.7 6.2 multiply_add_fusion.8
  225.9 7.8 %fusion.54 = f32[256,8,128]{2,1,0:T(8,128)S(1)} fusion(f32[256,8,128]{2,1,0:T(8,128)S(1)} %multiply_add_fusion.8, f32[1,32,8,8,128]{4,3,2,1,0:T(8,128)S(1)} %copy-done.5, f32[]{:T(128)} %bitcast.120, f32[]{:T(128)} %bitcast.119, f32[]{:T(128)} %bitcast.118, f32[]{:T(128)} %bitcast.117, f32[]{:T(128)} %bitcast.116, f32[]{:T(128)} %bitcast.115, f32[]{:T(128)} %bitcast.114, ...), kind=kLoop, calls=%fused_computation.209 | loop fusion | flops 4718592 | bytes 3145764 | tf_op jit(solution)/shard_map/div | solution.py:86
  233.6 7.8 %fusion.70 = f32[256,8,128]{2,1,0:T(8,128)S(1)} fusion(f32[256,8,128]{2,1,0:T(8,128)S(1)} %fusion.54, f32[]{:T(128)} %bitcast.120, f32[]{:T(128)} %bitcast.119, f32[]{:T(128)} %bitcast.118, f32[]{:T(128)} %bitcast.117, f32[]{:T(128)} %bitcast.116, f32[]{:T(128)} %bitcast.115, f32[]{:T(128)} %bitcast.114, f32[]{:T(128)} %bitcast.96, f32[]{:T(128)} %bitcast.95), kind=kLoop, calls=%fused_computation.225 | loop fusion | flops 4456448 | bytes 2097188 | tf_op jit(solution)/shard_map/add | solution.py:31
  241.4 6.1 add_bitcast_fusion.4
  247.5 10.0 %multiply_add_fusion.7 = f32[256,8,128]{2,1,0:T(8,128)S(1)} fusion(f32[256,8,128]{2,1,0:T(8,128)S(1)} %copy-done.1, f32[]{:T(128)} %bitcast.134, f32[]{:T(128)} %bitcast.133, f32[]{:T(128)} %bitcast.132, f32[]{:T(128)} %bitcast.131, f32[]{:T(128)S(6)} %mul.1946, f32[]{:T(128)} %bitcast.129, f32[]{:T(128)} %bitcast.128, f32[]{:T(128)} %bitcast.127, ...), kind=kLoop, calls=%fused_computation.560 | loop fusion | flops 6553600 | bytes 4194340 | tf_op jit(solution)/shard_map/add | solution.py:31
  257.5 6.1 multiply_add_fusion.6
  263.6 7.9 %fusion.87 = f32[256,8,128]{2,1,0:T(8,128)S(1)} fusion(f32[256,8,128]{2,1,0:T(8,128)S(1)} %multiply_add_fusion.6, f32[1,32,8,8,128]{4,3,2,1,0:T(8,128)S(1)} %copy.18, f32[]{:T(128)} %bitcast.148, f32[]{:T(128)} %bitcast.147, f32[]{:T(128)} %bitcast.146, f32[]{:T(128)} %bitcast.145, f32[]{:T(128)} %bitcast.144, f32[]{:T(128)} %bitcast.143, f32[]{:T(128)} %bitcast.142, ...), kind=kLoop, calls=%fused_computation.242 | loop fusion | flops 4718592 | bytes 3145764 | tf_op jit(solution)/shard_map/div | solution.py:86
  271.5 7.9 %fusion.103 = f32[256,8,128]{2,1,0:T(8,128)S(1)} fusion(f32[256,8,128]{2,1,0:T(8,128)S(1)} %fusion.87, f32[]{:T(128)} %bitcast.148, f32[]{:T(128)} %bitcast.147, f32[]{:T(128)} %bitcast.146, f32[]{:T(128)} %bitcast.145, f32[]{:T(128)} %bitcast.144, f32[]{:T(128)} %bitcast.143, f32[]{:T(128)} %bitcast.142, f32[]{:T(128)} %bitcast.124, f32[]{:T(128)} %bitcast.123), kind=kLoop, calls=%fused_computation.258 | loop fusion | flops 4456448 | bytes 2097188 | tf_op jit(solution)/shard_map/add | solution.py:31
  279.3 6.1 add_bitcast_fusion.3
  288.1 9.1 %collective-permute-start.3 = (f32[3,256,4,128]{3,2,1,0:T(4,128)S(1)}, f32[3,256,4,128]{3,2,1,0:T(4,128)S(1)}, u32[]{:S(2)}, u32[]{:S(2)}) collective-permute-start(f32[3,256,4,128]{3,2,1,0:T(4,128)S(1)} %get-tuple-element.15), channel_id=1, source_target_pairs={{1,0},{2,1},{3,2},{4,3},{5,4},{6,5},{7,6},{8,7},{9,8},{10,9},{11,1... | collective-permute-start | bytes 4718600 | tf_op jit(solution)/shard_map/ppermute | solution.py:17
  297.2 31.0 %collective-permute-done.2 = f32[3,256,4,128]{3,2,1,0:T(4,128)S(1)} collective-permute-done((f32[3,256,4,128]{3,2,1,0:T(4,128)S(1)}, f32[3,256,4,128]{3,2,1,0:T(4,128)S(1)}, u32[]{:S(2)}, u32[]{:S(2)}) %collective-permute-start.2) | collective-permute-done | bytes 1572896 | tf_op jit(solution)/shard_map/ppermute | solution.py:16
  332.3 28.9 %fusion.241 = f32[256,8,128]{2,1,0:T(8,128)} fusion(f32[256,16,128]{2,1,0:T(8,128)S(1)} %get-tuple-element.10, f32[256,16,128]{2,1,0:T(8,128)} %get-tuple-element.11, f32[256,16,128]{2,1,0:T(8,128)S(1)} %get-tuple-element.9, f32[]{:T(128)} %bitcast.130, f32[]{:T(128)} %bitcast.102, f32[]{:T(128)} %bitcast.75, f32[]{:T(128)} %bitcast.134, f32[]{:T(128)} %bitcast.133, ...), kind=kLoop, calls=%fused_computation.426 | loop fusion | flops 13893632 | bytes 29360236 | tf_op jit(solution)/shard_map/add | solution.py:92
  361.3 45.5 %all-reduce.30.cloned.1.call-done = f32[256,8,128]{2,1,0:T(8,128)} async-done(((f32[256,8,128]{2,1,0:T(8,128)}), f32[256,8,128]{2,1,0:T(8,128)}) %all-reduce.30.cloned.1.call-update) | async-done | bytes 1048592 | tf_op jit(solution)/shard_map/psum | solution.py:59
  408.7 7.0 %collective-permute-start.5 = (f32[256,4,128]{2,1,0:T(4,128)S(1)}, f32[256,4,128]{2,1,0:T(4,128)S(1)}, u32[]{:S(2)}, u32[]{:S(2)}) collective-permute-start(f32[256,4,128]{2,1,0:T(4,128)S(1)} %get-tuple-element.22), channel_id=1, source_target_pairs={{1,0},{2,1},{3,2},{4,3},{5,4},{6,5},{7,6},{8,7},{9,8},{10,9},{11,1... | collective-permute-start | bytes 1572872 | tf_op jit(solution)/shard_map/ppermute | solution.py:17
  417.8 8.9 %collective-permute-done.5 = f32[256,4,128]{2,1,0:T(4,128)S(1)} collective-permute-done((f32[256,4,128]{2,1,0:T(4,128)S(1)}, f32[256,4,128]{2,1,0:T(4,128)S(1)}, u32[]{:S(2)}, u32[]{:S(2)}) %collective-permute-start.5) | collective-permute-done | bytes 524320 | tf_op jit(solution)/shard_map/ppermute | solution.py:17
  426.7 9.7 %collective-permute-done.4 = f32[256,4,128]{2,1,0:T(4,128)S(1)} collective-permute-done((f32[256,4,128]{2,1,0:T(4,128)S(1)}, f32[256,4,128]{2,1,0:T(4,128)S(1)}, u32[]{:S(2)}, u32[]{:S(2)}) %collective-permute-start.4) | collective-permute-done | bytes 524320 | tf_op jit(solution)/shard_map/ppermute | solution.py:16
  436.4 7.9 %multiply_add_fusion.5 = f32[256,8,128]{2,1,0:T(8,128)S(1)} fusion(f32[256,8,128]{2,1,0:T(8,128)S(1)} %exponential_multiply_fusion.1, f32[]{:T(128)} %bitcast.75, f32[]{:T(128)} %bitcast.78, f32[]{:T(128)} %bitcast.77, f32[]{:T(128)} %bitcast.76, f32[]{:T(128)} %bitcast.74, f32[]{:T(128)} %bitcast.73, f32[]{:T(128)} %bitcast.72, f32[]{:T(128)} %bitcast.71, ...), kind=kLoop, calls=%fused_computation.540 | loop fusion | flops 6553600 | bytes 3145764 | tf_op jit(solution)/shard_map/add | solution.py:31
  444.3 6.2 multiply_add_fusion.4
  450.5 7.6 %fusion.120 = f32[256,8,128]{2,1,0:T(8,128)S(1)} fusion(f32[256,8,128]{2,1,0:T(8,128)S(1)} %multiply_add_fusion.4, f32[1,32,8,8,128]{4,3,2,1,0:T(8,128)S(1)} %copy-done.9, f32[]{:T(128)} %bitcast.92, f32[]{:T(128)} %bitcast.91, f32[]{:T(128)} %bitcast.90, f32[]{:T(128)} %bitcast.89, f32[]{:T(128)} %bitcast.88, f32[]{:T(128)} %bitcast.87, f32[]{:T(128)} %bitcast.86, ...), kind=kLoop, calls=%fused_computation.275 | loop fusion | flops 4718592 | bytes 3145764 | tf_op jit(solution)/shard_map/div | solution.py:86
  458.1 7.6 %fusion.136 = f32[256,8,128]{2,1,0:T(8,128)S(1)} fusion(f32[256,8,128]{2,1,0:T(8,128)S(1)} %fusion.120, f32[]{:T(128)} %bitcast.92, f32[]{:T(128)} %bitcast.91, f32[]{:T(128)} %bitcast.90, f32[]{:T(128)} %bitcast.89, f32[]{:T(128)} %bitcast.88, f32[]{:T(128)} %bitcast.87, f32[]{:T(128)} %bitcast.86, f32[]{:T(128)} %bitcast.69, f32[]{:T(128)} %bitcast.68), kind=kLoop, calls=%fused_computation.291 | loop fusion | flops 4456448 | bytes 2097188 | tf_op jit(solution)/shard_map/add | solution.py:31
  465.7 6.2 add_bitcast_fusion.2
  472.0 7.8 %multiply_add_fusion.3 = f32[256,8,128]{2,1,0:T(8,128)S(1)} fusion(f32[256,8,128]{2,1,0:T(8,128)S(1)} %exponential_multiply_fusion.1, f32[]{:T(128)} %bitcast.102, f32[]{:T(128)} %bitcast.106, f32[]{:T(128)} %bitcast.105, f32[]{:T(128)} %bitcast.104, f32[]{:T(128)} %bitcast.103, f32[]{:T(128)} %bitcast.101, f32[]{:T(128)} %bitcast.100, f32[]{:T(128)} %bitcast.99, ...), kind=kLoop, calls=%fused_computation.521 | loop fusion | flops 6553600 | bytes 3145764 | tf_op jit(solution)/shard_map/add | solution.py:31
  479.7 6.1 multiply_add_fusion.2
  485.8 7.8 %fusion.153 = f32[256,8,128]{2,1,0:T(8,128)S(1)} fusion(f32[256,8,128]{2,1,0:T(8,128)S(1)} %multiply_add_fusion.2, f32[1,32,8,8,128]{4,3,2,1,0:T(8,128)S(1)} %copy-done.6, f32[]{:T(128)} %bitcast.120, f32[]{:T(128)} %bitcast.119, f32[]{:T(128)} %bitcast.118, f32[]{:T(128)} %bitcast.117, f32[]{:T(128)} %bitcast.116, f32[]{:T(128)} %bitcast.115, ...), kind=kLoop, calls=%fused_computation.308 | loop fusion | flops 4718592 | bytes 3145764 | tf_op jit(solution)/shard_map/div | solution.py:86
  493.6 7.8 %fusion.169 = f32[256,8,128]{2,1,0:T(8,128)S(1)} fusion(f32[256,8,128]{2,1,0:T(8,128)S(1)} %fusion.153, f32[]{:T(128)} %bitcast.120, f32[]{:T(128)} %bitcast.119, f32[]{:T(128)} %bitcast.118, f32[]{:T(128)} %bitcast.117, f32[]{:T(128)} %bitcast.116, f32[]{:T(128)} %bitcast.115, f32[]{:T(128)} %bitcast.114, f32[]{:T(128)} %bitcast.96, f32[]{:T(128)} %bitcast.95), kind=kLoop, calls=%fused_computation.324 | loop fusion | flops 4456448 | bytes 2097188 | tf_op jit(solution)/shard_map/add | solution.py:31
  501.4 6.1 add_bitcast_fusion.1
  507.5 8.1 %multiply_add_fusion.1 = f32[256,8,128]{2,1,0:T(8,128)S(1)} fusion(f32[256,8,128]{2,1,0:T(8,128)S(1)} %exponential_multiply_fusion.1, f32[]{:T(128)} %bitcast.130, f32[]{:T(128)} %bitcast.134, f32[]{:T(128)} %bitcast.133, f32[]{:T(128)} %bitcast.132, f32[]{:T(128)} %bitcast.131, f32[]{:T(128)} %bitcast.129, f32[]{:T(128)} %bitcast.128, f32[]{:T(128)} %bitcast.127, ...), kind=kLoop, calls=%fused_computation.502 | loop fusion | flops 6553600 | bytes 3145764 | tf_op jit(solution)/shard_map/add | solution.py:31
  515.6 6.1 multiply_add_fusion
  521.7 7.9 %fusion.186 = f32[256,8,128]{2,1,0:T(8,128)S(1)} fusion(f32[256,8,128]{2,1,0:T(8,128)S(1)} %multiply_add_fusion, f32[1,32,8,8,128]{4,3,2,1,0:T(8,128)S(1)} %copy-done.3, f32[]{:T(128)} %bitcast.148, f32[]{:T(128)} %bitcast.147, f32[]{:T(128)} %bitcast.146, f32[]{:T(128)} %bitcast.145, f32[]{:T(128)} %bitcast.144, f32[]{:T(128)} %bitcast.143, f32[]{:T(128)} %bitcast.142, ...), kind=kLoop, calls=%fused_computation.341 | loop fusion | flops 4718592 | bytes 3145764 | tf_op jit(solution)/shard_map/div | solution.py:86
  529.6 7.9 %fusion.202 = f32[256,8,128]{2,1,0:T(8,128)S(1)} fusion(f32[256,8,128]{2,1,0:T(8,128)S(1)} %fusion.186, f32[]{:T(128)} %bitcast.148, f32[]{:T(128)} %bitcast.147, f32[]{:T(128)} %bitcast.146, f32[]{:T(128)} %bitcast.145, f32[]{:T(128)} %bitcast.144, f32[]{:T(128)} %bitcast.143, f32[]{:T(128)} %bitcast.142, f32[]{:T(128)} %bitcast.124, f32[]{:T(128)} %bitcast.123), kind=kLoop, calls=%fused_computation.357 | loop fusion | flops 4456448 | bytes 2097188 | tf_op jit(solution)/shard_map/add | solution.py:31
  537.4 6.1 add_bitcast_fusion
  546.2 9.1 %collective-permute-start.7 = (f32[3,256,4,128]{3,2,1,0:T(4,128)S(1)}, f32[3,256,4,128]{3,2,1,0:T(4,128)S(1)}, u32[]{:S(2)}, u32[]{:S(2)}) collective-permute-start(f32[3,256,4,128]{3,2,1,0:T(4,128)S(1)} %get-tuple-element.13), channel_id=1, source_target_pairs={{1,0},{2,1},{3,2},{4,3},{5,4},{6,5},{7,6},{8,7},{9,8},{10,9},{11,1... | collective-permute-start | bytes 4718600 | tf_op jit(solution)/shard_map/ppermute | solution.py:17
  555.3 31.0 %collective-permute-done.6 = f32[3,256,4,128]{3,2,1,0:T(4,128)S(1)} collective-permute-done((f32[3,256,4,128]{3,2,1,0:T(4,128)S(1)}, f32[3,256,4,128]{3,2,1,0:T(4,128)S(1)}, u32[]{:S(2)}, u32[]{:S(2)}) %collective-permute-start.6) | collective-permute-done | bytes 1572896 | tf_op jit(solution)/shard_map/ppermute | solution.py:16
  590.4 28.9 %fusion.212 = f32[256,8,128]{2,1,0:T(8,128)} fusion(f32[256,16,128]{2,1,0:T(8,128)S(1)} %get-tuple-element.7, f32[256,16,128]{2,1,0:T(8,128)} %get-tuple-element.8, f32[256,16,128]{2,1,0:T(8,128)S(1)} %get-tuple-element.6, f32[]{:T(128)} %bitcast.130, f32[]{:T(128)} %bitcast.102, f32[]{:T(128)} %bitcast.75, f32[]{:T(128)} %bitcast.134, f32[]{:T(128)} %bitcast.133, ...), kind=kLoop, calls=%fused_computation.368 | loop fusion | flops 13893632 | bytes 29360236 | tf_op jit(solution)/shard_map/add | solution.py:92
  619.3 45.6 %all-reduce.32.cloned.1.call-done = f32[256,8,128]{2,1,0:T(8,128)} async-done(((f32[256,8,128]{2,1,0:T(8,128)}), f32[256,8,128]{2,1,0:T(8,128)}) %all-reduce.32.cloned.1.call-update) | async-done | bytes 1048592 | tf_op jit(solution)/shard_map/psum | solution.py:59
  (147 shorter events, 77.4 us)
Async XLA Ops:
  6.5 135.6 %all-reduce.28.cloned.1.call-start = ((), (), s32[]{:S(2)}) async-start(), calls=%async_computation.1 | async-start | bytes 2097152 | tf_op jit(solution)/shard_map/psum | solution.py:80
  41.1 6.4 copy-start.10
  41.1 6.4 copy-start.11
  47.5 7.3 %copy-start.12 = (bf16[256,8,128]{2,1,0:T(8,128)(2,1)S(1)}, bf16[256,8,128]{2,1,0:T(8,128)(2,1)}, u32[]{:S(2)}) copy-start(bf16[256,8,128]{2,1,0:T(8,128)(2,1)} %gather_fusion.22) | copy-start | bytes 1572868
  47.5 7.3 %copy-start.13 = (bf16[256,8,128]{2,1,0:T(8,128)(2,1)S(1)}, bf16[256,8,128]{2,1,0:T(8,128)(2,1)}, u32[]{:S(2)}) copy-start(bf16[256,8,128]{2,1,0:T(8,128)(2,1)} %gather_fusion.21) | copy-start | bytes 1572868
  47.5 7.3 %copy-start.14 = (bf16[256,8,128]{2,1,0:T(8,128)(2,1)S(1)}, bf16[256,8,128]{2,1,0:T(8,128)(2,1)}, u32[]{:S(2)}) copy-start(bf16[256,8,128]{2,1,0:T(8,128)(2,1)} %gather_fusion.20) | copy-start | bytes 1572868
  47.6 7.3 %copy-start.15 = (bf16[256,8,128]{2,1,0:T(8,128)(2,1)S(1)}, bf16[256,8,128]{2,1,0:T(8,128)(2,1)}, u32[]{:S(2)}) copy-start(bf16[256,8,128]{2,1,0:T(8,128)(2,1)} %gather_fusion.19) | copy-start | bytes 1572868
  47.6 7.3 %copy-start.16 = (bf16[256,8,128]{2,1,0:T(8,128)(2,1)S(1)}, bf16[256,8,128]{2,1,0:T(8,128)(2,1)}, u32[]{:S(2)}) copy-start(bf16[256,8,128]{2,1,0:T(8,128)(2,1)} %gather_fusion.18) | copy-start | bytes 1572868
  47.6 7.3 %copy-start.18 = (bf16[256,8,128]{2,1,0:T(8,128)(2,1)S(1)}, bf16[256,8,128]{2,1,0:T(8,128)(2,1)}, u32[]{:S(2)}) copy-start(bf16[256,8,128]{2,1,0:T(8,128)(2,1)} %gather_fusion.17) | copy-start | bytes 1572868
  47.6 7.3 %copy-start.20 = (bf16[256,8,128]{2,1,0:T(8,128)(2,1)S(1)}, bf16[256,8,128]{2,1,0:T(8,128)(2,1)}, u32[]{:S(2)}) copy-start(bf16[256,8,128]{2,1,0:T(8,128)(2,1)} %gather_fusion.16) | copy-start | bytes 1572868
  54.9 5.3 copy-start.17
  54.9 5.3 copy-start.19
  54.9 5.3 copy-start.21
  54.9 5.3 copy-start.22
  55.0 5.3 copy-start.23
  55.0 5.3 copy-start.24
  55.0 5.3 copy-start.25
  55.0 5.3 copy-start.26
  98.4 1.0 copy-start.7
  98.6 165.0 %copy-start.2 = (f32[1,32,8,8,128]{4,3,2,1,0:T(8,128)}, f32[1,32,8,8,128]{4,3,2,1,0:T(8,128)S(1)}, u32[]{:S(2)}) copy-start(f32[1,32,8,8,128]{4,3,2,1,0:T(8,128)S(1)} %copy.18) | copy-start | bytes 3145732
  99.4 1.0 copy-start.4
  100.4 1.3 copy-start.27
  101.6 305.2 %all-reduce.30.cloned.1.call-start = ((), (), s32[]{:S(2)}) async-start(), calls=%async_computation.2 | async-start | bytes 2097152 | tf_op jit(solution)/shard_map/psum | solution.py:59
  142.2 30.4 %copy-start.1 = (f32[256,8,128]{2,1,0:T(8,128)S(1)}, f32[256,8,128]{2,1,0:T(8,128)}, u32[]{:S(2)}) copy-start(f32[256,8,128]{2,1,0:T(8,128)} %all-reduce.28.cloned.1.call-done) | copy-start | bytes 3145732
  144.7 18.3 %collective-permute-start.1 = (f32[256,4,128]{2,1,0:T(4,128)}, f32[256,4,128]{2,1,0:T(4,128)}, u32[]{:S(2)}, u32[]{:S(2)}) collective-permute-start(f32[256,4,128]{2,1,0:T(4,128)} %get-tuple-element.24), channel_id=1, source_target_pairs={{1,0},{2,1},{3,2},{4,3},{5,4},{6,5},{7,6},{8,7},{9,8},{10,9},{11,1... | collective-permute-start | bytes 1572872 | tf_op jit(solution)/shard_map/ppermute | solution.py:17
  151.7 20.8 %collective-permute-start = (f32[256,4,128]{2,1,0:T(4,128)}, f32[256,4,128]{2,1,0:T(4,128)}, u32[]{:S(2)}, u32[]{:S(2)}) collective-permute-start(f32[256,4,128]{2,1,0:T(4,128)} %get-tuple-element.25), channel_id=1, source_target_pairs={{0,1},{1,2},{2,3},{3,4},{4,5},{5,6},{6,7},{7,8},{8,9},{9,10},{10,1... | collective-permute-start | bytes 1572872 | tf_op jit(solution)/shard_map/ppermute | solution.py:16
  182.2 6.3 copy-start.8
  219.6 6.2 copy-start.5
  286.2 42.0 %collective-permute-start.2 = (f32[3,256,4,128]{3,2,1,0:T(4,128)S(1)}, f32[3,256,4,128]{3,2,1,0:T(4,128)S(1)}, u32[]{:S(2)}, u32[]{:S(2)}) collective-permute-start(f32[3,256,4,128]{3,2,1,0:T(4,128)S(1)} %get-tuple-element.14), channel_id=1, source_target_pairs={{0,1},{1,2},{2,3},{3,4},{4,5},{5,6},{6,7},{7,8},{8,9},{9,10},{10,1... | collective-permute-start | bytes 4718600 | tf_op jit(solution)/shard_map/ppermute | solution.py:16
  288.1 41.0 %collective-permute-start.3 = (f32[3,256,4,128]{3,2,1,0:T(4,128)S(1)}, f32[3,256,4,128]{3,2,1,0:T(4,128)S(1)}, u32[]{:S(2)}, u32[]{:S(2)}) collective-permute-start(f32[3,256,4,128]{3,2,1,0:T(4,128)S(1)} %get-tuple-element.15), channel_id=1, source_target_pairs={{1,0},{2,1},{3,2},{4,3},{5,4},{6,5},{7,6},{8,7},{9,8},{10,9},{11,1... | collective-permute-start | bytes 4718600 | tf_op jit(solution)/shard_map/ppermute | solution.py:17
  361.2 303.7 %all-reduce.32.cloned.1.call-start = ((), (), s32[]{:S(2)}) async-start(), calls=%async_computation.3 | async-start | bytes 2097152 | tf_op jit(solution)/shard_map/psum | solution.py:59
  408.6 98.9 %copy-start = (f32[256,8,128]{2,1,0:T(8,128)}, f32[256,8,128]{2,1,0:T(8,128)S(1)}, u32[]{:S(2)}) copy-start(f32[256,8,128]{2,1,0:T(8,128)S(1)} %exponential_multiply_fusion.1) | copy-start | bytes 3145732
  408.7 18.0 %collective-permute-start.5 = (f32[256,4,128]{2,1,0:T(4,128)S(1)}, f32[256,4,128]{2,1,0:T(4,128)S(1)}, u32[]{:S(2)}, u32[]{:S(2)}) collective-permute-start(f32[256,4,128]{2,1,0:T(4,128)S(1)} %get-tuple-element.22), channel_id=1, source_target_pairs={{1,0},{2,1},{3,2},{4,3},{5,4},{6,5},{7,6},{8,7},{9,8},{10,9},{11,1... | collective-permute-start | bytes 1572872 | tf_op jit(solution)/shard_map/ppermute | solution.py:17
  415.8 34.7 %copy-start.9 = (f32[1,32,8,8,128]{4,3,2,1,0:T(8,128)S(1)}, f32[1,32,8,8,128]{4,3,2,1,0:T(8,128)}, u32[]{:S(2)}) copy-start(f32[1,32,8,8,128]{4,3,2,1,0:T(8,128)} %copy-done.7) | copy-start | bytes 3145732
  415.8 20.6 %collective-permute-start.4 = (f32[256,4,128]{2,1,0:T(4,128)S(1)}, f32[256,4,128]{2,1,0:T(4,128)S(1)}, u32[]{:S(2)}, u32[]{:S(2)}) collective-permute-start(f32[256,4,128]{2,1,0:T(4,128)S(1)} %get-tuple-element.23), channel_id=1, source_target_pairs={{0,1},{1,2},{2,3},{3,4},{4,5},{5,6},{6,7},{7,8},{8,9},{9,10},{10,1... | collective-permute-start | bytes 1572872 | tf_op jit(solution)/shard_map/ppermute | solution.py:16
  471.9 13.9 %copy-start.6 = (f32[1,32,8,8,128]{4,3,2,1,0:T(8,128)S(1)}, f32[1,32,8,8,128]{4,3,2,1,0:T(8,128)}, u32[]{:S(2)}) copy-start(f32[1,32,8,8,128]{4,3,2,1,0:T(8,128)} %copy-done.4) | copy-start | bytes 3145732
  507.5 14.2 %copy-start.3 = (f32[1,32,8,8,128]{4,3,2,1,0:T(8,128)S(1)}, f32[1,32,8,8,128]{4,3,2,1,0:T(8,128)}, u32[]{:S(2)}) copy-start(f32[1,32,8,8,128]{4,3,2,1,0:T(8,128)} %copy-done.2) | copy-start | bytes 3145732
  544.3 42.0 %collective-permute-start.6 = (f32[3,256,4,128]{3,2,1,0:T(4,128)S(1)}, f32[3,256,4,128]{3,2,1,0:T(4,128)S(1)}, u32[]{:S(2)}, u32[]{:S(2)}) collective-permute-start(f32[3,256,4,128]{3,2,1,0:T(4,128)S(1)} %get-tuple-element.12), channel_id=1, source_target_pairs={{0,1},{1,2},{2,3},{3,4},{4,5},{5,6},{6,7},{7,8},{8,9},{9,10},{10,1... | collective-permute-start | bytes 4718600 | tf_op jit(solution)/shard_map/ppermute | solution.py:16
  546.2 41.0 %collective-permute-start.7 = (f32[3,256,4,128]{3,2,1,0:T(4,128)S(1)}, f32[3,256,4,128]{3,2,1,0:T(4,128)S(1)}, u32[]{:S(2)}, u32[]{:S(2)}) collective-permute-start(f32[3,256,4,128]{3,2,1,0:T(4,128)S(1)} %get-tuple-element.13), channel_id=1, source_target_pairs={{1,0},{2,1},{3,2},{4,3},{5,4},{6,5},{7,6},{8,7},{9,8},{10,9},{11,1... | collective-permute-start | bytes 4718600 | tf_op jit(solution)/shard_map/ppermute | solution.py:17
Sparse Core Ops, SparseCore 0:
  101.7 40.4 all-reduce.27
  361.4 45.3 all-reduce.29
  619.5 45.4 all-reduce.31
where the time goes:
time: 687 us; the launch traced here: 675 us
  other arithmetic  308 us (45%)
  waiting for transfers between devices  227 us (33%)
  local copies, waits for them, and re-layouts  51 us (7%)
  starting transfers between devices  40.1 us (6%)
  blocking collectives  31.9 us (5%)
  between operations  16.3 us (2%)
    add x18, other arithmetic, correlate(): result + taps[offset] * lax.slice_in_dim(extended, offset, offset + lengt...  136 us
    psum x2, waiting for transfers between devices, update_estimate(): summed = lax.psum(logs, 'view')  91.1 us
    ppermute x4, waiting for transfers between devices, extended_2(): before = lax.ppermute(last, axis, up)  81.2 us
    add x2, other arithmetic, per_device(): logs = logs + jnp.log(back)  57.9 us
    div x6, other arithmetic, per_device(): ratio = bricks[index].astype(jnp.float32) / blurred  46.5 us
    psum x1, waiting for transfers between devices, per_device(): joined_volume = lax.psum(local_sum, 'view') / total_views  40.4 us
    another operation x8, other arithmetic, per_device(): ratio_wide = extended_2(jnp.stack(partials), (('vol', 2),), rim_width)  37.3 us
    gather x24, local copies, waits for them, and re-layouts, resample_view(): gathered = jnp.take(planes, first_rows + offset, axis=1).astype(jnp.float32)  35.9 us
  transfers between devices with their start and end apart: 11, of which 11 were waited for; matrix products, arithmetic and copies ran while one was open for 1% of the time, Pallas kernels for 0%

commit v1 on v0

v1 whole, which is shorter than its diff:
```python
import functools

import jax
import jax.numpy as jnp
from jax import lax
from jax.experimental import pallas as pl
from jax.experimental.pallas import tpu as pltpu
from jax.sharding import PartitionSpec as P

ITERS = 2
CZ = 8


def extended_2(shard, sides, width):
    for axis, dim in sides:
        devices, length = (lax.axis_size(axis), shard.shape[dim])
        up = [(i, (i + 1) % devices) for i in range(devices - 1)]
        down = [(j, i) for i, j in up]
        last = lax.slice_in_dim(shard, length - width, length, axis=dim)
        first = lax.slice_in_dim(shard, 0, width, axis=dim)
        before = lax.ppermute(last, axis, up)
        after = lax.ppermute(first, axis, down)
        shard = jnp.concatenate([before, shard, after], axis=dim)
    return shard


def resample_views(raw_views, weight_norm, offsets):
    rows = raw_views.shape[2]
    band = weight_norm.shape[2]
    target = offsets[:, :, None] + jnp.arange(band, dtype=jnp.int32)[None, None, :]
    onehot = target[..., None] == jnp.arange(rows, dtype=jnp.int32)[None, None, None, :]
    matrix = jnp.sum(jnp.where(onehot, weight_norm[..., None], 0.0), axis=2)
    result = jnp.einsum(
        "vxr,vzry->vzxy",
        matrix,
        raw_views.astype(jnp.float32),
        precision=lax.Precision.HIGHEST,
        preferred_element_type=jnp.float32,
    )
    return result.astype(jnp.bfloat16)


def _lane_weights(taps, ny, reverse):
    lane = lax.broadcasted_iota(jnp.int32, (8, ny), 1)
    out = []
    for t in range(9):
        d = t - 4
        tap = taps[8 - t] if reverse else taps[t]
        valid = (lane + d >= 0) & (lane + d < ny)
        out.append(((-d) % ny, jnp.where(valid, tap, 0.0)))
    return out


def _lane_correlate(f, weights):
    acc = None
    for shift, w in weights:
        rolled = f if shift == 0 else pltpu.roll(f, shift, 2)
        term = rolled * w[None]
        acc = term if acc is None else acc + term
    return acc


def _forward_kernel(taps_ref, est_ref, brick_ref, out_ref, a_ref, c_ref):
    v = pl.program_id(0)
    nz, _, ny = out_ref.shape[1:]
    tx = [taps_ref[v * 27 + 9 + t] for t in range(9)]
    tz = [taps_ref[v * 27 + t] for t in range(9)]
    ty = [taps_ref[v * 27 + 18 + t] for t in range(9)]
    zeros = jnp.zeros((4,) + a_ref.shape[1:], jnp.float32)
    a_ref[0:4] = zeros
    a_ref[nz + 4 : nz + 8] = zeros
    c_ref[0:4] = zeros
    c_ref[nz + 4 : nz + 8] = zeros

    def along_x(c, carry):
        z0 = pl.multiple_of(c * CZ, CZ)
        acc = tx[0] * est_ref[pl.ds(z0, CZ), pl.ds(0, 8), :]
        for t in range(1, 9):
            acc = acc + tx[t] * est_ref[pl.ds(z0, CZ), pl.ds(t, 8), :]
        a_ref[pl.ds(z0 + 4, CZ)] = acc
        return carry

    lax.fori_loop(0, nz // CZ, along_x, 0)
    wy = _lane_weights(ty, ny, False)
    wy_rev = _lane_weights(ty, ny, True)

    def middle(c, carry):
        z0 = pl.multiple_of(c * CZ, CZ)
        acc = tz[0] * a_ref[pl.ds(z0, CZ)]
        for t in range(1, 9):
            acc = acc + tz[t] * a_ref[pl.ds(z0 + t, CZ)]
        blurred = _lane_correlate(acc, wy)
        ratio = brick_ref[0, pl.ds(z0, CZ)].astype(jnp.float32) / blurred
        c_ref[pl.ds(z0 + 4, CZ)] = _lane_correlate(ratio, wy_rev)
        return carry

    lax.fori_loop(0, nz // CZ, middle, 0)

    def along_z_back(c, carry):
        z0 = pl.multiple_of(c * CZ, CZ)
        acc = tz[8] * c_ref[pl.ds(z0, CZ)]
        for t in range(1, 9):
            acc = acc + tz[8 - t] * c_ref[pl.ds(z0 + t, CZ)]
        out_ref[0, pl.ds(z0, CZ)] = acc
        return carry

    lax.fori_loop(0, nz // CZ, along_z_back, 0)


def forward_partials(taps_flat, extended, bricks):
    count, nz, width, ny = bricks.shape
    return pl.pallas_call(
        _forward_kernel,
        grid=(count,),
        in_specs=[
            pl.BlockSpec(memory_space=pltpu.SMEM),
            pl.BlockSpec((nz, width + 8, ny), lambda v: (0, 0, 0)),
            pl.BlockSpec((1, nz, width, ny), lambda v: (v, 0, 0, 0)),
        ],
        out_specs=pl.BlockSpec((1, nz, width, ny), lambda v: (v, 0, 0, 0)),
        out_shape=jax.ShapeDtypeStruct((count, nz, width, ny), jnp.float32),
        scratch_shapes=[
            pltpu.VMEM((nz + 8, width, ny), jnp.float32),
            pltpu.VMEM((nz + 8, width, ny), jnp.float32),
        ],
    )(taps_flat, extended, bricks)


def _back_kernel(taps_ref, wide_ref, out_ref):
    count = wide_ref.shape[0]
    nz = out_ref.shape[0]
    tx = [[taps_ref[v * 27 + 9 + t] for t in range(9)] for v in range(count)]

    def body(c, carry):
        z0 = pl.multiple_of(c * CZ, CZ)
        total = None
        for v in range(count):
            acc = tx[v][8] * wide_ref[v, pl.ds(z0, CZ), pl.ds(0, 8), :]
            for t in range(1, 9):
                acc = acc + tx[v][8 - t] * wide_ref[v, pl.ds(z0, CZ), pl.ds(t, 8), :]
            term = jnp.log(acc)
            total = term if total is None else total + term
        out_ref[pl.ds(z0, CZ)] = total
        return carry

    lax.fori_loop(0, nz // CZ, body, 0)


def back_logs(taps_flat, wide):
    count, nz, width8, ny = wide.shape
    return pl.pallas_call(
        _back_kernel,
        in_specs=[
            pl.BlockSpec(memory_space=pltpu.SMEM),
            pl.BlockSpec(memory_space=pltpu.VMEM),
        ],
        out_specs=pl.BlockSpec(memory_space=pltpu.VMEM),
        out_shape=jax.ShapeDtypeStruct((nz, width8 - 8, ny), jnp.float32),
    )(taps_flat, wide)


def per_device(raw_views, weights, offsets, psf_taps):
    count = raw_views.shape[0]
    total_views = count * lax.axis_size("view")
    rim_width = (psf_taps.shape[2] - 1) // 2
    weight_norm = weights / jnp.sum(weights, axis=-1, keepdims=True)
    taps_norm = psf_taps / jnp.sum(psf_taps, axis=-1, keepdims=True)
    taps_flat = taps_norm.reshape(-1)
    local_views = resample_views(raw_views, weight_norm, offsets)
    bricks = lax.all_to_all(local_views, "vol", split_axis=2, concat_axis=1, tiled=True)
    local_sum = bricks[0].astype(jnp.float32)
    for index in range(1, count):
        local_sum = local_sum + bricks[index].astype(jnp.float32)
    joined_volume = lax.psum(local_sum, "view") / total_views
    for turn in range(ITERS):
        extended = extended_2(joined_volume, (("vol", 1),), rim_width)
        partials = forward_partials(taps_flat, extended, bricks)
        ratio_wide = extended_2(partials, (("vol", 2),), rim_width)
        logs = back_logs(taps_flat, ratio_wide)
        summed = lax.psum(logs, "view")
        joined_volume = joined_volume * jnp.exp(summed / total_views)
    return joined_volume


def solution(mesh):
    placed = (
        P("view", "vol", None, None),
        P("view", None, None),
        P("view", None),
        P("view", None, None),
    )
    return jax.shard_map(
        per_device, mesh=mesh, in_specs=placed, out_specs=P(None, "vol", None), check_vma=False
    )
```

time: 687 us -> 430 us (0.63); the launches traced: 675 us -> 429 us
  other arithmetic: 308 us -> 26 us
  Pallas kernels: 0 us -> 84.8 us
  local copies, waits for them, and re-layouts: 51 us -> 10.8 us
  waiting for transfers between devices: 227 us -> 215 us
    add x20 -> x1, other arithmetic: 194 us -> 0.85 us  [resample_views(): offsets[:, :, None] + jnp.arange(band, dtype=jnp.int32)[None, None, :]]
    pallas_call x0 -> x4, Pallas kernels: none -> 84.8 us  [the longest x2 72 us: forward_partials(): pl.pallas_call(_forward_kernel, grid=(count,), in_specs=[pl.BlockSpec(mem...]
    another operation x12 -> x0, other arithmetic: 55 us -> none  [the longest x8 37.3 us: per_device(): ratio_wide = extended_2(jnp.stack(partials), (('vol', 2),), rim_width)]
    div x6 -> x0, other arithmetic: 46.5 us -> none  [per_device(): ratio = bricks[index].astype(jnp.float32) / blurred]
    gather x24 -> x0, local copies, waits for them, and re-layouts: 35.9 us -> none  [resample_view(): gathered = jnp.take(planes, first_rows + offset, axis=1).astype(jnp.float32)]
    ppermute x4, waiting for transfers between devices: 14.7 us -> 3.63 us  [extended_2(): after = lax.ppermute(first, axis, down)]
    concatenate x2 -> x4, other arithmetic: 2.84 us -> 12.2 us  [extended_2(): shard = jnp.concatenate([before, shard, after], axis=dim)]
    slice x2 -> x4, local copies, waits for them, and re-layouts: 0.95 us -> 8.56 us  [extended_2(): last = lax.slice_in_dim(shard, length - width, length, axis=dim)]
  transfers between devices with their start and end apart: 11 -> 11, of which waited for: 11 -> 11; matrix products, arithmetic and copies ran while one was open for 1% -> 0% of each run, Pallas kernels for 0% -> 0%
where the time goes in v1:
time: 430 us; the launch traced here: 429 us
  waiting for transfers between devices  215 us (50%)
  Pallas kernels  84.8 us (20%)
  starting transfers between devices  45.5 us (11%)
  blocking collectives  31.5 us (7%)
  other arithmetic  26 us (6%)
  between operations  13.3 us (3%)
  local copies, waits for them, and re-layouts  10.8 us (3%)
    psum x2, waiting for transfers between devices, per_device(): summed = lax.psum(logs, 'view')  89.5 us
    ppermute x4, waiting for transfers between devices, extended_2(): before = lax.ppermute(last, axis, up)  81.7 us
    pallas_call x2, Pallas kernels, forward_partials(): pl.pallas_call(_forward_kernel, grid=(count,), in_specs=[pl.BlockSpec(mem...  72 us
    psum x1, waiting for transfers between devices, per_device(): joined_volume = lax.psum(local_sum, 'view') / total_views  40.4 us
    ppermute x4, starting transfers between devices, extended_2(): after = lax.ppermute(first, axis, down)  35.3 us
    all_to_all x1, blocking collectives, per_device(): lax.all_to_all(local_views, 'vol', split_axis=2, concat_axis=1, tiled=True)  31.5 us
    pallas_call x2, Pallas kernels, back_logs(): pl.pallas_call(_back_kernel, in_specs=[pl.BlockSpec(memory_space=pltpu.SM...  12.8 us
    concatenate x4, other arithmetic, extended_2(): shard = jnp.concatenate([before, shard, after], axis=dim)  12.2 us
  transfers between devices with their start and end apart: 11, of which 11 were waited for; matrix products, arithmetic and copies ran while one was open for 0% of the time, Pallas kernels for 0%

profile of v1, /device:TPU:5, one launch (start us, length us, event | category | flops | bytes accessed | tf_op | source)
XLA Modules:
  0.0 428.6 jit_solution(9046060091199766734)
XLA Ops:
  6.5 0.9 reduce_sum.27
  7.4 0.7 broadcast_divide_fusion
  8.2 0.2 copy.10
  8.3 0.9 iota_add_fusion
  9.2 4.4 %select_reduce_fusion = f32[3,256,256]{2,1,0:T(8,128)S(1)} fusion(f32[3,256,8]{2,1,0:T(8,128)S(1)} %copy.10, s32[3,256,8]{2,1,0:T(8,128)S(1)} %iota_add_fusion), kind=kLoop, calls=%fused_computation.3 | loop fusion | flops 4521984 | bytes 835584 | tf_op jit(solution)/shard_map/reduce_sum | solution.py:32
  13.6 1.4 fusion.1
  15.1 1.0 copy.11
  16.1 31.5 %all_to_all.18 = bf16[3,8,256,128]{3,1,0,2:T(8,128)(2,1)S(1)} all-to-all(bf16[3,8,256,128]{3,1,0,2:T(8,128)(2,1)S(1)} %copy.11), channel_id=1, replica_groups=mesh['view'=4,'vol'=32] {'vol'}, dimensions={2} | all-to-all | bytes 3145728 | tf_op jit(solution)/shard_map/all_to_all | solution.py:170
  47.6 0.5 copy.16
  48.1 1.4 convert_add_fusion
  49.6 0.0 all-reduce.6.cloned.1.call-start
  49.6 40.4 %all-reduce.4.cloned.1.call-done = f32[256,8,128]{2,1,0:T(8,128)} async-done(((f32[256,8,128]{2,1,0:T(8,128)}), f32[256,8,128]{2,1,0:T(8,128)}) %all-reduce.4.cloned.1.call-update) | async-done | bytes 1048592 | tf_op jit(solution)/shard_map/psum | solution.py:174
  90.0 1.3 broadcast_multiply_fusion
  91.3 1.4 fusion.8
  92.7 3.1 collective-permute-start
  95.8 7.9 %collective-permute-start.1 = (f32[256,4,128]{2,1,0:T(4,128)}, f32[256,4,128]{2,1,0:T(4,128)S(1)}, u32[]{:S(2)}, u32[]{:S(2)}) collective-permute-start(f32[256,4,128]{2,1,0:T(4,128)} %get-tuple-element.14), channel_id=1, source_target_pairs={{1,0},{2,1},{3,2},{4,3},{5,4},{6,5},{7,6},{8,7},{9,8},{10,9},{11,1... | collective-permute-start | bytes 1572872 | tf_op jit(solution)/shard_map/ppermute | solution.py:22
  103.7 0.1 fusion.2
  103.8 0.6 reshape.21.taps_ref
  104.3 9.3 %collective-permute-done = f32[256,4,128]{2,1,0:T(4,128)S(1)} collective-permute-done((f32[256,4,128]{2,1,0:T(4,128)}, f32[256,4,128]{2,1,0:T(4,128)S(1)}, u32[]{:S(2)}, u32[]{:S(2)}) %collective-permute-start) | collective-permute-done | bytes 524320 | tf_op jit(solution)/shard_map/ppermute | solution.py:21
  113.7 1.0 collective-permute-done.1
  114.6 2.9 pad_maximum_fusion.2.est_ref
  117.6 36.0 %shard_map.46 = f32[3,256,8,128]{3,2,1,0:T(8,128)} custom-call(f32[81]{0:T(128)} %reshape.21.taps_ref, f32[256,16,128]{2,1,0:T(8,128)} %pad_maximum_fusion.2.est_ref, bf16[3,256,8,128]{3,2,1,0:T(8,128)(2,1)} %bitcast.16), custom_call_target="tpu_custom_call" | custom-call | tf_op jit(solution)/shard_map/pallas_call | solution.py:112
  153.6 3.5 fusion.5
  157.1 1.9 collective-permute-start.2
  159.1 9.7 %collective-permute-start.3 = (f32[3,256,4,128]{3,2,1,0:T(4,128)S(1)}, f32[3,256,4,128]{3,2,1,0:T(4,128)S(1)}, u32[]{:S(2)}, u32[]{:S(2)}) collective-permute-start(f32[3,256,4,128]{3,2,1,0:T(4,128)S(1)} %get-tuple-element.8), channel_id=1, source_target_pairs={{1,0},{2,1},{3,2},{4,3},{5,4},{6,5},{7,6},{8,7},{9,8},{10,9},{11,1... | collective-permute-start | bytes 4718600 | tf_op jit(solution)/shard_map/ppermute | solution.py:22
  168.8 31.3 %collective-permute-done.2 = f32[3,256,4,128]{3,2,1,0:T(4,128)S(1)} collective-permute-done((f32[3,256,4,128]{3,2,1,0:T(4,128)S(1)}, f32[3,256,4,128]{3,2,1,0:T(4,128)S(1)}, u32[]{:S(2)}, u32[]{:S(2)}) %collective-permute-start.2) | collective-permute-done | bytes 1572896 | tf_op jit(solution)/shard_map/ppermute | solution.py:21
  200.1 0.9 collective-permute-done.3
  201.0 3.7 pad_maximum_fusion.wide_ref
  204.7 6.4 %shard_map.47 = f32[256,8,128]{2,1,0:T(8,128)} custom-call(f32[81]{0:T(128)} %reshape.21.taps_ref, f32[3,256,16,128]{3,2,1,0:T(8,128)} %pad_maximum_fusion.wide_ref), custom_call_target="tpu_custom_call" | custom-call | tf_op jit(solution)/shard_map/pallas_call | solution.py:151
  211.1 0.0 all-reduce.8.cloned.1.call-start
  211.2 44.8 %all-reduce.6.cloned.1.call-done = f32[256,8,128]{2,1,0:T(8,128)} async-done(((f32[256,8,128]{2,1,0:T(8,128)}), f32[256,8,128]{2,1,0:T(8,128)}) %all-reduce.6.cloned.1.call-update) | async-done | bytes 1048592 | tf_op jit(solution)/shard_map/psum | solution.py:180
  256.0 1.7 exponential_multiply_fusion.1
  257.7 0.2 fusion.7
  257.9 3.1 collective-permute-start.4
  261.0 7.9 %collective-permute-start.5 = (f32[256,4,128]{2,1,0:T(4,128)S(1)}, f32[256,4,128]{2,1,0:T(4,128)S(1)}, u32[]{:S(2)}, u32[]{:S(2)}) collective-permute-start(f32[256,4,128]{2,1,0:T(4,128)S(1)} %get-tuple-element.12), channel_id=1, source_target_pairs={{1,0},{2,1},{3,2},{4,3},{5,4},{6,5},{7,6},{8,7},{9,8},{10,9},{11,1... | collective-permute-start | bytes 1572872 | tf_op jit(solution)/shard_map/ppermute | solution.py:22
  268.9 9.8 %collective-permute-done.4 = f32[256,4,128]{2,1,0:T(4,128)S(1)} collective-permute-done((f32[256,4,128]{2,1,0:T(4,128)S(1)}, f32[256,4,128]{2,1,0:T(4,128)S(1)}, u32[]{:S(2)}, u32[]{:S(2)}) %collective-permute-start.4) | collective-permute-done | bytes 524320 | tf_op jit(solution)/shard_map/ppermute | solution.py:21
  278.7 0.9 collective-permute-done.5
  279.6 1.8 pad_maximum_fusion.3.est_ref
  281.3 36.0 %shard_map.48 = f32[3,256,8,128]{3,2,1,0:T(8,128)} custom-call(f32[81]{0:T(128)} %reshape.21.taps_ref, f32[256,16,128]{2,1,0:T(8,128)} %pad_maximum_fusion.3.est_ref, bf16[3,256,8,128]{3,2,1,0:T(8,128)(2,1)} %bitcast.17), custom_call_target="tpu_custom_call" | custom-call | tf_op jit(solution)/shard_map/pallas_call | solution.py:112
  317.4 3.5 fusion.4
  320.9 1.9 collective-permute-start.6
  322.8 9.8 %collective-permute-start.7 = (f32[3,256,4,128]{3,2,1,0:T(4,128)S(1)}, f32[3,256,4,128]{3,2,1,0:T(4,128)S(1)}, u32[]{:S(2)}, u32[]{:S(2)}) collective-permute-start(f32[3,256,4,128]{3,2,1,0:T(4,128)S(1)} %get-tuple-element.6), channel_id=1, source_target_pairs={{1,0},{2,1},{3,2},{4,3},{5,4},{6,5},{7,6},{8,7},{9,8},{10,9},{11,1... | collective-permute-start | bytes 4718600 | tf_op jit(solution)/shard_map/ppermute | solution.py:22
  332.7 31.3 %collective-permute-done.6 = f32[3,256,4,128]{3,2,1,0:T(4,128)S(1)} collective-permute-done((f32[3,256,4,128]{3,2,1,0:T(4,128)S(1)}, f32[3,256,4,128]{3,2,1,0:T(4,128)S(1)}, u32[]{:S(2)}, u32[]{:S(2)}) %collective-permute-start.6) | collective-permute-done | bytes 1572896 | tf_op jit(solution)/shard_map/ppermute | solution.py:21
  364.0 0.9 collective-permute-done.7
  364.9 3.7 pad_maximum_fusion.1.wide_ref
  368.6 6.4 %shard_map.49 = f32[256,8,128]{2,1,0:T(8,128)} custom-call(f32[81]{0:T(128)} %reshape.21.taps_ref, f32[3,256,16,128]{3,2,1,0:T(8,128)} %pad_maximum_fusion.1.wide_ref), custom_call_target="tpu_custom_call" | custom-call | tf_op jit(solution)/shard_map/pallas_call | solution.py:151
  375.0 44.7 %all-reduce.8.cloned.1.call-done = f32[256,8,128]{2,1,0:T(8,128)} async-done(((f32[256,8,128]{2,1,0:T(8,128)}), f32[256,8,128]{2,1,0:T(8,128)}) %all-reduce.8.cloned.1.call-update) | async-done | bytes 1048592 | tf_op jit(solution)/shard_map/psum | solution.py:180
  419.7 2.4 exponential_multiply_fusion
  (16 shorter events, 0.1 us)
Async XLA Ops:
  6.5 7.1 %copy-start = (bf16[3,8,256,128]{3,2,1,0:T(8,128)(2,1)S(1)}, bf16[3,8,256,128]{3,2,1,0:T(8,128)(2,1)}, u32[]{:S(2)}) copy-start(bf16[3,8,256,128]{3,2,1,0:T(8,128)(2,1)} %param.4) | copy-start | bytes 4718596
  6.5 83.4 %all-reduce.4.cloned.1.call-start = ((), (), s32[]{:S(2)}) async-start(), calls=%async_computation.1 | async-start | bytes 2097152 | tf_op jit(solution)/shard_map/psum | solution.py:174
  48.1 43.2 %copy-start.3 = (bf16[3,8,32,8,128]{4,3,1,2,0:T(8,128)(2,1)}, bf16[3,8,32,8,128]{4,3,1,2,0:T(8,128)(2,1)S(1)}, u32[]{:S(2)}) copy-start(bf16[3,8,32,8,128]{4,3,1,2,0:T(8,128)(2,1)S(1)} %copy.16) | copy-start | bytes 4718596
  49.5 54.1 %copy-start.5 = (f32[3,3,9]{2,1,0:T(4,128)S(1)}, f32[3,3,9]{2,1,0:T(4,128)}, u32[]{:S(2)}) copy-start(f32[3,3,9]{2,1,0:T(4,128)} %param.7) | copy-start | bytes 976
  49.6 206.4 %all-reduce.6.cloned.1.call-start = ((), (), s32[]{:S(2)}) async-start(), calls=%async_computation.2 | async-start | bytes 2097152 | tf_op jit(solution)/shard_map/psum | solution.py:180
  91.3 1.4 copy-start.4
  92.7 21.0 %collective-permute-start = (f32[256,4,128]{2,1,0:T(4,128)}, f32[256,4,128]{2,1,0:T(4,128)S(1)}, u32[]{:S(2)}, u32[]{:S(2)}) collective-permute-start(f32[256,4,128]{2,1,0:T(4,128)} %get-tuple-element.13), channel_id=1, source_target_pairs={{0,1},{1,2},{2,3},{3,4},{4,5},{5,6},{6,7},{7,8},{8,9},{9,10},{10,1... | collective-permute-start | bytes 1572872 | tf_op jit(solution)/shard_map/ppermute | solution.py:21
  95.8 18.9 %collective-permute-start.1 = (f32[256,4,128]{2,1,0:T(4,128)}, f32[256,4,128]{2,1,0:T(4,128)S(1)}, u32[]{:S(2)}, u32[]{:S(2)}) collective-permute-start(f32[256,4,128]{2,1,0:T(4,128)} %get-tuple-element.14), channel_id=1, source_target_pairs={{1,0},{2,1},{3,2},{4,3},{5,4},{6,5},{7,6},{8,7},{9,8},{10,9},{11,1... | collective-permute-start | bytes 1572872 | tf_op jit(solution)/shard_map/ppermute | solution.py:22
  153.6 47.4 %copy-start.2 = (f32[3,256,8,128]{3,2,1,0:T(8,128)S(1)}, f32[3,256,8,128]{3,2,1,0:T(8,128)}, u32[]{:S(2)}) copy-start(f32[3,256,8,128]{3,2,1,0:T(8,128)} %shard_map.46) | copy-start | bytes 9437188
  157.1 43.0 %collective-permute-start.2 = (f32[3,256,4,128]{3,2,1,0:T(4,128)S(1)}, f32[3,256,4,128]{3,2,1,0:T(4,128)S(1)}, u32[]{:S(2)}, u32[]{:S(2)}) collective-permute-start(f32[3,256,4,128]{3,2,1,0:T(4,128)S(1)} %get-tuple-element.7), channel_id=1, source_target_pairs={{0,1},{1,2},{2,3},{3,4},{4,5},{5,6},{6,7},{7,8},{8,9},{9,10},{10,1... | collective-permute-start | bytes 4718600 | tf_op jit(solution)/shard_map/ppermute | solution.py:21
  159.1 41.9 %collective-permute-start.3 = (f32[3,256,4,128]{3,2,1,0:T(4,128)S(1)}, f32[3,256,4,128]{3,2,1,0:T(4,128)S(1)}, u32[]{:S(2)}, u32[]{:S(2)}) collective-permute-start(f32[3,256,4,128]{3,2,1,0:T(4,128)S(1)} %get-tuple-element.8), channel_id=1, source_target_pairs={{1,0},{2,1},{3,2},{4,3},{5,4},{6,5},{7,6},{8,7},{9,8},{10,9},{11,1... | collective-permute-start | bytes 4718600 | tf_op jit(solution)/shard_map/ppermute | solution.py:22
  211.1 208.6 %all-reduce.8.cloned.1.call-start = ((), (), s32[]{:S(2)}) async-start(), calls=%async_computation.3 | async-start | bytes 2097152 | tf_op jit(solution)/shard_map/psum | solution.py:180
  257.9 20.8 %collective-permute-start.4 = (f32[256,4,128]{2,1,0:T(4,128)S(1)}, f32[256,4,128]{2,1,0:T(4,128)S(1)}, u32[]{:S(2)}, u32[]{:S(2)}) collective-permute-start(f32[256,4,128]{2,1,0:T(4,128)S(1)} %get-tuple-element.11), channel_id=1, source_target_pairs={{0,1},{1,2},{2,3},{3,4},{4,5},{5,6},{6,7},{7,8},{8,9},{9,10},{10,1... | collective-permute-start | bytes 1572872 | tf_op jit(solution)/shard_map/ppermute | solution.py:21
  261.0 18.6 %collective-permute-start.5 = (f32[256,4,128]{2,1,0:T(4,128)S(1)}, f32[256,4,128]{2,1,0:T(4,128)S(1)}, u32[]{:S(2)}, u32[]{:S(2)}) collective-permute-start(f32[256,4,128]{2,1,0:T(4,128)S(1)} %get-tuple-element.12), channel_id=1, source_target_pairs={{1,0},{2,1},{3,2},{4,3},{5,4},{6,5},{7,6},{8,7},{9,8},{10,9},{11,1... | collective-permute-start | bytes 1572872 | tf_op jit(solution)/shard_map/ppermute | solution.py:22
  317.4 47.5 %copy-start.1 = (f32[3,256,8,128]{3,2,1,0:T(8,128)S(1)}, f32[3,256,8,128]{3,2,1,0:T(8,128)}, u32[]{:S(2)}) copy-start(f32[3,256,8,128]{3,2,1,0:T(8,128)} %shard_map.48) | copy-start | bytes 9437188
  320.9 43.1 %collective-permute-start.6 = (f32[3,256,4,128]{3,2,1,0:T(4,128)S(1)}, f32[3,256,4,128]{3,2,1,0:T(4,128)S(1)}, u32[]{:S(2)}, u32[]{:S(2)}) collective-permute-start(f32[3,256,4,128]{3,2,1,0:T(4,128)S(1)} %get-tuple-element.5), channel_id=1, source_target_pairs={{0,1},{1,2},{2,3},{3,4},{4,5},{5,6},{6,7},{7,8},{8,9},{9,10},{10,1... | collective-permute-start | bytes 4718600 | tf_op jit(solution)/shard_map/ppermute | solution.py:21
  322.8 42.0 %collective-permute-start.7 = (f32[3,256,4,128]{3,2,1,0:T(4,128)S(1)}, f32[3,256,4,128]{3,2,1,0:T(4,128)S(1)}, u32[]{:S(2)}, u32[]{:S(2)}) collective-permute-start(f32[3,256,4,128]{3,2,1,0:T(4,128)S(1)} %get-tuple-element.6), channel_id=1, source_target_pairs={{1,0},{2,1},{3,2},{4,3},{5,4},{6,5},{7,6},{8,7},{9,8},{10,9},{11,1... | collective-permute-start | bytes 4718600 | tf_op jit(solution)/shard_map/ppermute | solution.py:22
Sparse Core Ops, SparseCore 0:
  49.7 40.2 all-reduce.3
  211.3 44.6 all-reduce.5
  375.1 44.5 all-reduce.7

commit v2 on v1

--- a/solution.py
+++ b/solution.py
@@ -60,9 +60,8 @@
     return acc
 
 
-def _forward_kernel(taps_ref, est_ref, brick_ref, out_ref, a_ref, c_ref):
-    v = pl.program_id(0)
-    nz, _, ny = out_ref.shape[1:]
+def _forward_kernel(v, taps_ref, est_ref, brick_ref, out_ref, a_ref, c_ref):
+    nz, _, ny = out_ref.shape
     tx = [taps_ref[v * 27 + 9 + t] for t in range(9)]
     tz = [taps_ref[v * 27 + t] for t in range(9)]
     ty = [taps_ref[v * 27 + 18 + t] for t in range(9)]
@@ -90,7 +89,7 @@
         for t in range(1, 9):
             acc = acc + tz[t] * a_ref[pl.ds(z0 + t, CZ)]
         blurred = _lane_correlate(acc, wy)
-        ratio = brick_ref[0, pl.ds(z0, CZ)].astype(jnp.float32) / blurred
+        ratio = brick_ref[pl.ds(z0, CZ)].astype(jnp.float32) / blurred
         c_ref[pl.ds(z0 + 4, CZ)] = _lane_correlate(ratio, wy_rev)
         return carry
 
@@ -101,33 +100,33 @@
         acc = tz[8] * c_ref[pl.ds(z0, CZ)]
         for t in range(1, 9):
             acc = acc + tz[8 - t] * c_ref[pl.ds(z0 + t, CZ)]
-        out_ref[0, pl.ds(z0, CZ)] = acc
+        out_ref[pl.ds(z0, CZ)] = acc
         return carry
 
     lax.fori_loop(0, nz // CZ, along_z_back, 0)
 
 
-def forward_partials(taps_flat, extended, bricks):
-    count, nz, width, ny = bricks.shape
+def forward_partial(taps_flat, v, extended, brick):
+    nz, width, ny = brick.shape
     return pl.pallas_call(
-        _forward_kernel,
-        grid=(count,),
+        functools.partial(_forward_kernel, v),
         in_specs=[
             pl.BlockSpec(memory_space=pltpu.SMEM),
-            pl.BlockSpec((nz, width + 8, ny), lambda v: (0, 0, 0)),
-            pl.BlockSpec((1, nz, width, ny), lambda v: (v, 0, 0, 0)),
+            pl.BlockSpec(memory_space=pltpu.VMEM),
+            pl.BlockSpec(memory_space=pltpu.VMEM),
         ],
-        out_specs=pl.BlockSpec((1, nz, width, ny), lambda v: (v, 0, 0, 0)),
-        out_shape=jax.ShapeDtypeStruct((count, nz, width, ny), jnp.float32),
+        out_specs=pl.BlockSpec(memory_space=pltpu.VMEM),
+        out_shape=jax.ShapeDtypeStruct((nz, width, ny), jnp.float32),
         scratch_shapes=[
             pltpu.VMEM((nz + 8, width, ny), jnp.float32),
             pltpu.VMEM((nz + 8, width, ny), jnp.float32),
         ],
-    )(taps_flat, extended, bricks)
-
-
-def _back_kernel(taps_ref, wide_ref, out_ref):
-    count = wide_ref.shape[0]
+    )(taps_flat, extended, brick)
+
+
+def _back_kernel(taps_ref, *refs):
+    wide_refs, out_ref = refs[:-1], refs[-1]
+    count = len(wide_refs)
     nz = out_ref.shape[0]
     tx = [[taps_ref[v * 27 + 9 + t] for t in range(9)] for v in range(count)]
 
@@ -135,9 +134,9 @@
         z0 = pl.multiple_of(c * CZ, CZ)
         total = None
         for v in range(count):
-            acc = tx[v][8] * wide_ref[v, pl.ds(z0, CZ), pl.ds(0, 8), :]
+            acc = tx[v][8] * wide_refs[v][pl.ds(z0, CZ), pl.ds(0, 8), :]
             for t in range(1, 9):
-                acc = acc + tx[v][8 - t] * wide_ref[v, pl.ds(z0, CZ), pl.ds(t, 8), :]
+                acc = acc + tx[v][8 - t] * wide_refs[v][pl.ds(z0, CZ), pl.ds(t, 8), :]
             term = jnp.log(acc)
             total = term if total is None else total + term
         out_ref[pl.ds(z0, CZ)] = total
@@ -146,17 +145,31 @@
     lax.fori_loop(0, nz // CZ, body, 0)
 
 
-def back_logs(taps_flat, wide):
-    count, nz, width8, ny = wide.shape
+def back_logs(taps_flat, wides):
+    nz, width8, ny = wides[0].shape
     return pl.pallas_call(
         _back_kernel,
-        in_specs=[
-            pl.BlockSpec(memory_space=pltpu.SMEM),
-            pl.BlockSpec(memory_space=pltpu.VMEM),
-        ],
+        in_specs=[pl.BlockSpec(memory_space=pltpu.SMEM)]
+        + [pl.BlockSpec(memory_space=pltpu.VMEM)] * len(wides),
         out_specs=pl.BlockSpec(memory_space=pltpu.VMEM),
         out_shape=jax.ShapeDtypeStruct((nz, width8 - 8, ny), jnp.float32),
-    )(taps_flat, wide)
+    )(taps_flat, *wides)
+
+
+def view_sum(part):
+    count = lax.axis_size("view")
+    core_swap = [(i, i ^ 1) for i in range(count)]
+    chip_swap = [(i, i ^ 2) for i in range(count)]
+    half = part.shape[0] // 2
+    core = lax.axis_index("view") % 2
+    own = lax.dynamic_slice_in_dim(part, core * half, half, axis=0)
+    give = lax.dynamic_slice_in_dim(part, (1 - core) * half, half, axis=0)
+    own = own + lax.ppermute(give, "view", core_swap)
+    own = own + lax.ppermute(own, "view", chip_swap)
+    other = lax.ppermute(own, "view", core_swap)
+    low = jnp.where(core == 0, own, other)
+    high = jnp.where(core == 0, other, own)
+    return jnp.concatenate([low, high], axis=0)
 
 
 def per_device(raw_views, weights, offsets, psf_taps):
@@ -171,13 +184,15 @@
     local_sum = bricks[0].astype(jnp.float32)
     for index in range(1, count):
         local_sum = local_sum + bricks[index].astype(jnp.float32)
-    joined_volume = lax.psum(local_sum, "view") / total_views
+    joined_volume = view_sum(local_sum) / total_views
     for turn in range(ITERS):
         extended = extended_2(joined_volume, (("vol", 1),), rim_width)
-        partials = forward_partials(taps_flat, extended, bricks)
-        ratio_wide = extended_2(partials, (("vol", 2),), rim_width)
-        logs = back_logs(taps_flat, ratio_wide)
-        summed = lax.psum(logs, "view")
+        wides = []
+        for index in range(count):
+            partial_value = forward_partial(taps_flat, index, extended, bricks[index])
+            wides.append(extended_2(partial_value, (("vol", 1),), rim_width))
+        logs = back_logs(taps_flat, wides)
+        summed = view_sum(logs)
         joined_volume = joined_volume * jnp.exp(summed / total_views)
     return joined_volume
 

time: 430 us -> 360 us (0.84)
  waiting for transfers between devices: 215 us -> 94.5 us
  starting transfers between devices: 45.5 us -> 118 us
  blocking collectives: 31.5 us -> 0 us
  between operations: 13.3 us -> 0.48 us
  Pallas kernels: 84.8 us -> 95 us
  local copies, waits for them, and re-layouts: 10.8 us -> 18.8 us
    psum x3 -> x0, waiting for transfers between devices: 130 us -> none  [the longest x2 89.5 us: per_device(): summed = lax.psum(logs, 'view')]
    ppermute x4 -> x8, waiting for transfers between devices: 81.7 us -> 25.1 us  [extended_2(): before = lax.ppermute(last, axis, up)]
    ppermute x0 -> x9, waiting for transfers between devices: none -> 46.1 us  [the longest x3 36.6 us: view_sum(): own = own + lax.ppermute(own, 'view', chip_swap)]
    ppermute x4 -> x8, starting transfers between devices: 35.3 us -> 74.8 us  [extended_2(): after = lax.ppermute(first, axis, down)]
    all_to_all x1 -> x0, blocking collectives: 31.5 us -> none  [per_device(): lax.all_to_all(local_views, 'vol', split_axis=2, concat_axis=1, tiled=True)]
    all_to_all x0 -> x1, waiting for transfers between devices: none -> 19.8 us  [per_device(): lax.all_to_all(local_views, 'vol', split_axis=2, concat_axis=1, tiled=True)]
    ppermute x0 -> x9, starting transfers between devices: none -> 17.1 us  [the longest x3 10.3 us: view_sum(): own = own + lax.ppermute(give, 'view', core_swap)]
    all_to_all x0 -> x1, starting transfers between devices: none -> 10.5 us  [per_device(): lax.all_to_all(local_views, 'vol', split_axis=2, concat_axis=1, tiled=True)]
  transfers between devices with their start and end apart: 11 -> 26, of which waited for: 11 -> 18; matrix products, arithmetic and copies ran while one was open for 0% -> 4% of each run, Pallas kernels for 0% -> 8%
where the time goes in v2:
time: 360 us; the launch traced here: 357 us
  starting transfers between devices  118 us (33%)
  Pallas kernels  95 us (26%)
  waiting for transfers between devices  94.5 us (26%)
  other arithmetic  28.8 us (8%)
  local copies, waits for them, and re-layouts  18.8 us (5%)
    pallas_call x6, Pallas kernels, forward_partial(): pl.pallas_call(functools.partial(_forward_kernel, v), in_specs=[pl.BlockS...  82.1 us
    ppermute x8, starting transfers between devices, extended_2(): after = lax.ppermute(first, axis, down)  74.8 us
    ppermute x3, waiting for transfers between devices, view_sum(): own = own + lax.ppermute(own, 'view', chip_swap)  36.6 us
    ppermute x8, waiting for transfers between devices, extended_2(): before = lax.ppermute(last, axis, up)  25.1 us
    all_to_all x1, waiting for transfers between devices, per_device(): lax.all_to_all(local_views, 'vol', split_axis=2, concat_axis=1, tiled=True)  19.8 us
    concatenate x8, other arithmetic, extended_2(): shard = jnp.concatenate([before, shard, after], axis=dim)  17.4 us
    ppermute x8, starting transfers between devices, extended_2(): before = lax.ppermute(last, axis, up)  15.9 us
    pallas_call x2, Pallas kernels, back_logs(): pl.pallas_call(_back_kernel, in_specs=[pl.BlockSpec(memory_space=pltpu.SM...  12.9 us
  transfers between devices with their start and end apart: 26, of which 18 were waited for; matrix products, arithmetic and copies ran while one was open for 4% of the time, Pallas kernels for 8%

profile of v2, /device:TPU:5, one launch (start us, length us, event | category | flops | bytes accessed | tf_op | source)
XLA Modules:
  0.0 357.3 jit_solution(14407971792488965046)
XLA Ops:
  2.7 4.4 %select_reduce_fusion = f32[3,256,256]{2,1,0:T(8,128)S(1)} fusion(f32[3,256,8]{2,1,0:T(8,128)S(1)} %copy.10, s32[3,256,8]{2,1,0:T(8,128)S(1)} %iota_add_fusion), kind=kLoop, calls=%fused_computation.1 | loop fusion | flops 4521984 | bytes 835584 | tf_op jit(solution)/shard_map/reduce_sum | solution.py:32
  8.5 2.2 copy.11
  10.7 10.5 %all-to-all-start = ((bf16[3,8,256,128]{3,1,0,2:T(8,128)(2,1)}), bf16[3,8,256,128]{3,1,0,2:T(8,128)(2,1)S(1)}, u32[]{:S(2)}, u32[]{:S(2)}) async-start(bf16[3,8,256,128]{3,1,0,2:T(8,128)(2,1)} %copy.11), calls=%async_computation | async-start | bytes 3145728 | tf_op jit(solution)/shard_map/all_to_all | solution.py:183
  21.2 19.8 %all-to-all-done = bf16[3,8,256,128]{3,1,0,2:T(8,128)(2,1)S(1)} async-done(((bf16[3,8,256,128]{3,1,0,2:T(8,128)(2,1)}), bf16[3,8,256,128]{3,1,0,2:T(8,128)(2,1)S(1)}, u32[]{:S(2)}, u32[]{:S(2)}) %all-to-all-start) | async-done | bytes 1572896 | tf_op jit(solution)/shard_map/all_to_all | solution.py:183
  43.0 3.3 collective-permute-start
  46.3 1.7 collective-permute-done
  49.2 12.2 %collective-permute-done.1 = f32[128,8,128]{2,1,0:T(8,128)S(1)} collective-permute-done((f32[128,8,128]{2,1,0:T(8,128)S(1)}, f32[128,8,128]{2,1,0:T(8,128)S(1)}, u32[]{:S(2)}, u32[]{:S(2)}) %collective-permute-start.1) | collective-permute-done | bytes 524320 | tf_op jit(solution)/shard_map/ppermute | solution.py:168
  65.2 2.3 collective-permute-start.3
  67.5 8.7 %collective-permute-start.4 = (f32[256,4,128]{2,1,0:T(4,128)S(1)}, f32[256,4,128]{2,1,0:T(4,128)}, u32[]{:S(2)}, u32[]{:S(2)}) collective-permute-start(f32[256,4,128]{2,1,0:T(4,128)S(1)} %get-tuple-element.27), channel_id=1, source_target_pairs={{1,0},{2,1},{3,2},{4,3},{5,4},{6,5},{7,6},{8,7},{9,8},{10,9},{11,1... | collective-permute-start | bytes 1572872 | tf_op jit(solution)/shard_map/ppermute | solution.py:22
  76.9 9.0 %collective-permute-done.3 = f32[256,4,128]{2,1,0:T(4,128)S(1)} collective-permute-done((f32[256,4,128]{2,1,0:T(4,128)S(1)}, f32[256,4,128]{2,1,0:T(4,128)S(1)}, u32[]{:S(2)}, u32[]{:S(2)}) %collective-permute-start.3) | collective-permute-done | bytes 524320 | tf_op jit(solution)/shard_map/ppermute | solution.py:21
  86.8 2.8 pad_maximum_fusion.est_ref
  89.5 13.6 %shard_map.47 = f32[256,8,128]{2,1,0:T(8,128)} custom-call(f32[81]{0:T(128)} %reshape.16.taps_ref, f32[256,16,128]{2,1,0:T(8,128)} %pad_maximum_fusion.est_ref, bf16[256,8,128]{2,1,0:T(8,128)(2,1)} %bitcast.23), custom_call_target="tpu_custom_call" | custom-call | tf_op jit(solution)/shard_map/pallas_call | solution.py:111
  103.2 13.7 %shard_map.46 = f32[256,8,128]{2,1,0:T(8,128)} custom-call(f32[81]{0:T(128)} %reshape.16.taps_ref, f32[256,16,128]{2,1,0:T(8,128)} %pad_maximum_fusion.est_ref, bf16[256,8,128]{2,1,0:T(8,128)(2,1)} %bitcast.21), custom_call_target="tpu_custom_call" | custom-call | tf_op jit(solution)/shard_map/pallas_call | solution.py:111
  116.9 2.5 fusion.15
  119.4 1.9 collective-permute-start.5
  121.3 9.9 %collective-permute-start.6 = (f32[256,4,128]{2,1,0:T(4,128)S(1)}, f32[256,4,128]{2,1,0:T(4,128)}, u32[]{:S(2)}, u32[]{:S(2)}) collective-permute-start(f32[256,4,128]{2,1,0:T(4,128)S(1)} %get-tuple-element.25), channel_id=1, source_target_pairs={{1,0},{2,1},{3,2},{4,3},{5,4},{6,5},{7,6},{8,7},{9,8},{10,9},{11,1... | collective-permute-start | bytes 1572872 | tf_op jit(solution)/shard_map/ppermute | solution.py:22
  132.4 13.8 %shard_map.48 = f32[256,8,128]{2,1,0:T(8,128)} custom-call(f32[81]{0:T(128)} %reshape.16.taps_ref, f32[256,16,128]{2,1,0:T(8,128)} %pad_maximum_fusion.est_ref, bf16[256,8,128]{2,1,0:T(8,128)(2,1)} %bitcast.19), custom_call_target="tpu_custom_call" | custom-call | tf_op jit(solution)/shard_map/pallas_call | solution.py:111
  146.2 1.9 collective-permute-start.7
  148.1 9.1 %collective-permute-start.8 = (f32[256,4,128]{2,1,0:T(4,128)}, f32[256,4,128]{2,1,0:T(4,128)S(1)}, u32[]{:S(2)}, u32[]{:S(2)}) collective-permute-start(f32[256,4,128]{2,1,0:T(4,128)} %get-tuple-element.23), channel_id=1, source_target_pairs={{1,0},{2,1},{3,2},{4,3},{5,4},{6,5},{7,6},{8,7},{9,8},{10,9},{11,1... | collective-permute-start | bytes 1572872 | tf_op jit(solution)/shard_map/ppermute | solution.py:22
  157.2 1.7 fusion.13
  158.9 1.9 collective-permute-start.9
  160.9 9.1 %collective-permute-start.10 = (f32[256,4,128]{2,1,0:T(4,128)S(1)}, f32[256,4,128]{2,1,0:T(4,128)S(1)}, u32[]{:S(2)}, u32[]{:S(2)}) collective-permute-start(f32[256,4,128]{2,1,0:T(4,128)S(1)} %get-tuple-element.21), channel_id=1, source_target_pairs={{1,0},{2,1},{3,2},{4,3},{5,4},{6,5},{7,6},{8,7},{9,8},{10,9},{11,1... | collective-permute-start | bytes 1572872 | tf_op jit(solution)/shard_map/ppermute | solution.py:22
  170.0 2.9 pad_maximum_fusion.1.refs_0_
  174.7 3.0 collective-permute-done.9
  178.5 1.8 pad_maximum_fusion.3.refs_2_
  180.3 6.5 %shard_map.49 = f32[256,8,128]{2,1,0:T(8,128)} custom-call(f32[81]{0:T(128)} %reshape.16.taps_ref, f32[256,16,128]{2,1,0:T(8,128)} %pad_maximum_fusion.1.refs_0_, f32[256,16,128]{2,1,0:T(8,128)} %pad_maximum_fusion.2.refs_1_, f32[256,16,128]{2,1,0:T(8,128)} %pad_maximum_fusion.3.refs_2_), custom_call_target="tpu_custom_call" | custom-call | tf_op jit(solution)/shard_map/pallas_call | solution.py:150
  187.9 3.6 %collective-permute-start.11 = (f32[128,8,128]{2,1,0:T(8,128)S(1)}, f32[128,8,128]{2,1,0:T(8,128)S(1)}, u32[]{:S(2)}, u32[]{:S(2)}) collective-permute-start(f32[128,8,128]{2,1,0:T(8,128)S(1)} %constant_dynamic-slice_fusion.1), channel_id=1, source_target_pairs={{0,32},{32,0},{64,96},{96,64},{1,33},{33,1},{65,97},{97,65},{2,34}... | collective-permute-start | bytes 1572872 | tf_op jit(solution)/shard_map/ppermute | solution.py:167
  195.2 12.2 %collective-permute-done.12 = f32[128,8,128]{2,1,0:T(8,128)S(1)} collective-permute-done((f32[128,8,128]{2,1,0:T(8,128)S(1)}, f32[128,8,128]{2,1,0:T(8,128)S(1)}, u32[]{:S(2)}, u32[]{:S(2)}) %collective-permute-start.12) | collective-permute-done | bytes 524320 | tf_op jit(solution)/shard_map/ppermute | solution.py:168
  210.7 1.9 collective-permute-start.14
  212.6 10.0 %collective-permute-start.15 = (f32[256,4,128]{2,1,0:T(4,128)S(1)}, f32[256,4,128]{2,1,0:T(4,128)S(1)}, u32[]{:S(2)}, u32[]{:S(2)}) collective-permute-start(f32[256,4,128]{2,1,0:T(4,128)S(1)} %get-tuple-element.17), channel_id=1, source_target_pairs={{1,0},{2,1},{3,2},{4,3},{5,4},{6,5},{7,6},{8,7},{9,8},{10,9},{11,1... | collective-permute-start | bytes 1572872 | tf_op jit(solution)/shard_map/ppermute | solution.py:22
  222.7 9.9 %collective-permute-done.14 = f32[256,4,128]{2,1,0:T(4,128)S(1)} collective-permute-done((f32[256,4,128]{2,1,0:T(4,128)S(1)}, f32[256,4,128]{2,1,0:T(4,128)S(1)}, u32[]{:S(2)}, u32[]{:S(2)}) %collective-permute-start.14) | collective-permute-done | bytes 524320 | tf_op jit(solution)/shard_map/ppermute | solution.py:21
  235.1 13.6 %shard_map.51 = f32[256,8,128]{2,1,0:T(8,128)} custom-call(f32[81]{0:T(128)} %reshape.16.taps_ref, f32[256,16,128]{2,1,0:T(8,128)} %pad_maximum_fusion.4.est_ref, bf16[256,8,128]{2,1,0:T(8,128)(2,1)} %bitcast.24), custom_call_target="tpu_custom_call" | custom-call | tf_op jit(solution)/shard_map/pallas_call | solution.py:111
  248.8 13.7 %shard_map.50 = f32[256,8,128]{2,1,0:T(8,128)} custom-call(f32[81]{0:T(128)} %reshape.16.taps_ref, f32[256,16,128]{2,1,0:T(8,128)} %pad_maximum_fusion.4.est_ref, bf16[256,8,128]{2,1,0:T(8,128)(2,1)} %bitcast.22), custom_call_target="tpu_custom_call" | custom-call | tf_op jit(solution)/shard_map/pallas_call | solution.py:111
  262.5 2.5 fusion.11
  265.0 1.9 collective-permute-start.16
  266.9 9.8 %collective-permute-start.17 = (f32[256,4,128]{2,1,0:T(4,128)S(1)}, f32[256,4,128]{2,1,0:T(4,128)}, u32[]{:S(2)}, u32[]{:S(2)}) collective-permute-start(f32[256,4,128]{2,1,0:T(4,128)S(1)} %get-tuple-element.15), channel_id=1, source_target_pairs={{1,0},{2,1},{3,2},{4,3},{5,4},{6,5},{7,6},{8,7},{9,8},{10,9},{11,1... | collective-permute-start | bytes 1572872 | tf_op jit(solution)/shard_map/ppermute | solution.py:22
  277.8 13.7 %shard_map.52 = f32[256,8,128]{2,1,0:T(8,128)} custom-call(f32[81]{0:T(128)} %reshape.16.taps_ref, f32[256,16,128]{2,1,0:T(8,128)} %pad_maximum_fusion.4.est_ref, bf16[256,8,128]{2,1,0:T(8,128)(2,1)} %bitcast.20), custom_call_target="tpu_custom_call" | custom-call | tf_op jit(solution)/shard_map/pallas_call | solution.py:111
  291.4 2.0 collective-permute-start.18
  293.5 9.1 %collective-permute-start.19 = (f32[256,4,128]{2,1,0:T(4,128)S(1)}, f32[256,4,128]{2,1,0:T(4,128)S(1)}, u32[]{:S(2)}, u32[]{:S(2)}) collective-permute-start(f32[256,4,128]{2,1,0:T(4,128)S(1)} %get-tuple-element.13), channel_id=1, source_target_pairs={{1,0},{2,1},{3,2},{4,3},{5,4},{6,5},{7,6},{8,7},{9,8},{10,9},{11,1... | collective-permute-start | bytes 1572872 | tf_op jit(solution)/shard_map/ppermute | solution.py:22
  302.6 1.7 fusion.9
  304.3 1.9 collective-permute-start.20
  306.2 9.1 %collective-permute-start.21 = (f32[256,4,128]{2,1,0:T(4,128)S(1)}, f32[256,4,128]{2,1,0:T(4,128)S(1)}, u32[]{:S(2)}, u32[]{:S(2)}) collective-permute-start(f32[256,4,128]{2,1,0:T(4,128)S(1)} %get-tuple-element.11), channel_id=1, source_target_pairs={{1,0},{2,1},{3,2},{4,3},{5,4},{6,5},{7,6},{8,7},{9,8},{10,9},{11,1... | collective-permute-start | bytes 1572872 | tf_op jit(solution)/shard_map/ppermute | solution.py:22
  315.3 3.0 pad_maximum_fusion.5.refs_0_
  320.1 3.2 collective-permute-done.20
  324.2 1.7 pad_maximum_fusion.7.refs_2_
  326.0 6.5 %shard_map.53 = f32[256,8,128]{2,1,0:T(8,128)} custom-call(f32[81]{0:T(128)} %reshape.16.taps_ref, f32[256,16,128]{2,1,0:T(8,128)} %pad_maximum_fusion.5.refs_0_, f32[256,16,128]{2,1,0:T(8,128)} %pad_maximum_fusion.6.refs_1_, f32[256,16,128]{2,1,0:T(8,128)} %pad_maximum_fusion.7.refs_2_), custom_call_target="tpu_custom_call" | custom-call | tf_op jit(solution)/shard_map/pallas_call | solution.py:150
  333.5 3.3 collective-permute-start.22
  340.4 12.2 %collective-permute-done.23 = f32[128,8,128]{2,1,0:T(8,128)S(1)} collective-permute-done((f32[128,8,128]{2,1,0:T(8,128)S(1)}, f32[128,8,128]{2,1,0:T(8,128)S(1)}, u32[]{:S(2)}, u32[]{:S(2)}) %collective-permute-start.23) | collective-permute-done | bytes 524320 | tf_op jit(solution)/shard_map/ppermute | solution.py:168
  (83 shorter events, 39.7 us)
Async XLA Ops:
  0.0 7.1 %copy-start = (bf16[3,8,256,128]{3,2,1,0:T(8,128)(2,1)S(1)}, bf16[3,8,256,128]{3,2,1,0:T(8,128)(2,1)}, u32[]{:S(2)}) copy-start(bf16[3,8,256,128]{3,2,1,0:T(8,128)(2,1)} %param.4) | copy-start | bytes 4718596
  10.7 30.4 %all-to-all-start = ((bf16[3,8,256,128]{3,1,0,2:T(8,128)(2,1)}), bf16[3,8,256,128]{3,1,0,2:T(8,128)(2,1)S(1)}, u32[]{:S(2)}, u32[]{:S(2)}) async-start(bf16[3,8,256,128]{3,1,0,2:T(8,128)(2,1)} %copy.11), calls=%async_computation | async-start | bytes 3145728 | tf_op jit(solution)/shard_map/all_to_all | solution.py:183
  41.7 6.5 %copy-start.8 = (bf16[1,32,8,8,128]{4,3,2,1,0:T(8,128)(2,1)}, bf16[1,32,8,8,128]{4,3,2,1,0:T(8,128)(2,1)S(1)}, u32[]{:S(2)}) copy-start(bf16[1,32,8,8,128]{4,3,2,1,0:T(8,128)(2,1)S(1)} %get-tuple-element.6) | copy-start | bytes 1572868
  41.7 6.5 %copy-start.9 = (bf16[1,32,8,8,128]{4,3,2,1,0:T(8,128)(2,1)}, bf16[1,32,8,8,128]{4,3,2,1,0:T(8,128)(2,1)S(1)}, u32[]{:S(2)}) copy-start(bf16[1,32,8,8,128]{4,3,2,1,0:T(8,128)(2,1)S(1)} %get-tuple-element.5) | copy-start | bytes 1572868
  41.7 6.5 %copy-start.10 = (bf16[1,32,8,8,128]{4,3,2,1,0:T(8,128)(2,1)}, bf16[1,32,8,8,128]{4,3,2,1,0:T(8,128)(2,1)S(1)}, u32[]{:S(2)}) copy-start(bf16[1,32,8,8,128]{4,3,2,1,0:T(8,128)(2,1)S(1)} %get-tuple-element.7) | copy-start | bytes 1572868
  43.0 5.1 %collective-permute-start = (f32[128,8,128]{2,1,0:T(8,128)}, f32[128,8,128]{2,1,0:T(8,128)S(1)}, u32[]{:S(2)}, u32[]{:S(2)}) collective-permute-start(f32[128,8,128]{2,1,0:T(8,128)} %constant_dynamic-slice_fusion.2), channel_id=1, source_target_pairs={{0,32},{32,0},{64,96},{96,64},{1,33},{33,1},{65,97},{97,65},{2,34}... | collective-permute-start | bytes 1572872 | tf_op jit(solution)/shard_map/ppermute | solution.py:167
  48.2 13.2 %collective-permute-start.1 = (f32[128,8,128]{2,1,0:T(8,128)S(1)}, f32[128,8,128]{2,1,0:T(8,128)S(1)}, u32[]{:S(2)}, u32[]{:S(2)}) collective-permute-start(f32[128,8,128]{2,1,0:T(8,128)S(1)} %dynamic-slice_add_fusion.2), channel_id=1, source_target_pairs={{0,64},{32,96},{64,0},{96,32},{1,65},{33,97},{65,1},{97,33},{2,66}... | collective-permute-start | bytes 1572872 | tf_op jit(solution)/shard_map/ppermute | solution.py:168
  61.4 2.8 collective-permute-start.2
  64.3 0.8 copy-start.11
  64.3 11.8 %copy-start.13 = (f32[3,3,9]{2,1,0:T(4,128)S(1)}, f32[3,3,9]{2,1,0:T(4,128)}, u32[]{:S(2)}) copy-start(f32[3,3,9]{2,1,0:T(4,128)} %param.7) | copy-start | bytes 976
  65.2 20.7 %collective-permute-start.3 = (f32[256,4,128]{2,1,0:T(4,128)S(1)}, f32[256,4,128]{2,1,0:T(4,128)S(1)}, u32[]{:S(2)}, u32[]{:S(2)}) collective-permute-start(f32[256,4,128]{2,1,0:T(4,128)S(1)} %get-tuple-element.26), channel_id=1, source_target_pairs={{0,1},{1,2},{2,3},{3,4},{4,5},{5,6},{6,7},{7,8},{8,9},{9,10},{10,1... | collective-permute-start | bytes 1572872 | tf_op jit(solution)/shard_map/ppermute | solution.py:21
  67.5 19.3 %collective-permute-start.4 = (f32[256,4,128]{2,1,0:T(4,128)S(1)}, f32[256,4,128]{2,1,0:T(4,128)}, u32[]{:S(2)}, u32[]{:S(2)}) collective-permute-start(f32[256,4,128]{2,1,0:T(4,128)S(1)} %get-tuple-element.27), channel_id=1, source_target_pairs={{1,0},{2,1},{3,2},{4,3},{5,4},{6,5},{7,6},{8,7},{9,8},{10,9},{11,1... | collective-permute-start | bytes 1572872 | tf_op jit(solution)/shard_map/ppermute | solution.py:22
  103.2 28.1 %copy-start.3 = (f32[256,8,128]{2,1,0:T(8,128)S(1)}, f32[256,8,128]{2,1,0:T(8,128)}, u32[]{:S(2)}) copy-start(f32[256,8,128]{2,1,0:T(8,128)} %shard_map.47) | copy-start | bytes 3145732
  119.4 41.5 %collective-permute-start.5 = (f32[256,4,128]{2,1,0:T(4,128)}, f32[256,4,128]{2,1,0:T(4,128)}, u32[]{:S(2)}, u32[]{:S(2)}) collective-permute-start(f32[256,4,128]{2,1,0:T(4,128)} %get-tuple-element.24), channel_id=1, source_target_pairs={{0,1},{1,2},{2,3},{3,4},{4,5},{5,6},{6,7},{7,8},{8,9},{9,10},{10,1... | collective-permute-start | bytes 1572872 | tf_op jit(solution)/shard_map/ppermute | solution.py:21
  121.3 48.7 %collective-permute-start.6 = (f32[256,4,128]{2,1,0:T(4,128)S(1)}, f32[256,4,128]{2,1,0:T(4,128)}, u32[]{:S(2)}, u32[]{:S(2)}) collective-permute-start(f32[256,4,128]{2,1,0:T(4,128)S(1)} %get-tuple-element.25), channel_id=1, source_target_pairs={{1,0},{2,1},{3,2},{4,3},{5,4},{6,5},{7,6},{8,7},{9,8},{10,9},{11,1... | collective-permute-start | bytes 1572872 | tf_op jit(solution)/shard_map/ppermute | solution.py:22
  132.4 37.5 %copy-start.7 = (f32[256,8,128]{2,1,0:T(8,128)S(1)}, f32[256,8,128]{2,1,0:T(8,128)}, u32[]{:S(2)}) copy-start(f32[256,8,128]{2,1,0:T(8,128)} %shard_map.46) | copy-start | bytes 3145732
  146.2 26.7 %collective-permute-start.7 = (f32[256,4,128]{2,1,0:T(4,128)}, f32[256,4,128]{2,1,0:T(4,128)S(1)}, u32[]{:S(2)}, u32[]{:S(2)}) collective-permute-start(f32[256,4,128]{2,1,0:T(4,128)} %get-tuple-element.22), channel_id=1, source_target_pairs={{0,1},{1,2},{2,3},{3,4},{4,5},{5,6},{6,7},{7,8},{8,9},{9,10},{10,1... | collective-permute-start | bytes 1572872 | tf_op jit(solution)/shard_map/ppermute | solution.py:21
  148.1 24.8 %collective-permute-start.8 = (f32[256,4,128]{2,1,0:T(4,128)}, f32[256,4,128]{2,1,0:T(4,128)S(1)}, u32[]{:S(2)}, u32[]{:S(2)}) collective-permute-start(f32[256,4,128]{2,1,0:T(4,128)} %get-tuple-element.23), channel_id=1, source_target_pairs={{1,0},{2,1},{3,2},{4,3},{5,4},{6,5},{7,6},{8,7},{9,8},{10,9},{11,1... | collective-permute-start | bytes 1572872 | tf_op jit(solution)/shard_map/ppermute | solution.py:22
  158.9 18.7 %collective-permute-start.9 = (f32[256,4,128]{2,1,0:T(4,128)S(1)}, f32[256,4,128]{2,1,0:T(4,128)S(1)}, u32[]{:S(2)}, u32[]{:S(2)}) collective-permute-start(f32[256,4,128]{2,1,0:T(4,128)S(1)} %get-tuple-element.20), channel_id=1, source_target_pairs={{0,1},{1,2},{2,3},{3,4},{4,5},{5,6},{6,7},{7,8},{8,9},{9,10},{10,1... | collective-permute-start | bytes 1572872 | tf_op jit(solution)/shard_map/ppermute | solution.py:21
  160.9 17.6 %collective-permute-start.10 = (f32[256,4,128]{2,1,0:T(4,128)S(1)}, f32[256,4,128]{2,1,0:T(4,128)S(1)}, u32[]{:S(2)}, u32[]{:S(2)}) collective-permute-start(f32[256,4,128]{2,1,0:T(4,128)S(1)} %get-tuple-element.21), channel_id=1, source_target_pairs={{1,0},{2,1},{3,2},{4,3},{5,4},{6,5},{7,6},{8,7},{9,8},{10,9},{11,1... | collective-permute-start | bytes 1572872 | tf_op jit(solution)/shard_map/ppermute | solution.py:22
  172.9 5.6 %copy-start.5 = (f32[256,8,128]{2,1,0:T(8,128)S(1)}, f32[256,8,128]{2,1,0:T(8,128)}, u32[]{:S(2)}) copy-start(f32[256,8,128]{2,1,0:T(8,128)} %shard_map.48) | copy-start | bytes 3145732
  187.9 5.2 %collective-permute-start.11 = (f32[128,8,128]{2,1,0:T(8,128)S(1)}, f32[128,8,128]{2,1,0:T(8,128)S(1)}, u32[]{:S(2)}, u32[]{:S(2)}) collective-permute-start(f32[128,8,128]{2,1,0:T(8,128)S(1)} %constant_dynamic-slice_fusion.1), channel_id=1, source_target_pairs={{0,32},{32,0},{64,96},{96,64},{1,33},{33,1},{65,97},{97,65},{2,34}... | collective-permute-start | bytes 1572872 | tf_op jit(solution)/shard_map/ppermute | solution.py:167
  194.1 16.2 %copy-start.12 = (f32[128,8,128]{2,1,0:T(8,128)S(1)}, f32[128,8,128]{2,1,0:T(8,128)}, u32[]{:S(2)}) copy-start(f32[128,8,128]{2,1,0:T(8,128)} %copy-done.11) | copy-start | bytes 1572868
  194.2 13.2 %collective-permute-start.12 = (f32[128,8,128]{2,1,0:T(8,128)S(1)}, f32[128,8,128]{2,1,0:T(8,128)S(1)}, u32[]{:S(2)}, u32[]{:S(2)}) collective-permute-start(f32[128,8,128]{2,1,0:T(8,128)S(1)} %dynamic-slice_add_fusion.1), channel_id=1, source_target_pairs={{0,64},{32,96},{64,0},{96,32},{1,65},{33,97},{65,1},{97,33},{2,66}... | collective-permute-start | bytes 1572872 | tf_op jit(solution)/shard_map/ppermute | solution.py:168
  207.4 2.8 collective-permute-start.13
  210.7 21.8 %collective-permute-start.14 = (f32[256,4,128]{2,1,0:T(4,128)S(1)}, f32[256,4,128]{2,1,0:T(4,128)S(1)}, u32[]{:S(2)}, u32[]{:S(2)}) collective-permute-start(f32[256,4,128]{2,1,0:T(4,128)S(1)} %get-tuple-element.16), channel_id=1, source_target_pairs={{0,1},{1,2},{2,3},{3,4},{4,5},{5,6},{6,7},{7,8},{8,9},{9,10},{10,1... | collective-permute-start | bytes 1572872 | tf_op jit(solution)/shard_map/ppermute | solution.py:21
  212.6 20.8 %collective-permute-start.15 = (f32[256,4,128]{2,1,0:T(4,128)S(1)}, f32[256,4,128]{2,1,0:T(4,128)S(1)}, u32[]{:S(2)}, u32[]{:S(2)}) collective-permute-start(f32[256,4,128]{2,1,0:T(4,128)S(1)} %get-tuple-element.17), channel_id=1, source_target_pairs={{1,0},{2,1},{3,2},{4,3},{5,4},{6,5},{7,6},{8,7},{9,8},{10,9},{11,1... | collective-permute-start | bytes 1572872 | tf_op jit(solution)/shard_map/ppermute | solution.py:22
  248.8 28.0 %copy-start.2 = (f32[256,8,128]{2,1,0:T(8,128)S(1)}, f32[256,8,128]{2,1,0:T(8,128)}, u32[]{:S(2)}) copy-start(f32[256,8,128]{2,1,0:T(8,128)} %shard_map.51) | copy-start | bytes 3145732
  265.0 41.2 %collective-permute-start.16 = (f32[256,4,128]{2,1,0:T(4,128)}, f32[256,4,128]{2,1,0:T(4,128)}, u32[]{:S(2)}, u32[]{:S(2)}) collective-permute-start(f32[256,4,128]{2,1,0:T(4,128)} %get-tuple-element.14), channel_id=1, source_target_pairs={{0,1},{1,2},{2,3},{3,4},{4,5},{5,6},{6,7},{7,8},{8,9},{9,10},{10,1... | collective-permute-start | bytes 1572872 | tf_op jit(solution)/shard_map/ppermute | solution.py:21
  266.9 48.4 %collective-permute-start.17 = (f32[256,4,128]{2,1,0:T(4,128)S(1)}, f32[256,4,128]{2,1,0:T(4,128)}, u32[]{:S(2)}, u32[]{:S(2)}) collective-permute-start(f32[256,4,128]{2,1,0:T(4,128)S(1)} %get-tuple-element.15), channel_id=1, source_target_pairs={{1,0},{2,1},{3,2},{4,3},{5,4},{6,5},{7,6},{8,7},{9,8},{10,9},{11,1... | collective-permute-start | bytes 1572872 | tf_op jit(solution)/shard_map/ppermute | solution.py:22
  291.4 23.9 %copy-start.6 = (f32[256,8,128]{2,1,0:T(8,128)S(1)}, f32[256,8,128]{2,1,0:T(8,128)}, u32[]{:S(2)}) copy-start(f32[256,8,128]{2,1,0:T(8,128)} %shard_map.50) | copy-start | bytes 3145732
  291.4 26.9 %collective-permute-start.18 = (f32[256,4,128]{2,1,0:T(4,128)}, f32[256,4,128]{2,1,0:T(4,128)S(1)}, u32[]{:S(2)}, u32[]{:S(2)}) collective-permute-start(f32[256,4,128]{2,1,0:T(4,128)} %get-tuple-element.12), channel_id=1, source_target_pairs={{0,1},{1,2},{2,3},{3,4},{4,5},{5,6},{6,7},{7,8},{8,9},{9,10},{10,1... | collective-permute-start | bytes 1572872 | tf_op jit(solution)/shard_map/ppermute | solution.py:21
  293.5 24.9 %collective-permute-start.19 = (f32[256,4,128]{2,1,0:T(4,128)S(1)}, f32[256,4,128]{2,1,0:T(4,128)S(1)}, u32[]{:S(2)}, u32[]{:S(2)}) collective-permute-start(f32[256,4,128]{2,1,0:T(4,128)S(1)} %get-tuple-element.13), channel_id=1, source_target_pairs={{1,0},{2,1},{3,2},{4,3},{5,4},{6,5},{7,6},{8,7},{9,8},{10,9},{11,1... | collective-permute-start | bytes 1572872 | tf_op jit(solution)/shard_map/ppermute | solution.py:22
  304.3 19.0 %collective-permute-start.20 = (f32[256,4,128]{2,1,0:T(4,128)S(1)}, f32[256,4,128]{2,1,0:T(4,128)S(1)}, u32[]{:S(2)}, u32[]{:S(2)}) collective-permute-start(f32[256,4,128]{2,1,0:T(4,128)S(1)} %get-tuple-element.10), channel_id=1, source_target_pairs={{0,1},{1,2},{2,3},{3,4},{4,5},{5,6},{6,7},{7,8},{8,9},{9,10},{10,1... | collective-permute-start | bytes 1572872 | tf_op jit(solution)/shard_map/ppermute | solution.py:21
  306.2 18.0 %collective-permute-start.21 = (f32[256,4,128]{2,1,0:T(4,128)S(1)}, f32[256,4,128]{2,1,0:T(4,128)S(1)}, u32[]{:S(2)}, u32[]{:S(2)}) collective-permute-start(f32[256,4,128]{2,1,0:T(4,128)S(1)} %get-tuple-element.11), channel_id=1, source_target_pairs={{1,0},{2,1},{3,2},{4,3},{5,4},{6,5},{7,6},{8,7},{9,8},{10,9},{11,1... | collective-permute-start | bytes 1572872 | tf_op jit(solution)/shard_map/ppermute | solution.py:22
  318.3 5.9 %copy-start.4 = (f32[256,8,128]{2,1,0:T(8,128)S(1)}, f32[256,8,128]{2,1,0:T(8,128)}, u32[]{:S(2)}) copy-start(f32[256,8,128]{2,1,0:T(8,128)} %shard_map.52) | copy-start | bytes 3145732
  333.5 4.9 %collective-permute-start.22 = (f32[128,8,128]{2,1,0:T(8,128)S(1)}, f32[128,8,128]{2,1,0:T(8,128)S(1)}, u32[]{:S(2)}, u32[]{:S(2)}) collective-permute-start(f32[128,8,128]{2,1,0:T(8,128)S(1)} %constant_dynamic-slice_fusion), channel_id=1, source_target_pairs={{0,32},{32,0},{64,96},{96,64},{1,33},{33,1},{65,97},{97,65},{2,34}... | collective-permute-start | bytes 1572872 | tf_op jit(solution)/shard_map/ppermute | solution.py:167
  339.4 13.2 %collective-permute-start.23 = (f32[128,8,128]{2,1,0:T(8,128)S(1)}, f32[128,8,128]{2,1,0:T(8,128)S(1)}, u32[]{:S(2)}, u32[]{:S(2)}) collective-permute-start(f32[128,8,128]{2,1,0:T(8,128)S(1)} %dynamic-slice_add_fusion), channel_id=1, source_target_pairs={{0,64},{32,96},{64,0},{96,32},{1,65},{33,97},{65,1},{97,33},{2,66}... | collective-permute-start | bytes 1572872 | tf_op jit(solution)/shard_map/ppermute | solution.py:168
  352.7 2.8 collective-permute-start.24
  355.5 1.8 copy-start.1

commit v3 on v2

--- a/solution.py
+++ b/solution.py
@@ -11,17 +11,23 @@
 CZ = 8
 
 
-def extended_2(shard, sides, width):
-    for axis, dim in sides:
-        devices, length = (lax.axis_size(axis), shard.shape[dim])
-        up = [(i, (i + 1) % devices) for i in range(devices - 1)]
-        down = [(j, i) for i, j in up]
-        last = lax.slice_in_dim(shard, length - width, length, axis=dim)
-        first = lax.slice_in_dim(shard, 0, width, axis=dim)
-        before = lax.ppermute(last, axis, up)
-        after = lax.ppermute(first, axis, down)
-        shard = jnp.concatenate([before, shard, after], axis=dim)
-    return shard
+def halos(shard, axis, dim, width):
+    devices, length = (lax.axis_size(axis), shard.shape[dim])
+    up = [(i, (i + 1) % devices) for i in range(devices - 1)]
+    down = [(j, i) for i, j in up]
+    last = lax.slice_in_dim(shard, length - width, length, axis=dim)
+    first = lax.slice_in_dim(shard, 0, width, axis=dim)
+    before = lax.ppermute(last, axis, up)
+    after = lax.ppermute(first, axis, down)
+    return before, after
+
+
+def _fill_wide(wide_ref, before_ref, mid_ref, after_ref, z0):
+    rim = before_ref.shape[1]
+    width = mid_ref.shape[1]
+    wide_ref[:, 0:rim, :] = before_ref[pl.ds(z0, CZ)]
+    wide_ref[:, rim : rim + width, :] = mid_ref[pl.ds(z0, CZ)]
+    wide_ref[:, rim + width :, :] = after_ref[pl.ds(z0, CZ)]
 
 
 def resample_views(raw_views, weight_norm, offsets):
@@ -60,7 +66,7 @@
     return acc
 
 
-def _forward_kernel(v, taps_ref, est_ref, brick_ref, out_ref, a_ref, c_ref):
+def _forward_kernel(v, taps_ref, before_ref, mid_ref, after_ref, brick_ref, out_ref, a_ref, c_ref, est_ref):
     nz, _, ny = out_ref.shape
     tx = [taps_ref[v * 27 + 9 + t] for t in range(9)]
     tz = [taps_ref[v * 27 + t] for t in range(9)]
@@ -73,9 +79,10 @@
 
     def along_x(c, carry):
         z0 = pl.multiple_of(c * CZ, CZ)
-        acc = tx[0] * est_ref[pl.ds(z0, CZ), pl.ds(0, 8), :]
+        _fill_wide(est_ref, before_ref, mid_ref, after_ref, z0)
+        acc = tx[0] * est_ref[:, pl.ds(0, 8), :]
         for t in range(1, 9):
-            acc = acc + tx[t] * est_ref[pl.ds(z0, CZ), pl.ds(t, 8), :]
+            acc = acc + tx[t] * est_ref[:, pl.ds(t, 8), :]
         a_ref[pl.ds(z0 + 4, CZ)] = acc
         return carry
 
@@ -106,27 +113,24 @@
     lax.fori_loop(0, nz // CZ, along_z_back, 0)
 
 
-def forward_partial(taps_flat, v, extended, brick):
+def forward_partial(taps_flat, v, before, mid, after, brick):
     nz, width, ny = brick.shape
     return pl.pallas_call(
         functools.partial(_forward_kernel, v),
-        in_specs=[
-            pl.BlockSpec(memory_space=pltpu.SMEM),
-            pl.BlockSpec(memory_space=pltpu.VMEM),
-            pl.BlockSpec(memory_space=pltpu.VMEM),
-        ],
+        in_specs=[pl.BlockSpec(memory_space=pltpu.SMEM)] + [pl.BlockSpec(memory_space=pltpu.VMEM)] * 4,
         out_specs=pl.BlockSpec(memory_space=pltpu.VMEM),
         out_shape=jax.ShapeDtypeStruct((nz, width, ny), jnp.float32),
         scratch_shapes=[
             pltpu.VMEM((nz + 8, width, ny), jnp.float32),
             pltpu.VMEM((nz + 8, width, ny), jnp.float32),
+            pltpu.VMEM((CZ, width + 8, ny), jnp.float32),
         ],
-    )(taps_flat, extended, brick)
+    )(taps_flat, before, mid, after, brick)
 
 
 def _back_kernel(taps_ref, *refs):
-    wide_refs, out_ref = refs[:-1], refs[-1]
-    count = len(wide_refs)
+    parts, out_ref, wide_ref = refs[:-2], refs[-2], refs[-1]
+    count = len(parts) // 3
     nz = out_ref.shape[0]
     tx = [[taps_ref[v * 27 + 9 + t] for t in range(9)] for v in range(count)]
 
@@ -134,9 +138,10 @@
         z0 = pl.multiple_of(c * CZ, CZ)
         total = None
         for v in range(count):
-            acc = tx[v][8] * wide_refs[v][pl.ds(z0, CZ), pl.ds(0, 8), :]
+            _fill_wide(wide_ref, *parts[3 * v : 3 * v + 3], z0)
+            acc = tx[v][8] * wide_ref[:, pl.ds(0, 8), :]
             for t in range(1, 9):
-                acc = acc + tx[v][8 - t] * wide_refs[v][pl.ds(z0, CZ), pl.ds(t, 8), :]
+                acc = acc + tx[v][8 - t] * wide_ref[:, pl.ds(t, 8), :]
             term = jnp.log(acc)
             total = term if total is None else total + term
         out_ref[pl.ds(z0, CZ)] = total
@@ -145,15 +150,16 @@
     lax.fori_loop(0, nz // CZ, body, 0)
 
 
-def back_logs(taps_flat, wides):
-    nz, width8, ny = wides[0].shape
+def back_logs(taps_flat, parts):
+    nz, width, ny = parts[1].shape
     return pl.pallas_call(
         _back_kernel,
         in_specs=[pl.BlockSpec(memory_space=pltpu.SMEM)]
-        + [pl.BlockSpec(memory_space=pltpu.VMEM)] * len(wides),
+        + [pl.BlockSpec(memory_space=pltpu.VMEM)] * len(parts),
         out_specs=pl.BlockSpec(memory_space=pltpu.VMEM),
-        out_shape=jax.ShapeDtypeStruct((nz, width8 - 8, ny), jnp.float32),
-    )(taps_flat, *wides)
+        out_shape=jax.ShapeDtypeStruct((nz, width, ny), jnp.float32),
+        scratch_shapes=[pltpu.VMEM((CZ, width + 8, ny), jnp.float32)],
+    )(taps_flat, *parts)
 
 
 def view_sum(part):
@@ -186,12 +192,15 @@
         local_sum = local_sum + bricks[index].astype(jnp.float32)
     joined_volume = view_sum(local_sum) / total_views
     for turn in range(ITERS):
-        extended = extended_2(joined_volume, (("vol", 1),), rim_width)
-        wides = []
+        before, after = halos(joined_volume, "vol", 1, rim_width)
+        parts = []
         for index in range(count):
-            partial_value = forward_partial(taps_flat, index, extended, bricks[index])
-            wides.append(extended_2(partial_value, (("vol", 1),), rim_width))
-        logs = back_logs(taps_flat, wides)
+            partial_value = forward_partial(
+                taps_flat, index, before, joined_volume, after, bricks[index]
+            )
+            low, high = halos(partial_value, "vol", 1, rim_width)
+            parts += [low, partial_value, high]
+        logs = back_logs(taps_flat, parts)
         summed = view_sum(logs)
         joined_volume = joined_volume * jnp.exp(summed / total_views)
     return joined_volume

time: 360 us -> 362 us (level)
  waiting for transfers between devices: 94.5 us -> 133 us
  starting transfers between devices: 118 us -> 91.8 us
  other arithmetic: 28.8 us -> 12.4 us
  local copies, waits for them, and re-layouts: 18.8 us -> 24.2 us
    ppermute x16, waiting for transfers between devices: 28.6 us -> 67.3 us  [the longest x8 34.8 us: halos(): before = lax.ppermute(last, axis, up)]
    ppermute x16, starting transfers between devices: 90.6 us -> 64.1 us  [the longest x8 44.4 us: halos(): after = lax.ppermute(first, axis, down)]
    concatenate x8 -> x0, other arithmetic: 17.4 us -> none  [extended_2(): shard = jnp.concatenate([before, shard, after], axis=dim)]
  transfers between devices with their start and end apart: 26 -> 26, of which waited for: 18 -> 18; matrix products, arithmetic and copies ran while one was open for 4% -> 3% of each run, Pallas kernels for 8% -> 15%
where the time goes in v3:
time: 362 us; the launch traced here: 360 us
  waiting for transfers between devices  133 us (37%)
  Pallas kernels  96.7 us (27%)
  starting transfers between devices  91.8 us (25%)
  local copies, waits for them, and re-layouts  24.2 us (7%)
  other arithmetic  12.4 us (3%)
    pallas_call x6, Pallas kernels, forward_partial(): pl.pallas_call(functools.partial(_forward_kernel, v), in_specs=[pl.BlockS...  82.8 us
    ppermute x8, starting transfers between devices, halos(): after = lax.ppermute(first, axis, down)  44.4 us
    ppermute x3, waiting for transfers between devices, view_sum(): own = own + lax.ppermute(own, 'view', chip_swap)  36.7 us
    ppermute x8, waiting for transfers between devices, halos(): before = lax.ppermute(last, axis, up)  34.8 us
    ppermute x8, waiting for transfers between devices, halos(): after = lax.ppermute(first, axis, down)  32.4 us
    all_to_all x1, waiting for transfers between devices, per_device(): lax.all_to_all(local_views, 'vol', split_axis=2, concat_axis=1, tiled=True)  19.9 us
    ppermute x8, starting transfers between devices, halos(): before = lax.ppermute(last, axis, up)  19.7 us
    slice x8, local copies, waits for them, and re-layouts, halos(): first = lax.slice_in_dim(shard, 0, width, axis=dim)  14.2 us
  transfers between devices with their start and end apart: 26, of which 18 were waited for; matrix products, arithmetic and copies ran while one was open for 3% of the time, Pallas kernels for 15%

profile of v3, /device:TPU:5, one launch (start us, length us, event | category | flops | bytes accessed | tf_op | source)
XLA Modules:
  0.0 360.4 jit_solution(7307158760102033999)
XLA Ops:
  2.7 4.4 %select_reduce_fusion = f32[3,256,256]{2,1,0:T(8,128)S(1)} fusion(f32[3,256,8]{2,1,0:T(8,128)S(1)} %copy.10, s32[3,256,8]{2,1,0:T(8,128)S(1)} %iota_add_fusion), kind=kLoop, calls=%fused_computation.1 | loop fusion | flops 4521984 | bytes 835584 | tf_op jit(solution)/shard_map/reduce_sum | solution.py:38
  8.5 2.2 copy.11
  10.7 10.5 %all-to-all-start = ((bf16[3,8,256,128]{3,1,0,2:T(8,128)(2,1)}), bf16[3,8,256,128]{3,1,0,2:T(8,128)(2,1)S(1)}, u32[]{:S(2)}, u32[]{:S(2)}) async-start(bf16[3,8,256,128]{3,1,0,2:T(8,128)(2,1)} %copy.11), calls=%async_computation | async-start | bytes 3145728 | tf_op jit(solution)/shard_map/all_to_all | solution.py:189
  21.3 19.9 %all-to-all-done = bf16[3,8,256,128]{3,1,0,2:T(8,128)(2,1)S(1)} async-done(((bf16[3,8,256,128]{3,1,0,2:T(8,128)(2,1)}), bf16[3,8,256,128]{3,1,0,2:T(8,128)(2,1)S(1)}, u32[]{:S(2)}, u32[]{:S(2)}) %all-to-all-start) | async-done | bytes 1572896 | tf_op jit(solution)/shard_map/all_to_all | solution.py:189
  43.0 3.4 collective-permute-start
  46.5 1.9 collective-permute-done
  50.4 12.2 %collective-permute-done.1 = f32[128,8,128]{2,1,0:T(8,128)S(1)} collective-permute-done((f32[128,8,128]{2,1,0:T(8,128)S(1)}, f32[128,8,128]{2,1,0:T(8,128)S(1)}, u32[]{:S(2)}, u32[]{:S(2)}) %collective-permute-start.1) | collective-permute-done | bytes 524320 | tf_op jit(solution)/shard_map/ppermute | solution.py:174
  67.9 5.2 %collective-permute-start.4 = (f32[256,4,128]{2,1,0:T(4,128)}, f32[256,4,128]{2,1,0:T(4,128)}, u32[]{:S(2)}, u32[]{:S(2)}) collective-permute-start(f32[256,4,128]{2,1,0:T(4,128)} %get-tuple-element.26), channel_id=1, source_target_pairs={{1,0},{2,1},{3,2},{4,3},{5,4},{6,5},{7,6},{8,7},{9,8},{10,9},{11,1... | collective-permute-start | bytes 1572872 | tf_op jit(solution)/shard_map/ppermute | solution.py:21
  73.1 1.9 collective-permute-start.3
  75.8 8.5 %collective-permute-done.4.after_ref = f32[256,4,128]{2,1,0:T(4,128)} collective-permute-done((f32[256,4,128]{2,1,0:T(4,128)}, f32[256,4,128]{2,1,0:T(4,128)}, u32[]{:S(2)}, u32[]{:S(2)}) %collective-permute-start.4) | collective-permute-done | bytes 524320 | tf_op jit(solution)/shard_map/ppermute | solution.py:21
  84.3 9.5 %collective-permute-done.3.before_ref = f32[256,4,128]{2,1,0:T(4,128)} collective-permute-done((f32[256,4,128]{2,1,0:T(4,128)}, f32[256,4,128]{2,1,0:T(4,128)}, u32[]{:S(2)}, u32[]{:S(2)}) %collective-permute-start.3) | collective-permute-done | bytes 524320 | tf_op jit(solution)/shard_map/ppermute | solution.py:20
  93.8 13.8 %shard_map.46.refs_1_ = f32[256,8,128]{2,1,0:T(8,128)} custom-call(f32[81]{0:T(128)} %reshape.16.taps_ref, f32[256,4,128]{2,1,0:T(4,128)} %collective-permute-done.3.before_ref, f32[256,8,128]{2,1,0:T(8,128)} %copy-done.3, f32[256,4,128]{2,1,0:T(4,128)} %collective-permute-done.4.after_ref, bf16[256,8,128]{2,1,0:T(8,128)(2,1)} %bitcast.23), custom_call_target="tpu_custom_call" | custom-call | tf_op jit(solution)/shard_map/pallas_call | solution.py:118
  107.6 2.6 fusion.15
  110.2 1.9 collective-permute-start.6
  112.1 3.4 collective-permute-start.5
  115.5 13.8 %shard_map.47.refs_4_ = f32[256,8,128]{2,1,0:T(8,128)} custom-call(f32[81]{0:T(128)} %reshape.16.taps_ref, f32[256,4,128]{2,1,0:T(4,128)} %collective-permute-done.3.before_ref, f32[256,8,128]{2,1,0:T(8,128)} %copy-done.3, f32[256,4,128]{2,1,0:T(4,128)} %collective-permute-done.4.after_ref, bf16[256,8,128]{2,1,0:T(8,128)(2,1)} %bitcast.21), custom_call_target="tpu_custom_call" | custom-call | tf_op jit(solution)/shard_map/pallas_call | solution.py:118
  129.3 2.5 fusion.14
  131.8 7.6 %collective-permute-start.8 = (f32[256,4,128]{2,1,0:T(4,128)}, f32[256,4,128]{2,1,0:T(4,128)}, u32[]{:S(2)}, u32[]{:S(2)}) collective-permute-start(f32[256,4,128]{2,1,0:T(4,128)} %get-tuple-element.22), channel_id=1, source_target_pairs={{1,0},{2,1},{3,2},{4,3},{5,4},{6,5},{7,6},{8,7},{9,8},{10,9},{11,1... | collective-permute-start | bytes 1572872 | tf_op jit(solution)/shard_map/ppermute | solution.py:21
  139.4 1.9 collective-permute-start.7
  141.4 13.8 %shard_map.48.refs_7_ = f32[256,8,128]{2,1,0:T(8,128)} custom-call(f32[81]{0:T(128)} %reshape.16.taps_ref, f32[256,4,128]{2,1,0:T(4,128)} %collective-permute-done.3.before_ref, f32[256,8,128]{2,1,0:T(8,128)} %copy-done.3, f32[256,4,128]{2,1,0:T(4,128)} %collective-permute-done.4.after_ref, bf16[256,8,128]{2,1,0:T(8,128)(2,1)} %bitcast.19), custom_call_target="tpu_custom_call" | custom-call | tf_op jit(solution)/shard_map/pallas_call | solution.py:118
  155.2 1.7 fusion.13
  156.9 9.1 %collective-permute-start.10 = (f32[256,4,128]{2,1,0:T(4,128)S(1)}, f32[256,4,128]{2,1,0:T(4,128)S(1)}, u32[]{:S(2)}, u32[]{:S(2)}) collective-permute-start(f32[256,4,128]{2,1,0:T(4,128)S(1)} %get-tuple-element.20), channel_id=1, source_target_pairs={{1,0},{2,1},{3,2},{4,3},{5,4},{6,5},{7,6},{8,7},{9,8},{10,9},{11,1... | collective-permute-start | bytes 1572872 | tf_op jit(solution)/shard_map/ppermute | solution.py:21
  166.0 1.9 collective-permute-start.9
  168.0 6.9 %collective-permute-done.10.refs_8_ = f32[256,4,128]{2,1,0:T(4,128)S(1)} collective-permute-done((f32[256,4,128]{2,1,0:T(4,128)S(1)}, f32[256,4,128]{2,1,0:T(4,128)S(1)}, u32[]{:S(2)}, u32[]{:S(2)}) %collective-permute-start.10) | collective-permute-done | bytes 524320 | tf_op jit(solution)/shard_map/ppermute | solution.py:21
  175.6 8.9 %collective-permute-done.9.refs_6_ = f32[256,4,128]{2,1,0:T(4,128)} collective-permute-done((f32[256,4,128]{2,1,0:T(4,128)S(1)}, f32[256,4,128]{2,1,0:T(4,128)}, u32[]{:S(2)}, u32[]{:S(2)}) %collective-permute-start.9) | collective-permute-done | bytes 524320 | tf_op jit(solution)/shard_map/ppermute | solution.py:20
  184.5 6.9 %shard_map.49 = f32[256,8,128]{2,1,0:T(8,128)} custom-call(f32[81]{0:T(128)} %reshape.16.taps_ref, f32[256,4,128]{2,1,0:T(4,128)} %collective-permute-done.5.refs_0_, f32[256,8,128]{2,1,0:T(8,128)} %shard_map.46.refs_1_, f32[256,4,128]{2,1,0:T(4,128)} %collective-permute-done.6.refs_2_, f32[256,4,128]{2,1,0:T(4,128)} %collective-permute-done.7.refs_3_, ...), custom_call_target="tpu_custom_call" | custom-call | tf_op jit(solution)/shard_map/pallas_call | solution.py:155
  192.5 3.6 %collective-permute-start.11 = (f32[128,8,128]{2,1,0:T(8,128)S(1)}, f32[128,8,128]{2,1,0:T(8,128)S(1)}, u32[]{:S(2)}, u32[]{:S(2)}) collective-permute-start(f32[128,8,128]{2,1,0:T(8,128)S(1)} %constant_dynamic-slice_fusion.1), channel_id=1, source_target_pairs={{0,32},{32,0},{64,96},{96,64},{1,33},{33,1},{65,97},{97,65},{2,34}... | collective-permute-start | bytes 1572872 | tf_op jit(solution)/shard_map/ppermute | solution.py:173
  199.8 12.2 %collective-permute-done.12 = f32[128,8,128]{2,1,0:T(8,128)S(1)} collective-permute-done((f32[128,8,128]{2,1,0:T(8,128)S(1)}, f32[128,8,128]{2,1,0:T(8,128)S(1)}, u32[]{:S(2)}, u32[]{:S(2)}) %collective-permute-start.12) | collective-permute-done | bytes 524320 | tf_op jit(solution)/shard_map/ppermute | solution.py:174
  215.4 1.9 collective-permute-start.15
  217.3 3.4 collective-permute-start.14
  220.7 9.8 %collective-permute-done.15.after_ref = f32[256,4,128]{2,1,0:T(4,128)S(1)} collective-permute-done((f32[256,4,128]{2,1,0:T(4,128)S(1)}, f32[256,4,128]{2,1,0:T(4,128)S(1)}, u32[]{:S(2)}, u32[]{:S(2)}) %collective-permute-start.15) | collective-permute-done | bytes 524320 | tf_op jit(solution)/shard_map/ppermute | solution.py:21
  230.5 7.7 %collective-permute-done.14.before_ref = f32[256,4,128]{2,1,0:T(4,128)} collective-permute-done((f32[256,4,128]{2,1,0:T(4,128)S(1)}, f32[256,4,128]{2,1,0:T(4,128)}, u32[]{:S(2)}, u32[]{:S(2)}) %collective-permute-start.14) | collective-permute-done | bytes 524320 | tf_op jit(solution)/shard_map/ppermute | solution.py:20
  238.2 13.8 %shard_map.50.refs_1_ = f32[256,8,128]{2,1,0:T(8,128)} custom-call(f32[81]{0:T(128)} %reshape.16.taps_ref, f32[256,4,128]{2,1,0:T(4,128)} %collective-permute-done.14.before_ref, f32[256,8,128]{2,1,0:T(8,128)} %copy-done.1, f32[256,4,128]{2,1,0:T(4,128)} %copy-done.9, bf16[256,8,128]{2,1,0:T(8,128)(2,1)} %bitcast.24), custom_call_target="tpu_custom_call" | custom-call | tf_op jit(solution)/shard_map/pallas_call | solution.py:118
  252.0 1.7 fusion.11
  253.7 1.9 collective-permute-start.17
  255.7 3.4 collective-permute-start.16
  259.0 13.8 %shard_map.51.refs_4_ = f32[256,8,128]{2,1,0:T(8,128)} custom-call(f32[81]{0:T(128)} %reshape.16.taps_ref, f32[256,4,128]{2,1,0:T(4,128)} %collective-permute-done.14.before_ref, f32[256,8,128]{2,1,0:T(8,128)} %copy-done.1, f32[256,4,128]{2,1,0:T(4,128)} %copy-done.9, bf16[256,8,128]{2,1,0:T(8,128)(2,1)} %bitcast.22), custom_call_target="tpu_custom_call" | custom-call | tf_op jit(solution)/shard_map/pallas_call | solution.py:118
  272.8 2.5 fusion.10
  275.3 7.6 %collective-permute-start.19 = (f32[256,4,128]{2,1,0:T(4,128)}, f32[256,4,128]{2,1,0:T(4,128)}, u32[]{:S(2)}, u32[]{:S(2)}) collective-permute-start(f32[256,4,128]{2,1,0:T(4,128)} %get-tuple-element.12), channel_id=1, source_target_pairs={{1,0},{2,1},{3,2},{4,3},{5,4},{6,5},{7,6},{8,7},{9,8},{10,9},{11,1... | collective-permute-start | bytes 1572872 | tf_op jit(solution)/shard_map/ppermute | solution.py:21
  283.0 1.9 collective-permute-start.18
  284.9 13.8 %shard_map.52.refs_7_ = f32[256,8,128]{2,1,0:T(8,128)} custom-call(f32[81]{0:T(128)} %reshape.16.taps_ref, f32[256,4,128]{2,1,0:T(4,128)} %collective-permute-done.14.before_ref, f32[256,8,128]{2,1,0:T(8,128)} %copy-done.1, f32[256,4,128]{2,1,0:T(4,128)} %copy-done.9, bf16[256,8,128]{2,1,0:T(8,128)(2,1)} %bitcast.20), custom_call_target="tpu_custom_call" | custom-call | tf_op jit(solution)/shard_map/pallas_call | solution.py:118
  300.4 9.1 %collective-permute-start.21 = (f32[256,4,128]{2,1,0:T(4,128)S(1)}, f32[256,4,128]{2,1,0:T(4,128)S(1)}, u32[]{:S(2)}, u32[]{:S(2)}) collective-permute-start(f32[256,4,128]{2,1,0:T(4,128)S(1)} %get-tuple-element.10), channel_id=1, source_target_pairs={{1,0},{2,1},{3,2},{4,3},{5,4},{6,5},{7,6},{8,7},{9,8},{10,9},{11,1... | collective-permute-start | bytes 1572872 | tf_op jit(solution)/shard_map/ppermute | solution.py:21
  309.5 1.9 collective-permute-start.20
  311.5 7.2 %collective-permute-done.21.refs_8_ = f32[256,4,128]{2,1,0:T(4,128)S(1)} collective-permute-done((f32[256,4,128]{2,1,0:T(4,128)S(1)}, f32[256,4,128]{2,1,0:T(4,128)S(1)}, u32[]{:S(2)}, u32[]{:S(2)}) %collective-permute-start.21) | collective-permute-done | bytes 524320 | tf_op jit(solution)/shard_map/ppermute | solution.py:21
  319.5 8.8 %collective-permute-done.20.refs_6_ = f32[256,4,128]{2,1,0:T(4,128)S(1)} collective-permute-done((f32[256,4,128]{2,1,0:T(4,128)S(1)}, f32[256,4,128]{2,1,0:T(4,128)S(1)}, u32[]{:S(2)}, u32[]{:S(2)}) %collective-permute-start.20) | collective-permute-done | bytes 524320 | tf_op jit(solution)/shard_map/ppermute | solution.py:20
  329.0 6.9 %shard_map.53 = f32[256,8,128]{2,1,0:T(8,128)} custom-call(f32[81]{0:T(128)} %reshape.16.taps_ref, f32[256,4,128]{2,1,0:T(4,128)} %collective-permute-done.16.refs_0_, f32[256,8,128]{2,1,0:T(8,128)} %shard_map.50.refs_1_, f32[256,4,128]{2,1,0:T(4,128)} %collective-permute-done.17.refs_2_, f32[256,4,128]{2,1,0:T(4,128)} %collective-permute-done.18.refs_3_, ...), custom_call_target="tpu_custom_call" | custom-call | tf_op jit(solution)/shard_map/pallas_call | solution.py:155
  337.1 3.3 collective-permute-start.22
  344.0 12.2 %collective-permute-done.23 = f32[128,8,128]{2,1,0:T(8,128)S(1)} collective-permute-done((f32[128,8,128]{2,1,0:T(8,128)S(1)}, f32[128,8,128]{2,1,0:T(8,128)S(1)}, u32[]{:S(2)}, u32[]{:S(2)}) %collective-permute-start.23) | collective-permute-done | bytes 524320 | tf_op jit(solution)/shard_map/ppermute | solution.py:174
  (75 shorter events, 34.9 us)
Async XLA Ops:
  0.0 7.1 %copy-start = (bf16[3,8,256,128]{3,2,1,0:T(8,128)(2,1)S(1)}, bf16[3,8,256,128]{3,2,1,0:T(8,128)(2,1)}, u32[]{:S(2)}) copy-start(bf16[3,8,256,128]{3,2,1,0:T(8,128)(2,1)} %param.4) | copy-start | bytes 4718596
  10.7 30.4 %all-to-all-start = ((bf16[3,8,256,128]{3,1,0,2:T(8,128)(2,1)}), bf16[3,8,256,128]{3,1,0,2:T(8,128)(2,1)S(1)}, u32[]{:S(2)}, u32[]{:S(2)}) async-start(bf16[3,8,256,128]{3,1,0,2:T(8,128)(2,1)} %copy.11), calls=%async_computation | async-start | bytes 3145728 | tf_op jit(solution)/shard_map/all_to_all | solution.py:189
  41.7 1.3 copy-start.4
  41.7 1.3 copy-start.5
  41.7 1.3 copy-start.6
  43.0 5.3 %collective-permute-start = (f32[128,8,128]{2,1,0:T(8,128)}, f32[128,8,128]{2,1,0:T(8,128)}, u32[]{:S(2)}, u32[]{:S(2)}) collective-permute-start(f32[128,8,128]{2,1,0:T(8,128)} %constant_dynamic-slice_fusion.2), channel_id=1, source_target_pairs={{0,32},{32,0},{64,96},{96,64},{1,33},{33,1},{65,97},{97,65},{2,34}... | collective-permute-start | bytes 1572872 | tf_op jit(solution)/shard_map/ppermute | solution.py:173
  49.4 13.2 %collective-permute-start.1 = (f32[128,8,128]{2,1,0:T(8,128)S(1)}, f32[128,8,128]{2,1,0:T(8,128)S(1)}, u32[]{:S(2)}, u32[]{:S(2)}) collective-permute-start(f32[128,8,128]{2,1,0:T(8,128)S(1)} %dynamic-slice_add_fusion.2), channel_id=1, source_target_pairs={{0,64},{32,96},{64,0},{96,32},{1,65},{33,97},{65,1},{97,33},{2,66}... | collective-permute-start | bytes 1572872 | tf_op jit(solution)/shard_map/ppermute | solution.py:174
  62.7 2.8 collective-permute-start.2
  65.6 0.8 copy-start.7
  66.5 27.3 %copy-start.3 = (f32[256,8,128]{2,1,0:T(8,128)}, f32[256,8,128]{2,1,0:T(8,128)S(1)}, u32[]{:S(2)}) copy-start(f32[256,8,128]{2,1,0:T(8,128)S(1)} %maximum_multiply_fusion.mid_ref) | copy-start | bytes 3145732
  66.6 8.5 %copy-start.13 = (f32[3,3,9]{2,1,0:T(4,128)S(1)}, f32[3,3,9]{2,1,0:T(4,128)}, u32[]{:S(2)}) copy-start(f32[3,3,9]{2,1,0:T(4,128)} %param.7) | copy-start | bytes 976
  67.9 16.4 %collective-permute-start.4 = (f32[256,4,128]{2,1,0:T(4,128)}, f32[256,4,128]{2,1,0:T(4,128)}, u32[]{:S(2)}, u32[]{:S(2)}) collective-permute-start(f32[256,4,128]{2,1,0:T(4,128)} %get-tuple-element.26), channel_id=1, source_target_pairs={{1,0},{2,1},{3,2},{4,3},{5,4},{6,5},{7,6},{8,7},{9,8},{10,9},{11,1... | collective-permute-start | bytes 1572872 | tf_op jit(solution)/shard_map/ppermute | solution.py:21
  73.1 20.7 %collective-permute-start.3 = (f32[256,4,128]{2,1,0:T(4,128)}, f32[256,4,128]{2,1,0:T(4,128)}, u32[]{:S(2)}, u32[]{:S(2)}) collective-permute-start(f32[256,4,128]{2,1,0:T(4,128)} %get-tuple-element.27), channel_id=1, source_target_pairs={{0,1},{1,2},{2,3},{3,4},{4,5},{5,6},{6,7},{7,8},{8,9},{9,10},{10,1... | collective-permute-start | bytes 1572872 | tf_op jit(solution)/shard_map/ppermute | solution.py:20
  110.2 55.8 %collective-permute-start.6 = (f32[256,4,128]{2,1,0:T(4,128)}, f32[256,4,128]{2,1,0:T(4,128)}, u32[]{:S(2)}, u32[]{:S(2)}) collective-permute-start(f32[256,4,128]{2,1,0:T(4,128)} %get-tuple-element.24), channel_id=1, source_target_pairs={{1,0},{2,1},{3,2},{4,3},{5,4},{6,5},{7,6},{8,7},{9,8},{10,9},{11,1... | collective-permute-start | bytes 1572872 | tf_op jit(solution)/shard_map/ppermute | solution.py:21
  112.1 55.8 %collective-permute-start.5 = (f32[256,4,128]{2,1,0:T(4,128)S(1)}, f32[256,4,128]{2,1,0:T(4,128)}, u32[]{:S(2)}, u32[]{:S(2)}) collective-permute-start(f32[256,4,128]{2,1,0:T(4,128)S(1)} %get-tuple-element.25), channel_id=1, source_target_pairs={{0,1},{1,2},{2,3},{3,4},{4,5},{5,6},{6,7},{7,8},{8,9},{9,10},{10,1... | collective-permute-start | bytes 1572872 | tf_op jit(solution)/shard_map/ppermute | solution.py:20
  131.8 36.1 %collective-permute-start.8 = (f32[256,4,128]{2,1,0:T(4,128)}, f32[256,4,128]{2,1,0:T(4,128)}, u32[]{:S(2)}, u32[]{:S(2)}) collective-permute-start(f32[256,4,128]{2,1,0:T(4,128)} %get-tuple-element.22), channel_id=1, source_target_pairs={{1,0},{2,1},{3,2},{4,3},{5,4},{6,5},{7,6},{8,7},{9,8},{10,9},{11,1... | collective-permute-start | bytes 1572872 | tf_op jit(solution)/shard_map/ppermute | solution.py:21
  139.4 28.5 %collective-permute-start.7 = (f32[256,4,128]{2,1,0:T(4,128)S(1)}, f32[256,4,128]{2,1,0:T(4,128)}, u32[]{:S(2)}, u32[]{:S(2)}) collective-permute-start(f32[256,4,128]{2,1,0:T(4,128)S(1)} %get-tuple-element.23), channel_id=1, source_target_pairs={{0,1},{1,2},{2,3},{3,4},{4,5},{5,6},{6,7},{7,8},{8,9},{9,10},{10,1... | collective-permute-start | bytes 1572872 | tf_op jit(solution)/shard_map/ppermute | solution.py:20
  156.9 17.9 %collective-permute-start.10 = (f32[256,4,128]{2,1,0:T(4,128)S(1)}, f32[256,4,128]{2,1,0:T(4,128)S(1)}, u32[]{:S(2)}, u32[]{:S(2)}) collective-permute-start(f32[256,4,128]{2,1,0:T(4,128)S(1)} %get-tuple-element.20), channel_id=1, source_target_pairs={{1,0},{2,1},{3,2},{4,3},{5,4},{6,5},{7,6},{8,7},{9,8},{10,9},{11,1... | collective-permute-start | bytes 1572872 | tf_op jit(solution)/shard_map/ppermute | solution.py:21
  166.0 18.5 %collective-permute-start.9 = (f32[256,4,128]{2,1,0:T(4,128)S(1)}, f32[256,4,128]{2,1,0:T(4,128)}, u32[]{:S(2)}, u32[]{:S(2)}) collective-permute-start(f32[256,4,128]{2,1,0:T(4,128)S(1)} %get-tuple-element.21), channel_id=1, source_target_pairs={{0,1},{1,2},{2,3},{3,4},{4,5},{5,6},{6,7},{7,8},{8,9},{9,10},{10,1... | collective-permute-start | bytes 1572872 | tf_op jit(solution)/shard_map/ppermute | solution.py:20
  174.8 0.8 copy-start.11
  192.5 5.2 %collective-permute-start.11 = (f32[128,8,128]{2,1,0:T(8,128)S(1)}, f32[128,8,128]{2,1,0:T(8,128)S(1)}, u32[]{:S(2)}, u32[]{:S(2)}) collective-permute-start(f32[128,8,128]{2,1,0:T(8,128)S(1)} %constant_dynamic-slice_fusion.1), channel_id=1, source_target_pairs={{0,32},{32,0},{64,96},{96,64},{1,33},{33,1},{65,97},{97,65},{2,34}... | collective-permute-start | bytes 1572872 | tf_op jit(solution)/shard_map/ppermute | solution.py:173
  198.8 16.2 %copy-start.8 = (f32[128,8,128]{2,1,0:T(8,128)S(1)}, f32[128,8,128]{2,1,0:T(8,128)}, u32[]{:S(2)}) copy-start(f32[128,8,128]{2,1,0:T(8,128)} %copy-done.7) | copy-start | bytes 1572868
  198.8 13.2 %collective-permute-start.12 = (f32[128,8,128]{2,1,0:T(8,128)S(1)}, f32[128,8,128]{2,1,0:T(8,128)S(1)}, u32[]{:S(2)}, u32[]{:S(2)}) collective-permute-start(f32[128,8,128]{2,1,0:T(8,128)S(1)} %dynamic-slice_add_fusion.1), channel_id=1, source_target_pairs={{0,64},{32,96},{64,0},{96,32},{1,65},{33,97},{65,1},{97,33},{2,66}... | collective-permute-start | bytes 1572872 | tf_op jit(solution)/shard_map/ppermute | solution.py:174
  212.1 2.8 collective-permute-start.13
  215.2 23.0 %copy-start.1 = (f32[256,8,128]{2,1,0:T(8,128)}, f32[256,8,128]{2,1,0:T(8,128)S(1)}, u32[]{:S(2)}) copy-start(f32[256,8,128]{2,1,0:T(8,128)S(1)} %fusion.4.mid_ref) | copy-start | bytes 3145732
  215.4 15.1 %collective-permute-start.15 = (f32[256,4,128]{2,1,0:T(4,128)S(1)}, f32[256,4,128]{2,1,0:T(4,128)S(1)}, u32[]{:S(2)}, u32[]{:S(2)}) collective-permute-start(f32[256,4,128]{2,1,0:T(4,128)S(1)} %get-tuple-element.16), channel_id=1, source_target_pairs={{1,0},{2,1},{3,2},{4,3},{5,4},{6,5},{7,6},{8,7},{9,8},{10,9},{11,1... | collective-permute-start | bytes 1572872 | tf_op jit(solution)/shard_map/ppermute | solution.py:21
  217.3 20.9 %collective-permute-start.14 = (f32[256,4,128]{2,1,0:T(4,128)S(1)}, f32[256,4,128]{2,1,0:T(4,128)}, u32[]{:S(2)}, u32[]{:S(2)}) collective-permute-start(f32[256,4,128]{2,1,0:T(4,128)S(1)} %get-tuple-element.17), channel_id=1, source_target_pairs={{0,1},{1,2},{2,3},{3,4},{4,5},{5,6},{6,7},{7,8},{8,9},{9,10},{10,1... | collective-permute-start | bytes 1572872 | tf_op jit(solution)/shard_map/ppermute | solution.py:20
  230.5 7.7 %copy-start.9 = (f32[256,4,128]{2,1,0:T(4,128)}, f32[256,4,128]{2,1,0:T(4,128)S(1)}, u32[]{:S(2)}) copy-start(f32[256,4,128]{2,1,0:T(4,128)S(1)} %collective-permute-done.15.after_ref) | copy-start | bytes 1572868
  253.7 55.8 %collective-permute-start.17 = (f32[256,4,128]{2,1,0:T(4,128)S(1)}, f32[256,4,128]{2,1,0:T(4,128)}, u32[]{:S(2)}, u32[]{:S(2)}) collective-permute-start(f32[256,4,128]{2,1,0:T(4,128)S(1)} %get-tuple-element.14), channel_id=1, source_target_pairs={{1,0},{2,1},{3,2},{4,3},{5,4},{6,5},{7,6},{8,7},{9,8},{10,9},{11,1... | collective-permute-start | bytes 1572872 | tf_op jit(solution)/shard_map/ppermute | solution.py:21
  255.7 55.8 %collective-permute-start.16 = (f32[256,4,128]{2,1,0:T(4,128)S(1)}, f32[256,4,128]{2,1,0:T(4,128)}, u32[]{:S(2)}, u32[]{:S(2)}) collective-permute-start(f32[256,4,128]{2,1,0:T(4,128)S(1)} %get-tuple-element.15), channel_id=1, source_target_pairs={{0,1},{1,2},{2,3},{3,4},{4,5},{5,6},{6,7},{7,8},{8,9},{9,10},{10,1... | collective-permute-start | bytes 1572872 | tf_op jit(solution)/shard_map/ppermute | solution.py:20
  275.3 36.1 %collective-permute-start.19 = (f32[256,4,128]{2,1,0:T(4,128)}, f32[256,4,128]{2,1,0:T(4,128)}, u32[]{:S(2)}, u32[]{:S(2)}) collective-permute-start(f32[256,4,128]{2,1,0:T(4,128)} %get-tuple-element.12), channel_id=1, source_target_pairs={{1,0},{2,1},{3,2},{4,3},{5,4},{6,5},{7,6},{8,7},{9,8},{10,9},{11,1... | collective-permute-start | bytes 1572872 | tf_op jit(solution)/shard_map/ppermute | solution.py:21
  283.0 28.5 %collective-permute-start.18 = (f32[256,4,128]{2,1,0:T(4,128)S(1)}, f32[256,4,128]{2,1,0:T(4,128)}, u32[]{:S(2)}, u32[]{:S(2)}) collective-permute-start(f32[256,4,128]{2,1,0:T(4,128)S(1)} %get-tuple-element.13), channel_id=1, source_target_pairs={{0,1},{1,2},{2,3},{3,4},{4,5},{5,6},{6,7},{7,8},{8,9},{9,10},{10,1... | collective-permute-start | bytes 1572872 | tf_op jit(solution)/shard_map/ppermute | solution.py:20
  300.4 18.2 %collective-permute-start.21 = (f32[256,4,128]{2,1,0:T(4,128)S(1)}, f32[256,4,128]{2,1,0:T(4,128)S(1)}, u32[]{:S(2)}, u32[]{:S(2)}) collective-permute-start(f32[256,4,128]{2,1,0:T(4,128)S(1)} %get-tuple-element.10), channel_id=1, source_target_pairs={{1,0},{2,1},{3,2},{4,3},{5,4},{6,5},{7,6},{8,7},{9,8},{10,9},{11,1... | collective-permute-start | bytes 1572872 | tf_op jit(solution)/shard_map/ppermute | solution.py:21
  309.5 18.7 %collective-permute-start.20 = (f32[256,4,128]{2,1,0:T(4,128)S(1)}, f32[256,4,128]{2,1,0:T(4,128)S(1)}, u32[]{:S(2)}, u32[]{:S(2)}) collective-permute-start(f32[256,4,128]{2,1,0:T(4,128)S(1)} %get-tuple-element.11), channel_id=1, source_target_pairs={{0,1},{1,2},{2,3},{3,4},{4,5},{5,6},{6,7},{7,8},{8,9},{9,10},{10,1... | collective-permute-start | bytes 1572872 | tf_op jit(solution)/shard_map/ppermute | solution.py:20
  318.7 0.8 copy-start.10
  328.2 0.8 copy-start.12
  337.1 4.9 %collective-permute-start.22 = (f32[128,8,128]{2,1,0:T(8,128)S(1)}, f32[128,8,128]{2,1,0:T(8,128)S(1)}, u32[]{:S(2)}, u32[]{:S(2)}) collective-permute-start(f32[128,8,128]{2,1,0:T(8,128)S(1)} %constant_dynamic-slice_fusion), channel_id=1, source_target_pairs={{0,32},{32,0},{64,96},{96,64},{1,33},{33,1},{65,97},{97,65},{2,34}... | collective-permute-start | bytes 1572872 | tf_op jit(solution)/shard_map/ppermute | solution.py:173
  343.0 16.2 %copy-start.2 = (f32[256,8,128]{2,1,0:T(8,128)S(1)}, f32[256,8,128]{2,1,0:T(8,128)}, u32[]{:S(2)}) copy-start(f32[256,8,128]{2,1,0:T(8,128)} %copy-done.1) | copy-start | bytes 3145732
  343.1 13.2 %collective-permute-start.23 = (f32[128,8,128]{2,1,0:T(8,128)S(1)}, f32[128,8,128]{2,1,0:T(8,128)S(1)}, u32[]{:S(2)}, u32[]{:S(2)}) collective-permute-start(f32[128,8,128]{2,1,0:T(8,128)S(1)} %dynamic-slice_add_fusion), channel_id=1, source_target_pairs={{0,64},{32,96},{64,0},{96,32},{1,65},{33,97},{65,1},{97,33},{2,66}... | collective-permute-start | bytes 1572872 | tf_op jit(solution)/shard_map/ppermute | solution.py:174
  356.3 2.8 collective-permute-start.24

commit v4 on v3

--- a/solution.py
+++ b/solution.py
@@ -66,7 +66,9 @@
     return acc
 
 
-def _forward_kernel(v, taps_ref, before_ref, mid_ref, after_ref, brick_ref, out_ref, a_ref, c_ref, est_ref):
+def _forward_kernel(
+    v, taps_ref, toeplitz_ref, before_ref, mid_ref, after_ref, brick_ref, out_ref, a_ref, c_ref, est_ref
+):
     nz, _, ny = out_ref.shape
     tx = [taps_ref[v * 27 + 9 + t] for t in range(9)]
     tz = [taps_ref[v * 27 + t] for t in range(9)]
@@ -87,17 +89,22 @@
         return carry
 
     lax.fori_loop(0, nz // CZ, along_x, 0)
-    wy = _lane_weights(ty, ny, False)
-    wy_rev = _lane_weights(ty, ny, True)
+    forward_y = toeplitz_ref[0]
+    back_y = toeplitz_ref[1]
+
+    def along_y(f, matrix):
+        flat = f.reshape(CZ * f.shape[1], ny)
+        out = jnp.dot(flat, matrix, precision=lax.Precision.HIGHEST, preferred_element_type=jnp.float32)
+        return out.reshape(f.shape)
 
     def middle(c, carry):
         z0 = pl.multiple_of(c * CZ, CZ)
         acc = tz[0] * a_ref[pl.ds(z0, CZ)]
         for t in range(1, 9):
             acc = acc + tz[t] * a_ref[pl.ds(z0 + t, CZ)]
-        blurred = _lane_correlate(acc, wy)
+        blurred = along_y(acc, forward_y)
         ratio = brick_ref[pl.ds(z0, CZ)].astype(jnp.float32) / blurred
-        c_ref[pl.ds(z0 + 4, CZ)] = _lane_correlate(ratio, wy_rev)
+        c_ref[pl.ds(z0 + 4, CZ)] = along_y(ratio, back_y)
         return carry
 
     lax.fori_loop(0, nz // CZ, middle, 0)
@@ -113,11 +120,20 @@
     lax.fori_loop(0, nz // CZ, along_z_back, 0)
 
 
+def toeplitz_pair(taps_y, ny):
+    rows = jnp.arange(ny, dtype=jnp.int32)
+    lag = rows[:, None] - rows[None, :] + 4
+    inside = (lag >= 0) & (lag <= 8)
+    matrix = jnp.where(inside, taps_y[jnp.clip(lag, 0, 8)], 0.0)
+    return jnp.stack([matrix, matrix.T])
+
+
 def forward_partial(taps_flat, v, before, mid, after, brick):
     nz, width, ny = brick.shape
+    toeplitz = toeplitz_pair(taps_flat[v * 27 + 18 : v * 27 + 27], ny)
     return pl.pallas_call(
         functools.partial(_forward_kernel, v),
-        in_specs=[pl.BlockSpec(memory_space=pltpu.SMEM)] + [pl.BlockSpec(memory_space=pltpu.VMEM)] * 4,
+        in_specs=[pl.BlockSpec(memory_space=pltpu.SMEM)] + [pl.BlockSpec(memory_space=pltpu.VMEM)] * 5,
         out_specs=pl.BlockSpec(memory_space=pltpu.VMEM),
         out_shape=jax.ShapeDtypeStruct((nz, width, ny), jnp.float32),
         scratch_shapes=[
@@ -125,7 +141,7 @@
             pltpu.VMEM((nz + 8, width, ny), jnp.float32),
             pltpu.VMEM((CZ, width + 8, ny), jnp.float32),
         ],
-    )(taps_flat, before, mid, after, brick)
+    )(taps_flat, toeplitz, before, mid, after, brick)
 
 
 def _back_kernel(taps_ref, *refs):

time: 362 us -> 406 us (1.12)
  other arithmetic: 12.4 us -> 48.1 us
  Pallas kernels: 96.7 us -> 127 us
  waiting for transfers between devices: 133 us -> 112 us
    pallas_call x6, Pallas kernels: 82.8 us -> 113 us  [forward_partial(): pl.pallas_call(functools.partial(_forward_kernel, v), in_specs=[pl.BlockS...]
    select_n x0 -> x3, other arithmetic: none -> 16.9 us  [toeplitz_pair(): matrix = jnp.where(inside, taps_y[jnp.clip(lag, 0, 8)], 0.0)]
    gather x0 -> x3, other arithmetic: none -> 16.8 us  [toeplitz_pair(): matrix = jnp.where(inside, taps_y[jnp.clip(lag, 0, 8)], 0.0)]
    ppermute x3, waiting for transfers between devices: 36.7 us -> 23.7 us  [view_sum(): own = own + lax.ppermute(own, 'view', chip_swap)]
    ppermute x8, waiting for transfers between devices: 32.4 us -> 25.9 us  [halos(): after = lax.ppermute(first, axis, down)]
  transfers between devices with their start and end apart: 26 -> 26, of which waited for: 18 -> 17; matrix products, arithmetic and copies ran while one was open for 3% -> 11% of each run, Pallas kernels for 15% -> 19%
where the time goes in v4:
time: 406 us; the launch traced here: 404 us
  Pallas kernels  127 us (31%)
  waiting for transfers between devices  112 us (28%)
  starting transfers between devices  91.8 us (23%)
  other arithmetic  48.1 us (12%)
  local copies, waits for them, and re-layouts  24.2 us (6%)
    pallas_call x6, Pallas kernels, forward_partial(): pl.pallas_call(functools.partial(_forward_kernel, v), in_specs=[pl.BlockS...  113 us
    ppermute x8, starting transfers between devices, halos(): after = lax.ppermute(first, axis, down)  43.8 us
    ppermute x8, waiting for transfers between devices, halos(): before = lax.ppermute(last, axis, up)  34.9 us
    ppermute x8, waiting for transfers between devices, halos(): after = lax.ppermute(first, axis, down)  25.9 us
    ppermute x3, waiting for transfers between devices, view_sum(): own = own + lax.ppermute(own, 'view', chip_swap)  23.7 us
    all_to_all x1, waiting for transfers between devices, per_device(): lax.all_to_all(local_views, 'vol', split_axis=2, concat_axis=1, tiled=True)  19.8 us
    ppermute x8, starting transfers between devices, halos(): before = lax.ppermute(last, axis, up)  19.7 us
    select_n x3, other arithmetic, toeplitz_pair(): matrix = jnp.where(inside, taps_y[jnp.clip(lag, 0, 8)], 0.0)  16.9 us
  transfers between devices with their start and end apart: 26, of which 17 were waited for; matrix products, arithmetic and copies ran while one was open for 11% of the time, Pallas kernels for 19%

profile of v4, /device:TPU:5, one launch (start us, length us, event | category | flops | bytes accessed | tf_op | source)
XLA Modules:
  0.0 404.2 jit_solution(7349916420486902185)
XLA Ops:
  2.7 4.4 %select_reduce_fusion = f32[3,256,256]{2,1,0:T(8,128)S(1)} fusion(f32[3,256,8]{2,1,0:T(8,128)S(1)} %copy.16, s32[3,256,8]{2,1,0:T(8,128)S(1)} %iota_add_fusion), kind=kLoop, calls=%fused_computation.1 | loop fusion | flops 4521984 | bytes 835584 | tf_op jit(solution)/shard_map/reduce_sum | solution.py:38
  8.5 2.2 copy.17
  10.7 10.5 %all-to-all-start = ((bf16[3,8,256,128]{3,1,0,2:T(8,128)(2,1)}), bf16[3,8,256,128]{3,1,0,2:T(8,128)(2,1)S(1)}, u32[]{:S(2)}, u32[]{:S(2)}) async-start(bf16[3,8,256,128]{3,1,0,2:T(8,128)(2,1)} %copy.17), calls=%async_computation | async-start | bytes 3145728 | tf_op jit(solution)/shard_map/all_to_all | solution.py:205
  21.3 19.8 %all-to-all-done = bf16[3,8,256,128]{3,1,0,2:T(8,128)(2,1)S(1)} async-done(((bf16[3,8,256,128]{3,1,0,2:T(8,128)(2,1)}), bf16[3,8,256,128]{3,1,0,2:T(8,128)(2,1)S(1)}, u32[]{:S(2)}, u32[]{:S(2)}) %all-to-all-start) | async-done | bytes 1572896 | tf_op jit(solution)/shard_map/all_to_all | solution.py:205
  43.0 3.4 collective-permute-start
  50.4 5.5 %fusion.29 = f32[128,128]{0,1:T(8,128)S(1)} fusion(f32[]{:T(128)} %bitcast.44, f32[]{:T(128)} %bitcast.43, f32[]{:T(128)} %bitcast.42, f32[]{:T(128)} %bitcast.41, f32[]{:T(128)} %bitcast.40, f32[]{:T(128)} %bitcast.39, f32[]{:T(128)} %bitcast.38, f32[]{:T(128)} %bitcast.37, f32[]{:T(128)} %bitcast.36), kind=kLoop, calls=%fused_computation.62 | loop fusion | flops 360448 | bytes 65572 | tf_op jit(solution)/shard_map/gather | solution.py:127
  56.0 5.7 %fusion.28 = f32[128,128]{0,1:T(8,128)S(1)} fusion(f32[]{:T(128)} %bitcast.31, f32[]{:T(128)} %bitcast.30, f32[]{:T(128)} %bitcast.29, f32[]{:T(128)} %bitcast.28, f32[]{:T(128)} %bitcast.27, f32[]{:T(128)} %bitcast.26, f32[]{:T(128)} %bitcast.25, f32[]{:T(128)} %bitcast.24, f32[]{:T(128)} %bitcast.23), kind=kLoop, calls=%fused_computation.61 | loop fusion | flops 360448 | bytes 65572 | tf_op jit(solution)/shard_map/gather | solution.py:127
  61.8 5.7 %fusion.11 = f32[128,128]{1,0:T(8,128)S(1)} fusion(f32[]{:T(128)} %bitcast.12, f32[]{:T(128)} %bitcast.13, f32[]{:T(128)} %bitcast.14, f32[]{:T(128)} %bitcast.15, f32[]{:T(128)} %bitcast.16, f32[]{:T(128)} %bitcast.18, f32[]{:T(128)} %bitcast.17, f32[]{:T(128)} %bitcast.9, f32[]{:T(128)} %bitcast.11), kind=kLoop, calls=%fused_computation.40 | loop fusion | flops 360448 | bytes 65572 | tf_op jit(solution)/shard_map/gather | solution.py:127
  67.6 5.5 %bitcast_select_fusion = f32[1,128,128]{2,1,0:T(8,128)S(1)} fusion(f32[]{:T(128)} %bitcast.44, f32[]{:T(128)} %bitcast.43, f32[]{:T(128)} %bitcast.42, f32[]{:T(128)} %bitcast.41, f32[]{:T(128)} %bitcast.40, f32[]{:T(128)} %bitcast.39, f32[]{:T(128)} %bitcast.38, f32[]{:T(128)} %bitcast.37, f32[]{:T(128)} %bitcast.36), kind=kLoop, calls=%fused_computation.30 | loop fusion | flops 458752 | bytes 65572 | tf_op jit(solution)/shard_map/jit(_where)/select_n | solution.py:127
  73.1 5.7 %bitcast_select_fusion.2 = f32[1,128,128]{2,1,0:T(8,128)S(1)} fusion(f32[]{:T(128)} %bitcast.31, f32[]{:T(128)} %bitcast.30, f32[]{:T(128)} %bitcast.29, f32[]{:T(128)} %bitcast.28, f32[]{:T(128)} %bitcast.27, f32[]{:T(128)} %bitcast.26, f32[]{:T(128)} %bitcast.25, f32[]{:T(128)} %bitcast.24, f32[]{:T(128)} %bitcast.23), kind=kLoop, calls=%fused_computation.33 | loop fusion | flops 458752 | bytes 65572 | tf_op jit(solution)/shard_map/jit(_where)/select_n | solution.py:127
  82.3 4.6 %collective-permute-start.4 = (f32[256,4,128]{2,1,0:T(4,128)S(1)}, f32[256,4,128]{2,1,0:T(4,128)}, u32[]{:S(2)}, u32[]{:S(2)}) collective-permute-start(f32[256,4,128]{2,1,0:T(4,128)S(1)} %get-tuple-element.26), channel_id=1, source_target_pairs={{1,0},{2,1},{3,2},{4,3},{5,4},{6,5},{7,6},{8,7},{9,8},{10,9},{11,1... | collective-permute-start | bytes 1572872 | tf_op jit(solution)/shard_map/ppermute | solution.py:21
  86.9 1.9 collective-permute-start.3
  88.9 5.7 %bitcast_select_fusion.5 = f32[1,128,128]{2,1,0:T(8,128)S(1)} fusion(f32[]{:T(128)} %bitcast.18, f32[]{:T(128)} %bitcast.17, f32[]{:T(128)} %bitcast.16, f32[]{:T(128)} %bitcast.15, f32[]{:T(128)} %bitcast.14, f32[]{:T(128)} %bitcast.13, f32[]{:T(128)} %bitcast.12, f32[]{:T(128)} %bitcast.11, f32[]{:T(128)} %bitcast.9), kind=kLoop, calls=%fused_computation.38 | loop fusion | flops 458752 | bytes 65572 | tf_op jit(solution)/shard_map/jit(_where)/select_n | solution.py:127
  95.9 2.0 collective-permute-done.4.after_ref
  97.9 9.6 %collective-permute-done.3.before_ref = f32[256,4,128]{2,1,0:T(4,128)} collective-permute-done((f32[256,4,128]{2,1,0:T(4,128)S(1)}, f32[256,4,128]{2,1,0:T(4,128)}, u32[]{:S(2)}, u32[]{:S(2)}) %collective-permute-start.3) | collective-permute-done | bytes 524320 | tf_op jit(solution)/shard_map/ppermute | solution.py:20
  107.5 18.8 %shard_map.46.refs_1_ = f32[256,8,128]{2,1,0:T(8,128)} custom-call(f32[81]{0:T(128)} %copy-done.10, f32[2,128,128]{2,1,0:T(8,128)} %pad_maximum_fusion.toeplitz_ref, f32[256,4,128]{2,1,0:T(4,128)} %collective-permute-done.3.before_ref, f32[256,8,128]{2,1,0:T(8,128)} %copy-done.3, f32[256,4,128]{2,1,0:T(4,128)} %collective-permute-done.4.after_ref, ...), custom_call_target="tpu_custom_call" | custom-call | tf_op jit(solution)/shard_map/pallas_call | solution.py:134
  126.3 2.5 fusion.37
  130.7 3.4 collective-permute-start.5
  134.1 18.8 %shard_map.47.refs_4_ = f32[256,8,128]{2,1,0:T(8,128)} custom-call(f32[81]{0:T(128)} %copy-done.10, f32[2,128,128]{2,1,0:T(8,128)} %pad_maximum_fusion.1.toeplitz_ref, f32[256,4,128]{2,1,0:T(4,128)} %collective-permute-done.3.before_ref, f32[256,8,128]{2,1,0:T(8,128)} %copy-done.3, f32[256,4,128]{2,1,0:T(4,128)} %collective-permute-done.4.after_ref, ...), custom_call_target="tpu_custom_call" | custom-call | tf_op jit(solution)/shard_map/pallas_call | solution.py:134
  152.9 2.5 fusion.36
  155.4 7.6 %collective-permute-start.8 = (f32[256,4,128]{2,1,0:T(4,128)}, f32[256,4,128]{2,1,0:T(4,128)}, u32[]{:S(2)}, u32[]{:S(2)}) collective-permute-start(f32[256,4,128]{2,1,0:T(4,128)} %get-tuple-element.22), channel_id=1, source_target_pairs={{1,0},{2,1},{3,2},{4,3},{5,4},{6,5},{7,6},{8,7},{9,8},{10,9},{11,1... | collective-permute-start | bytes 1572872 | tf_op jit(solution)/shard_map/ppermute | solution.py:21
  163.0 1.9 collective-permute-start.7
  165.0 18.8 %shard_map.48.refs_7_ = f32[256,8,128]{2,1,0:T(8,128)} custom-call(f32[81]{0:T(128)} %copy-done.10, f32[2,128,128]{2,1,0:T(8,128)} %pad_maximum_fusion.2.toeplitz_ref, f32[256,4,128]{2,1,0:T(4,128)} %collective-permute-done.3.before_ref, f32[256,8,128]{2,1,0:T(8,128)} %copy-done.3, f32[256,4,128]{2,1,0:T(4,128)} %collective-permute-done.4.after_ref, ...), custom_call_target="tpu_custom_call" | custom-call | tf_op jit(solution)/shard_map/pallas_call | solution.py:134
  185.5 9.1 %collective-permute-start.10 = (f32[256,4,128]{2,1,0:T(4,128)S(1)}, f32[256,4,128]{2,1,0:T(4,128)S(1)}, u32[]{:S(2)}, u32[]{:S(2)}) collective-permute-start(f32[256,4,128]{2,1,0:T(4,128)S(1)} %get-tuple-element.20), channel_id=1, source_target_pairs={{1,0},{2,1},{3,2},{4,3},{5,4},{6,5},{7,6},{8,7},{9,8},{10,9},{11,1... | collective-permute-start | bytes 1572872 | tf_op jit(solution)/shard_map/ppermute | solution.py:21
  194.6 1.9 collective-permute-start.9
  196.5 6.9 %collective-permute-done.10.refs_8_ = f32[256,4,128]{2,1,0:T(4,128)S(1)} collective-permute-done((f32[256,4,128]{2,1,0:T(4,128)S(1)}, f32[256,4,128]{2,1,0:T(4,128)S(1)}, u32[]{:S(2)}, u32[]{:S(2)}) %collective-permute-start.10) | collective-permute-done | bytes 524320 | tf_op jit(solution)/shard_map/ppermute | solution.py:21
  204.2 8.9 %collective-permute-done.9.refs_6_ = f32[256,4,128]{2,1,0:T(4,128)} collective-permute-done((f32[256,4,128]{2,1,0:T(4,128)S(1)}, f32[256,4,128]{2,1,0:T(4,128)}, u32[]{:S(2)}, u32[]{:S(2)}) %collective-permute-start.9) | collective-permute-done | bytes 524320 | tf_op jit(solution)/shard_map/ppermute | solution.py:20
  213.1 6.9 %shard_map.49 = f32[256,8,128]{2,1,0:T(8,128)} custom-call(f32[81]{0:T(128)} %copy-done.10, f32[256,4,128]{2,1,0:T(4,128)} %collective-permute-done.5.refs_0_, f32[256,8,128]{2,1,0:T(8,128)} %shard_map.46.refs_1_, f32[256,4,128]{2,1,0:T(4,128)} %collective-permute-done.6.refs_2_, f32[256,4,128]{2,1,0:T(4,128)} %collective-permute-done.7.refs_3_, ...), custom_call_target="tpu_custom_call" | custom-call | tf_op jit(solution)/shard_map/pallas_call | solution.py:171
  221.1 3.6 collective-permute-start.11
  229.2 12.0 %collective-permute-done.12 = f32[128,8,128]{2,1,0:T(8,128)S(1)} collective-permute-done((f32[128,8,128]{2,1,0:T(8,128)S(1)}, f32[128,8,128]{2,1,0:T(8,128)S(1)}, u32[]{:S(2)}, u32[]{:S(2)}) %collective-permute-start.12) | collective-permute-done | bytes 524320 | tf_op jit(solution)/shard_map/ppermute | solution.py:190
  244.3 1.9 collective-permute-start.15
  246.2 3.4 collective-permute-start.14
  249.6 9.8 %collective-permute-done.15.after_ref = f32[256,4,128]{2,1,0:T(4,128)S(1)} collective-permute-done((f32[256,4,128]{2,1,0:T(4,128)S(1)}, f32[256,4,128]{2,1,0:T(4,128)S(1)}, u32[]{:S(2)}, u32[]{:S(2)}) %collective-permute-start.15) | collective-permute-done | bytes 524320 | tf_op jit(solution)/shard_map/ppermute | solution.py:21
  259.4 7.7 %collective-permute-done.14.before_ref = f32[256,4,128]{2,1,0:T(4,128)} collective-permute-done((f32[256,4,128]{2,1,0:T(4,128)S(1)}, f32[256,4,128]{2,1,0:T(4,128)}, u32[]{:S(2)}, u32[]{:S(2)}) %collective-permute-start.14) | collective-permute-done | bytes 524320 | tf_op jit(solution)/shard_map/ppermute | solution.py:20
  267.1 18.8 %shard_map.50.refs_1_ = f32[256,8,128]{2,1,0:T(8,128)} custom-call(f32[81]{0:T(128)} %copy-done.10, f32[2,128,128]{2,1,0:T(8,128)} %pad_maximum_fusion.toeplitz_ref, f32[256,4,128]{2,1,0:T(4,128)} %collective-permute-done.14.before_ref, f32[256,8,128]{2,1,0:T(8,128)} %copy-done.1, f32[256,4,128]{2,1,0:T(4,128)} %copy-done.9, bf16[256,8,128]{2,1,0:T(8,128)(2,1)} %bitcast.129), custom_call_target="tpu_custom_call" | custom-call | tf_op jit(solution)/shard_map/pallas_call | solution.py:134
  287.6 1.9 collective-permute-start.17
  289.5 3.4 collective-permute-start.16
  292.9 18.8 %shard_map.51.refs_4_ = f32[256,8,128]{2,1,0:T(8,128)} custom-call(f32[81]{0:T(128)} %copy-done.10, f32[2,128,128]{2,1,0:T(8,128)} %pad_maximum_fusion.1.toeplitz_ref, f32[256,4,128]{2,1,0:T(4,128)} %collective-permute-done.14.before_ref, f32[256,8,128]{2,1,0:T(8,128)} %copy-done.1, f32[256,4,128]{2,1,0:T(4,128)} %copy-done.9, bf16[256,8,128]{2,1,0:T(8,128)(2,1)} %bitcast.127), custom_call_target="tpu_custom_call" | custom-call | tf_op jit(solution)/shard_map/pallas_call | solution.py:134
  311.7 2.5 fusion.32
  314.2 7.6 %collective-permute-start.19 = (f32[256,4,128]{2,1,0:T(4,128)}, f32[256,4,128]{2,1,0:T(4,128)}, u32[]{:S(2)}, u32[]{:S(2)}) collective-permute-start(f32[256,4,128]{2,1,0:T(4,128)} %get-tuple-element.12), channel_id=1, source_target_pairs={{1,0},{2,1},{3,2},{4,3},{5,4},{6,5},{7,6},{8,7},{9,8},{10,9},{11,1... | collective-permute-start | bytes 1572872 | tf_op jit(solution)/shard_map/ppermute | solution.py:21
  321.8 1.9 collective-permute-start.18
  323.7 18.8 %shard_map.52.refs_7_ = f32[256,8,128]{2,1,0:T(8,128)} custom-call(f32[81]{0:T(128)} %copy-done.10, f32[2,128,128]{2,1,0:T(8,128)} %pad_maximum_fusion.2.toeplitz_ref, f32[256,4,128]{2,1,0:T(4,128)} %collective-permute-done.14.before_ref, f32[256,8,128]{2,1,0:T(8,128)} %copy-done.1, f32[256,4,128]{2,1,0:T(4,128)} %copy-done.9, bf16[256,8,128]{2,1,0:T(8,128)(2,1)} %bitcast.125), custom_call_target="tpu_custom_call" | custom-call | tf_op jit(solution)/shard_map/pallas_call | solution.py:134
  344.2 9.1 %collective-permute-start.21 = (f32[256,4,128]{2,1,0:T(4,128)S(1)}, f32[256,4,128]{2,1,0:T(4,128)S(1)}, u32[]{:S(2)}, u32[]{:S(2)}) collective-permute-start(f32[256,4,128]{2,1,0:T(4,128)S(1)} %get-tuple-element.10), channel_id=1, source_target_pairs={{1,0},{2,1},{3,2},{4,3},{5,4},{6,5},{7,6},{8,7},{9,8},{10,9},{11,1... | collective-permute-start | bytes 1572872 | tf_op jit(solution)/shard_map/ppermute | solution.py:21
  355.3 7.2 %collective-permute-done.21.refs_8_ = f32[256,4,128]{2,1,0:T(4,128)S(1)} collective-permute-done((f32[256,4,128]{2,1,0:T(4,128)S(1)}, f32[256,4,128]{2,1,0:T(4,128)S(1)}, u32[]{:S(2)}, u32[]{:S(2)}) %collective-permute-start.21) | collective-permute-done | bytes 524320 | tf_op jit(solution)/shard_map/ppermute | solution.py:21
  363.3 8.8 %collective-permute-done.20.refs_6_ = f32[256,4,128]{2,1,0:T(4,128)S(1)} collective-permute-done((f32[256,4,128]{2,1,0:T(4,128)S(1)}, f32[256,4,128]{2,1,0:T(4,128)S(1)}, u32[]{:S(2)}, u32[]{:S(2)}) %collective-permute-start.20) | collective-permute-done | bytes 524320 | tf_op jit(solution)/shard_map/ppermute | solution.py:20
  372.8 6.9 %shard_map.53 = f32[256,8,128]{2,1,0:T(8,128)} custom-call(f32[81]{0:T(128)} %copy-done.10, f32[256,4,128]{2,1,0:T(4,128)} %collective-permute-done.16.refs_0_, f32[256,8,128]{2,1,0:T(8,128)} %shard_map.50.refs_1_, f32[256,4,128]{2,1,0:T(4,128)} %collective-permute-done.17.refs_2_, f32[256,4,128]{2,1,0:T(4,128)} %collective-permute-done.18.refs_3_, ...), custom_call_target="tpu_custom_call" | custom-call | tf_op jit(solution)/shard_map/pallas_call | solution.py:171
  380.9 3.3 collective-permute-start.22
  388.4 11.7 %collective-permute-done.23 = f32[128,8,128]{2,1,0:T(8,128)S(1)} collective-permute-done((f32[128,8,128]{2,1,0:T(8,128)S(1)}, f32[128,8,128]{2,1,0:T(8,128)S(1)}, u32[]{:S(2)}, u32[]{:S(2)}) %collective-permute-start.23) | collective-permute-done | bytes 524320 | tf_op jit(solution)/shard_map/ppermute | solution.py:190
  (94 shorter events, 44.3 us)
Async XLA Ops:
  0.0 7.1 %copy-start = (bf16[3,8,256,128]{3,2,1,0:T(8,128)(2,1)S(1)}, bf16[3,8,256,128]{3,2,1,0:T(8,128)(2,1)}, u32[]{:S(2)}) copy-start(bf16[3,8,256,128]{3,2,1,0:T(8,128)(2,1)} %param.4) | copy-start | bytes 4718596
  10.7 30.4 %all-to-all-start = ((bf16[3,8,256,128]{3,1,0,2:T(8,128)(2,1)}), bf16[3,8,256,128]{3,1,0,2:T(8,128)(2,1)S(1)}, u32[]{:S(2)}, u32[]{:S(2)}) async-start(bf16[3,8,256,128]{3,1,0,2:T(8,128)(2,1)} %copy.17), calls=%async_computation | async-start | bytes 3145728 | tf_op jit(solution)/shard_map/all_to_all | solution.py:205
  41.7 1.3 copy-start.4
  41.7 1.3 copy-start.5
  41.7 1.3 copy-start.6
  41.7 4.7 %copy-start.14 = (f32[3,3,9]{2,1,0:T(4,128)S(1)}, f32[3,3,9]{2,1,0:T(4,128)}, u32[]{:S(2)}) copy-start(f32[3,3,9]{2,1,0:T(4,128)} %param.7) | copy-start | bytes 976
  43.0 5.3 %collective-permute-start = (f32[128,8,128]{2,1,0:T(8,128)}, f32[128,8,128]{2,1,0:T(8,128)}, u32[]{:S(2)}, u32[]{:S(2)}) collective-permute-start(f32[128,8,128]{2,1,0:T(8,128)} %constant_dynamic-slice_fusion.2), channel_id=1, source_target_pairs={{0,32},{32,0},{64,96},{96,64},{1,33},{33,1},{65,97},{97,65},{2,34}... | collective-permute-start | bytes 1572872 | tf_op jit(solution)/shard_map/ppermute | solution.py:189
  46.6 32.2 %copy-start.10 = (f32[81]{0:T(128)}, f32[81]{0:T(128)S(1)}, u32[]{:S(2)}) copy-start(f32[81]{0:T(128)S(1)} %reshape.110.taps_ref) | copy-start | bytes 976
  49.4 29.4 %collective-permute-start.1 = (f32[128,8,128]{2,1,0:T(8,128)S(1)}, f32[128,8,128]{2,1,0:T(8,128)S(1)}, u32[]{:S(2)}, u32[]{:S(2)}) collective-permute-start(f32[128,8,128]{2,1,0:T(8,128)S(1)} %dynamic-slice_add_fusion.2), channel_id=1, source_target_pairs={{0,64},{32,96},{64,0},{96,32},{1,65},{33,97},{65,1},{97,33},{2,66}... | collective-permute-start | bytes 1572872 | tf_op jit(solution)/shard_map/ppermute | solution.py:190
  78.8 2.3 collective-permute-start.2
  81.2 0.8 copy-start.7
  82.1 25.4 %copy-start.3 = (f32[256,8,128]{2,1,0:T(8,128)}, f32[256,8,128]{2,1,0:T(8,128)S(1)}, u32[]{:S(2)}) copy-start(f32[256,8,128]{2,1,0:T(8,128)S(1)} %maximum_multiply_fusion.mid_ref) | copy-start | bytes 3145732
  82.3 15.6 %collective-permute-start.4 = (f32[256,4,128]{2,1,0:T(4,128)S(1)}, f32[256,4,128]{2,1,0:T(4,128)}, u32[]{:S(2)}, u32[]{:S(2)}) collective-permute-start(f32[256,4,128]{2,1,0:T(4,128)S(1)} %get-tuple-element.26), channel_id=1, source_target_pairs={{1,0},{2,1},{3,2},{4,3},{5,4},{6,5},{7,6},{8,7},{9,8},{10,9},{11,1... | collective-permute-start | bytes 1572872 | tf_op jit(solution)/shard_map/ppermute | solution.py:21
  86.9 20.5 %collective-permute-start.3 = (f32[256,4,128]{2,1,0:T(4,128)S(1)}, f32[256,4,128]{2,1,0:T(4,128)}, u32[]{:S(2)}, u32[]{:S(2)}) collective-permute-start(f32[256,4,128]{2,1,0:T(4,128)S(1)} %get-tuple-element.27), channel_id=1, source_target_pairs={{0,1},{1,2},{2,3},{3,4},{4,5},{5,6},{6,7},{7,8},{8,9},{9,10},{10,1... | collective-permute-start | bytes 1572872 | tf_op jit(solution)/shard_map/ppermute | solution.py:20
  128.8 65.7 %collective-permute-start.6 = (f32[256,4,128]{2,1,0:T(4,128)}, f32[256,4,128]{2,1,0:T(4,128)}, u32[]{:S(2)}, u32[]{:S(2)}) collective-permute-start(f32[256,4,128]{2,1,0:T(4,128)} %get-tuple-element.24), channel_id=1, source_target_pairs={{1,0},{2,1},{3,2},{4,3},{5,4},{6,5},{7,6},{8,7},{9,8},{10,9},{11,1... | collective-permute-start | bytes 1572872 | tf_op jit(solution)/shard_map/ppermute | solution.py:21
  130.7 65.8 %collective-permute-start.5 = (f32[256,4,128]{2,1,0:T(4,128)S(1)}, f32[256,4,128]{2,1,0:T(4,128)}, u32[]{:S(2)}, u32[]{:S(2)}) collective-permute-start(f32[256,4,128]{2,1,0:T(4,128)S(1)} %get-tuple-element.25), channel_id=1, source_target_pairs={{0,1},{1,2},{2,3},{3,4},{4,5},{5,6},{6,7},{7,8},{8,9},{9,10},{10,1... | collective-permute-start | bytes 1572872 | tf_op jit(solution)/shard_map/ppermute | solution.py:20
  155.4 41.1 %collective-permute-start.8 = (f32[256,4,128]{2,1,0:T(4,128)}, f32[256,4,128]{2,1,0:T(4,128)}, u32[]{:S(2)}, u32[]{:S(2)}) collective-permute-start(f32[256,4,128]{2,1,0:T(4,128)} %get-tuple-element.22), channel_id=1, source_target_pairs={{1,0},{2,1},{3,2},{4,3},{5,4},{6,5},{7,6},{8,7},{9,8},{10,9},{11,1... | collective-permute-start | bytes 1572872 | tf_op jit(solution)/shard_map/ppermute | solution.py:21
  163.0 33.5 %collective-permute-start.7 = (f32[256,4,128]{2,1,0:T(4,128)S(1)}, f32[256,4,128]{2,1,0:T(4,128)}, u32[]{:S(2)}, u32[]{:S(2)}) collective-permute-start(f32[256,4,128]{2,1,0:T(4,128)S(1)} %get-tuple-element.23), channel_id=1, source_target_pairs={{0,1},{1,2},{2,3},{3,4},{4,5},{5,6},{6,7},{7,8},{8,9},{9,10},{10,1... | collective-permute-start | bytes 1572872 | tf_op jit(solution)/shard_map/ppermute | solution.py:20
  185.5 17.9 %collective-permute-start.10 = (f32[256,4,128]{2,1,0:T(4,128)S(1)}, f32[256,4,128]{2,1,0:T(4,128)S(1)}, u32[]{:S(2)}, u32[]{:S(2)}) collective-permute-start(f32[256,4,128]{2,1,0:T(4,128)S(1)} %get-tuple-element.20), channel_id=1, source_target_pairs={{1,0},{2,1},{3,2},{4,3},{5,4},{6,5},{7,6},{8,7},{9,8},{10,9},{11,1... | collective-permute-start | bytes 1572872 | tf_op jit(solution)/shard_map/ppermute | solution.py:21
  194.6 18.5 %collective-permute-start.9 = (f32[256,4,128]{2,1,0:T(4,128)S(1)}, f32[256,4,128]{2,1,0:T(4,128)}, u32[]{:S(2)}, u32[]{:S(2)}) collective-permute-start(f32[256,4,128]{2,1,0:T(4,128)S(1)} %get-tuple-element.21), channel_id=1, source_target_pairs={{0,1},{1,2},{2,3},{3,4},{4,5},{5,6},{6,7},{7,8},{8,9},{9,10},{10,1... | collective-permute-start | bytes 1572872 | tf_op jit(solution)/shard_map/ppermute | solution.py:20
  203.4 0.8 copy-start.12
  221.1 5.2 %collective-permute-start.11 = (f32[128,8,128]{2,1,0:T(8,128)S(1)}, f32[128,8,128]{2,1,0:T(8,128)S(1)}, u32[]{:S(2)}, u32[]{:S(2)}) collective-permute-start(f32[128,8,128]{2,1,0:T(8,128)S(1)} %constant_dynamic-slice_fusion.1), channel_id=1, source_target_pairs={{0,32},{32,0},{64,96},{96,64},{1,33},{33,1},{65,97},{97,65},{2,34}... | collective-permute-start | bytes 1572872 | tf_op jit(solution)/shard_map/ppermute | solution.py:189
  227.4 16.5 %copy-start.8 = (f32[128,8,128]{2,1,0:T(8,128)S(1)}, f32[128,8,128]{2,1,0:T(8,128)}, u32[]{:S(2)}) copy-start(f32[128,8,128]{2,1,0:T(8,128)} %copy-done.7) | copy-start | bytes 1572868
  227.4 13.8 %collective-permute-start.12 = (f32[128,8,128]{2,1,0:T(8,128)S(1)}, f32[128,8,128]{2,1,0:T(8,128)S(1)}, u32[]{:S(2)}, u32[]{:S(2)}) collective-permute-start(f32[128,8,128]{2,1,0:T(8,128)S(1)} %dynamic-slice_add_fusion.1), channel_id=1, source_target_pairs={{0,64},{32,96},{64,0},{96,32},{1,65},{33,97},{65,1},{97,33},{2,66}... | collective-permute-start | bytes 1572872 | tf_op jit(solution)/shard_map/ppermute | solution.py:190
  241.3 2.5 collective-permute-start.13
  244.1 23.0 %copy-start.1 = (f32[256,8,128]{2,1,0:T(8,128)}, f32[256,8,128]{2,1,0:T(8,128)S(1)}, u32[]{:S(2)}) copy-start(f32[256,8,128]{2,1,0:T(8,128)S(1)} %fusion.4.mid_ref) | copy-start | bytes 3145732
  244.3 15.1 %collective-permute-start.15 = (f32[256,4,128]{2,1,0:T(4,128)S(1)}, f32[256,4,128]{2,1,0:T(4,128)S(1)}, u32[]{:S(2)}, u32[]{:S(2)}) collective-permute-start(f32[256,4,128]{2,1,0:T(4,128)S(1)} %get-tuple-element.16), channel_id=1, source_target_pairs={{1,0},{2,1},{3,2},{4,3},{5,4},{6,5},{7,6},{8,7},{9,8},{10,9},{11,1... | collective-permute-start | bytes 1572872 | tf_op jit(solution)/shard_map/ppermute | solution.py:21
  246.2 20.9 %collective-permute-start.14 = (f32[256,4,128]{2,1,0:T(4,128)S(1)}, f32[256,4,128]{2,1,0:T(4,128)}, u32[]{:S(2)}, u32[]{:S(2)}) collective-permute-start(f32[256,4,128]{2,1,0:T(4,128)S(1)} %get-tuple-element.17), channel_id=1, source_target_pairs={{0,1},{1,2},{2,3},{3,4},{4,5},{5,6},{6,7},{7,8},{8,9},{9,10},{10,1... | collective-permute-start | bytes 1572872 | tf_op jit(solution)/shard_map/ppermute | solution.py:20
  259.4 7.7 %copy-start.9 = (f32[256,4,128]{2,1,0:T(4,128)}, f32[256,4,128]{2,1,0:T(4,128)S(1)}, u32[]{:S(2)}) copy-start(f32[256,4,128]{2,1,0:T(4,128)S(1)} %collective-permute-done.15.after_ref) | copy-start | bytes 1572868
  287.6 65.7 %collective-permute-start.17 = (f32[256,4,128]{2,1,0:T(4,128)S(1)}, f32[256,4,128]{2,1,0:T(4,128)}, u32[]{:S(2)}, u32[]{:S(2)}) collective-permute-start(f32[256,4,128]{2,1,0:T(4,128)S(1)} %get-tuple-element.14), channel_id=1, source_target_pairs={{1,0},{2,1},{3,2},{4,3},{5,4},{6,5},{7,6},{8,7},{9,8},{10,9},{11,1... | collective-permute-start | bytes 1572872 | tf_op jit(solution)/shard_map/ppermute | solution.py:21
  289.5 65.7 %collective-permute-start.16 = (f32[256,4,128]{2,1,0:T(4,128)S(1)}, f32[256,4,128]{2,1,0:T(4,128)}, u32[]{:S(2)}, u32[]{:S(2)}) collective-permute-start(f32[256,4,128]{2,1,0:T(4,128)S(1)} %get-tuple-element.15), channel_id=1, source_target_pairs={{0,1},{1,2},{2,3},{3,4},{4,5},{5,6},{6,7},{7,8},{8,9},{9,10},{10,1... | collective-permute-start | bytes 1572872 | tf_op jit(solution)/shard_map/ppermute | solution.py:20
  314.2 41.1 %collective-permute-start.19 = (f32[256,4,128]{2,1,0:T(4,128)}, f32[256,4,128]{2,1,0:T(4,128)}, u32[]{:S(2)}, u32[]{:S(2)}) collective-permute-start(f32[256,4,128]{2,1,0:T(4,128)} %get-tuple-element.12), channel_id=1, source_target_pairs={{1,0},{2,1},{3,2},{4,3},{5,4},{6,5},{7,6},{8,7},{9,8},{10,9},{11,1... | collective-permute-start | bytes 1572872 | tf_op jit(solution)/shard_map/ppermute | solution.py:21
  321.8 33.5 %collective-permute-start.18 = (f32[256,4,128]{2,1,0:T(4,128)S(1)}, f32[256,4,128]{2,1,0:T(4,128)}, u32[]{:S(2)}, u32[]{:S(2)}) collective-permute-start(f32[256,4,128]{2,1,0:T(4,128)S(1)} %get-tuple-element.13), channel_id=1, source_target_pairs={{0,1},{1,2},{2,3},{3,4},{4,5},{5,6},{6,7},{7,8},{8,9},{9,10},{10,1... | collective-permute-start | bytes 1572872 | tf_op jit(solution)/shard_map/ppermute | solution.py:20
  344.2 18.2 %collective-permute-start.21 = (f32[256,4,128]{2,1,0:T(4,128)S(1)}, f32[256,4,128]{2,1,0:T(4,128)S(1)}, u32[]{:S(2)}, u32[]{:S(2)}) collective-permute-start(f32[256,4,128]{2,1,0:T(4,128)S(1)} %get-tuple-element.10), channel_id=1, source_target_pairs={{1,0},{2,1},{3,2},{4,3},{5,4},{6,5},{7,6},{8,7},{9,8},{10,9},{11,1... | collective-permute-start | bytes 1572872 | tf_op jit(solution)/shard_map/ppermute | solution.py:21
  353.3 18.7 %collective-permute-start.20 = (f32[256,4,128]{2,1,0:T(4,128)S(1)}, f32[256,4,128]{2,1,0:T(4,128)S(1)}, u32[]{:S(2)}, u32[]{:S(2)}) collective-permute-start(f32[256,4,128]{2,1,0:T(4,128)S(1)} %get-tuple-element.11), channel_id=1, source_target_pairs={{0,1},{1,2},{2,3},{3,4},{4,5},{5,6},{6,7},{7,8},{8,9},{9,10},{10,1... | collective-permute-start | bytes 1572872 | tf_op jit(solution)/shard_map/ppermute | solution.py:20
  362.5 0.8 copy-start.11
  372.0 0.8 copy-start.13
  380.9 4.9 %collective-permute-start.22 = (f32[128,8,128]{2,1,0:T(8,128)S(1)}, f32[128,8,128]{2,1,0:T(8,128)S(1)}, u32[]{:S(2)}, u32[]{:S(2)}) collective-permute-start(f32[128,8,128]{2,1,0:T(8,128)S(1)} %constant_dynamic-slice_fusion), channel_id=1, source_target_pairs={{0,32},{32,0},{64,96},{96,64},{1,33},{33,1},{65,97},{97,65},{2,34}... | collective-permute-start | bytes 1572872 | tf_op jit(solution)/shard_map/ppermute | solution.py:189
  386.9 16.2 %copy-start.2 = (f32[256,8,128]{2,1,0:T(8,128)S(1)}, f32[256,8,128]{2,1,0:T(8,128)}, u32[]{:S(2)}) copy-start(f32[256,8,128]{2,1,0:T(8,128)} %copy-done.1) | copy-start | bytes 3145732
  386.9 13.2 %collective-permute-start.23 = (f32[128,8,128]{2,1,0:T(8,128)S(1)}, f32[128,8,128]{2,1,0:T(8,128)S(1)}, u32[]{:S(2)}, u32[]{:S(2)}) collective-permute-start(f32[128,8,128]{2,1,0:T(8,128)S(1)} %dynamic-slice_add_fusion), channel_id=1, source_target_pairs={{0,64},{32,96},{64,0},{96,32},{1,65},{33,97},{65,1},{97,33},{2,66}... | collective-permute-start | bytes 1572872 | tf_op jit(solution)/shard_map/ppermute | solution.py:190
  400.1 2.8 collective-permute-start.24

commit v5 on v3

--- a/solution.py
+++ b/solution.py
@@ -8,15 +8,20 @@
 from jax.sharding import PartitionSpec as P
 
 ITERS = 2
-CZ = 8
+CZ = 32
 
 
 def halos(shard, axis, dim, width):
-    devices, length = (lax.axis_size(axis), shard.shape[dim])
+    length = shard.shape[dim]
+    last = lax.slice_in_dim(shard, length - width, length, axis=dim)
+    first = lax.slice_in_dim(shard, 0, width, axis=dim)
+    return swap_rims(first, last, axis)
+
+
+def swap_rims(first, last, axis):
+    devices = lax.axis_size(axis)
     up = [(i, (i + 1) % devices) for i in range(devices - 1)]
     down = [(j, i) for i, j in up]
-    last = lax.slice_in_dim(shard, length - width, length, axis=dim)
-    first = lax.slice_in_dim(shard, 0, width, axis=dim)
     before = lax.ppermute(last, axis, up)
     after = lax.ppermute(first, axis, down)
     return before, after
@@ -33,9 +38,10 @@
 def resample_views(raw_views, weight_norm, offsets):
     rows = raw_views.shape[2]
     band = weight_norm.shape[2]
-    target = offsets[:, :, None] + jnp.arange(band, dtype=jnp.int32)[None, None, :]
-    onehot = target[..., None] == jnp.arange(rows, dtype=jnp.int32)[None, None, None, :]
-    matrix = jnp.sum(jnp.where(onehot, weight_norm[..., None], 0.0), axis=2)
+    lag = jnp.arange(rows, dtype=jnp.int32)[None, None, :] - offsets[:, :, None]
+    matrix = jnp.zeros(lag.shape, jnp.float32)
+    for k in range(band):
+        matrix = matrix + jnp.where(lag == k, weight_norm[:, :, k : k + 1], 0.0)
     result = jnp.einsum(
         "vxr,vzry->vzxy",
         matrix,
@@ -66,8 +72,11 @@
     return acc
 
 
-def _forward_kernel(v, taps_ref, before_ref, mid_ref, after_ref, brick_ref, out_ref, a_ref, c_ref, est_ref):
-    nz, _, ny = out_ref.shape
+def _forward_kernel(
+    v, taps_ref, before_ref, mid_ref, after_ref, brick_ref, out_ref, first_ref, last_ref, a_ref, c_ref, est_ref
+):
+    nz, width, ny = out_ref.shape
+    rim = first_ref.shape[1]
     tx = [taps_ref[v * 27 + 9 + t] for t in range(9)]
     tz = [taps_ref[v * 27 + t] for t in range(9)]
     ty = [taps_ref[v * 27 + 18 + t] for t in range(9)]
@@ -108,6 +117,8 @@
         for t in range(1, 9):
             acc = acc + tz[8 - t] * c_ref[pl.ds(z0 + t, CZ)]
         out_ref[pl.ds(z0, CZ)] = acc
+        first_ref[pl.ds(z0, CZ)] = acc[:, :rim, :]
+        last_ref[pl.ds(z0, CZ)] = acc[:, width - rim :, :]
         return carry
 
     lax.fori_loop(0, nz // CZ, along_z_back, 0)
@@ -118,8 +129,12 @@
     return pl.pallas_call(
         functools.partial(_forward_kernel, v),
         in_specs=[pl.BlockSpec(memory_space=pltpu.SMEM)] + [pl.BlockSpec(memory_space=pltpu.VMEM)] * 4,
-        out_specs=pl.BlockSpec(memory_space=pltpu.VMEM),
-        out_shape=jax.ShapeDtypeStruct((nz, width, ny), jnp.float32),
+        out_specs=[pl.BlockSpec(memory_space=pltpu.VMEM)] * 3,
+        out_shape=[
+            jax.ShapeDtypeStruct((nz, width, ny), jnp.float32),
+            jax.ShapeDtypeStruct((nz, 4, ny), jnp.float32),
+            jax.ShapeDtypeStruct((nz, 4, ny), jnp.float32),
+        ],
         scratch_shapes=[
             pltpu.VMEM((nz + 8, width, ny), jnp.float32),
             pltpu.VMEM((nz + 8, width, ny), jnp.float32),
@@ -195,10 +210,10 @@
         before, after = halos(joined_volume, "vol", 1, rim_width)
         parts = []
         for index in range(count):
-            partial_value = forward_partial(
+            partial_value, first, last = forward_partial(
                 taps_flat, index, before, joined_volume, after, bricks[index]
             )
-            low, high = halos(partial_value, "vol", 1, rim_width)
+            low, high = swap_rims(first, last, "vol")
             parts += [low, partial_value, high]
         logs = back_logs(taps_flat, parts)
         summed = view_sum(logs)

time: 362 us -> 332 us (0.917)
  starting transfers between devices: 91.8 us -> 114 us
  Pallas kernels: 96.7 us -> 76.5 us
  local copies, waits for them, and re-layouts: 24.2 us -> 8.99 us
  waiting for transfers between devices: 133 us -> 120 us
  other arithmetic: 12.4 us -> 6.08 us
    ppermute x16, starting transfers between devices: 64.1 us -> 85.1 us  [the longest x8 69.8 us: swap_rims(): after = lax.ppermute(first, axis, down)]
    pallas_call x6, Pallas kernels: 82.8 us -> 62.2 us  [forward_partial(): pl.pallas_call(functools.partial(_forward_kernel, v), in_specs=[pl.BlockS...]
    ppermute x16, waiting for transfers between devices: 67.3 us -> 53.8 us  [the longest x8 34.4 us: swap_rims(): before = lax.ppermute(last, axis, up)]
    slice x8 -> x2, local copies, waits for them, and re-layouts: 14.2 us -> 1.52 us  [halos(): first = lax.slice_in_dim(shard, 0, width, axis=dim)]
    reduce_sum x1 -> x0, other arithmetic: 4.43 us -> none  [resample_views(): matrix = jnp.sum(jnp.where(onehot, weight_norm[..., None], 0.0), axis=2)]
  transfers between devices with their start and end apart: 26 -> 26, of which waited for: 18 -> 18; matrix products, arithmetic and copies ran while one was open for 3% -> 0% of each run, Pallas kernels for 15% -> 13%
where the time goes in v5:
time: 332 us; the launch traced here: 329 us
  waiting for transfers between devices  120 us (36%)
  starting transfers between devices  114 us (34%)
  Pallas kernels  76.5 us (23%)
  local copies, waits for them, and re-layouts  8.99 us (3%)
  other arithmetic  6.08 us (2%)
  matrix products  3.33 us (1%)
    ppermute x8, starting transfers between devices, swap_rims(): after = lax.ppermute(first, axis, down)  69.8 us
    pallas_call x6, Pallas kernels, forward_partial(): pl.pallas_call(functools.partial(_forward_kernel, v), in_specs=[pl.BlockS...  62.2 us
    ppermute x3, waiting for transfers between devices, view_sum(): own = own + lax.ppermute(own, 'view', chip_swap)  36.7 us
    ppermute x8, waiting for transfers between devices, swap_rims(): before = lax.ppermute(last, axis, up)  34.4 us
    all_to_all x1, waiting for transfers between devices, per_device(): lax.all_to_all(local_views, 'vol', split_axis=2, concat_axis=1, tiled=True)  19.8 us
    ppermute x8, waiting for transfers between devices, swap_rims(): after = lax.ppermute(first, axis, down)  19.4 us
    ppermute x8, starting transfers between devices, swap_rims(): before = lax.ppermute(last, axis, up)  15.3 us
    pallas_call x2, Pallas kernels, back_logs(): pl.pallas_call(_back_kernel, in_specs=[pl.BlockSpec(memory_space=pltpu.SM...  14.4 us
  transfers between devices with their start and end apart: 26, of which 18 were waited for; matrix products, arithmetic and copies ran while one was open for 0% of the time, Pallas kernels for 13%

profile of v5, /device:TPU:5, one launch (start us, length us, event | category | flops | bytes accessed | tf_op | source)
XLA Modules:
  0.0 328.8 jit_solution(6941222759120232160)
XLA Ops:
  1.7 3.3 %fusion.1 = bf16[3,8,256,128]{3,2,1,0:T(8,128)(2,1)S(1)} fusion(bf16[3,8,256,128]{3,2,1,0:T(8,128)(2,1)S(1)} %copy-done, f32[3,256]{1,0:T(4,128)S(1)} %get-tuple-element.62, f32[3,256]{1,0:T(4,128)S(1)} %get-tuple-element.63, f32[3,256]{1,0:T(4,128)S(1)} %get-tuple-element.64, f32[3,256]{1,0:T(4,128)S(1)} %get-tuple-element.65, ...), kind=kOutput, calls=%fused_computation.3 | convolution fusion | flops 2421424128 | bytes 3173376 | tf_op jit(solution)/shard_map/vxr,vzry->vzxy/dot_general | solution.py:45
  5.0 2.2 copy.7
  7.2 10.5 %all-to-all-start = ((bf16[3,8,256,128]{3,1,0,2:T(8,128)(2,1)}), bf16[3,8,256,128]{3,1,0,2:T(8,128)(2,1)S(1)}, u32[]{:S(2)}, u32[]{:S(2)}) async-start(bf16[3,8,256,128]{3,1,0,2:T(8,128)(2,1)} %copy.7), calls=%async_computation | async-start | bytes 3145728 | tf_op jit(solution)/shard_map/all_to_all | solution.py:204
  17.8 19.8 %all-to-all-done = bf16[3,8,256,128]{3,1,0,2:T(8,128)(2,1)S(1)} async-done(((bf16[3,8,256,128]{3,1,0,2:T(8,128)(2,1)}), bf16[3,8,256,128]{3,1,0,2:T(8,128)(2,1)S(1)}, u32[]{:S(2)}, u32[]{:S(2)}) %all-to-all-start) | async-done | bytes 1572896 | tf_op jit(solution)/shard_map/all_to_all | solution.py:204
  39.5 3.4 %collective-permute-start = (f32[128,8,128]{2,1,0:T(8,128)}, f32[128,8,128]{2,1,0:T(8,128)S(1)}, u32[]{:S(2)}, u32[]{:S(2)}) collective-permute-start(f32[128,8,128]{2,1,0:T(8,128)} %constant_dynamic-slice_fusion.2), channel_id=1, source_target_pairs={{0,32},{32,0},{64,96},{96,64},{1,33},{33,1},{65,97},{97,65},{2,34}... | collective-permute-start | bytes 1572872 | tf_op jit(solution)/shard_map/ppermute | solution.py:188
  42.9 1.7 collective-permute-done
  45.7 12.2 %collective-permute-done.1 = f32[128,8,128]{2,1,0:T(8,128)S(1)} collective-permute-done((f32[128,8,128]{2,1,0:T(8,128)S(1)}, f32[128,8,128]{2,1,0:T(8,128)S(1)}, u32[]{:S(2)}, u32[]{:S(2)}) %collective-permute-start.1) | collective-permute-done | bytes 524320 | tf_op jit(solution)/shard_map/ppermute | solution.py:189
  58.0 1.3 collective-permute-start.2
  59.3 1.5 collective-permute-done.2
  61.8 1.4 fusion.68
  63.2 5.2 %collective-permute-start.4 = (f32[256,4,128]{2,1,0:T(4,128)}, f32[256,4,128]{2,1,0:T(4,128)}, u32[]{:S(2)}, u32[]{:S(2)}) collective-permute-start(f32[256,4,128]{2,1,0:T(4,128)} %get-tuple-element.50), channel_id=1, source_target_pairs={{1,0},{2,1},{3,2},{4,3},{5,4},{6,5},{7,6},{8,7},{9,8},{10,9},{11,1... | collective-permute-start | bytes 1572872 | tf_op jit(solution)/shard_map/ppermute | solution.py:26
  68.4 1.9 collective-permute-start.3
  71.1 8.5 %collective-permute-done.4.after_ref = f32[256,4,128]{2,1,0:T(4,128)} collective-permute-done((f32[256,4,128]{2,1,0:T(4,128)}, f32[256,4,128]{2,1,0:T(4,128)}, u32[]{:S(2)}, u32[]{:S(2)}) %collective-permute-start.4) | collective-permute-done | bytes 524320 | tf_op jit(solution)/shard_map/ppermute | solution.py:26
  79.7 9.5 %collective-permute-done.3.before_ref = f32[256,4,128]{2,1,0:T(4,128)} collective-permute-done((f32[256,4,128]{2,1,0:T(4,128)}, f32[256,4,128]{2,1,0:T(4,128)}, u32[]{:S(2)}, u32[]{:S(2)}) %collective-permute-start.3) | collective-permute-done | bytes 524320 | tf_op jit(solution)/shard_map/ppermute | solution.py:25
  89.2 10.3 %shard_map.48 = (f32[256,8,128]{2,1,0:T(8,128)}, f32[256,4,128]{2,1,0:T(4,128)}, f32[256,4,128]{2,1,0:T(4,128)}) custom-call(f32[81]{0:T(128)} %reshape.12.taps_ref, f32[256,4,128]{2,1,0:T(4,128)} %collective-permute-done.3.before_ref, f32[256,8,128]{2,1,0:T(8,128)} %copy-done.3, f32[256,4,128]{2,1,0:T(4,128)} %collective-permute-done.4.after_ref, ...), custom_call_target="tpu_custom_call" | custom-call | tf_op jit(solution)/shard_map/pallas_call | solution.py:129
  99.5 1.9 collective-permute-start.9
  101.4 9.1 %collective-permute-start.10 = (f32[256,4,128]{2,1,0:T(4,128)}, f32[256,4,128]{2,1,0:T(4,128)S(1)}, u32[]{:S(2)}, u32[]{:S(2)}) collective-permute-start(f32[256,4,128]{2,1,0:T(4,128)} %get-tuple-element.31), channel_id=1, source_target_pairs={{1,0},{2,1},{3,2},{4,3},{5,4},{6,5},{7,6},{8,7},{9,8},{10,9},{11,1... | collective-permute-start | bytes 1572872 | tf_op jit(solution)/shard_map/ppermute | solution.py:26
  110.5 10.4 %shard_map.46 = (f32[256,8,128]{2,1,0:T(8,128)}, f32[256,4,128]{2,1,0:T(4,128)}, f32[256,4,128]{2,1,0:T(4,128)}) custom-call(f32[81]{0:T(128)} %reshape.12.taps_ref, f32[256,4,128]{2,1,0:T(4,128)} %collective-permute-done.3.before_ref, f32[256,8,128]{2,1,0:T(8,128)} %copy-done.3, f32[256,4,128]{2,1,0:T(4,128)} %collective-permute-done.4.after_ref, ...), custom_call_target="tpu_custom_call" | custom-call | tf_op jit(solution)/shard_map/pallas_call | solution.py:129
  120.9 1.9 collective-permute-start.5
  122.8 9.1 %collective-permute-start.6 = (f32[256,4,128]{2,1,0:T(4,128)}, f32[256,4,128]{2,1,0:T(4,128)}, u32[]{:S(2)}, u32[]{:S(2)}) collective-permute-start(f32[256,4,128]{2,1,0:T(4,128)} %get-tuple-element.25), channel_id=1, source_target_pairs={{1,0},{2,1},{3,2},{4,3},{5,4},{6,5},{7,6},{8,7},{9,8},{10,9},{11,1... | collective-permute-start | bytes 1572872 | tf_op jit(solution)/shard_map/ppermute | solution.py:26
  131.9 10.4 %shard_map.47 = (f32[256,8,128]{2,1,0:T(8,128)}, f32[256,4,128]{2,1,0:T(4,128)}, f32[256,4,128]{2,1,0:T(4,128)}) custom-call(f32[81]{0:T(128)} %reshape.12.taps_ref, f32[256,4,128]{2,1,0:T(4,128)} %collective-permute-done.3.before_ref, f32[256,8,128]{2,1,0:T(8,128)} %copy-done.3, f32[256,4,128]{2,1,0:T(4,128)} %collective-permute-done.4.after_ref, ...), custom_call_target="tpu_custom_call" | custom-call | tf_op jit(solution)/shard_map/pallas_call | solution.py:129
  142.2 1.9 collective-permute-start.7
  144.2 9.1 %collective-permute-start.8 = (f32[256,4,128]{2,1,0:T(4,128)}, f32[256,4,128]{2,1,0:T(4,128)}, u32[]{:S(2)}, u32[]{:S(2)}) collective-permute-start(f32[256,4,128]{2,1,0:T(4,128)} %get-tuple-element.28), channel_id=1, source_target_pairs={{1,0},{2,1},{3,2},{4,3},{5,4},{6,5},{7,6},{8,7},{9,8},{10,9},{11,1... | collective-permute-start | bytes 1572872 | tf_op jit(solution)/shard_map/ppermute | solution.py:26
  153.3 7.6 %collective-permute-done.7.refs_3_ = f32[256,4,128]{2,1,0:T(4,128)} collective-permute-done((f32[256,4,128]{2,1,0:T(4,128)}, f32[256,4,128]{2,1,0:T(4,128)}, u32[]{:S(2)}, u32[]{:S(2)}) %collective-permute-start.7) | collective-permute-done | bytes 524320 | tf_op jit(solution)/shard_map/ppermute | solution.py:25
  161.9 7.2 %shard_map.49 = f32[256,8,128]{2,1,0:T(8,128)} custom-call(f32[81]{0:T(128)} %reshape.12.taps_ref, f32[256,4,128]{2,1,0:T(4,128)} %collective-permute-done.5.refs_0_, f32[256,8,128]{2,1,0:T(8,128)} %get-tuple-element.24.refs_1_, f32[256,4,128]{2,1,0:T(4,128)} %collective-permute-done.6.refs_2_, f32[256,4,128]{2,1,0:T(4,128)} %collective-permute-done.7.refs_3_, ...), custom_call_target="tpu_custom_call" | custom-call | tf_op jit(solution)/shard_map/pallas_call | solution.py:170
  170.1 3.9 %collective-permute-start.11 = (f32[128,8,128]{2,1,0:T(8,128)S(1)}, f32[128,8,128]{2,1,0:T(8,128)S(1)}, u32[]{:S(2)}, u32[]{:S(2)}) collective-permute-start(f32[128,8,128]{2,1,0:T(8,128)S(1)} %constant_dynamic-slice_fusion.1), channel_id=1, source_target_pairs={{0,32},{32,0},{64,96},{96,64},{1,33},{33,1},{65,97},{97,65},{2,34}... | collective-permute-start | bytes 1572872 | tf_op jit(solution)/shard_map/ppermute | solution.py:188
  174.1 1.5 collective-permute-done.11
  177.7 12.2 %collective-permute-done.12 = f32[128,8,128]{2,1,0:T(8,128)S(1)} collective-permute-done((f32[128,8,128]{2,1,0:T(8,128)S(1)}, f32[128,8,128]{2,1,0:T(8,128)S(1)}, u32[]{:S(2)}, u32[]{:S(2)}) %collective-permute-start.12) | collective-permute-done | bytes 524320 | tf_op jit(solution)/shard_map/ppermute | solution.py:189
  191.3 1.5 collective-permute-done.13
  193.3 9.8 %collective-permute-start.15 = (f32[256,4,128]{2,1,0:T(4,128)S(1)}, f32[256,4,128]{2,1,0:T(4,128)S(1)}, u32[]{:S(2)}, u32[]{:S(2)}) collective-permute-start(f32[256,4,128]{2,1,0:T(4,128)S(1)} %get-tuple-element.46), channel_id=1, source_target_pairs={{1,0},{2,1},{3,2},{4,3},{5,4},{6,5},{7,6},{8,7},{9,8},{10,9},{11,1... | collective-permute-start | bytes 1572872 | tf_op jit(solution)/shard_map/ppermute | solution.py:26
  203.1 1.9 collective-permute-start.14
  205.1 9.0 %collective-permute-done.15.after_ref = f32[256,4,128]{2,1,0:T(4,128)S(1)} collective-permute-done((f32[256,4,128]{2,1,0:T(4,128)S(1)}, f32[256,4,128]{2,1,0:T(4,128)S(1)}, u32[]{:S(2)}, u32[]{:S(2)}) %collective-permute-start.15) | collective-permute-done | bytes 524320 | tf_op jit(solution)/shard_map/ppermute | solution.py:26
  214.1 9.6 %collective-permute-done.14.before_ref = f32[256,4,128]{2,1,0:T(4,128)} collective-permute-done((f32[256,4,128]{2,1,0:T(4,128)S(1)}, f32[256,4,128]{2,1,0:T(4,128)}, u32[]{:S(2)}, u32[]{:S(2)}) %collective-permute-start.14) | collective-permute-done | bytes 524320 | tf_op jit(solution)/shard_map/ppermute | solution.py:25
  223.7 10.4 %shard_map.52 = (f32[256,8,128]{2,1,0:T(8,128)}, f32[256,4,128]{2,1,0:T(4,128)}, f32[256,4,128]{2,1,0:T(4,128)}) custom-call(f32[81]{0:T(128)} %reshape.12.taps_ref, f32[256,4,128]{2,1,0:T(4,128)} %collective-permute-done.14.before_ref, f32[256,8,128]{2,1,0:T(8,128)} %copy-done.1, f32[256,4,128]{2,1,0:T(4,128)} %copy-done.9, bf16[256,8,128]{2,1,0:T(8,128)(2,1)} %bitcast.40), custom_call_target="tpu_custom_call" | custom-call | tf_op jit(solution)/shard_map/pallas_call | solution.py:129
  234.1 1.9 collective-permute-start.20
  236.0 9.3 %collective-permute-start.21 = (f32[256,4,128]{2,1,0:T(4,128)}, f32[256,4,128]{2,1,0:T(4,128)S(1)}, u32[]{:S(2)}, u32[]{:S(2)}) collective-permute-start(f32[256,4,128]{2,1,0:T(4,128)} %get-tuple-element.40), channel_id=1, source_target_pairs={{1,0},{2,1},{3,2},{4,3},{5,4},{6,5},{7,6},{8,7},{9,8},{10,9},{11,1... | collective-permute-start | bytes 1572872 | tf_op jit(solution)/shard_map/ppermute | solution.py:26
  245.2 10.3 %shard_map.50 = (f32[256,8,128]{2,1,0:T(8,128)}, f32[256,4,128]{2,1,0:T(4,128)}, f32[256,4,128]{2,1,0:T(4,128)}) custom-call(f32[81]{0:T(128)} %reshape.12.taps_ref, f32[256,4,128]{2,1,0:T(4,128)} %collective-permute-done.14.before_ref, f32[256,8,128]{2,1,0:T(8,128)} %copy-done.1, f32[256,4,128]{2,1,0:T(4,128)} %copy-done.9, bf16[256,8,128]{2,1,0:T(8,128)(2,1)} %bitcast.38), custom_call_target="tpu_custom_call" | custom-call | tf_op jit(solution)/shard_map/pallas_call | solution.py:129
  255.5 1.9 collective-permute-start.16
  257.5 9.1 %collective-permute-start.17 = (f32[256,4,128]{2,1,0:T(4,128)}, f32[256,4,128]{2,1,0:T(4,128)}, u32[]{:S(2)}, u32[]{:S(2)}) collective-permute-start(f32[256,4,128]{2,1,0:T(4,128)} %get-tuple-element.34), channel_id=1, source_target_pairs={{1,0},{2,1},{3,2},{4,3},{5,4},{6,5},{7,6},{8,7},{9,8},{10,9},{11,1... | collective-permute-start | bytes 1572872 | tf_op jit(solution)/shard_map/ppermute | solution.py:26
  266.5 10.4 %shard_map.51 = (f32[256,8,128]{2,1,0:T(8,128)}, f32[256,4,128]{2,1,0:T(4,128)}, f32[256,4,128]{2,1,0:T(4,128)}) custom-call(f32[81]{0:T(128)} %reshape.12.taps_ref, f32[256,4,128]{2,1,0:T(4,128)} %collective-permute-done.14.before_ref, f32[256,8,128]{2,1,0:T(8,128)} %copy-done.1, f32[256,4,128]{2,1,0:T(4,128)} %copy-done.9, bf16[256,8,128]{2,1,0:T(8,128)(2,1)} %bitcast.36), custom_call_target="tpu_custom_call" | custom-call | tf_op jit(solution)/shard_map/pallas_call | solution.py:129
  277.0 1.9 collective-permute-start.18
  278.9 9.1 %collective-permute-start.19 = (f32[256,4,128]{2,1,0:T(4,128)}, f32[256,4,128]{2,1,0:T(4,128)}, u32[]{:S(2)}, u32[]{:S(2)}) collective-permute-start(f32[256,4,128]{2,1,0:T(4,128)} %get-tuple-element.37), channel_id=1, source_target_pairs={{1,0},{2,1},{3,2},{4,3},{5,4},{6,5},{7,6},{8,7},{9,8},{10,9},{11,1... | collective-permute-start | bytes 1572872 | tf_op jit(solution)/shard_map/ppermute | solution.py:26
  288.1 7.6 %collective-permute-done.18.refs_3_ = f32[256,4,128]{2,1,0:T(4,128)} collective-permute-done((f32[256,4,128]{2,1,0:T(4,128)}, f32[256,4,128]{2,1,0:T(4,128)}, u32[]{:S(2)}, u32[]{:S(2)}) %collective-permute-start.18) | collective-permute-done | bytes 524320 | tf_op jit(solution)/shard_map/ppermute | solution.py:25
  296.6 7.2 %shard_map.53 = f32[256,8,128]{2,1,0:T(8,128)} custom-call(f32[81]{0:T(128)} %reshape.12.taps_ref, f32[256,4,128]{2,1,0:T(4,128)} %copy-done.14, f32[256,8,128]{2,1,0:T(8,128)} %get-tuple-element.33.refs_1_, f32[256,4,128]{2,1,0:T(4,128)} %collective-permute-done.17.refs_2_, f32[256,4,128]{2,1,0:T(4,128)} %collective-permute-done.18.refs_3_, ...), custom_call_target="tpu_custom_call" | custom-call | tf_op jit(solution)/shard_map/pallas_call | solution.py:170
  304.9 3.9 %collective-permute-start.22 = (f32[128,8,128]{2,1,0:T(8,128)S(1)}, f32[128,8,128]{2,1,0:T(8,128)S(1)}, u32[]{:S(2)}, u32[]{:S(2)}) collective-permute-start(f32[128,8,128]{2,1,0:T(8,128)S(1)} %constant_dynamic-slice_fusion), channel_id=1, source_target_pairs={{0,32},{32,0},{64,96},{96,64},{1,33},{33,1},{65,97},{97,65},{2,34}... | collective-permute-start | bytes 1572872 | tf_op jit(solution)/shard_map/ppermute | solution.py:188
  308.8 1.5 collective-permute-done.22
  312.5 12.2 %collective-permute-done.23 = f32[128,8,128]{2,1,0:T(8,128)S(1)} collective-permute-done((f32[128,8,128]{2,1,0:T(8,128)S(1)}, f32[128,8,128]{2,1,0:T(8,128)S(1)}, u32[]{:S(2)}, u32[]{:S(2)}) %collective-permute-start.23) | collective-permute-done | bytes 524320 | tf_op jit(solution)/shard_map/ppermute | solution.py:189
  326.0 1.5 collective-permute-done.24
  (75 shorter events, 19.0 us)
Async XLA Ops:
  0.0 1.7 copy-start
  7.2 30.4 %all-to-all-start = ((bf16[3,8,256,128]{3,1,0,2:T(8,128)(2,1)}), bf16[3,8,256,128]{3,1,0,2:T(8,128)(2,1)S(1)}, u32[]{:S(2)}, u32[]{:S(2)}) async-start(bf16[3,8,256,128]{3,1,0,2:T(8,128)(2,1)} %copy.7), calls=%async_computation | async-start | bytes 3145728 | tf_op jit(solution)/shard_map/all_to_all | solution.py:204
  38.2 1.3 copy-start.4
  38.2 1.3 copy-start.5
  38.2 1.3 copy-start.6
  39.5 5.2 %collective-permute-start = (f32[128,8,128]{2,1,0:T(8,128)}, f32[128,8,128]{2,1,0:T(8,128)S(1)}, u32[]{:S(2)}, u32[]{:S(2)}) collective-permute-start(f32[128,8,128]{2,1,0:T(8,128)} %constant_dynamic-slice_fusion.2), channel_id=1, source_target_pairs={{0,32},{32,0},{64,96},{96,64},{1,33},{33,1},{65,97},{97,65},{2,34}... | collective-permute-start | bytes 1572872 | tf_op jit(solution)/shard_map/ppermute | solution.py:188
  44.7 13.2 %collective-permute-start.1 = (f32[128,8,128]{2,1,0:T(8,128)S(1)}, f32[128,8,128]{2,1,0:T(8,128)S(1)}, u32[]{:S(2)}, u32[]{:S(2)}) collective-permute-start(f32[128,8,128]{2,1,0:T(8,128)S(1)} %dynamic-slice_add_fusion.2), channel_id=1, source_target_pairs={{0,64},{32,96},{64,0},{96,32},{1,65},{33,97},{65,1},{97,33},{2,66}... | collective-permute-start | bytes 1572872 | tf_op jit(solution)/shard_map/ppermute | solution.py:189
  58.0 2.8 collective-permute-start.2
  60.9 0.8 copy-start.7
  61.8 27.4 %copy-start.3 = (f32[256,8,128]{2,1,0:T(8,128)}, f32[256,8,128]{2,1,0:T(8,128)S(1)}, u32[]{:S(2)}) copy-start(f32[256,8,128]{2,1,0:T(8,128)S(1)} %maximum_multiply_fusion.mid_ref) | copy-start | bytes 3145732
  61.8 8.5 %copy-start.15 = (f32[3,3,9]{2,1,0:T(4,128)S(1)}, f32[3,3,9]{2,1,0:T(4,128)}, u32[]{:S(2)}) copy-start(f32[3,3,9]{2,1,0:T(4,128)} %param.7) | copy-start | bytes 976
  63.2 16.5 %collective-permute-start.4 = (f32[256,4,128]{2,1,0:T(4,128)}, f32[256,4,128]{2,1,0:T(4,128)}, u32[]{:S(2)}, u32[]{:S(2)}) collective-permute-start(f32[256,4,128]{2,1,0:T(4,128)} %get-tuple-element.50), channel_id=1, source_target_pairs={{1,0},{2,1},{3,2},{4,3},{5,4},{6,5},{7,6},{8,7},{9,8},{10,9},{11,1... | collective-permute-start | bytes 1572872 | tf_op jit(solution)/shard_map/ppermute | solution.py:26
  68.4 20.7 %collective-permute-start.3 = (f32[256,4,128]{2,1,0:T(4,128)}, f32[256,4,128]{2,1,0:T(4,128)}, u32[]{:S(2)}, u32[]{:S(2)}) collective-permute-start(f32[256,4,128]{2,1,0:T(4,128)} %get-tuple-element.51), channel_id=1, source_target_pairs={{0,1},{1,2},{2,3},{3,4},{4,5},{5,6},{6,7},{7,8},{8,9},{9,10},{10,1... | collective-permute-start | bytes 1572872 | tf_op jit(solution)/shard_map/ppermute | solution.py:25
  99.5 44.7 %collective-permute-start.9 = (f32[256,4,128]{2,1,0:T(4,128)}, f32[256,4,128]{2,1,0:T(4,128)S(1)}, u32[]{:S(2)}, u32[]{:S(2)}) collective-permute-start(f32[256,4,128]{2,1,0:T(4,128)} %get-tuple-element.29), channel_id=1, source_target_pairs={{0,1},{1,2},{2,3},{3,4},{4,5},{5,6},{6,7},{7,8},{8,9},{9,10},{10,1... | collective-permute-start | bytes 1572872 | tf_op jit(solution)/shard_map/ppermute | solution.py:25
  101.4 51.9 %collective-permute-start.10 = (f32[256,4,128]{2,1,0:T(4,128)}, f32[256,4,128]{2,1,0:T(4,128)S(1)}, u32[]{:S(2)}, u32[]{:S(2)}) collective-permute-start(f32[256,4,128]{2,1,0:T(4,128)} %get-tuple-element.31), channel_id=1, source_target_pairs={{1,0},{2,1},{3,2},{4,3},{5,4},{6,5},{7,6},{8,7},{9,8},{10,9},{11,1... | collective-permute-start | bytes 1572872 | tf_op jit(solution)/shard_map/ppermute | solution.py:26
  120.9 32.4 %collective-permute-start.5 = (f32[256,4,128]{2,1,0:T(4,128)}, f32[256,4,128]{2,1,0:T(4,128)}, u32[]{:S(2)}, u32[]{:S(2)}) collective-permute-start(f32[256,4,128]{2,1,0:T(4,128)} %get-tuple-element.23), channel_id=1, source_target_pairs={{0,1},{1,2},{2,3},{3,4},{4,5},{5,6},{6,7},{7,8},{8,9},{9,10},{10,1... | collective-permute-start | bytes 1572872 | tf_op jit(solution)/shard_map/ppermute | solution.py:25
  122.8 30.5 %collective-permute-start.6 = (f32[256,4,128]{2,1,0:T(4,128)}, f32[256,4,128]{2,1,0:T(4,128)}, u32[]{:S(2)}, u32[]{:S(2)}) collective-permute-start(f32[256,4,128]{2,1,0:T(4,128)} %get-tuple-element.25), channel_id=1, source_target_pairs={{1,0},{2,1},{3,2},{4,3},{5,4},{6,5},{7,6},{8,7},{9,8},{10,9},{11,1... | collective-permute-start | bytes 1572872 | tf_op jit(solution)/shard_map/ppermute | solution.py:26
  142.2 18.7 %collective-permute-start.7 = (f32[256,4,128]{2,1,0:T(4,128)}, f32[256,4,128]{2,1,0:T(4,128)}, u32[]{:S(2)}, u32[]{:S(2)}) collective-permute-start(f32[256,4,128]{2,1,0:T(4,128)} %get-tuple-element.26), channel_id=1, source_target_pairs={{0,1},{1,2},{2,3},{3,4},{4,5},{5,6},{6,7},{7,8},{8,9},{9,10},{10,1... | collective-permute-start | bytes 1572872 | tf_op jit(solution)/shard_map/ppermute | solution.py:25
  144.2 17.7 %copy-start.11 = (f32[256,4,128]{2,1,0:T(4,128)}, f32[256,4,128]{2,1,0:T(4,128)S(1)}, u32[]{:S(2)}) copy-start(f32[256,4,128]{2,1,0:T(4,128)S(1)} %collective-permute-done.9.refs_6_) | copy-start | bytes 1572868
  144.2 17.7 %collective-permute-start.8 = (f32[256,4,128]{2,1,0:T(4,128)}, f32[256,4,128]{2,1,0:T(4,128)}, u32[]{:S(2)}, u32[]{:S(2)}) collective-permute-start(f32[256,4,128]{2,1,0:T(4,128)} %get-tuple-element.28), channel_id=1, source_target_pairs={{1,0},{2,1},{3,2},{4,3},{5,4},{6,5},{7,6},{8,7},{9,8},{10,9},{11,1... | collective-permute-start | bytes 1572872 | tf_op jit(solution)/shard_map/ppermute | solution.py:26
  153.3 8.6 %copy-start.13 = (f32[256,4,128]{2,1,0:T(4,128)}, f32[256,4,128]{2,1,0:T(4,128)S(1)}, u32[]{:S(2)}) copy-start(f32[256,4,128]{2,1,0:T(4,128)S(1)} %collective-permute-done.10.refs_8_) | copy-start | bytes 1572868
  170.1 5.5 %collective-permute-start.11 = (f32[128,8,128]{2,1,0:T(8,128)S(1)}, f32[128,8,128]{2,1,0:T(8,128)S(1)}, u32[]{:S(2)}, u32[]{:S(2)}) collective-permute-start(f32[128,8,128]{2,1,0:T(8,128)S(1)} %constant_dynamic-slice_fusion.1), channel_id=1, source_target_pairs={{0,32},{32,0},{64,96},{96,64},{1,33},{33,1},{65,97},{97,65},{2,34}... | collective-permute-start | bytes 1572872 | tf_op jit(solution)/shard_map/ppermute | solution.py:188
  176.7 16.2 %copy-start.8 = (f32[128,8,128]{2,1,0:T(8,128)S(1)}, f32[128,8,128]{2,1,0:T(8,128)}, u32[]{:S(2)}) copy-start(f32[128,8,128]{2,1,0:T(8,128)} %copy-done.7) | copy-start | bytes 1572868
  176.7 13.2 %collective-permute-start.12 = (f32[128,8,128]{2,1,0:T(8,128)S(1)}, f32[128,8,128]{2,1,0:T(8,128)S(1)}, u32[]{:S(2)}, u32[]{:S(2)}) collective-permute-start(f32[128,8,128]{2,1,0:T(8,128)S(1)} %dynamic-slice_add_fusion.1), channel_id=1, source_target_pairs={{0,64},{32,96},{64,0},{96,32},{1,65},{33,97},{65,1},{97,33},{2,66}... | collective-permute-start | bytes 1572872 | tf_op jit(solution)/shard_map/ppermute | solution.py:189
  190.0 2.8 collective-permute-start.13
  193.1 30.6 %copy-start.1 = (f32[256,8,128]{2,1,0:T(8,128)}, f32[256,8,128]{2,1,0:T(8,128)S(1)}, u32[]{:S(2)}) copy-start(f32[256,8,128]{2,1,0:T(8,128)S(1)} %fusion.4.mid_ref) | copy-start | bytes 3145732
  193.3 20.8 %collective-permute-start.15 = (f32[256,4,128]{2,1,0:T(4,128)S(1)}, f32[256,4,128]{2,1,0:T(4,128)S(1)}, u32[]{:S(2)}, u32[]{:S(2)}) collective-permute-start(f32[256,4,128]{2,1,0:T(4,128)S(1)} %get-tuple-element.46), channel_id=1, source_target_pairs={{1,0},{2,1},{3,2},{4,3},{5,4},{6,5},{7,6},{8,7},{9,8},{10,9},{11,1... | collective-permute-start | bytes 1572872 | tf_op jit(solution)/shard_map/ppermute | solution.py:26
  203.1 20.5 %collective-permute-start.14 = (f32[256,4,128]{2,1,0:T(4,128)S(1)}, f32[256,4,128]{2,1,0:T(4,128)}, u32[]{:S(2)}, u32[]{:S(2)}) collective-permute-start(f32[256,4,128]{2,1,0:T(4,128)S(1)} %get-tuple-element.47), channel_id=1, source_target_pairs={{0,1},{1,2},{2,3},{3,4},{4,5},{5,6},{6,7},{7,8},{8,9},{9,10},{10,1... | collective-permute-start | bytes 1572872 | tf_op jit(solution)/shard_map/ppermute | solution.py:25
  214.1 9.6 %copy-start.9 = (f32[256,4,128]{2,1,0:T(4,128)}, f32[256,4,128]{2,1,0:T(4,128)S(1)}, u32[]{:S(2)}) copy-start(f32[256,4,128]{2,1,0:T(4,128)S(1)} %collective-permute-done.15.after_ref) | copy-start | bytes 1572868
  234.1 44.9 %collective-permute-start.20 = (f32[256,4,128]{2,1,0:T(4,128)}, f32[256,4,128]{2,1,0:T(4,128)S(1)}, u32[]{:S(2)}, u32[]{:S(2)}) collective-permute-start(f32[256,4,128]{2,1,0:T(4,128)} %get-tuple-element.38), channel_id=1, source_target_pairs={{0,1},{1,2},{2,3},{3,4},{4,5},{5,6},{6,7},{7,8},{8,9},{9,10},{10,1... | collective-permute-start | bytes 1572872 | tf_op jit(solution)/shard_map/ppermute | solution.py:25
  236.0 52.1 %collective-permute-start.21 = (f32[256,4,128]{2,1,0:T(4,128)}, f32[256,4,128]{2,1,0:T(4,128)S(1)}, u32[]{:S(2)}, u32[]{:S(2)}) collective-permute-start(f32[256,4,128]{2,1,0:T(4,128)} %get-tuple-element.40), channel_id=1, source_target_pairs={{1,0},{2,1},{3,2},{4,3},{5,4},{6,5},{7,6},{8,7},{9,8},{10,9},{11,1... | collective-permute-start | bytes 1572872 | tf_op jit(solution)/shard_map/ppermute | solution.py:26
  255.5 32.5 %collective-permute-start.16 = (f32[256,4,128]{2,1,0:T(4,128)}, f32[256,4,128]{2,1,0:T(4,128)S(1)}, u32[]{:S(2)}, u32[]{:S(2)}) collective-permute-start(f32[256,4,128]{2,1,0:T(4,128)} %get-tuple-element.32), channel_id=1, source_target_pairs={{0,1},{1,2},{2,3},{3,4},{4,5},{5,6},{6,7},{7,8},{8,9},{9,10},{10,1... | collective-permute-start | bytes 1572872 | tf_op jit(solution)/shard_map/ppermute | solution.py:25
  257.5 30.6 %collective-permute-start.17 = (f32[256,4,128]{2,1,0:T(4,128)}, f32[256,4,128]{2,1,0:T(4,128)}, u32[]{:S(2)}, u32[]{:S(2)}) collective-permute-start(f32[256,4,128]{2,1,0:T(4,128)} %get-tuple-element.34), channel_id=1, source_target_pairs={{1,0},{2,1},{3,2},{4,3},{5,4},{6,5},{7,6},{8,7},{9,8},{10,9},{11,1... | collective-permute-start | bytes 1572872 | tf_op jit(solution)/shard_map/ppermute | solution.py:26
  277.0 18.7 %collective-permute-start.18 = (f32[256,4,128]{2,1,0:T(4,128)}, f32[256,4,128]{2,1,0:T(4,128)}, u32[]{:S(2)}, u32[]{:S(2)}) collective-permute-start(f32[256,4,128]{2,1,0:T(4,128)} %get-tuple-element.35), channel_id=1, source_target_pairs={{0,1},{1,2},{2,3},{3,4},{4,5},{5,6},{6,7},{7,8},{8,9},{9,10},{10,1... | collective-permute-start | bytes 1572872 | tf_op jit(solution)/shard_map/ppermute | solution.py:25
  278.9 17.7 %copy-start.10 = (f32[256,4,128]{2,1,0:T(4,128)}, f32[256,4,128]{2,1,0:T(4,128)S(1)}, u32[]{:S(2)}) copy-start(f32[256,4,128]{2,1,0:T(4,128)S(1)} %collective-permute-done.20.refs_6_) | copy-start | bytes 1572868
  278.9 17.7 %collective-permute-start.19 = (f32[256,4,128]{2,1,0:T(4,128)}, f32[256,4,128]{2,1,0:T(4,128)}, u32[]{:S(2)}, u32[]{:S(2)}) collective-permute-start(f32[256,4,128]{2,1,0:T(4,128)} %get-tuple-element.37), channel_id=1, source_target_pairs={{1,0},{2,1},{3,2},{4,3},{5,4},{6,5},{7,6},{8,7},{9,8},{10,9},{11,1... | collective-permute-start | bytes 1572872 | tf_op jit(solution)/shard_map/ppermute | solution.py:26
  288.0 8.6 %copy-start.12 = (f32[256,4,128]{2,1,0:T(4,128)}, f32[256,4,128]{2,1,0:T(4,128)S(1)}, u32[]{:S(2)}) copy-start(f32[256,4,128]{2,1,0:T(4,128)S(1)} %collective-permute-done.21.refs_8_) | copy-start | bytes 1572868
  288.1 8.6 %copy-start.14 = (f32[256,4,128]{2,1,0:T(4,128)}, f32[256,4,128]{2,1,0:T(4,128)S(1)}, u32[]{:S(2)}) copy-start(f32[256,4,128]{2,1,0:T(4,128)S(1)} %collective-permute-done.16.refs_0_) | copy-start | bytes 1572868
  304.9 5.5 %collective-permute-start.22 = (f32[128,8,128]{2,1,0:T(8,128)S(1)}, f32[128,8,128]{2,1,0:T(8,128)S(1)}, u32[]{:S(2)}, u32[]{:S(2)}) collective-permute-start(f32[128,8,128]{2,1,0:T(8,128)S(1)} %constant_dynamic-slice_fusion), channel_id=1, source_target_pairs={{0,32},{32,0},{64,96},{96,64},{1,33},{33,1},{65,97},{97,65},{2,34}... | collective-permute-start | bytes 1572872 | tf_op jit(solution)/shard_map/ppermute | solution.py:188
  311.5 16.2 %copy-start.2 = (f32[256,8,128]{2,1,0:T(8,128)S(1)}, f32[256,8,128]{2,1,0:T(8,128)}, u32[]{:S(2)}) copy-start(f32[256,8,128]{2,1,0:T(8,128)} %copy-done.1) | copy-start | bytes 3145732
  311.5 13.2 %collective-permute-start.23 = (f32[128,8,128]{2,1,0:T(8,128)S(1)}, f32[128,8,128]{2,1,0:T(8,128)S(1)}, u32[]{:S(2)}, u32[]{:S(2)}) collective-permute-start(f32[128,8,128]{2,1,0:T(8,128)S(1)} %dynamic-slice_add_fusion), channel_id=1, source_target_pairs={{0,64},{32,96},{64,0},{96,32},{1,65},{33,97},{65,1},{97,33},{2,66}... | collective-permute-start | bytes 1572872 | tf_op jit(solution)/shard_map/ppermute | solution.py:189
  324.8 2.8 collective-permute-start.24

commit v6 on v5

--- a/solution.py
+++ b/solution.py
@@ -177,6 +177,173 @@
     )(taps_flat, *parts)
 
 
+def _pack(acc, first_ref, last_ref, p0):
+    half = acc.shape[0] // 2
+    upper, lower = acc[:half], acc[half:]
+    row = lax.broadcasted_iota(jnp.int32, upper.shape, 1)
+    first_ref[pl.ds(p0, half)] = jnp.where(row < 4, upper, pltpu.roll(lower, 4, 1))
+    last_ref[pl.ds(p0, half)] = jnp.where(row < 4, pltpu.roll(upper, 4, 1), lower)
+
+
+def _unpack(packed_ref, p0):
+    packed = packed_ref[pl.ds(p0, CZ // 2)]
+    return jnp.concatenate([packed, pltpu.roll(packed, 4, 1)], axis=0)
+
+
+def _iteration_kernel(
+    taps_ref, before_ref, mid_ref, after_ref, brick_ref, logs_ref,
+    a_ref, c_ref, ext_ref, part_ref, send_ref, recv_ref, send_sem, recv_sem,
+):
+    count, nz, width, ny = part_ref.shape
+    me = lax.axis_index("vol")
+    view = lax.axis_index("view")
+    has_lo = me > 0
+    has_hi = me < lax.axis_size("vol") - 1
+    barrier = pltpu.get_barrier_semaphore()
+
+    @pl.when(has_lo)
+    def _():
+        pl.semaphore_signal(barrier, inc=1, device_id=(view, me - 1), device_id_type=pl.DeviceIdType.MESH)
+
+    @pl.when(has_hi)
+    def _():
+        pl.semaphore_signal(barrier, inc=1, device_id=(view, me + 1), device_id_type=pl.DeviceIdType.MESH)
+
+    pl.semaphore_wait(barrier, has_lo.astype(jnp.int32) + has_hi.astype(jnp.int32))
+
+    @pl.when(jnp.logical_not(has_lo))
+    def _():
+        recv_ref[:, 0] = jnp.zeros(recv_ref.shape[:1] + recv_ref.shape[2:], jnp.float32)
+
+    @pl.when(jnp.logical_not(has_hi))
+    def _():
+        recv_ref[:, 1] = jnp.zeros(recv_ref.shape[:1] + recv_ref.shape[2:], jnp.float32)
+
+    def copies(v):
+        up = pltpu.make_async_remote_copy(
+            src_ref=send_ref.at[v, 1], dst_ref=recv_ref.at[v, 0],
+            send_sem=send_sem.at[v, 1], recv_sem=recv_sem.at[v, 0],
+            device_id=(view, me + 1), device_id_type=pl.DeviceIdType.MESH,
+        )
+        down = pltpu.make_async_remote_copy(
+            src_ref=send_ref.at[v, 0], dst_ref=recv_ref.at[v, 1],
+            send_sem=send_sem.at[v, 0], recv_sem=recv_sem.at[v, 1],
+            device_id=(view, me - 1), device_id_type=pl.DeviceIdType.MESH,
+        )
+        return up, down
+
+    zeros = jnp.zeros((4, width, ny), jnp.float32)
+    a_ref[0:4] = zeros
+    a_ref[nz + 4 : nz + 8] = zeros
+    c_ref[0:4] = zeros
+    c_ref[nz + 4 : nz + 8] = zeros
+    for v in range(count):
+        tx = [taps_ref[v * 27 + 9 + t] for t in range(9)]
+        tz = [taps_ref[v * 27 + t] for t in range(9)]
+        ty = [taps_ref[v * 27 + 18 + t] for t in range(9)]
+
+        def along_x(c, carry):
+            z0 = pl.multiple_of(c * CZ, CZ)
+            _fill_wide(ext_ref, before_ref, mid_ref, after_ref, z0)
+            acc = tx[0] * ext_ref[:, pl.ds(0, 8), :]
+            for t in range(1, 9):
+                acc = acc + tx[t] * ext_ref[:, pl.ds(t, 8), :]
+            a_ref[pl.ds(z0 + 4, CZ)] = acc
+            return carry
+
+        lax.fori_loop(0, nz // CZ, along_x, 0)
+        wy = _lane_weights(ty, ny, False)
+        wy_rev = _lane_weights(ty, ny, True)
+
+        def middle(c, carry):
+            z0 = pl.multiple_of(c * CZ, CZ)
+            acc = tz[0] * a_ref[pl.ds(z0, CZ)]
+            for t in range(1, 9):
+                acc = acc + tz[t] * a_ref[pl.ds(z0 + t, CZ)]
+            blurred = _lane_correlate(acc, wy)
+            ratio = brick_ref[v, pl.ds(z0, CZ)].astype(jnp.float32) / blurred
+            c_ref[pl.ds(z0 + 4, CZ)] = _lane_correlate(ratio, wy_rev)
+            return carry
+
+        lax.fori_loop(0, nz // CZ, middle, 0)
+
+        def along_z_back(c, carry):
+            z0 = pl.multiple_of(c * CZ, CZ)
+            acc = tz[8] * c_ref[pl.ds(z0, CZ)]
+            for t in range(1, 9):
+                acc = acc + tz[8 - t] * c_ref[pl.ds(z0 + t, CZ)]
+            part_ref[v, pl.ds(z0, CZ)] = acc
+            _pack(acc, send_ref.at[v, 0], send_ref.at[v, 1], pl.multiple_of(c * (CZ // 2), CZ // 2))
+            return carry
+
+        lax.fori_loop(0, nz // CZ, along_z_back, 0)
+        up, down = copies(v)
+
+        @pl.when(has_hi)
+        def _():
+            up.start()
+
+        @pl.when(has_lo)
+        def _():
+            down.start()
+
+    for v in range(count):
+        up, down = copies(v)
+
+        @pl.when(has_hi)
+        def _():
+            up.wait_send()
+            down.wait_recv()
+
+        @pl.when(has_lo)
+        def _():
+            down.wait_send()
+            up.wait_recv()
+
+    tb = [[taps_ref[v * 27 + 9 + t] for t in range(9)] for v in range(count)]
+
+    def back(c, carry):
+        z0 = pl.multiple_of(c * CZ, CZ)
+        p0 = pl.multiple_of(c * (CZ // 2), CZ // 2)
+        total = None
+        for v in range(count):
+            ext_ref[:, 0:4, :] = _unpack(recv_ref.at[v, 0], p0)[:, 0:4, :]
+            ext_ref[:, 4 : 4 + width, :] = part_ref[v, pl.ds(z0, CZ)]
+            ext_ref[:, 4 + width :, :] = _unpack(recv_ref.at[v, 1], p0)[:, 0:4, :]
+            acc = tb[v][8] * ext_ref[:, pl.ds(0, 8), :]
+            for t in range(1, 9):
+                acc = acc + tb[v][8 - t] * ext_ref[:, pl.ds(t, 8), :]
+            term = jnp.log(acc)
+            total = term if total is None else total + term
+        logs_ref[pl.ds(z0, CZ)] = total
+        return carry
+
+    lax.fori_loop(0, nz // CZ, back, 0)
+
+
+def iteration_logs(taps_flat, before, mid, after, bricks):
+    count, nz, width, ny = bricks.shape
+    return pl.pallas_call(
+        _iteration_kernel,
+        in_specs=[pl.BlockSpec(memory_space=pltpu.SMEM)] + [pl.BlockSpec(memory_space=pltpu.VMEM)] * 4,
+        out_specs=pl.BlockSpec(memory_space=pltpu.VMEM),
+        out_shape=jax.ShapeDtypeStruct((nz, width, ny), jnp.float32),
+        scratch_shapes=[
+            pltpu.VMEM((nz + 8, width, ny), jnp.float32),
+            pltpu.VMEM((nz + 8, width, ny), jnp.float32),
+            pltpu.VMEM((CZ, width + 8, ny), jnp.float32),
+            pltpu.VMEM((count, nz, width, ny), jnp.float32),
+            pltpu.VMEM((count, 2, nz // 2, width, ny), jnp.float32),
+            pltpu.VMEM((count, 2, nz // 2, width, ny), jnp.float32),
+            pltpu.SemaphoreType.DMA((count, 2)),
+            pltpu.SemaphoreType.DMA((count, 2)),
+        ],
+        compiler_params=pltpu.CompilerParams(
+            collective_id=0, has_side_effects=True, vmem_limit_bytes=48 * 1024 * 1024
+        ),
+    )(taps_flat, before, mid, after, bricks)
+
+
 def view_sum(part):
     count = lax.axis_size("view")
     core_swap = [(i, i ^ 1) for i in range(count)]
@@ -208,14 +375,7 @@
     joined_volume = view_sum(local_sum) / total_views
     for turn in range(ITERS):
         before, after = halos(joined_volume, "vol", 1, rim_width)
-        parts = []
-        for index in range(count):
-            partial_value, first, last = forward_partial(
-                taps_flat, index, before, joined_volume, after, bricks[index]
-            )
-            low, high = swap_rims(first, last, "vol")
-            parts += [low, partial_value, high]
-        logs = back_logs(taps_flat, parts)
+        logs = iteration_logs(taps_flat, before, joined_volume, after, bricks)
         summed = view_sum(logs)
         joined_volume = joined_volume * jnp.exp(summed / total_views)
     return joined_volume

time: 332 us -> 267 us (0.80)
  starting transfers between devices: 114 us -> 38.1 us
  Pallas kernels: 76.5 us -> 104 us
  waiting for transfers between devices: 120 us -> 102 us
    ppermute x8 -> x2, starting transfers between devices: 69.8 us -> 7.18 us  [swap_rims(): after = lax.ppermute(first, axis, down)]
    pallas_call x8 -> x2, Pallas kernels: 76.5 us -> 104 us  [iteration_logs(): pl.pallas_call(_iteration_kernel, in_specs=[pl.BlockSpec(memory_space=plt...]
    ppermute x8 -> x2, waiting for transfers between devices: 34.4 us -> 16.9 us  [swap_rims(): before = lax.ppermute(last, axis, up)]
    ppermute x8 -> x2, starting transfers between devices: 15.3 us -> 5.26 us  [swap_rims(): before = lax.ppermute(last, axis, up)]
    unnamed x36 -> x24, local copies, waits for them, and re-layouts: 0.88 us -> 5.38 us
    ppermute x8 -> x2, waiting for transfers between devices: 19.4 us -> 18.9 us  [swap_rims(): after = lax.ppermute(first, axis, down)]
  transfers between devices with their start and end apart: 26 -> 14, of which waited for: 18 -> 14; matrix products, arithmetic and copies ran while one was open for 0% -> 0% of each run, Pallas kernels for 13% -> 0%
where the time goes in v6:
time: 267 us
  Pallas kernels  104 us (39%)
  waiting for transfers between devices  102 us (38%)
  starting transfers between devices  38.1 us (14%)
  local copies, waits for them, and re-layouts  11.7 us (4%)
  other arithmetic  7.22 us (3%)
  matrix products  3.33 us (1%)
    pallas_call x2, Pallas kernels, iteration_logs(): pl.pallas_call(_iteration_kernel, in_specs=[pl.BlockSpec(memory_space=plt...  104 us
    ppermute x3, waiting for transfers between devices, view_sum(): own = own + lax.ppermute(own, 'view', chip_swap)  36.7 us
    all_to_all x1, waiting for transfers between devices, per_device(): lax.all_to_all(local_views, 'vol', split_axis=2, concat_axis=1, tiled=True)  19.8 us
    ppermute x2, waiting for transfers between devices, swap_rims(): after = lax.ppermute(first, axis, down)  18.9 us
    ppermute x2, waiting for transfers between devices, swap_rims(): before = lax.ppermute(last, axis, up)  16.9 us
    all_to_all x1, starting transfers between devices, per_device(): lax.all_to_all(local_views, 'vol', split_axis=2, concat_axis=1, tiled=True)  10.5 us
    ppermute x3, starting transfers between devices, view_sum(): own = own + lax.ppermute(give, 'view', core_swap)  8.39 us
    ppermute x2, starting transfers between devices, swap_rims(): after = lax.ppermute(first, axis, down)  7.18 us
  transfers between devices with their start and end apart: 14, of which 14 were waited for; matrix products, arithmetic and copies ran while one was open for 0% of the time, Pallas kernels for 0%

profile of v6, /device:TPU:5, one launch (start us, length us, event | category | flops | bytes accessed | tf_op | source)
XLA Modules:
  0.0 266.5 jit_solution(9492251560038266915)
XLA Ops:
  0.0 0.9 reduce_sum.18
  0.9 0.7 broadcast_divide_fusion
  1.7 3.3 %fusion.1 = bf16[3,8,256,128]{3,2,1,0:T(8,128)(2,1)S(1)} fusion(bf16[3,8,256,128]{3,2,1,0:T(8,128)(2,1)S(1)} %copy-done, f32[3,256]{1,0:T(4,128)S(1)} %get-tuple-element.25, f32[3,256]{1,0:T(4,128)S(1)} %get-tuple-element.26, f32[3,256]{1,0:T(4,128)S(1)} %get-tuple-element.27, f32[3,256]{1,0:T(4,128)S(1)} %get-tuple-element.28, ...), kind=kOutput, calls=%fused_computation.2 | convolution fusion | flops 2421424128 | bytes 3173376 | tf_op jit(solution)/shard_map/vxr,vzry->vzxy/dot_general | solution.py:45
  5.0 2.2 copy.7
  7.2 10.5 %all-to-all-start = ((bf16[3,8,256,128]{3,1,0,2:T(8,128)(2,1)}), bf16[3,8,256,128]{3,1,0,2:T(8,128)(2,1)S(1)}, u32[]{:S(2)}, u32[]{:S(2)}) async-start(bf16[3,8,256,128]{3,1,0,2:T(8,128)(2,1)} %copy.7), calls=%async_computation | async-start | bytes 3145728 | tf_op jit(solution)/shard_map/all_to_all | solution.py:371
  17.8 19.8 %all-to-all-done = bf16[3,8,256,128]{3,1,0,2:T(8,128)(2,1)S(1)} async-done(((bf16[3,8,256,128]{3,1,0,2:T(8,128)(2,1)}), bf16[3,8,256,128]{3,1,0,2:T(8,128)(2,1)S(1)}, u32[]{:S(2)}, u32[]{:S(2)}) %all-to-all-start) | async-done | bytes 1572896 | tf_op jit(solution)/shard_map/all_to_all | solution.py:371
  37.6 1.2 copy-done.3
  38.8 1.8 copy.28
  40.7 0.3 convert_add_fusion
  40.9 1.0 copy-done.8
  41.9 0.8 constant_dynamic-slice_fusion.2
  42.8 3.3 %collective-permute-start = (f32[128,8,128]{2,1,0:T(8,128)}, f32[128,8,128]{2,1,0:T(8,128)}, u32[]{:S(2)}, u32[]{:S(2)}) collective-permute-start(f32[128,8,128]{2,1,0:T(8,128)} %constant_dynamic-slice_fusion.2), channel_id=1, source_target_pairs={{0,32},{32,0},{64,96},{96,64},{1,33},{33,1},{65,97},{97,65},{2,34}... | collective-permute-start | bytes 1572872 | tf_op jit(solution)/shard_map/ppermute | solution.py:355
  46.1 1.9 collective-permute-done
  48.0 1.3 dynamic-slice_add_fusion.2
  49.2 1.0 collective-permute-start.1
  50.2 12.2 %collective-permute-done.1 = f32[128,8,128]{2,1,0:T(8,128)S(1)} collective-permute-done((f32[128,8,128]{2,1,0:T(8,128)S(1)}, f32[128,8,128]{2,1,0:T(8,128)S(1)}, u32[]{:S(2)}, u32[]{:S(2)}) %collective-permute-start.1) | collective-permute-done | bytes 524320 | tf_op jit(solution)/shard_map/ppermute | solution.py:356
  62.4 0.8 add.79
  63.3 1.2 collective-permute-start.2
  64.5 1.9 collective-permute-done.2
  66.4 1.3 broadcast_select_fusion.5
  67.7 0.8 copy-done.4
  68.8 1.1 fusion.68
  69.9 1.0 copy-done.1
  70.9 5.2 %collective-permute-start.4 = (f32[256,4,128]{2,1,0:T(4,128)}, f32[256,4,128]{2,1,0:T(4,128)}, u32[]{:S(2)}, u32[]{:S(2)}) collective-permute-start(f32[256,4,128]{2,1,0:T(4,128)} %get-tuple-element.13), channel_id=1, source_target_pairs={{1,0},{2,1},{3,2},{4,3},{5,4},{6,5},{7,6},{8,7},{9,8},{10,9},{11,1... | collective-permute-start | bytes 1572872 | tf_op jit(solution)/shard_map/ppermute | solution.py:26
  76.1 1.9 collective-permute-start.3
  78.2 9.1 %collective-permute-done.4.after_ref = f32[256,4,128]{2,1,0:T(4,128)} collective-permute-done((f32[256,4,128]{2,1,0:T(4,128)}, f32[256,4,128]{2,1,0:T(4,128)}, u32[]{:S(2)}, u32[]{:S(2)}) %collective-permute-start.4) | collective-permute-done | bytes 524320 | tf_op jit(solution)/shard_map/ppermute | solution.py:26
  87.3 9.5 %collective-permute-done.3.before_ref = f32[256,4,128]{2,1,0:T(4,128)} collective-permute-done((f32[256,4,128]{2,1,0:T(4,128)}, f32[256,4,128]{2,1,0:T(4,128)}, u32[]{:S(2)}, u32[]{:S(2)}) %collective-permute-start.3) | collective-permute-done | bytes 524320 | tf_op jit(solution)/shard_map/ppermute | solution.py:25
  96.8 1.2 copy-done.2
  98.1 52.2 %shard_map.46 = f32[256,8,128]{2,1,0:T(8,128)S(1)} custom-call(f32[81]{0:T(128)S(1)} %reshape.17.taps_ref, f32[256,4,128]{2,1,0:T(4,128)} %collective-permute-done.3.before_ref, f32[256,8,128]{2,1,0:T(8,128)S(1)} %copy-done.2, f32[256,4,128]{2,1,0:T(4,128)} %collective-permute-done.4.after_ref, bf16[3,256,8,128]{3,2,1,0:T(8,128)(2,1)S(1)} %bitcast.32), custom_call_target="tpu_custom_call" | custom-call | tf_op jit(solution)/shard_map/pallas_call | solution.py:326
  150.3 2.5 collective-permute-start.5
  152.9 1.5 collective-permute-done.5
  154.5 1.0 collective-permute-start.6
  155.5 12.2 %collective-permute-done.6 = f32[128,8,128]{2,1,0:T(8,128)S(1)} collective-permute-done((f32[128,8,128]{2,1,0:T(8,128)S(1)}, f32[128,8,128]{2,1,0:T(8,128)S(1)}, u32[]{:S(2)}, u32[]{:S(2)}) %collective-permute-start.6) | collective-permute-done | bytes 524320 | tf_op jit(solution)/shard_map/ppermute | solution.py:356
  167.7 1.3 collective-permute-start.7
  169.0 1.5 collective-permute-done.7
  170.7 0.2 fusion.4.mid_ref
  171.0 1.9 collective-permute-start.9
  173.0 3.3 %collective-permute-start.8 = (f32[256,4,128]{2,1,0:T(4,128)S(1)}, f32[256,4,128]{2,1,0:T(4,128)S(1)}, u32[]{:S(2)}, u32[]{:S(2)}) collective-permute-start(f32[256,4,128]{2,1,0:T(4,128)S(1)} %get-tuple-element.10), channel_id=1, source_target_pairs={{0,1},{1,2},{2,3},{3,4},{4,5},{5,6},{6,7},{7,8},{8,9},{9,10},{10,1... | collective-permute-start | bytes 1572872 | tf_op jit(solution)/shard_map/ppermute | solution.py:25
  176.3 9.7 %collective-permute-done.9.after_ref = f32[256,4,128]{2,1,0:T(4,128)S(1)} collective-permute-done((f32[256,4,128]{2,1,0:T(4,128)S(1)}, f32[256,4,128]{2,1,0:T(4,128)S(1)}, u32[]{:S(2)}, u32[]{:S(2)}) %collective-permute-start.9) | collective-permute-done | bytes 524320 | tf_op jit(solution)/shard_map/ppermute | solution.py:26
  186.1 7.4 %collective-permute-done.8.before_ref = f32[256,4,128]{2,1,0:T(4,128)S(1)} collective-permute-done((f32[256,4,128]{2,1,0:T(4,128)S(1)}, f32[256,4,128]{2,1,0:T(4,128)S(1)}, u32[]{:S(2)}, u32[]{:S(2)}) %collective-permute-start.8) | collective-permute-done | bytes 524320 | tf_op jit(solution)/shard_map/ppermute | solution.py:25
  193.4 51.5 %shard_map.47 = f32[256,8,128]{2,1,0:T(8,128)S(1)} custom-call(f32[81]{0:T(128)S(1)} %reshape.17.taps_ref, f32[256,4,128]{2,1,0:T(4,128)S(1)} %collective-permute-done.8.before_ref, f32[256,8,128]{2,1,0:T(8,128)S(1)} %fusion.4.mid_ref, f32[256,4,128]{2,1,0:T(4,128)S(1)} %collective-permute-done.9.after_ref, bf16[3,256,8,128]{3,2,1,0:T(8,128)(2,1)S(1)} %bitcast.33), custom_call_target="tpu_custom_call" | custom-call | tf_op jit(solution)/shard_map/pallas_call | solution.py:326
  245.0 2.5 collective-permute-start.10
  247.6 1.5 collective-permute-done.10
  249.2 1.0 collective-permute-start.11
  250.2 12.2 %collective-permute-done.11 = f32[128,8,128]{2,1,0:T(8,128)S(1)} collective-permute-done((f32[128,8,128]{2,1,0:T(8,128)S(1)}, f32[128,8,128]{2,1,0:T(8,128)S(1)}, u32[]{:S(2)}, u32[]{:S(2)}) %collective-permute-start.11) | collective-permute-done | bytes 524320 | tf_op jit(solution)/shard_map/ppermute | solution.py:356
  262.5 1.3 collective-permute-start.12
  263.7 1.5 collective-permute-done.12
  265.4 1.2 fusion.6
  (32 shorter events, 1.2 us)
Async XLA Ops:
  0.0 1.7 copy-start
  7.2 30.4 %all-to-all-start = ((bf16[3,8,256,128]{3,1,0,2:T(8,128)(2,1)}), bf16[3,8,256,128]{3,1,0,2:T(8,128)(2,1)S(1)}, u32[]{:S(2)}, u32[]{:S(2)}) async-start(bf16[3,8,256,128]{3,1,0,2:T(8,128)(2,1)} %copy.7), calls=%async_computation | async-start | bytes 3145728 | tf_op jit(solution)/shard_map/all_to_all | solution.py:371
  37.6 1.2 copy-start.3
  40.9 1.0 copy-start.8
  42.8 5.2 %collective-permute-start = (f32[128,8,128]{2,1,0:T(8,128)}, f32[128,8,128]{2,1,0:T(8,128)}, u32[]{:S(2)}, u32[]{:S(2)}) collective-permute-start(f32[128,8,128]{2,1,0:T(8,128)} %constant_dynamic-slice_fusion.2), channel_id=1, source_target_pairs={{0,32},{32,0},{64,96},{96,64},{1,33},{33,1},{65,97},{97,65},{2,34}... | collective-permute-start | bytes 1572872 | tf_op jit(solution)/shard_map/ppermute | solution.py:355
  49.2 13.2 %collective-permute-start.1 = (f32[128,8,128]{2,1,0:T(8,128)S(1)}, f32[128,8,128]{2,1,0:T(8,128)S(1)}, u32[]{:S(2)}, u32[]{:S(2)}) collective-permute-start(f32[128,8,128]{2,1,0:T(8,128)S(1)} %dynamic-slice_add_fusion.2), channel_id=1, source_target_pairs={{0,64},{32,96},{64,0},{96,32},{1,65},{33,97},{65,1},{97,33},{2,66}... | collective-permute-start | bytes 1572872 | tf_op jit(solution)/shard_map/ppermute | solution.py:356
  63.3 3.1 %collective-permute-start.2 = (f32[128,8,128]{2,1,0:T(8,128)}, f32[128,8,128]{2,1,0:T(8,128)}, u32[]{:S(2)}, u32[]{:S(2)}) collective-permute-start(f32[128,8,128]{2,1,0:T(8,128)} %add.79), channel_id=1, source_target_pairs={{0,32},{32,0},{64,96},{96,64},{1,33},{33,1},{65,97},{97,65},{2,34}... | collective-permute-start | bytes 1572872 | tf_op jit(solution)/shard_map/ppermute | solution.py:357
  67.6 0.8 copy-start.4
  67.7 1.0 copy-start.6
  68.8 9.3 %copy-start.9 = (f32[3,3,9]{2,1,0:T(4,128)S(1)}, f32[3,3,9]{2,1,0:T(4,128)}, u32[]{:S(2)}) copy-start(f32[3,3,9]{2,1,0:T(4,128)} %param.7) | copy-start | bytes 976
  69.9 1.0 copy-start.1
  70.9 16.5 %collective-permute-start.4 = (f32[256,4,128]{2,1,0:T(4,128)}, f32[256,4,128]{2,1,0:T(4,128)}, u32[]{:S(2)}, u32[]{:S(2)}) collective-permute-start(f32[256,4,128]{2,1,0:T(4,128)} %get-tuple-element.13), channel_id=1, source_target_pairs={{1,0},{2,1},{3,2},{4,3},{5,4},{6,5},{7,6},{8,7},{9,8},{10,9},{11,1... | collective-permute-start | bytes 1572872 | tf_op jit(solution)/shard_map/ppermute | solution.py:26
  76.1 20.7 %collective-permute-start.3 = (f32[256,4,128]{2,1,0:T(4,128)}, f32[256,4,128]{2,1,0:T(4,128)}, u32[]{:S(2)}, u32[]{:S(2)}) collective-permute-start(f32[256,4,128]{2,1,0:T(4,128)} %get-tuple-element.14), channel_id=1, source_target_pairs={{0,1},{1,2},{2,3},{3,4},{4,5},{5,6},{6,7},{7,8},{8,9},{9,10},{10,1... | collective-permute-start | bytes 1572872 | tf_op jit(solution)/shard_map/ppermute | solution.py:25
  96.8 1.2 copy-start.2
  150.3 4.1 %collective-permute-start.5 = (f32[128,8,128]{2,1,0:T(8,128)S(1)}, f32[128,8,128]{2,1,0:T(8,128)S(1)}, u32[]{:S(2)}, u32[]{:S(2)}) collective-permute-start(f32[128,8,128]{2,1,0:T(8,128)S(1)} %constant_dynamic-slice_fusion.1), channel_id=1, source_target_pairs={{0,32},{32,0},{64,96},{96,64},{1,33},{33,1},{65,97},{97,65},{2,34}... | collective-permute-start | bytes 1572872 | tf_op jit(solution)/shard_map/ppermute | solution.py:355
  154.4 16.2 %copy-start.5 = (f32[128,8,128]{2,1,0:T(8,128)S(1)}, f32[128,8,128]{2,1,0:T(8,128)}, u32[]{:S(2)}) copy-start(f32[128,8,128]{2,1,0:T(8,128)} %copy-done.4) | copy-start | bytes 1572868
  154.5 16.2 %copy-start.7 = (f32[128,8,128]{2,1,0:T(8,128)S(1)}, f32[128,8,128]{2,1,0:T(8,128)}, u32[]{:S(2)}) copy-start(f32[128,8,128]{2,1,0:T(8,128)} %copy-done.6) | copy-start | bytes 1572868
  154.5 13.2 %collective-permute-start.6 = (f32[128,8,128]{2,1,0:T(8,128)S(1)}, f32[128,8,128]{2,1,0:T(8,128)S(1)}, u32[]{:S(2)}, u32[]{:S(2)}) collective-permute-start(f32[128,8,128]{2,1,0:T(8,128)S(1)} %dynamic-slice_add_fusion.1), channel_id=1, source_target_pairs={{0,64},{32,96},{64,0},{96,32},{1,65},{33,97},{65,1},{97,33},{2,66}... | collective-permute-start | bytes 1572872 | tf_op jit(solution)/shard_map/ppermute | solution.py:356
  167.7 2.8 %collective-permute-start.7 = (f32[128,8,128]{2,1,0:T(8,128)S(1)}, f32[128,8,128]{2,1,0:T(8,128)S(1)}, u32[]{:S(2)}, u32[]{:S(2)}) collective-permute-start(f32[128,8,128]{2,1,0:T(8,128)S(1)} %add.81), channel_id=1, source_target_pairs={{0,32},{32,0},{64,96},{96,64},{1,33},{33,1},{65,97},{97,65},{2,34}... | collective-permute-start | bytes 1572872 | tf_op jit(solution)/shard_map/ppermute | solution.py:357
  171.0 15.0 %collective-permute-start.9 = (f32[256,4,128]{2,1,0:T(4,128)S(1)}, f32[256,4,128]{2,1,0:T(4,128)S(1)}, u32[]{:S(2)}, u32[]{:S(2)}) collective-permute-start(f32[256,4,128]{2,1,0:T(4,128)S(1)} %get-tuple-element.9), channel_id=1, source_target_pairs={{1,0},{2,1},{3,2},{4,3},{5,4},{6,5},{7,6},{8,7},{9,8},{10,9},{11,1... | collective-permute-start | bytes 1572872 | tf_op jit(solution)/shard_map/ppermute | solution.py:26
  173.0 20.4 %collective-permute-start.8 = (f32[256,4,128]{2,1,0:T(4,128)S(1)}, f32[256,4,128]{2,1,0:T(4,128)S(1)}, u32[]{:S(2)}, u32[]{:S(2)}) collective-permute-start(f32[256,4,128]{2,1,0:T(4,128)S(1)} %get-tuple-element.10), channel_id=1, source_target_pairs={{0,1},{1,2},{2,3},{3,4},{4,5},{5,6},{6,7},{7,8},{8,9},{9,10},{10,1... | collective-permute-start | bytes 1572872 | tf_op jit(solution)/shard_map/ppermute | solution.py:25
  245.0 4.1 %collective-permute-start.10 = (f32[128,8,128]{2,1,0:T(8,128)S(1)}, f32[128,8,128]{2,1,0:T(8,128)S(1)}, u32[]{:S(2)}, u32[]{:S(2)}) collective-permute-start(f32[128,8,128]{2,1,0:T(8,128)S(1)} %constant_dynamic-slice_fusion), channel_id=1, source_target_pairs={{0,32},{32,0},{64,96},{96,64},{1,33},{33,1},{65,97},{97,65},{2,34}... | collective-permute-start | bytes 1572872 | tf_op jit(solution)/shard_map/ppermute | solution.py:355
  249.2 13.2 %collective-permute-start.11 = (f32[128,8,128]{2,1,0:T(8,128)S(1)}, f32[128,8,128]{2,1,0:T(8,128)S(1)}, u32[]{:S(2)}, u32[]{:S(2)}) collective-permute-start(f32[128,8,128]{2,1,0:T(8,128)S(1)} %dynamic-slice_add_fusion), channel_id=1, source_target_pairs={{0,64},{32,96},{64,0},{96,32},{1,65},{33,97},{65,1},{97,33},{2,66}... | collective-permute-start | bytes 1572872 | tf_op jit(solution)/shard_map/ppermute | solution.py:356
  262.5 2.8 %collective-permute-start.12 = (f32[128,8,128]{2,1,0:T(8,128)S(1)}, f32[128,8,128]{2,1,0:T(8,128)S(1)}, u32[]{:S(2)}, u32[]{:S(2)}) collective-permute-start(f32[128,8,128]{2,1,0:T(8,128)S(1)} %add.83), channel_id=1, source_target_pairs={{0,32},{32,0},{64,96},{96,64},{1,33},{33,1},{65,97},{97,65},{2,34}... | collective-permute-start | bytes 1572872 | tf_op jit(solution)/shard_map/ppermute | solution.py:357

commit v7 on v6

--- a/solution.py
+++ b/solution.py
@@ -232,6 +232,39 @@
         )
         return up, down
 
+    tb = [[taps_ref[v * 27 + 9 + t] for t in range(9)] for v in range(count)]
+
+    def finish(v):
+        up, down = copies(v)
+
+        @pl.when(has_hi)
+        def _():
+            up.wait_send()
+            down.wait_recv()
+
+        @pl.when(has_lo)
+        def _():
+            down.wait_send()
+            up.wait_recv()
+
+        def back(c, carry):
+            z0 = pl.multiple_of(c * CZ, CZ)
+            p0 = pl.multiple_of(c * (CZ // 2), CZ // 2)
+            ext_ref[:, 0:4, :] = _unpack(recv_ref.at[v, 0], p0)[:, 0:4, :]
+            ext_ref[:, 4 : 4 + width, :] = part_ref[v, pl.ds(z0, CZ)]
+            ext_ref[:, 4 + width :, :] = _unpack(recv_ref.at[v, 1], p0)[:, 0:4, :]
+            acc = tb[v][8] * ext_ref[:, pl.ds(0, 8), :]
+            for t in range(1, 9):
+                acc = acc + tb[v][8 - t] * ext_ref[:, pl.ds(t, 8), :]
+            term = jnp.log(acc)
+            if v == 0:
+                logs_ref[pl.ds(z0, CZ)] = term
+            else:
+                logs_ref[pl.ds(z0, CZ)] = logs_ref[pl.ds(z0, CZ)] + term
+            return carry
+
+        lax.fori_loop(0, nz // CZ, back, 0)
+
     zeros = jnp.zeros((4, width, ny), jnp.float32)
     a_ref[0:4] = zeros
     a_ref[nz + 4 : nz + 8] = zeros
@@ -287,38 +320,9 @@
         def _():
             down.start()
 
-    for v in range(count):
-        up, down = copies(v)
-
-        @pl.when(has_hi)
-        def _():
-            up.wait_send()
-            down.wait_recv()
-
-        @pl.when(has_lo)
-        def _():
-            down.wait_send()
-            up.wait_recv()
-
-    tb = [[taps_ref[v * 27 + 9 + t] for t in range(9)] for v in range(count)]
-
-    def back(c, carry):
-        z0 = pl.multiple_of(c * CZ, CZ)
-        p0 = pl.multiple_of(c * (CZ // 2), CZ // 2)
-        total = None
-        for v in range(count):
-            ext_ref[:, 0:4, :] = _unpack(recv_ref.at[v, 0], p0)[:, 0:4, :]
-            ext_ref[:, 4 : 4 + width, :] = part_ref[v, pl.ds(z0, CZ)]
-            ext_ref[:, 4 + width :, :] = _unpack(recv_ref.at[v, 1], p0)[:, 0:4, :]
-            acc = tb[v][8] * ext_ref[:, pl.ds(0, 8), :]
-            for t in range(1, 9):
-                acc = acc + tb[v][8 - t] * ext_ref[:, pl.ds(t, 8), :]
-            term = jnp.log(acc)
-            total = term if total is None else total + term
-        logs_ref[pl.ds(z0, CZ)] = total
-        return carry
-
-    lax.fori_loop(0, nz // CZ, back, 0)
+        if v >= 1:
+            finish(v - 1)
+    finish(count - 1)
 
 
 def iteration_logs(taps_flat, before, mid, after, bricks):

time: 267 us -> 266 us (level)
  Pallas kernels: 104 us -> 99.1 us
    pallas_call x2, Pallas kernels: 104 us -> 99.1 us  [iteration_logs(): pl.pallas_call(_iteration_kernel, in_specs=[pl.BlockSpec(memory_space=plt...]
    ppermute x2, starting transfers between devices: 7.18 us -> 10.7 us  [swap_rims(): after = lax.ppermute(first, axis, down)]
where the time goes in v7:
time: 266 us; the launch traced here: 265 us
  waiting for transfers between devices  104 us (39%)
  Pallas kernels  99.1 us (37%)
  starting transfers between devices  40.2 us (15%)
  local copies, waits for them, and re-layouts  11.7 us (4%)
  other arithmetic  7.22 us (3%)
  matrix products  3.33 us (1%)
    pallas_call x2, Pallas kernels, iteration_logs(): pl.pallas_call(_iteration_kernel, in_specs=[pl.BlockSpec(memory_space=plt...  99.1 us
    ppermute x3, waiting for transfers between devices, view_sum(): own = own + lax.ppermute(own, 'view', chip_swap)  36.7 us
    all_to_all x1, waiting for transfers between devices, per_device(): lax.all_to_all(local_views, 'vol', split_axis=2, concat_axis=1, tiled=True)  19.8 us
    ppermute x2, waiting for transfers between devices, swap_rims(): before = lax.ppermute(last, axis, up)  19 us
    ppermute x2, waiting for transfers between devices, swap_rims(): after = lax.ppermute(first, axis, down)  18.1 us
    ppermute x2, starting transfers between devices, swap_rims(): after = lax.ppermute(first, axis, down)  10.7 us
    all_to_all x1, starting transfers between devices, per_device(): lax.all_to_all(local_views, 'vol', split_axis=2, concat_axis=1, tiled=True)  10.5 us
    ppermute x3, starting transfers between devices, view_sum(): own = own + lax.ppermute(give, 'view', core_swap)  8.39 us
  transfers between devices with their start and end apart: 14, of which 14 were waited for; matrix products, arithmetic and copies ran while one was open for 0% of the time, Pallas kernels for 0%

profile of v7, /device:TPU:5, one launch (start us, length us, event | category | flops | bytes accessed | tf_op | source)
XLA Modules:
  0.0 265.5 jit_solution(11624128755259690617)
XLA Ops:
  0.0 0.9 reduce_sum.18
  0.9 0.7 broadcast_divide_fusion
  1.7 3.3 %fusion.1 = bf16[3,8,256,128]{3,2,1,0:T(8,128)(2,1)S(1)} fusion(bf16[3,8,256,128]{3,2,1,0:T(8,128)(2,1)S(1)} %copy-done, f32[3,256]{1,0:T(4,128)S(1)} %get-tuple-element.25, f32[3,256]{1,0:T(4,128)S(1)} %get-tuple-element.26, f32[3,256]{1,0:T(4,128)S(1)} %get-tuple-element.27, f32[3,256]{1,0:T(4,128)S(1)} %get-tuple-element.28, ...), kind=kOutput, calls=%fused_computation.2 | convolution fusion | flops 2421424128 | bytes 3173376 | tf_op jit(solution)/shard_map/vxr,vzry->vzxy/dot_general | solution.py:45
  5.0 2.2 copy.7
  7.2 10.5 %all-to-all-start = ((bf16[3,8,256,128]{3,1,0,2:T(8,128)(2,1)}), bf16[3,8,256,128]{3,1,0,2:T(8,128)(2,1)S(1)}, u32[]{:S(2)}, u32[]{:S(2)}) async-start(bf16[3,8,256,128]{3,1,0,2:T(8,128)(2,1)} %copy.7), calls=%async_computation | async-start | bytes 3145728 | tf_op jit(solution)/shard_map/all_to_all | solution.py:375
  17.8 19.8 %all-to-all-done = bf16[3,8,256,128]{3,1,0,2:T(8,128)(2,1)S(1)} async-done(((bf16[3,8,256,128]{3,1,0,2:T(8,128)(2,1)}), bf16[3,8,256,128]{3,1,0,2:T(8,128)(2,1)S(1)}, u32[]{:S(2)}, u32[]{:S(2)}) %all-to-all-start) | async-done | bytes 1572896 | tf_op jit(solution)/shard_map/all_to_all | solution.py:375
  37.6 1.2 copy-done.3
  38.8 1.8 copy.28
  40.7 0.3 convert_add_fusion
  40.9 1.0 copy-done.8
  41.9 0.8 constant_dynamic-slice_fusion.2
  42.8 3.3 %collective-permute-start = (f32[128,8,128]{2,1,0:T(8,128)}, f32[128,8,128]{2,1,0:T(8,128)}, u32[]{:S(2)}, u32[]{:S(2)}) collective-permute-start(f32[128,8,128]{2,1,0:T(8,128)} %constant_dynamic-slice_fusion.2), channel_id=1, source_target_pairs={{0,32},{32,0},{64,96},{96,64},{1,33},{33,1},{65,97},{97,65},{2,34}... | collective-permute-start | bytes 1572872 | tf_op jit(solution)/shard_map/ppermute | solution.py:359
  46.1 1.9 collective-permute-done
  48.0 1.3 dynamic-slice_add_fusion.2
  49.2 1.0 collective-permute-start.1
  50.2 12.2 %collective-permute-done.1 = f32[128,8,128]{2,1,0:T(8,128)S(1)} collective-permute-done((f32[128,8,128]{2,1,0:T(8,128)S(1)}, f32[128,8,128]{2,1,0:T(8,128)S(1)}, u32[]{:S(2)}, u32[]{:S(2)}) %collective-permute-start.1) | collective-permute-done | bytes 524320 | tf_op jit(solution)/shard_map/ppermute | solution.py:360
  62.4 0.8 add.79
  63.3 1.2 collective-permute-start.2
  64.5 1.9 collective-permute-done.2
  66.4 1.3 broadcast_select_fusion.5
  67.7 0.8 copy-done.4
  68.8 1.1 fusion.68
  69.9 1.0 copy-done.1
  70.9 5.2 %collective-permute-start.4 = (f32[256,4,128]{2,1,0:T(4,128)}, f32[256,4,128]{2,1,0:T(4,128)}, u32[]{:S(2)}, u32[]{:S(2)}) collective-permute-start(f32[256,4,128]{2,1,0:T(4,128)} %get-tuple-element.13), channel_id=1, source_target_pairs={{1,0},{2,1},{3,2},{4,3},{5,4},{6,5},{7,6},{8,7},{9,8},{10,9},{11,1... | collective-permute-start | bytes 1572872 | tf_op jit(solution)/shard_map/ppermute | solution.py:26
  76.1 1.9 collective-permute-start.3
  78.2 9.1 %collective-permute-done.4.after_ref = f32[256,4,128]{2,1,0:T(4,128)} collective-permute-done((f32[256,4,128]{2,1,0:T(4,128)}, f32[256,4,128]{2,1,0:T(4,128)}, u32[]{:S(2)}, u32[]{:S(2)}) %collective-permute-start.4) | collective-permute-done | bytes 524320 | tf_op jit(solution)/shard_map/ppermute | solution.py:26
  87.3 9.5 %collective-permute-done.3.before_ref = f32[256,4,128]{2,1,0:T(4,128)} collective-permute-done((f32[256,4,128]{2,1,0:T(4,128)}, f32[256,4,128]{2,1,0:T(4,128)}, u32[]{:S(2)}, u32[]{:S(2)}) %collective-permute-start.3) | collective-permute-done | bytes 524320 | tf_op jit(solution)/shard_map/ppermute | solution.py:25
  96.8 1.2 copy-done.2
  98.1 49.9 %shard_map.46 = f32[256,8,128]{2,1,0:T(8,128)S(1)} custom-call(f32[81]{0:T(128)S(1)} %reshape.17.taps_ref, f32[256,4,128]{2,1,0:T(4,128)} %collective-permute-done.3.before_ref, f32[256,8,128]{2,1,0:T(8,128)S(1)} %copy-done.2, f32[256,4,128]{2,1,0:T(4,128)} %collective-permute-done.4.after_ref, bf16[3,256,8,128]{3,2,1,0:T(8,128)(2,1)S(1)} %bitcast.32), custom_call_target="tpu_custom_call" | custom-call | tf_op jit(solution)/shard_map/pallas_call | solution.py:330
  148.0 2.5 collective-permute-start.5
  150.5 1.5 collective-permute-done.5
  152.2 1.0 collective-permute-start.6
  153.2 12.2 %collective-permute-done.6 = f32[128,8,128]{2,1,0:T(8,128)S(1)} collective-permute-done((f32[128,8,128]{2,1,0:T(8,128)S(1)}, f32[128,8,128]{2,1,0:T(8,128)S(1)}, u32[]{:S(2)}, u32[]{:S(2)}) %collective-permute-start.6) | collective-permute-done | bytes 524320 | tf_op jit(solution)/shard_map/ppermute | solution.py:360
  165.4 1.3 collective-permute-start.7
  166.7 1.5 collective-permute-done.7
  168.4 0.2 fusion.4.mid_ref
  168.7 5.5 %collective-permute-start.9 = (f32[256,4,128]{2,1,0:T(4,128)S(1)}, f32[256,4,128]{2,1,0:T(4,128)S(1)}, u32[]{:S(2)}, u32[]{:S(2)}) collective-permute-start(f32[256,4,128]{2,1,0:T(4,128)S(1)} %get-tuple-element.9), channel_id=1, source_target_pairs={{1,0},{2,1},{3,2},{4,3},{5,4},{6,5},{7,6},{8,7},{9,8},{10,9},{11,1... | collective-permute-start | bytes 1572872 | tf_op jit(solution)/shard_map/ppermute | solution.py:26
  174.2 1.9 collective-permute-start.8
  176.2 9.0 %collective-permute-done.9.after_ref = f32[256,4,128]{2,1,0:T(4,128)S(1)} collective-permute-done((f32[256,4,128]{2,1,0:T(4,128)S(1)}, f32[256,4,128]{2,1,0:T(4,128)S(1)}, u32[]{:S(2)}, u32[]{:S(2)}) %collective-permute-start.9) | collective-permute-done | bytes 524320 | tf_op jit(solution)/shard_map/ppermute | solution.py:26
  185.2 9.5 %collective-permute-done.8.before_ref = f32[256,4,128]{2,1,0:T(4,128)S(1)} collective-permute-done((f32[256,4,128]{2,1,0:T(4,128)S(1)}, f32[256,4,128]{2,1,0:T(4,128)S(1)}, u32[]{:S(2)}, u32[]{:S(2)}) %collective-permute-start.8) | collective-permute-done | bytes 524320 | tf_op jit(solution)/shard_map/ppermute | solution.py:25
  194.7 49.2 %shard_map.47 = f32[256,8,128]{2,1,0:T(8,128)S(1)} custom-call(f32[81]{0:T(128)S(1)} %reshape.17.taps_ref, f32[256,4,128]{2,1,0:T(4,128)S(1)} %collective-permute-done.8.before_ref, f32[256,8,128]{2,1,0:T(8,128)S(1)} %fusion.4.mid_ref, f32[256,4,128]{2,1,0:T(4,128)S(1)} %collective-permute-done.9.after_ref, bf16[3,256,8,128]{3,2,1,0:T(8,128)(2,1)S(1)} %bitcast.33), custom_call_target="tpu_custom_call" | custom-call | tf_op jit(solution)/shard_map/pallas_call | solution.py:330
  244.0 2.5 collective-permute-start.10
  246.5 1.5 collective-permute-done.10
  248.1 1.0 collective-permute-start.11
  249.1 12.2 %collective-permute-done.11 = f32[128,8,128]{2,1,0:T(8,128)S(1)} collective-permute-done((f32[128,8,128]{2,1,0:T(8,128)S(1)}, f32[128,8,128]{2,1,0:T(8,128)S(1)}, u32[]{:S(2)}, u32[]{:S(2)}) %collective-permute-start.11) | collective-permute-done | bytes 524320 | tf_op jit(solution)/shard_map/ppermute | solution.py:360
  261.4 1.3 collective-permute-start.12
  262.7 1.5 collective-permute-done.12
  264.3 1.2 fusion.6
  (32 shorter events, 1.2 us)
Async XLA Ops:
  0.0 1.7 copy-start
  7.2 30.4 %all-to-all-start = ((bf16[3,8,256,128]{3,1,0,2:T(8,128)(2,1)}), bf16[3,8,256,128]{3,1,0,2:T(8,128)(2,1)S(1)}, u32[]{:S(2)}, u32[]{:S(2)}) async-start(bf16[3,8,256,128]{3,1,0,2:T(8,128)(2,1)} %copy.7), calls=%async_computation | async-start | bytes 3145728 | tf_op jit(solution)/shard_map/all_to_all | solution.py:375
  37.6 1.2 copy-start.3
  40.9 1.0 copy-start.8
  42.8 5.2 %collective-permute-start = (f32[128,8,128]{2,1,0:T(8,128)}, f32[128,8,128]{2,1,0:T(8,128)}, u32[]{:S(2)}, u32[]{:S(2)}) collective-permute-start(f32[128,8,128]{2,1,0:T(8,128)} %constant_dynamic-slice_fusion.2), channel_id=1, source_target_pairs={{0,32},{32,0},{64,96},{96,64},{1,33},{33,1},{65,97},{97,65},{2,34}... | collective-permute-start | bytes 1572872 | tf_op jit(solution)/shard_map/ppermute | solution.py:359
  49.2 13.2 %collective-permute-start.1 = (f32[128,8,128]{2,1,0:T(8,128)S(1)}, f32[128,8,128]{2,1,0:T(8,128)S(1)}, u32[]{:S(2)}, u32[]{:S(2)}) collective-permute-start(f32[128,8,128]{2,1,0:T(8,128)S(1)} %dynamic-slice_add_fusion.2), channel_id=1, source_target_pairs={{0,64},{32,96},{64,0},{96,32},{1,65},{33,97},{65,1},{97,33},{2,66}... | collective-permute-start | bytes 1572872 | tf_op jit(solution)/shard_map/ppermute | solution.py:360
  63.3 3.1 %collective-permute-start.2 = (f32[128,8,128]{2,1,0:T(8,128)}, f32[128,8,128]{2,1,0:T(8,128)}, u32[]{:S(2)}, u32[]{:S(2)}) collective-permute-start(f32[128,8,128]{2,1,0:T(8,128)} %add.79), channel_id=1, source_target_pairs={{0,32},{32,0},{64,96},{96,64},{1,33},{33,1},{65,97},{97,65},{2,34}... | collective-permute-start | bytes 1572872 | tf_op jit(solution)/shard_map/ppermute | solution.py:361
  67.6 0.8 copy-start.4
  67.7 1.0 copy-start.6
  68.8 9.3 %copy-start.9 = (f32[3,3,9]{2,1,0:T(4,128)S(1)}, f32[3,3,9]{2,1,0:T(4,128)}, u32[]{:S(2)}) copy-start(f32[3,3,9]{2,1,0:T(4,128)} %param.7) | copy-start | bytes 976
  69.9 1.0 copy-start.1
  70.9 16.5 %collective-permute-start.4 = (f32[256,4,128]{2,1,0:T(4,128)}, f32[256,4,128]{2,1,0:T(4,128)}, u32[]{:S(2)}, u32[]{:S(2)}) collective-permute-start(f32[256,4,128]{2,1,0:T(4,128)} %get-tuple-element.13), channel_id=1, source_target_pairs={{1,0},{2,1},{3,2},{4,3},{5,4},{6,5},{7,6},{8,7},{9,8},{10,9},{11,1... | collective-permute-start | bytes 1572872 | tf_op jit(solution)/shard_map/ppermute | solution.py:26
  76.1 20.7 %collective-permute-start.3 = (f32[256,4,128]{2,1,0:T(4,128)}, f32[256,4,128]{2,1,0:T(4,128)}, u32[]{:S(2)}, u32[]{:S(2)}) collective-permute-start(f32[256,4,128]{2,1,0:T(4,128)} %get-tuple-element.14), channel_id=1, source_target_pairs={{0,1},{1,2},{2,3},{3,4},{4,5},{5,6},{6,7},{7,8},{8,9},{9,10},{10,1... | collective-permute-start | bytes 1572872 | tf_op jit(solution)/shard_map/ppermute | solution.py:25
  96.8 1.2 copy-start.2
  148.0 4.1 %collective-permute-start.5 = (f32[128,8,128]{2,1,0:T(8,128)S(1)}, f32[128,8,128]{2,1,0:T(8,128)S(1)}, u32[]{:S(2)}, u32[]{:S(2)}) collective-permute-start(f32[128,8,128]{2,1,0:T(8,128)S(1)} %constant_dynamic-slice_fusion.1), channel_id=1, source_target_pairs={{0,32},{32,0},{64,96},{96,64},{1,33},{33,1},{65,97},{97,65},{2,34}... | collective-permute-start | bytes 1572872 | tf_op jit(solution)/shard_map/ppermute | solution.py:359
  152.1 16.2 %copy-start.5 = (f32[128,8,128]{2,1,0:T(8,128)S(1)}, f32[128,8,128]{2,1,0:T(8,128)}, u32[]{:S(2)}) copy-start(f32[128,8,128]{2,1,0:T(8,128)} %copy-done.4) | copy-start | bytes 1572868
  152.2 16.2 %copy-start.7 = (f32[128,8,128]{2,1,0:T(8,128)S(1)}, f32[128,8,128]{2,1,0:T(8,128)}, u32[]{:S(2)}) copy-start(f32[128,8,128]{2,1,0:T(8,128)} %copy-done.6) | copy-start | bytes 1572868
  152.2 13.2 %collective-permute-start.6 = (f32[128,8,128]{2,1,0:T(8,128)S(1)}, f32[128,8,128]{2,1,0:T(8,128)S(1)}, u32[]{:S(2)}, u32[]{:S(2)}) collective-permute-start(f32[128,8,128]{2,1,0:T(8,128)S(1)} %dynamic-slice_add_fusion.1), channel_id=1, source_target_pairs={{0,64},{32,96},{64,0},{96,32},{1,65},{33,97},{65,1},{97,33},{2,66}... | collective-permute-start | bytes 1572872 | tf_op jit(solution)/shard_map/ppermute | solution.py:360
  165.4 2.8 %collective-permute-start.7 = (f32[128,8,128]{2,1,0:T(8,128)S(1)}, f32[128,8,128]{2,1,0:T(8,128)S(1)}, u32[]{:S(2)}, u32[]{:S(2)}) collective-permute-start(f32[128,8,128]{2,1,0:T(8,128)S(1)} %add.81), channel_id=1, source_target_pairs={{0,32},{32,0},{64,96},{96,64},{1,33},{33,1},{65,97},{97,65},{2,34}... | collective-permute-start | bytes 1572872 | tf_op jit(solution)/shard_map/ppermute | solution.py:361
  168.7 16.4 %collective-permute-start.9 = (f32[256,4,128]{2,1,0:T(4,128)S(1)}, f32[256,4,128]{2,1,0:T(4,128)S(1)}, u32[]{:S(2)}, u32[]{:S(2)}) collective-permute-start(f32[256,4,128]{2,1,0:T(4,128)S(1)} %get-tuple-element.9), channel_id=1, source_target_pairs={{1,0},{2,1},{3,2},{4,3},{5,4},{6,5},{7,6},{8,7},{9,8},{10,9},{11,1... | collective-permute-start | bytes 1572872 | tf_op jit(solution)/shard_map/ppermute | solution.py:26
  174.2 20.4 %collective-permute-start.8 = (f32[256,4,128]{2,1,0:T(4,128)S(1)}, f32[256,4,128]{2,1,0:T(4,128)S(1)}, u32[]{:S(2)}, u32[]{:S(2)}) collective-permute-start(f32[256,4,128]{2,1,0:T(4,128)S(1)} %get-tuple-element.10), channel_id=1, source_target_pairs={{0,1},{1,2},{2,3},{3,4},{4,5},{5,6},{6,7},{7,8},{8,9},{9,10},{10,1... | collective-permute-start | bytes 1572872 | tf_op jit(solution)/shard_map/ppermute | solution.py:25
  244.0 4.1 %collective-permute-start.10 = (f32[128,8,128]{2,1,0:T(8,128)S(1)}, f32[128,8,128]{2,1,0:T(8,128)S(1)}, u32[]{:S(2)}, u32[]{:S(2)}) collective-permute-start(f32[128,8,128]{2,1,0:T(8,128)S(1)} %constant_dynamic-slice_fusion), channel_id=1, source_target_pairs={{0,32},{32,0},{64,96},{96,64},{1,33},{33,1},{65,97},{97,65},{2,34}... | collective-permute-start | bytes 1572872 | tf_op jit(solution)/shard_map/ppermute | solution.py:359
  248.1 13.2 %collective-permute-start.11 = (f32[128,8,128]{2,1,0:T(8,128)S(1)}, f32[128,8,128]{2,1,0:T(8,128)S(1)}, u32[]{:S(2)}, u32[]{:S(2)}) collective-permute-start(f32[128,8,128]{2,1,0:T(8,128)S(1)} %dynamic-slice_add_fusion), channel_id=1, source_target_pairs={{0,64},{32,96},{64,0},{96,32},{1,65},{33,97},{65,1},{97,33},{2,66}... | collective-permute-start | bytes 1572872 | tf_op jit(solution)/shard_map/ppermute | solution.py:360
  261.4 2.8 %collective-permute-start.12 = (f32[128,8,128]{2,1,0:T(8,128)S(1)}, f32[128,8,128]{2,1,0:T(8,128)S(1)}, u32[]{:S(2)}, u32[]{:S(2)}) collective-permute-start(f32[128,8,128]{2,1,0:T(8,128)S(1)} %add.83), channel_id=1, source_target_pairs={{0,32},{32,0},{64,96},{96,64},{1,33},{33,1},{65,97},{97,65},{2,34}... | collective-permute-start | bytes 1572872 | tf_op jit(solution)/shard_map/ppermute | solution.py:361

commit v8 on v7

--- a/solution.py
+++ b/solution.py
@@ -348,7 +348,13 @@
     )(taps_flat, before, mid, after, bricks)
 
 
-def view_sum(part):
+def _by_core(core, mine, theirs):
+    low = jnp.where(core == 0, mine, theirs)
+    high = jnp.where(core == 0, theirs, mine)
+    return jnp.concatenate([low, high], axis=0)
+
+
+def view_sum_update(part, update, rim_width):
     count = lax.axis_size("view")
     core_swap = [(i, i ^ 1) for i in range(count)]
     chip_swap = [(i, i ^ 2) for i in range(count)]
@@ -358,10 +364,14 @@
     give = lax.dynamic_slice_in_dim(part, (1 - core) * half, half, axis=0)
     own = own + lax.ppermute(give, "view", core_swap)
     own = own + lax.ppermute(own, "view", chip_swap)
-    other = lax.ppermute(own, "view", core_swap)
-    low = jnp.where(core == 0, own, other)
-    high = jnp.where(core == 0, other, own)
-    return jnp.concatenate([low, high], axis=0)
+    fresh = update(own, core * half, half)
+    whole = _by_core(core, fresh, lax.ppermute(fresh, "view", core_swap))
+    if rim_width is None:
+        return whole
+    before, after = halos(fresh, "vol", 1, rim_width)
+    before = _by_core(core, before, lax.ppermute(before, "view", core_swap))
+    after = _by_core(core, after, lax.ppermute(after, "view", core_swap))
+    return whole, before, after
 
 
 def per_device(raw_views, weights, offsets, psf_taps):
@@ -376,12 +386,20 @@
     local_sum = bricks[0].astype(jnp.float32)
     for index in range(1, count):
         local_sum = local_sum + bricks[index].astype(jnp.float32)
-    joined_volume = view_sum(local_sum) / total_views
+    joined_volume, before, after = view_sum_update(
+        local_sum, lambda own, at, size: own / total_views, rim_width
+    )
     for turn in range(ITERS):
-        before, after = halos(joined_volume, "vol", 1, rim_width)
         logs = iteration_logs(taps_flat, before, joined_volume, after, bricks)
-        summed = view_sum(logs)
-        joined_volume = joined_volume * jnp.exp(summed / total_views)
+
+        def update(own, at, size, previous=joined_volume):
+            return lax.dynamic_slice_in_dim(previous, at, size, axis=0) * jnp.exp(own / total_views)
+
+        result = view_sum_update(logs, update, rim_width if turn < ITERS - 1 else None)
+        if turn < ITERS - 1:
+            joined_volume, before, after = result
+        else:
+            joined_volume = result
     return joined_volume
 
 

time: 266 us -> 253 us (0.951)
  waiting for transfers between devices: 104 us -> 86.2 us
  starting transfers between devices: 40.2 us -> 44.3 us
  Pallas kernels: 99.1 us -> 102 us
    ppermute x2, waiting for transfers between devices: 18.1 us -> 6.22 us  [swap_rims(): after = lax.ppermute(first, axis, down)]
    ppermute x2, waiting for transfers between devices: 19 us -> 16.2 us  [swap_rims(): before = lax.ppermute(last, axis, up)]
    ppermute x9 -> x13, waiting for transfers between devices: 46.6 us -> 44 us  [the longest x3 36.6 us: view_sum_update(): own = own + lax.ppermute(own, 'view', chip_swap)]
    ppermute x9 -> x13, starting transfers between devices: 15.1 us -> 17.5 us  [the longest x3 5.48 us: view_sum_update(): own = own + lax.ppermute(give, 'view', core_swap)]
    unnamed x24 -> x16, local copies, waits for them, and re-layouts: 5.38 us -> 3.69 us
  transfers between devices with their start and end apart: 14 -> 18, of which waited for: 14 -> 13; matrix products, arithmetic and copies ran while one was open for 0% -> 1% of each run, Pallas kernels for 0% -> 0%
where the time goes in v8:
time: 253 us; the launch traced here: 252 us
  Pallas kernels  102 us (40%)
  waiting for transfers between devices  86.2 us (34%)
  starting transfers between devices  44.3 us (18%)
  local copies, waits for them, and re-layouts  9.62 us (4%)
  other arithmetic  7.05 us (3%)
  matrix products  3.32 us (1%)
    pallas_call x2, Pallas kernels, iteration_logs(): pl.pallas_call(_iteration_kernel, in_specs=[pl.BlockSpec(memory_space=plt...  102 us
    ppermute x3, waiting for transfers between devices, view_sum_update(): own = own + lax.ppermute(own, 'view', chip_swap)  36.6 us
    all_to_all x1, waiting for transfers between devices, per_device(): lax.all_to_all(local_views, 'vol', split_axis=2, concat_axis=1, tiled=True)  19.8 us
    ppermute x2, waiting for transfers between devices, swap_rims(): before = lax.ppermute(last, axis, up)  16.2 us
    ppermute x2, starting transfers between devices, swap_rims(): after = lax.ppermute(first, axis, down)  12.4 us
    all_to_all x1, starting transfers between devices, per_device(): lax.all_to_all(local_views, 'vol', split_axis=2, concat_axis=1, tiled=True)  10.5 us
    ppermute x2, waiting for transfers between devices, swap_rims(): after = lax.ppermute(first, axis, down)  6.22 us
    ppermute x3, starting transfers between devices, view_sum_update(): own = own + lax.ppermute(give, 'view', core_swap)  5.48 us
  transfers between devices with their start and end apart: 18, of which 13 were waited for; matrix products, arithmetic and copies ran while one was open for 1% of the time, Pallas kernels for 0%

profile of v8, /device:TPU:5, one launch (start us, length us, event | category | flops | bytes accessed | tf_op | source)
XLA Modules:
  0.0 252.3 jit_solution(6432053409074334127)
XLA Ops:
  0.0 0.9 reduce_sum.18
  0.9 0.7 broadcast_divide_fusion
  1.7 3.3 %fusion.1 = bf16[3,8,256,128]{3,2,1,0:T(8,128)(2,1)S(1)} fusion(bf16[3,8,256,128]{3,2,1,0:T(8,128)(2,1)S(1)} %copy-done, f32[3,256]{1,0:T(4,128)S(1)} %get-tuple-element.33, f32[3,256]{1,0:T(4,128)S(1)} %get-tuple-element.34, f32[3,256]{1,0:T(4,128)S(1)} %get-tuple-element.35, f32[3,256]{1,0:T(4,128)S(1)} %get-tuple-element.36, ...), kind=kOutput, calls=%fused_computation.2 | convolution fusion | flops 2421424128 | bytes 3173376 | tf_op jit(solution)/shard_map/vxr,vzry->vzxy/dot_general | solution.py:45
  5.0 2.2 copy.7
  7.2 10.5 %all-to-all-start = ((bf16[3,8,256,128]{3,1,0,2:T(8,128)(2,1)}), bf16[3,8,256,128]{3,1,0,2:T(8,128)(2,1)S(1)}, u32[]{:S(2)}, u32[]{:S(2)}) async-start(bf16[3,8,256,128]{3,1,0,2:T(8,128)(2,1)} %copy.7), calls=%async_computation | async-start | bytes 3145728 | tf_op jit(solution)/shard_map/all_to_all | solution.py:385
  17.8 19.8 %all-to-all-done = bf16[3,8,256,128]{3,1,0,2:T(8,128)(2,1)S(1)} async-done(((bf16[3,8,256,128]{3,1,0,2:T(8,128)(2,1)}), bf16[3,8,256,128]{3,1,0,2:T(8,128)(2,1)S(1)}, u32[]{:S(2)}, u32[]{:S(2)}) %all-to-all-start) | async-done | bytes 1572896 | tf_op jit(solution)/shard_map/all_to_all | solution.py:385
  37.6 1.2 copy-done.1
  38.8 1.9 copy.28
  41.0 1.0 copy-done.4
  41.9 0.8 constant_dynamic-slice_fusion.2
  42.7 3.3 %collective-permute-start = (f32[128,8,128]{2,1,0:T(8,128)}, f32[128,8,128]{2,1,0:T(8,128)}, u32[]{:S(2)}, u32[]{:S(2)}) collective-permute-start(f32[128,8,128]{2,1,0:T(8,128)} %constant_dynamic-slice_fusion.2), channel_id=1, source_target_pairs={{0,32},{32,0},{64,96},{96,64},{1,33},{33,1},{65,97},{97,65},{2,34}... | collective-permute-start | bytes 1572872 | tf_op jit(solution)/shard_map/ppermute | solution.py:365
  46.1 1.9 collective-permute-done
  48.0 1.3 dynamic-slice_add_fusion.2
  49.2 1.0 collective-permute-start.1
  50.2 12.2 %collective-permute-done.1 = f32[128,8,128]{2,1,0:T(8,128)S(1)} collective-permute-done((f32[128,8,128]{2,1,0:T(8,128)S(1)}, f32[128,8,128]{2,1,0:T(8,128)S(1)}, u32[]{:S(2)}, u32[]{:S(2)}) %collective-permute-start.1) | collective-permute-done | bytes 524320 | tf_op jit(solution)/shard_map/ppermute | solution.py:366
  62.5 0.8 copy-done.2
  63.3 0.8 fusion.68
  64.1 5.2 %collective-permute-start.5 = (f32[128,4,128]{2,1,0:T(4,128)S(1)}, f32[128,4,128]{2,1,0:T(4,128)}, u32[]{:S(2)}, u32[]{:S(2)}) collective-permute-start(f32[128,4,128]{2,1,0:T(4,128)S(1)} %get-tuple-element.21), channel_id=1, source_target_pairs={{1,0},{2,1},{3,2},{4,3},{5,4},{6,5},{7,6},{8,7},{9,8},{10,9},{11,1... | collective-permute-start | bytes 786440 | tf_op jit(solution)/shard_map/ppermute | solution.py:26
  69.3 1.9 collective-permute-start.3
  71.2 2.4 collective-permute-done.5
  73.7 2.1 collective-permute-start.6
  76.0 7.4 %collective-permute-done.3 = f32[128,4,128]{2,1,0:T(4,128)S(1)} collective-permute-done((f32[128,4,128]{2,1,0:T(4,128)}, f32[128,4,128]{2,1,0:T(4,128)S(1)}, u32[]{:S(2)}, u32[]{:S(2)}) %collective-permute-start.3) | collective-permute-done | bytes 262176 | tf_op jit(solution)/shard_map/ppermute | solution.py:25
  83.5 2.4 collective-permute-start.4
  85.9 1.1 broadcast_select_fusion.11
  87.3 0.7 copy-done.3
  88.1 51.0 %shard_map.46 = f32[256,8,128]{2,1,0:T(8,128)S(1)} custom-call(f32[81]{0:T(128)S(1)} %reshape.17.taps_ref, f32[256,4,128]{2,1,0:T(4,128)S(1)} %pad_maximum_fusion.3.before_ref, f32[256,8,128]{2,1,0:T(8,128)S(1)} %pad_maximum_fusion.mid_ref, f32[256,4,128]{2,1,0:T(4,128)S(1)} %pad_maximum_fusion.4.after_ref, bf16[3,256,8,128]{3,2,1,0:T(8,128)(2,1)S(1)} %bitcast.48), custom_call_target="tpu_custom_call" | custom-call | tf_op jit(solution)/shard_map/pallas_call | solution.py:330
  139.2 0.9 collective-permute-start.7
  140.0 1.5 collective-permute-done.7
  141.6 1.0 collective-permute-start.8
  142.6 12.2 %collective-permute-done.8 = f32[128,8,128]{2,1,0:T(8,128)S(1)} collective-permute-done((f32[128,8,128]{2,1,0:T(8,128)S(1)}, f32[128,8,128]{2,1,0:T(8,128)S(1)}, u32[]{:S(2)}, u32[]{:S(2)}) %collective-permute-start.8) | collective-permute-done | bytes 524320 | tf_op jit(solution)/shard_map/ppermute | solution.py:366
  154.8 0.3 fusion.38
  155.2 1.3 collective-permute-start.9
  156.5 7.2 %collective-permute-start.12 = (f32[128,4,128]{2,1,0:T(4,128)S(1)}, f32[128,4,128]{2,1,0:T(4,128)S(1)}, u32[]{:S(2)}, u32[]{:S(2)}) collective-permute-start(f32[128,4,128]{2,1,0:T(4,128)S(1)} %get-tuple-element.15), channel_id=1, source_target_pairs={{1,0},{2,1},{3,2},{4,3},{5,4},{6,5},{7,6},{8,7},{9,8},{10,9},{11,1... | collective-permute-start | bytes 786440 | tf_op jit(solution)/shard_map/ppermute | solution.py:26
  163.7 1.9 collective-permute-start.10
  165.6 3.8 %collective-permute-done.12 = f32[128,4,128]{2,1,0:T(4,128)S(1)} collective-permute-done((f32[128,4,128]{2,1,0:T(4,128)S(1)}, f32[128,4,128]{2,1,0:T(4,128)S(1)}, u32[]{:S(2)}, u32[]{:S(2)}) %collective-permute-start.12) | collective-permute-done | bytes 262176 | tf_op jit(solution)/shard_map/ppermute | solution.py:26
  169.4 0.8 collective-permute-start.13
  170.2 8.7 %collective-permute-done.10 = f32[128,4,128]{2,1,0:T(4,128)S(1)} collective-permute-done((f32[128,4,128]{2,1,0:T(4,128)S(1)}, f32[128,4,128]{2,1,0:T(4,128)S(1)}, u32[]{:S(2)}, u32[]{:S(2)}) %collective-permute-start.10) | collective-permute-done | bytes 262176 | tf_op jit(solution)/shard_map/ppermute | solution.py:25
  178.9 1.1 collective-permute-start.11
  180.4 0.8 collective-permute-done.11
  181.4 50.6 %shard_map.47 = f32[256,8,128]{2,1,0:T(8,128)S(1)} custom-call(f32[81]{0:T(128)S(1)} %reshape.17.taps_ref, f32[256,4,128]{2,1,0:T(4,128)S(1)} %pad_maximum_fusion.5.before_ref, f32[256,8,128]{2,1,0:T(8,128)S(1)} %pad_maximum_fusion.1.mid_ref, f32[256,4,128]{2,1,0:T(4,128)S(1)} %pad_maximum_fusion.6.after_ref, bf16[3,256,8,128]{3,2,1,0:T(8,128)(2,1)S(1)} %bitcast.49), custom_call_target="tpu_custom_call" | custom-call | tf_op jit(solution)/shard_map/pallas_call | solution.py:330
  232.0 1.3 collective-permute-start.14
  233.3 1.5 collective-permute-done.14
  234.8 1.0 collective-permute-start.15
  235.8 12.2 %collective-permute-done.15 = f32[128,8,128]{2,1,0:T(8,128)S(1)} collective-permute-done((f32[128,8,128]{2,1,0:T(8,128)S(1)}, f32[128,8,128]{2,1,0:T(8,128)S(1)}, u32[]{:S(2)}, u32[]{:S(2)}) %collective-permute-start.15) | collective-permute-done | bytes 524320 | tf_op jit(solution)/shard_map/ppermute | solution.py:366
  248.1 0.3 fusion.36
  248.4 1.3 collective-permute-start.16
  249.7 1.5 collective-permute-done.16
  251.3 1.0 pad_maximum_fusion.2
  (40 shorter events, 1.8 us)
Async XLA Ops:
  0.0 1.7 copy-start
  7.2 30.4 %all-to-all-start = ((bf16[3,8,256,128]{3,1,0,2:T(8,128)(2,1)}), bf16[3,8,256,128]{3,1,0,2:T(8,128)(2,1)S(1)}, u32[]{:S(2)}, u32[]{:S(2)}) async-start(bf16[3,8,256,128]{3,1,0,2:T(8,128)(2,1)} %copy.7), calls=%async_computation | async-start | bytes 3145728 | tf_op jit(solution)/shard_map/all_to_all | solution.py:385
  37.6 1.2 copy-start.1
  40.9 1.0 copy-start.4
  42.7 5.2 %collective-permute-start = (f32[128,8,128]{2,1,0:T(8,128)}, f32[128,8,128]{2,1,0:T(8,128)}, u32[]{:S(2)}, u32[]{:S(2)}) collective-permute-start(f32[128,8,128]{2,1,0:T(8,128)} %constant_dynamic-slice_fusion.2), channel_id=1, source_target_pairs={{0,32},{32,0},{64,96},{96,64},{1,33},{33,1},{65,97},{97,65},{2,34}... | collective-permute-start | bytes 1572872 | tf_op jit(solution)/shard_map/ppermute | solution.py:365
  49.2 26.6 %copy-start.5 = (f32[3,3,9]{2,1,0:T(4,128)S(1)}, f32[3,3,9]{2,1,0:T(4,128)}, u32[]{:S(2)}) copy-start(f32[3,3,9]{2,1,0:T(4,128)} %param.7) | copy-start | bytes 976
  49.2 13.2 %collective-permute-start.1 = (f32[128,8,128]{2,1,0:T(8,128)S(1)}, f32[128,8,128]{2,1,0:T(8,128)S(1)}, u32[]{:S(2)}, u32[]{:S(2)}) collective-permute-start(f32[128,8,128]{2,1,0:T(8,128)S(1)} %dynamic-slice_add_fusion.2), channel_id=1, source_target_pairs={{0,64},{32,96},{64,0},{96,32},{1,65},{33,97},{65,1},{97,33},{2,66}... | collective-permute-start | bytes 1572872 | tf_op jit(solution)/shard_map/ppermute | solution.py:366
  62.5 0.8 copy-start.2
  64.1 9.6 %collective-permute-start.5 = (f32[128,4,128]{2,1,0:T(4,128)S(1)}, f32[128,4,128]{2,1,0:T(4,128)}, u32[]{:S(2)}, u32[]{:S(2)}) collective-permute-start(f32[128,4,128]{2,1,0:T(4,128)S(1)} %get-tuple-element.21), channel_id=1, source_target_pairs={{1,0},{2,1},{3,2},{4,3},{5,4},{6,5},{7,6},{8,7},{9,8},{10,9},{11,1... | collective-permute-start | bytes 786440 | tf_op jit(solution)/shard_map/ppermute | solution.py:26
  69.3 14.1 %collective-permute-start.3 = (f32[128,4,128]{2,1,0:T(4,128)}, f32[128,4,128]{2,1,0:T(4,128)S(1)}, u32[]{:S(2)}, u32[]{:S(2)}) collective-permute-start(f32[128,4,128]{2,1,0:T(4,128)} %get-tuple-element.22), channel_id=1, source_target_pairs={{0,1},{1,2},{2,3},{3,4},{4,5},{5,6},{6,7},{7,8},{8,9},{9,10},{10,1... | collective-permute-start | bytes 786440 | tf_op jit(solution)/shard_map/ppermute | solution.py:25
  73.7 12.2 %collective-permute-start.6 = (f32[128,4,128]{2,1,0:T(4,128)}, f32[128,4,128]{2,1,0:T(4,128)}, u32[]{:S(2)}, u32[]{:S(2)}) collective-permute-start(f32[128,4,128]{2,1,0:T(4,128)} %collective-permute-done.5), channel_id=1, source_target_pairs={{0,32},{32,0},{64,96},{96,64},{1,33},{33,1},{65,97},{97,65},{2,34}... | collective-permute-start | bytes 786440 | tf_op jit(solution)/shard_map/ppermute | solution.py:373
  76.0 11.3 %collective-permute-start.2 = (f32[128,8,128]{2,1,0:T(8,128)}, f32[128,8,128]{2,1,0:T(8,128)S(1)}, u32[]{:S(2)}, u32[]{:S(2)}) collective-permute-start(f32[128,8,128]{2,1,0:T(8,128)} %copy-done.2), channel_id=1, source_target_pairs={{0,32},{32,0},{64,96},{96,64},{1,33},{33,1},{65,97},{97,65},{2,34}... | collective-permute-start | bytes 1572872 | tf_op jit(solution)/shard_map/ppermute | solution.py:368
  83.5 3.6 %collective-permute-start.4 = (f32[128,4,128]{2,1,0:T(4,128)S(1)}, f32[128,4,128]{2,1,0:T(4,128)S(1)}, u32[]{:S(2)}, u32[]{:S(2)}) collective-permute-start(f32[128,4,128]{2,1,0:T(4,128)S(1)} %collective-permute-done.3), channel_id=1, source_target_pairs={{0,32},{32,0},{64,96},{96,64},{1,33},{33,1},{65,97},{97,65},{2,34}... | collective-permute-start | bytes 786440 | tf_op jit(solution)/shard_map/ppermute | solution.py:372
  86.9 1.0 copy-start.3
  139.2 2.4 collective-permute-start.7
  141.6 13.2 %collective-permute-start.8 = (f32[128,8,128]{2,1,0:T(8,128)S(1)}, f32[128,8,128]{2,1,0:T(8,128)S(1)}, u32[]{:S(2)}, u32[]{:S(2)}) collective-permute-start(f32[128,8,128]{2,1,0:T(8,128)S(1)} %dynamic-slice_add_fusion.1), channel_id=1, source_target_pairs={{0,64},{32,96},{64,0},{96,32},{1,65},{33,97},{65,1},{97,33},{2,66}... | collective-permute-start | bytes 1572872 | tf_op jit(solution)/shard_map/ppermute | solution.py:366
  155.2 24.9 %collective-permute-start.9 = (f32[128,8,128]{2,1,0:T(8,128)S(1)}, f32[128,8,128]{2,1,0:T(8,128)S(1)}, u32[]{:S(2)}, u32[]{:S(2)}) collective-permute-start(f32[128,8,128]{2,1,0:T(8,128)S(1)} %fusion.38), channel_id=1, source_target_pairs={{0,32},{32,0},{64,96},{96,64},{1,33},{33,1},{65,97},{97,65},{2,34}... | collective-permute-start | bytes 1572872 | tf_op jit(solution)/shard_map/ppermute | solution.py:368
  156.5 12.9 %collective-permute-start.12 = (f32[128,4,128]{2,1,0:T(4,128)S(1)}, f32[128,4,128]{2,1,0:T(4,128)S(1)}, u32[]{:S(2)}, u32[]{:S(2)}) collective-permute-start(f32[128,4,128]{2,1,0:T(4,128)S(1)} %get-tuple-element.15), channel_id=1, source_target_pairs={{1,0},{2,1},{3,2},{4,3},{5,4},{6,5},{7,6},{8,7},{9,8},{10,9},{11,1... | collective-permute-start | bytes 786440 | tf_op jit(solution)/shard_map/ppermute | solution.py:26
  163.7 15.2 %collective-permute-start.10 = (f32[128,4,128]{2,1,0:T(4,128)S(1)}, f32[128,4,128]{2,1,0:T(4,128)S(1)}, u32[]{:S(2)}, u32[]{:S(2)}) collective-permute-start(f32[128,4,128]{2,1,0:T(4,128)S(1)} %get-tuple-element.16), channel_id=1, source_target_pairs={{0,1},{1,2},{2,3},{3,4},{4,5},{5,6},{6,7},{7,8},{8,9},{9,10},{10,1... | collective-permute-start | bytes 786440 | tf_op jit(solution)/shard_map/ppermute | solution.py:25
  169.4 10.8 %collective-permute-start.13 = (f32[128,4,128]{2,1,0:T(4,128)S(1)}, f32[128,4,128]{2,1,0:T(4,128)S(1)}, u32[]{:S(2)}, u32[]{:S(2)}) collective-permute-start(f32[128,4,128]{2,1,0:T(4,128)S(1)} %collective-permute-done.12), channel_id=1, source_target_pairs={{0,32},{32,0},{64,96},{96,64},{1,33},{33,1},{65,97},{97,65},{2,34}... | collective-permute-start | bytes 786440 | tf_op jit(solution)/shard_map/ppermute | solution.py:373
  178.9 2.3 collective-permute-start.11
  232.0 2.8 %collective-permute-start.14 = (f32[128,8,128]{2,1,0:T(8,128)S(1)}, f32[128,8,128]{2,1,0:T(8,128)S(1)}, u32[]{:S(2)}, u32[]{:S(2)}) collective-permute-start(f32[128,8,128]{2,1,0:T(8,128)S(1)} %constant_dynamic-slice_fusion), channel_id=1, source_target_pairs={{0,32},{32,0},{64,96},{96,64},{1,33},{33,1},{65,97},{97,65},{2,34}... | collective-permute-start | bytes 1572872 | tf_op jit(solution)/shard_map/ppermute | solution.py:365
  234.8 13.2 %collective-permute-start.15 = (f32[128,8,128]{2,1,0:T(8,128)S(1)}, f32[128,8,128]{2,1,0:T(8,128)S(1)}, u32[]{:S(2)}, u32[]{:S(2)}) collective-permute-start(f32[128,8,128]{2,1,0:T(8,128)S(1)} %dynamic-slice_add_fusion), channel_id=1, source_target_pairs={{0,64},{32,96},{64,0},{96,32},{1,65},{33,97},{65,1},{97,33},{2,66}... | collective-permute-start | bytes 1572872 | tf_op jit(solution)/shard_map/ppermute | solution.py:366
  248.4 2.8 %collective-permute-start.16 = (f32[128,8,128]{2,1,0:T(8,128)S(1)}, f32[128,8,128]{2,1,0:T(8,128)S(1)}, u32[]{:S(2)}, u32[]{:S(2)}) collective-permute-start(f32[128,8,128]{2,1,0:T(8,128)S(1)} %fusion.36), channel_id=1, source_target_pairs={{0,32},{32,0},{64,96},{96,64},{1,33},{33,1},{65,97},{97,65},{2,34}... | collective-permute-start | bytes 1572872 | tf_op jit(solution)/shard_map/ppermute | solution.py:368

commit v9 on v8

--- a/solution.py
+++ b/solution.py
@@ -266,33 +266,40 @@
         lax.fori_loop(0, nz // CZ, back, 0)
 
     zeros = jnp.zeros((4, width, ny), jnp.float32)
-    a_ref[0:4] = zeros
-    a_ref[nz + 4 : nz + 8] = zeros
     c_ref[0:4] = zeros
     c_ref[nz + 4 : nz + 8] = zeros
+    tx_all = [[taps_ref[v * 27 + 9 + t] for t in range(9)] for v in range(count)]
     for v in range(count):
-        tx = [taps_ref[v * 27 + 9 + t] for t in range(9)]
+        a_ref[v, 0:4] = zeros
+        a_ref[v, nz + 4 : nz + 8] = zeros
+
+    def along_x(c, carry):
+        z0 = pl.multiple_of(c * CZ, CZ)
+        _fill_wide(ext_ref, before_ref, mid_ref, after_ref, z0)
+        for sub in range(0, CZ, 8):
+            accs = [None] * count
+            for t in range(9):
+                shifted = ext_ref[pl.ds(sub, 8), pl.ds(t, 8), :]
+                for v in range(count):
+                    term = tx_all[v][t] * shifted
+                    accs[v] = term if accs[v] is None else accs[v] + term
+            for v in range(count):
+                a_ref[v, pl.ds(z0 + 4 + sub, 8)] = accs[v]
+        return carry
+
+    lax.fori_loop(0, nz // CZ, along_x, 0)
+    for v in range(count):
         tz = [taps_ref[v * 27 + t] for t in range(9)]
         ty = [taps_ref[v * 27 + 18 + t] for t in range(9)]
 
-        def along_x(c, carry):
-            z0 = pl.multiple_of(c * CZ, CZ)
-            _fill_wide(ext_ref, before_ref, mid_ref, after_ref, z0)
-            acc = tx[0] * ext_ref[:, pl.ds(0, 8), :]
-            for t in range(1, 9):
-                acc = acc + tx[t] * ext_ref[:, pl.ds(t, 8), :]
-            a_ref[pl.ds(z0 + 4, CZ)] = acc
-            return carry
-
-        lax.fori_loop(0, nz // CZ, along_x, 0)
         wy = _lane_weights(ty, ny, False)
         wy_rev = _lane_weights(ty, ny, True)
 
         def middle(c, carry):
             z0 = pl.multiple_of(c * CZ, CZ)
-            acc = tz[0] * a_ref[pl.ds(z0, CZ)]
+            acc = tz[0] * a_ref[v, pl.ds(z0, CZ)]
             for t in range(1, 9):
-                acc = acc + tz[t] * a_ref[pl.ds(z0 + t, CZ)]
+                acc = acc + tz[t] * a_ref[v, pl.ds(z0 + t, CZ)]
             blurred = _lane_correlate(acc, wy)
             ratio = brick_ref[v, pl.ds(z0, CZ)].astype(jnp.float32) / blurred
             c_ref[pl.ds(z0 + 4, CZ)] = _lane_correlate(ratio, wy_rev)
@@ -320,9 +327,8 @@
         def _():
             down.start()
 
-        if v >= 1:
-            finish(v - 1)
-    finish(count - 1)
+    for v in range(count):
+        finish(v)
 
 
 def iteration_logs(taps_flat, before, mid, after, bricks):
@@ -333,7 +339,7 @@
         out_specs=pl.BlockSpec(memory_space=pltpu.VMEM),
         out_shape=jax.ShapeDtypeStruct((nz, width, ny), jnp.float32),
         scratch_shapes=[
-            pltpu.VMEM((nz + 8, width, ny), jnp.float32),
+            pltpu.VMEM((count, nz + 8, width, ny), jnp.float32),
             pltpu.VMEM((nz + 8, width, ny), jnp.float32),
             pltpu.VMEM((CZ, width + 8, ny), jnp.float32),
             pltpu.VMEM((count, nz, width, ny), jnp.float32),

time: 253 us -> 250 us (0.988)
  starting transfers between devices: 44.3 us -> 40.5 us
    ppermute x2, starting transfers between devices: 12.4 us -> 7.18 us  [swap_rims(): after = lax.ppermute(first, axis, down)]
where the time goes in v9:
time: 250 us; the launch traced here: 249 us
  Pallas kernels  104 us (42%)
  waiting for transfers between devices  84.8 us (34%)
  starting transfers between devices  40.5 us (16%)
  local copies, waits for them, and re-layouts  9.62 us (4%)
  other arithmetic  7.05 us (3%)
  matrix products  3.32 us (1%)
    pallas_call x2, Pallas kernels, iteration_logs(): pl.pallas_call(_iteration_kernel, in_specs=[pl.BlockSpec(memory_space=plt...  104 us
    ppermute x3, waiting for transfers between devices, view_sum_update(): own = own + lax.ppermute(own, 'view', chip_swap)  36.6 us
    all_to_all x1, waiting for transfers between devices, per_device(): lax.all_to_all(local_views, 'vol', split_axis=2, concat_axis=1, tiled=True)  19.8 us
    ppermute x2, waiting for transfers between devices, swap_rims(): before = lax.ppermute(last, axis, up)  14 us
    all_to_all x1, starting transfers between devices, per_device(): lax.all_to_all(local_views, 'vol', split_axis=2, concat_axis=1, tiled=True)  10.5 us
    ppermute x2, starting transfers between devices, swap_rims(): after = lax.ppermute(first, axis, down)  7.18 us
    ppermute x2, waiting for transfers between devices, swap_rims(): after = lax.ppermute(first, axis, down)  6.96 us
    ppermute x3, starting transfers between devices, view_sum_update(): own = own + lax.ppermute(give, 'view', core_swap)  5.48 us
  transfers between devices with their start and end apart: 18, of which 13 were waited for; matrix products, arithmetic and copies ran while one was open for 1% of the time, Pallas kernels for 0%

profile of v9, /device:TPU:5, one launch (start us, length us, event | category | flops | bytes accessed | tf_op | source)
XLA Modules:
  0.0 249.1 jit_solution(11515627253259550800)
XLA Ops:
  0.0 0.9 reduce_sum.18
  0.9 0.7 broadcast_divide_fusion
  1.7 3.3 %fusion.1 = bf16[3,8,256,128]{3,2,1,0:T(8,128)(2,1)S(1)} fusion(bf16[3,8,256,128]{3,2,1,0:T(8,128)(2,1)S(1)} %copy-done, f32[3,256]{1,0:T(4,128)S(1)} %get-tuple-element.33, f32[3,256]{1,0:T(4,128)S(1)} %get-tuple-element.34, f32[3,256]{1,0:T(4,128)S(1)} %get-tuple-element.35, f32[3,256]{1,0:T(4,128)S(1)} %get-tuple-element.36, ...), kind=kOutput, calls=%fused_computation.2 | convolution fusion | flops 2421424128 | bytes 3173376 | tf_op jit(solution)/shard_map/vxr,vzry->vzxy/dot_general | solution.py:45
  5.0 2.2 copy.7
  7.2 10.5 %all-to-all-start = ((bf16[3,8,256,128]{3,1,0,2:T(8,128)(2,1)}), bf16[3,8,256,128]{3,1,0,2:T(8,128)(2,1)S(1)}, u32[]{:S(2)}, u32[]{:S(2)}) async-start(bf16[3,8,256,128]{3,1,0,2:T(8,128)(2,1)} %copy.7), calls=%async_computation | async-start | bytes 3145728 | tf_op jit(solution)/shard_map/all_to_all | solution.py:391
  17.8 19.8 %all-to-all-done = bf16[3,8,256,128]{3,1,0,2:T(8,128)(2,1)S(1)} async-done(((bf16[3,8,256,128]{3,1,0,2:T(8,128)(2,1)}), bf16[3,8,256,128]{3,1,0,2:T(8,128)(2,1)S(1)}, u32[]{:S(2)}, u32[]{:S(2)}) %all-to-all-start) | async-done | bytes 1572896 | tf_op jit(solution)/shard_map/all_to_all | solution.py:391
  37.6 1.2 copy-done.1
  38.8 1.9 copy.28
  41.0 1.0 copy-done.4
  41.9 0.8 constant_dynamic-slice_fusion.2
  42.7 3.3 %collective-permute-start = (f32[128,8,128]{2,1,0:T(8,128)}, f32[128,8,128]{2,1,0:T(8,128)}, u32[]{:S(2)}, u32[]{:S(2)}) collective-permute-start(f32[128,8,128]{2,1,0:T(8,128)} %constant_dynamic-slice_fusion.2), channel_id=1, source_target_pairs={{0,32},{32,0},{64,96},{96,64},{1,33},{33,1},{65,97},{97,65},{2,34}... | collective-permute-start | bytes 1572872 | tf_op jit(solution)/shard_map/ppermute | solution.py:371
  46.1 1.9 collective-permute-done
  48.0 1.3 dynamic-slice_add_fusion.2
  49.2 1.0 collective-permute-start.1
  50.2 12.2 %collective-permute-done.1 = f32[128,8,128]{2,1,0:T(8,128)S(1)} collective-permute-done((f32[128,8,128]{2,1,0:T(8,128)S(1)}, f32[128,8,128]{2,1,0:T(8,128)S(1)}, u32[]{:S(2)}, u32[]{:S(2)}) %collective-permute-start.1) | collective-permute-done | bytes 524320 | tf_op jit(solution)/shard_map/ppermute | solution.py:372
  62.5 0.8 copy-done.2
  63.3 0.8 fusion.68
  64.1 5.2 %collective-permute-start.5 = (f32[128,4,128]{2,1,0:T(4,128)S(1)}, f32[128,4,128]{2,1,0:T(4,128)}, u32[]{:S(2)}, u32[]{:S(2)}) collective-permute-start(f32[128,4,128]{2,1,0:T(4,128)S(1)} %get-tuple-element.21), channel_id=1, source_target_pairs={{1,0},{2,1},{3,2},{4,3},{5,4},{6,5},{7,6},{8,7},{9,8},{10,9},{11,1... | collective-permute-start | bytes 786440 | tf_op jit(solution)/shard_map/ppermute | solution.py:26
  69.3 1.9 collective-permute-start.3
  71.2 2.4 collective-permute-done.5
  73.7 2.1 collective-permute-start.6
  76.0 7.4 %collective-permute-done.3 = f32[128,4,128]{2,1,0:T(4,128)S(1)} collective-permute-done((f32[128,4,128]{2,1,0:T(4,128)}, f32[128,4,128]{2,1,0:T(4,128)S(1)}, u32[]{:S(2)}, u32[]{:S(2)}) %collective-permute-start.3) | collective-permute-done | bytes 262176 | tf_op jit(solution)/shard_map/ppermute | solution.py:25
  83.5 2.4 collective-permute-start.4
  85.9 1.1 broadcast_select_fusion.11
  87.3 0.7 copy-done.3
  88.1 52.0 %shard_map.46 = f32[256,8,128]{2,1,0:T(8,128)S(1)} custom-call(f32[81]{0:T(128)S(1)} %reshape.17.taps_ref, f32[256,4,128]{2,1,0:T(4,128)S(1)} %pad_maximum_fusion.3.before_ref, f32[256,8,128]{2,1,0:T(8,128)S(1)} %pad_maximum_fusion.mid_ref, f32[256,4,128]{2,1,0:T(4,128)S(1)} %pad_maximum_fusion.4.after_ref, bf16[3,256,8,128]{3,2,1,0:T(8,128)(2,1)S(1)} %bitcast.48), custom_call_target="tpu_custom_call" | custom-call | tf_op jit(solution)/shard_map/pallas_call | solution.py:336
  140.2 0.9 collective-permute-start.7
  141.0 1.5 collective-permute-done.7
  142.6 1.0 collective-permute-start.8
  143.6 12.2 %collective-permute-done.8 = f32[128,8,128]{2,1,0:T(8,128)S(1)} collective-permute-done((f32[128,8,128]{2,1,0:T(8,128)S(1)}, f32[128,8,128]{2,1,0:T(8,128)S(1)}, u32[]{:S(2)}, u32[]{:S(2)}) %collective-permute-start.8) | collective-permute-done | bytes 524320 | tf_op jit(solution)/shard_map/ppermute | solution.py:372
  155.8 0.3 fusion.38
  156.2 1.3 collective-permute-start.9
  157.5 1.9 collective-permute-start.12
  159.5 3.3 %collective-permute-start.10 = (f32[128,4,128]{2,1,0:T(4,128)S(1)}, f32[128,4,128]{2,1,0:T(4,128)S(1)}, u32[]{:S(2)}, u32[]{:S(2)}) collective-permute-start(f32[128,4,128]{2,1,0:T(4,128)S(1)} %get-tuple-element.16), channel_id=1, source_target_pairs={{0,1},{1,2},{2,3},{3,4},{4,5},{5,6},{6,7},{7,8},{8,9},{9,10},{10,1... | collective-permute-start | bytes 786440 | tf_op jit(solution)/shard_map/ppermute | solution.py:25
  162.8 4.5 %collective-permute-done.12 = f32[128,4,128]{2,1,0:T(4,128)S(1)} collective-permute-done((f32[128,4,128]{2,1,0:T(4,128)S(1)}, f32[128,4,128]{2,1,0:T(4,128)S(1)}, u32[]{:S(2)}, u32[]{:S(2)}) %collective-permute-start.12) | collective-permute-done | bytes 262176 | tf_op jit(solution)/shard_map/ppermute | solution.py:26
  167.3 0.8 collective-permute-start.13
  168.1 6.6 %collective-permute-done.10 = f32[128,4,128]{2,1,0:T(4,128)S(1)} collective-permute-done((f32[128,4,128]{2,1,0:T(4,128)S(1)}, f32[128,4,128]{2,1,0:T(4,128)S(1)}, u32[]{:S(2)}, u32[]{:S(2)}) %collective-permute-start.10) | collective-permute-done | bytes 262176 | tf_op jit(solution)/shard_map/ppermute | solution.py:25
  174.7 1.1 collective-permute-start.11
  176.2 0.8 collective-permute-done.11
  177.1 51.6 %shard_map.47 = f32[256,8,128]{2,1,0:T(8,128)S(1)} custom-call(f32[81]{0:T(128)S(1)} %reshape.17.taps_ref, f32[256,4,128]{2,1,0:T(4,128)S(1)} %pad_maximum_fusion.5.before_ref, f32[256,8,128]{2,1,0:T(8,128)S(1)} %pad_maximum_fusion.1.mid_ref, f32[256,4,128]{2,1,0:T(4,128)S(1)} %pad_maximum_fusion.6.after_ref, bf16[3,256,8,128]{3,2,1,0:T(8,128)(2,1)S(1)} %bitcast.49), custom_call_target="tpu_custom_call" | custom-call | tf_op jit(solution)/shard_map/pallas_call | solution.py:336
  228.8 1.3 collective-permute-start.14
  230.0 1.5 collective-permute-done.14
  231.6 1.0 collective-permute-start.15
  232.6 12.2 %collective-permute-done.15 = f32[128,8,128]{2,1,0:T(8,128)S(1)} collective-permute-done((f32[128,8,128]{2,1,0:T(8,128)S(1)}, f32[128,8,128]{2,1,0:T(8,128)S(1)}, u32[]{:S(2)}, u32[]{:S(2)}) %collective-permute-start.15) | collective-permute-done | bytes 524320 | tf_op jit(solution)/shard_map/ppermute | solution.py:372
  244.8 0.3 fusion.36
  245.2 1.3 collective-permute-start.16
  246.4 1.5 collective-permute-done.16
  248.1 1.0 pad_maximum_fusion.2
  (40 shorter events, 1.8 us)
Async XLA Ops:
  0.0 1.7 copy-start
  7.2 30.4 %all-to-all-start = ((bf16[3,8,256,128]{3,1,0,2:T(8,128)(2,1)}), bf16[3,8,256,128]{3,1,0,2:T(8,128)(2,1)S(1)}, u32[]{:S(2)}, u32[]{:S(2)}) async-start(bf16[3,8,256,128]{3,1,0,2:T(8,128)(2,1)} %copy.7), calls=%async_computation | async-start | bytes 3145728 | tf_op jit(solution)/shard_map/all_to_all | solution.py:391
  37.6 1.2 copy-start.1
  40.9 1.0 copy-start.4
  42.7 5.2 %collective-permute-start = (f32[128,8,128]{2,1,0:T(8,128)}, f32[128,8,128]{2,1,0:T(8,128)}, u32[]{:S(2)}, u32[]{:S(2)}) collective-permute-start(f32[128,8,128]{2,1,0:T(8,128)} %constant_dynamic-slice_fusion.2), channel_id=1, source_target_pairs={{0,32},{32,0},{64,96},{96,64},{1,33},{33,1},{65,97},{97,65},{2,34}... | collective-permute-start | bytes 1572872 | tf_op jit(solution)/shard_map/ppermute | solution.py:371
  49.2 26.6 %copy-start.5 = (f32[3,3,9]{2,1,0:T(4,128)S(1)}, f32[3,3,9]{2,1,0:T(4,128)}, u32[]{:S(2)}) copy-start(f32[3,3,9]{2,1,0:T(4,128)} %param.7) | copy-start | bytes 976
  49.2 13.2 %collective-permute-start.1 = (f32[128,8,128]{2,1,0:T(8,128)S(1)}, f32[128,8,128]{2,1,0:T(8,128)S(1)}, u32[]{:S(2)}, u32[]{:S(2)}) collective-permute-start(f32[128,8,128]{2,1,0:T(8,128)S(1)} %dynamic-slice_add_fusion.2), channel_id=1, source_target_pairs={{0,64},{32,96},{64,0},{96,32},{1,65},{33,97},{65,1},{97,33},{2,66}... | collective-permute-start | bytes 1572872 | tf_op jit(solution)/shard_map/ppermute | solution.py:372
  62.5 0.8 copy-start.2
  64.1 9.6 %collective-permute-start.5 = (f32[128,4,128]{2,1,0:T(4,128)S(1)}, f32[128,4,128]{2,1,0:T(4,128)}, u32[]{:S(2)}, u32[]{:S(2)}) collective-permute-start(f32[128,4,128]{2,1,0:T(4,128)S(1)} %get-tuple-element.21), channel_id=1, source_target_pairs={{1,0},{2,1},{3,2},{4,3},{5,4},{6,5},{7,6},{8,7},{9,8},{10,9},{11,1... | collective-permute-start | bytes 786440 | tf_op jit(solution)/shard_map/ppermute | solution.py:26
  69.3 14.1 %collective-permute-start.3 = (f32[128,4,128]{2,1,0:T(4,128)}, f32[128,4,128]{2,1,0:T(4,128)S(1)}, u32[]{:S(2)}, u32[]{:S(2)}) collective-permute-start(f32[128,4,128]{2,1,0:T(4,128)} %get-tuple-element.22), channel_id=1, source_target_pairs={{0,1},{1,2},{2,3},{3,4},{4,5},{5,6},{6,7},{7,8},{8,9},{9,10},{10,1... | collective-permute-start | bytes 786440 | tf_op jit(solution)/shard_map/ppermute | solution.py:25
  73.7 12.2 %collective-permute-start.6 = (f32[128,4,128]{2,1,0:T(4,128)}, f32[128,4,128]{2,1,0:T(4,128)}, u32[]{:S(2)}, u32[]{:S(2)}) collective-permute-start(f32[128,4,128]{2,1,0:T(4,128)} %collective-permute-done.5), channel_id=1, source_target_pairs={{0,32},{32,0},{64,96},{96,64},{1,33},{33,1},{65,97},{97,65},{2,34}... | collective-permute-start | bytes 786440 | tf_op jit(solution)/shard_map/ppermute | solution.py:379
  76.0 11.3 %collective-permute-start.2 = (f32[128,8,128]{2,1,0:T(8,128)}, f32[128,8,128]{2,1,0:T(8,128)S(1)}, u32[]{:S(2)}, u32[]{:S(2)}) collective-permute-start(f32[128,8,128]{2,1,0:T(8,128)} %copy-done.2), channel_id=1, source_target_pairs={{0,32},{32,0},{64,96},{96,64},{1,33},{33,1},{65,97},{97,65},{2,34}... | collective-permute-start | bytes 1572872 | tf_op jit(solution)/shard_map/ppermute | solution.py:374
  83.5 3.6 %collective-permute-start.4 = (f32[128,4,128]{2,1,0:T(4,128)S(1)}, f32[128,4,128]{2,1,0:T(4,128)S(1)}, u32[]{:S(2)}, u32[]{:S(2)}) collective-permute-start(f32[128,4,128]{2,1,0:T(4,128)S(1)} %collective-permute-done.3), channel_id=1, source_target_pairs={{0,32},{32,0},{64,96},{96,64},{1,33},{33,1},{65,97},{97,65},{2,34}... | collective-permute-start | bytes 786440 | tf_op jit(solution)/shard_map/ppermute | solution.py:378
  86.9 1.0 copy-start.3
  140.2 2.4 collective-permute-start.7
  142.6 13.2 %collective-permute-start.8 = (f32[128,8,128]{2,1,0:T(8,128)S(1)}, f32[128,8,128]{2,1,0:T(8,128)S(1)}, u32[]{:S(2)}, u32[]{:S(2)}) collective-permute-start(f32[128,8,128]{2,1,0:T(8,128)S(1)} %dynamic-slice_add_fusion.1), channel_id=1, source_target_pairs={{0,64},{32,96},{64,0},{96,32},{1,65},{33,97},{65,1},{97,33},{2,66}... | collective-permute-start | bytes 1572872 | tf_op jit(solution)/shard_map/ppermute | solution.py:372
  156.2 19.7 %collective-permute-start.9 = (f32[128,8,128]{2,1,0:T(8,128)S(1)}, f32[128,8,128]{2,1,0:T(8,128)S(1)}, u32[]{:S(2)}, u32[]{:S(2)}) collective-permute-start(f32[128,8,128]{2,1,0:T(8,128)S(1)} %fusion.38), channel_id=1, source_target_pairs={{0,32},{32,0},{64,96},{96,64},{1,33},{33,1},{65,97},{97,65},{2,34}... | collective-permute-start | bytes 1572872 | tf_op jit(solution)/shard_map/ppermute | solution.py:374
  157.5 9.8 %collective-permute-start.12 = (f32[128,4,128]{2,1,0:T(4,128)S(1)}, f32[128,4,128]{2,1,0:T(4,128)S(1)}, u32[]{:S(2)}, u32[]{:S(2)}) collective-permute-start(f32[128,4,128]{2,1,0:T(4,128)S(1)} %get-tuple-element.15), channel_id=1, source_target_pairs={{1,0},{2,1},{3,2},{4,3},{5,4},{6,5},{7,6},{8,7},{9,8},{10,9},{11,1... | collective-permute-start | bytes 786440 | tf_op jit(solution)/shard_map/ppermute | solution.py:26
  159.5 15.2 %collective-permute-start.10 = (f32[128,4,128]{2,1,0:T(4,128)S(1)}, f32[128,4,128]{2,1,0:T(4,128)S(1)}, u32[]{:S(2)}, u32[]{:S(2)}) collective-permute-start(f32[128,4,128]{2,1,0:T(4,128)S(1)} %get-tuple-element.16), channel_id=1, source_target_pairs={{0,1},{1,2},{2,3},{3,4},{4,5},{5,6},{6,7},{7,8},{8,9},{9,10},{10,1... | collective-permute-start | bytes 786440 | tf_op jit(solution)/shard_map/ppermute | solution.py:25
  167.3 8.6 %collective-permute-start.13 = (f32[128,4,128]{2,1,0:T(4,128)S(1)}, f32[128,4,128]{2,1,0:T(4,128)S(1)}, u32[]{:S(2)}, u32[]{:S(2)}) collective-permute-start(f32[128,4,128]{2,1,0:T(4,128)S(1)} %collective-permute-done.12), channel_id=1, source_target_pairs={{0,32},{32,0},{64,96},{96,64},{1,33},{33,1},{65,97},{97,65},{2,34}... | collective-permute-start | bytes 786440 | tf_op jit(solution)/shard_map/ppermute | solution.py:379
  174.7 2.3 collective-permute-start.11
  228.8 2.8 %collective-permute-start.14 = (f32[128,8,128]{2,1,0:T(8,128)S(1)}, f32[128,8,128]{2,1,0:T(8,128)S(1)}, u32[]{:S(2)}, u32[]{:S(2)}) collective-permute-start(f32[128,8,128]{2,1,0:T(8,128)S(1)} %constant_dynamic-slice_fusion), channel_id=1, source_target_pairs={{0,32},{32,0},{64,96},{96,64},{1,33},{33,1},{65,97},{97,65},{2,34}... | collective-permute-start | bytes 1572872 | tf_op jit(solution)/shard_map/ppermute | solution.py:371
  231.6 13.2 %collective-permute-start.15 = (f32[128,8,128]{2,1,0:T(8,128)S(1)}, f32[128,8,128]{2,1,0:T(8,128)S(1)}, u32[]{:S(2)}, u32[]{:S(2)}) collective-permute-start(f32[128,8,128]{2,1,0:T(8,128)S(1)} %dynamic-slice_add_fusion), channel_id=1, source_target_pairs={{0,64},{32,96},{64,0},{96,32},{1,65},{33,97},{65,1},{97,33},{2,66}... | collective-permute-start | bytes 1572872 | tf_op jit(solution)/shard_map/ppermute | solution.py:372
  245.2 2.8 %collective-permute-start.16 = (f32[128,8,128]{2,1,0:T(8,128)S(1)}, f32[128,8,128]{2,1,0:T(8,128)S(1)}, u32[]{:S(2)}, u32[]{:S(2)}) collective-permute-start(f32[128,8,128]{2,1,0:T(8,128)S(1)} %fusion.36), channel_id=1, source_target_pairs={{0,32},{32,0},{64,96},{96,64},{1,33},{33,1},{65,97},{97,65},{2,34}... | collective-permute-start | bytes 1572872 | tf_op jit(solution)/shard_map/ppermute | solution.py:374

commit v10 on v9

--- a/solution.py
+++ b/solution.py
@@ -72,111 +72,6 @@
     return acc
 
 
-def _forward_kernel(
-    v, taps_ref, before_ref, mid_ref, after_ref, brick_ref, out_ref, first_ref, last_ref, a_ref, c_ref, est_ref
-):
-    nz, width, ny = out_ref.shape
-    rim = first_ref.shape[1]
-    tx = [taps_ref[v * 27 + 9 + t] for t in range(9)]
-    tz = [taps_ref[v * 27 + t] for t in range(9)]
-    ty = [taps_ref[v * 27 + 18 + t] for t in range(9)]
-    zeros = jnp.zeros((4,) + a_ref.shape[1:], jnp.float32)
-    a_ref[0:4] = zeros
-    a_ref[nz + 4 : nz + 8] = zeros
-    c_ref[0:4] = zeros
-    c_ref[nz + 4 : nz + 8] = zeros
-
-    def along_x(c, carry):
-        z0 = pl.multiple_of(c * CZ, CZ)
-        _fill_wide(est_ref, before_ref, mid_ref, after_ref, z0)
-        acc = tx[0] * est_ref[:, pl.ds(0, 8), :]
-        for t in range(1, 9):
-            acc = acc + tx[t] * est_ref[:, pl.ds(t, 8), :]
-        a_ref[pl.ds(z0 + 4, CZ)] = acc
-        return carry
-
-    lax.fori_loop(0, nz // CZ, along_x, 0)
-    wy = _lane_weights(ty, ny, False)
-    wy_rev = _lane_weights(ty, ny, True)
-
-    def middle(c, carry):
-        z0 = pl.multiple_of(c * CZ, CZ)
-        acc = tz[0] * a_ref[pl.ds(z0, CZ)]
-        for t in range(1, 9):
-            acc = acc + tz[t] * a_ref[pl.ds(z0 + t, CZ)]
-        blurred = _lane_correlate(acc, wy)
-        ratio = brick_ref[pl.ds(z0, CZ)].astype(jnp.float32) / blurred
-        c_ref[pl.ds(z0 + 4, CZ)] = _lane_correlate(ratio, wy_rev)
-        return carry
-
-    lax.fori_loop(0, nz // CZ, middle, 0)
-
-    def along_z_back(c, carry):
-        z0 = pl.multiple_of(c * CZ, CZ)
-        acc = tz[8] * c_ref[pl.ds(z0, CZ)]
-        for t in range(1, 9):
-            acc = acc + tz[8 - t] * c_ref[pl.ds(z0 + t, CZ)]
-        out_ref[pl.ds(z0, CZ)] = acc
-        first_ref[pl.ds(z0, CZ)] = acc[:, :rim, :]
-        last_ref[pl.ds(z0, CZ)] = acc[:, width - rim :, :]
-        return carry
-
-    lax.fori_loop(0, nz // CZ, along_z_back, 0)
-
-
-def forward_partial(taps_flat, v, before, mid, after, brick):
-    nz, width, ny = brick.shape
-    return pl.pallas_call(
-        functools.partial(_forward_kernel, v),
-        in_specs=[pl.BlockSpec(memory_space=pltpu.SMEM)] + [pl.BlockSpec(memory_space=pltpu.VMEM)] * 4,
-        out_specs=[pl.BlockSpec(memory_space=pltpu.VMEM)] * 3,
-        out_shape=[
-            jax.ShapeDtypeStruct((nz, width, ny), jnp.float32),
-            jax.ShapeDtypeStruct((nz, 4, ny), jnp.float32),
-            jax.ShapeDtypeStruct((nz, 4, ny), jnp.float32),
-        ],
-        scratch_shapes=[
-            pltpu.VMEM((nz + 8, width, ny), jnp.float32),
-            pltpu.VMEM((nz + 8, width, ny), jnp.float32),
-            pltpu.VMEM((CZ, width + 8, ny), jnp.float32),
-        ],
-    )(taps_flat, before, mid, after, brick)
-
-
-def _back_kernel(taps_ref, *refs):
-    parts, out_ref, wide_ref = refs[:-2], refs[-2], refs[-1]
-    count = len(parts) // 3
-    nz = out_ref.shape[0]
-    tx = [[taps_ref[v * 27 + 9 + t] for t in range(9)] for v in range(count)]
-
-    def body(c, carry):
-        z0 = pl.multiple_of(c * CZ, CZ)
-        total = None
-        for v in range(count):
-            _fill_wide(wide_ref, *parts[3 * v : 3 * v + 3], z0)
-            acc = tx[v][8] * wide_ref[:, pl.ds(0, 8), :]
-            for t in range(1, 9):
-                acc = acc + tx[v][8 - t] * wide_ref[:, pl.ds(t, 8), :]
-            term = jnp.log(acc)
-            total = term if total is None else total + term
-        out_ref[pl.ds(z0, CZ)] = total
-        return carry
-
-    lax.fori_loop(0, nz // CZ, body, 0)
-
-
-def back_logs(taps_flat, parts):
-    nz, width, ny = parts[1].shape
-    return pl.pallas_call(
-        _back_kernel,
-        in_specs=[pl.BlockSpec(memory_space=pltpu.SMEM)]
-        + [pl.BlockSpec(memory_space=pltpu.VMEM)] * len(parts),
-        out_specs=pl.BlockSpec(memory_space=pltpu.VMEM),
-        out_shape=jax.ShapeDtypeStruct((nz, width, ny), jnp.float32),
-        scratch_shapes=[pltpu.VMEM((CZ, width + 8, ny), jnp.float32)],
-    )(taps_flat, *parts)
-
-
 def _pack(acc, first_ref, last_ref, p0):
     half = acc.shape[0] // 2
     upper, lower = acc[:half], acc[half:]
@@ -219,33 +114,48 @@
     def _():
         recv_ref[:, 1] = jnp.zeros(recv_ref.shape[:1] + recv_ref.shape[2:], jnp.float32)
 
-    def copies(v):
+    rows = nz // 4
+
+    def copies(v, h):
+        rows_h = pl.ds(h * rows, rows)
         up = pltpu.make_async_remote_copy(
-            src_ref=send_ref.at[v, 1], dst_ref=recv_ref.at[v, 0],
-            send_sem=send_sem.at[v, 1], recv_sem=recv_sem.at[v, 0],
+            src_ref=send_ref.at[v, 1, rows_h], dst_ref=recv_ref.at[v, 0, rows_h],
+            send_sem=send_sem.at[v, 1, h], recv_sem=recv_sem.at[v, 0, h],
             device_id=(view, me + 1), device_id_type=pl.DeviceIdType.MESH,
         )
         down = pltpu.make_async_remote_copy(
-            src_ref=send_ref.at[v, 0], dst_ref=recv_ref.at[v, 1],
-            send_sem=send_sem.at[v, 0], recv_sem=recv_sem.at[v, 1],
+            src_ref=send_ref.at[v, 0, rows_h], dst_ref=recv_ref.at[v, 1, rows_h],
+            send_sem=send_sem.at[v, 0, h], recv_sem=recv_sem.at[v, 1, h],
             device_id=(view, me - 1), device_id_type=pl.DeviceIdType.MESH,
         )
         return up, down
 
-    tb = [[taps_ref[v * 27 + 9 + t] for t in range(9)] for v in range(count)]
-
-    def finish(v):
-        up, down = copies(v)
+    def launch(v, h):
+        up, down = copies(v, h)
 
         @pl.when(has_hi)
         def _():
-            up.wait_send()
-            down.wait_recv()
+            up.start()
 
         @pl.when(has_lo)
         def _():
-            down.wait_send()
-            up.wait_recv()
+            down.start()
+
+    tb = [[taps_ref[v * 27 + 9 + t] for t in range(9)] for v in range(count)]
+
+    def finish(v):
+        for h in range(2):
+            up, down = copies(v, h)
+
+            @pl.when(has_hi)
+            def _():
+                up.wait_send()
+                down.wait_recv()
+
+            @pl.when(has_lo)
+            def _():
+                down.wait_send()
+                up.wait_recv()
 
         def back(c, carry):
             z0 = pl.multiple_of(c * CZ, CZ)
@@ -305,7 +215,6 @@
             c_ref[pl.ds(z0 + 4, CZ)] = _lane_correlate(ratio, wy_rev)
             return carry
 
-        lax.fori_loop(0, nz // CZ, middle, 0)
 
         def along_z_back(c, carry):
             z0 = pl.multiple_of(c * CZ, CZ)
@@ -316,16 +225,13 @@
             _pack(acc, send_ref.at[v, 0], send_ref.at[v, 1], pl.multiple_of(c * (CZ // 2), CZ // 2))
             return carry
 
-        lax.fori_loop(0, nz // CZ, along_z_back, 0)
-        up, down = copies(v)
-
-        @pl.when(has_hi)
-        def _():
-            up.start()
-
-        @pl.when(has_lo)
-        def _():
-            down.start()
+        chunks = nz // CZ
+        lax.fori_loop(0, chunks // 2 + 1, middle, 0)
+        lax.fori_loop(0, chunks // 2, along_z_back, 0)
+        launch(v, 0)
+        lax.fori_loop(chunks // 2 + 1, chunks, middle, 0)
+        lax.fori_loop(chunks // 2, chunks, along_z_back, 0)
+        launch(v, 1)
 
     for v in range(count):
         finish(v)
@@ -345,8 +251,8 @@
             pltpu.VMEM((count, nz, width, ny), jnp.float32),
             pltpu.VMEM((count, 2, nz // 2, width, ny), jnp.float32),
             pltpu.VMEM((count, 2, nz // 2, width, ny), jnp.float32),
-            pltpu.SemaphoreType.DMA((count, 2)),
-            pltpu.SemaphoreType.DMA((count, 2)),
+            pltpu.SemaphoreType.DMA((count, 2, 2)),
+            pltpu.SemaphoreType.DMA((count, 2, 2)),
         ],
         compiler_params=pltpu.CompilerParams(
             collective_id=0, has_side_effects=True, vmem_limit_bytes=48 * 1024 * 1024

time: 250 us -> 245 us (0.980)
  Pallas kernels: 104 us -> 98.8 us
    pallas_call x2, Pallas kernels: 104 us -> 98.8 us  [iteration_logs(): pl.pallas_call(_iteration_kernel, in_specs=[pl.BlockSpec(memory_space=plt...]
where the time goes in v10:
time: 245 us
  Pallas kernels  98.8 us (40%)
  waiting for transfers between devices  84.8 us (35%)
  starting transfers between devices  40.6 us (17%)
  local copies, waits for them, and re-layouts  9.62 us (4%)
  other arithmetic  7.05 us (3%)
  matrix products  3.32 us (1%)
    pallas_call x2, Pallas kernels, iteration_logs(): pl.pallas_call(_iteration_kernel, in_specs=[pl.BlockSpec(memory_space=plt...  98.8 us
    ppermute x3, waiting for transfers between devices, view_sum_update(): own = own + lax.ppermute(own, 'view', chip_swap)  36.6 us
    all_to_all x1, waiting for transfers between devices, per_device(): lax.all_to_all(local_views, 'vol', split_axis=2, concat_axis=1, tiled=True)  19.8 us
    ppermute x2, waiting for transfers between devices, swap_rims(): before = lax.ppermute(last, axis, up)  14 us
    all_to_all x1, starting transfers between devices, per_device(): lax.all_to_all(local_views, 'vol', split_axis=2, concat_axis=1, tiled=True)  10.5 us
    ppermute x2, starting transfers between devices, swap_rims(): after = lax.ppermute(first, axis, down)  7.18 us
    ppermute x2, waiting for transfers between devices, swap_rims(): after = lax.ppermute(first, axis, down)  6.96 us
    ppermute x3, starting transfers between devices, view_sum_update(): own = own + lax.ppermute(give, 'view', core_swap)  5.48 us
  transfers between devices with their start and end apart: 18, of which 13 were waited for; matrix products, arithmetic and copies ran while one was open for 1% of the time, Pallas kernels for 0%

profile of v10, /device:TPU:5, one launch (start us, length us, event | category | flops | bytes accessed | tf_op | source)
XLA Modules:
  0.0 244.6 jit_solution(6406898713462537455)
XLA Ops:
  0.0 0.9 reduce_sum.18
  0.9 0.7 broadcast_divide_fusion
  1.7 3.3 %fusion.1 = bf16[3,8,256,128]{3,2,1,0:T(8,128)(2,1)S(1)} fusion(bf16[3,8,256,128]{3,2,1,0:T(8,128)(2,1)S(1)} %copy-done, f32[3,256]{1,0:T(4,128)S(1)} %get-tuple-element.33, f32[3,256]{1,0:T(4,128)S(1)} %get-tuple-element.34, f32[3,256]{1,0:T(4,128)S(1)} %get-tuple-element.35, f32[3,256]{1,0:T(4,128)S(1)} %get-tuple-element.36, ...), kind=kOutput, calls=%fused_computation.2 | convolution fusion | flops 2421424128 | bytes 3173376 | tf_op jit(solution)/shard_map/vxr,vzry->vzxy/dot_general | solution.py:45
  5.0 2.2 copy.7
  7.2 10.5 %all-to-all-start = ((bf16[3,8,256,128]{3,1,0,2:T(8,128)(2,1)}), bf16[3,8,256,128]{3,1,0,2:T(8,128)(2,1)S(1)}, u32[]{:S(2)}, u32[]{:S(2)}) async-start(bf16[3,8,256,128]{3,1,0,2:T(8,128)(2,1)} %copy.7), calls=%async_computation | async-start | bytes 3145728 | tf_op jit(solution)/shard_map/all_to_all | solution.py:297
  17.8 19.8 %all-to-all-done = bf16[3,8,256,128]{3,1,0,2:T(8,128)(2,1)S(1)} async-done(((bf16[3,8,256,128]{3,1,0,2:T(8,128)(2,1)}), bf16[3,8,256,128]{3,1,0,2:T(8,128)(2,1)S(1)}, u32[]{:S(2)}, u32[]{:S(2)}) %all-to-all-start) | async-done | bytes 1572896 | tf_op jit(solution)/shard_map/all_to_all | solution.py:297
  37.6 1.2 copy-done.1
  38.8 1.9 copy.28
  41.0 1.0 copy-done.4
  41.9 0.8 constant_dynamic-slice_fusion.2
  42.7 3.3 %collective-permute-start = (f32[128,8,128]{2,1,0:T(8,128)}, f32[128,8,128]{2,1,0:T(8,128)}, u32[]{:S(2)}, u32[]{:S(2)}) collective-permute-start(f32[128,8,128]{2,1,0:T(8,128)} %constant_dynamic-slice_fusion.2), channel_id=1, source_target_pairs={{0,32},{32,0},{64,96},{96,64},{1,33},{33,1},{65,97},{97,65},{2,34}... | collective-permute-start | bytes 1572872 | tf_op jit(solution)/shard_map/ppermute | solution.py:277
  46.1 1.9 collective-permute-done
  48.0 1.3 dynamic-slice_add_fusion.2
  49.2 1.0 collective-permute-start.1
  50.2 12.2 %collective-permute-done.1 = f32[128,8,128]{2,1,0:T(8,128)S(1)} collective-permute-done((f32[128,8,128]{2,1,0:T(8,128)S(1)}, f32[128,8,128]{2,1,0:T(8,128)S(1)}, u32[]{:S(2)}, u32[]{:S(2)}) %collective-permute-start.1) | collective-permute-done | bytes 524320 | tf_op jit(solution)/shard_map/ppermute | solution.py:278
  62.5 0.8 copy-done.2
  63.3 0.8 fusion.68
  64.1 5.2 %collective-permute-start.5 = (f32[128,4,128]{2,1,0:T(4,128)S(1)}, f32[128,4,128]{2,1,0:T(4,128)}, u32[]{:S(2)}, u32[]{:S(2)}) collective-permute-start(f32[128,4,128]{2,1,0:T(4,128)S(1)} %get-tuple-element.21), channel_id=1, source_target_pairs={{1,0},{2,1},{3,2},{4,3},{5,4},{6,5},{7,6},{8,7},{9,8},{10,9},{11,1... | collective-permute-start | bytes 786440 | tf_op jit(solution)/shard_map/ppermute | solution.py:26
  69.3 1.9 collective-permute-start.3
  71.2 2.4 %collective-permute-done.5 = f32[128,4,128]{2,1,0:T(4,128)} collective-permute-done((f32[128,4,128]{2,1,0:T(4,128)S(1)}, f32[128,4,128]{2,1,0:T(4,128)}, u32[]{:S(2)}, u32[]{:S(2)}) %collective-permute-start.5) | collective-permute-done | bytes 262176 | tf_op jit(solution)/shard_map/ppermute | solution.py:26
  73.7 2.1 collective-permute-start.6
  76.0 7.4 %collective-permute-done.3 = f32[128,4,128]{2,1,0:T(4,128)S(1)} collective-permute-done((f32[128,4,128]{2,1,0:T(4,128)}, f32[128,4,128]{2,1,0:T(4,128)S(1)}, u32[]{:S(2)}, u32[]{:S(2)}) %collective-permute-start.3) | collective-permute-done | bytes 262176 | tf_op jit(solution)/shard_map/ppermute | solution.py:25
  83.5 2.4 collective-permute-start.4
  85.9 1.1 broadcast_select_fusion.11
  87.3 0.7 copy-done.3
  88.1 49.6 %shard_map.46 = f32[256,8,128]{2,1,0:T(8,128)S(1)} custom-call(f32[81]{0:T(128)S(1)} %reshape.17.taps_ref, f32[256,4,128]{2,1,0:T(4,128)S(1)} %pad_maximum_fusion.3.before_ref, f32[256,8,128]{2,1,0:T(8,128)S(1)} %pad_maximum_fusion.mid_ref, f32[256,4,128]{2,1,0:T(4,128)S(1)} %pad_maximum_fusion.4.after_ref, bf16[3,256,8,128]{3,2,1,0:T(8,128)(2,1)S(1)} %bitcast.48), custom_call_target="tpu_custom_call" | custom-call | tf_op jit(solution)/shard_map/pallas_call | solution.py:242
  137.8 0.9 collective-permute-start.7
  138.7 1.5 collective-permute-done.7
  140.3 1.2 collective-permute-start.8
  141.5 12.2 %collective-permute-done.8 = f32[128,8,128]{2,1,0:T(8,128)S(1)} collective-permute-done((f32[128,8,128]{2,1,0:T(8,128)S(1)}, f32[128,8,128]{2,1,0:T(8,128)S(1)}, u32[]{:S(2)}, u32[]{:S(2)}) %collective-permute-start.8) | collective-permute-done | bytes 524320 | tf_op jit(solution)/shard_map/ppermute | solution.py:278
  153.7 0.3 fusion.38
  154.0 1.3 collective-permute-start.9
  155.4 1.9 collective-permute-start.12
  157.3 3.3 %collective-permute-start.10 = (f32[128,4,128]{2,1,0:T(4,128)S(1)}, f32[128,4,128]{2,1,0:T(4,128)S(1)}, u32[]{:S(2)}, u32[]{:S(2)}) collective-permute-start(f32[128,4,128]{2,1,0:T(4,128)S(1)} %get-tuple-element.16), channel_id=1, source_target_pairs={{0,1},{1,2},{2,3},{3,4},{4,5},{5,6},{6,7},{7,8},{8,9},{9,10},{10,1... | collective-permute-start | bytes 786440 | tf_op jit(solution)/shard_map/ppermute | solution.py:25
  160.7 4.5 %collective-permute-done.12 = f32[128,4,128]{2,1,0:T(4,128)S(1)} collective-permute-done((f32[128,4,128]{2,1,0:T(4,128)S(1)}, f32[128,4,128]{2,1,0:T(4,128)S(1)}, u32[]{:S(2)}, u32[]{:S(2)}) %collective-permute-start.12) | collective-permute-done | bytes 262176 | tf_op jit(solution)/shard_map/ppermute | solution.py:26
  165.2 0.8 collective-permute-start.13
  166.0 6.6 %collective-permute-done.10 = f32[128,4,128]{2,1,0:T(4,128)S(1)} collective-permute-done((f32[128,4,128]{2,1,0:T(4,128)S(1)}, f32[128,4,128]{2,1,0:T(4,128)S(1)}, u32[]{:S(2)}, u32[]{:S(2)}) %collective-permute-start.10) | collective-permute-done | bytes 262176 | tf_op jit(solution)/shard_map/ppermute | solution.py:25
  172.5 1.1 collective-permute-start.11
  174.0 0.8 collective-permute-done.11
  175.0 49.2 %shard_map.47 = f32[256,8,128]{2,1,0:T(8,128)S(1)} custom-call(f32[81]{0:T(128)S(1)} %reshape.17.taps_ref, f32[256,4,128]{2,1,0:T(4,128)S(1)} %pad_maximum_fusion.5.before_ref, f32[256,8,128]{2,1,0:T(8,128)S(1)} %pad_maximum_fusion.1.mid_ref, f32[256,4,128]{2,1,0:T(4,128)S(1)} %pad_maximum_fusion.6.after_ref, bf16[3,256,8,128]{3,2,1,0:T(8,128)(2,1)S(1)} %bitcast.49), custom_call_target="tpu_custom_call" | custom-call | tf_op jit(solution)/shard_map/pallas_call | solution.py:242
  224.2 1.3 collective-permute-start.14
  225.5 1.5 collective-permute-done.14
  227.1 1.0 collective-permute-start.15
  228.1 12.2 %collective-permute-done.15 = f32[128,8,128]{2,1,0:T(8,128)S(1)} collective-permute-done((f32[128,8,128]{2,1,0:T(8,128)S(1)}, f32[128,8,128]{2,1,0:T(8,128)S(1)}, u32[]{:S(2)}, u32[]{:S(2)}) %collective-permute-start.15) | collective-permute-done | bytes 524320 | tf_op jit(solution)/shard_map/ppermute | solution.py:278
  240.3 0.3 fusion.36
  240.7 1.3 collective-permute-start.16
  241.9 1.5 collective-permute-done.16
  243.6 1.0 pad_maximum_fusion.2
  (40 shorter events, 1.8 us)
Async XLA Ops:
  0.0 1.7 copy-start
  7.2 30.4 %all-to-all-start = ((bf16[3,8,256,128]{3,1,0,2:T(8,128)(2,1)}), bf16[3,8,256,128]{3,1,0,2:T(8,128)(2,1)S(1)}, u32[]{:S(2)}, u32[]{:S(2)}) async-start(bf16[3,8,256,128]{3,1,0,2:T(8,128)(2,1)} %copy.7), calls=%async_computation | async-start | bytes 3145728 | tf_op jit(solution)/shard_map/all_to_all | solution.py:297
  37.6 1.2 copy-start.1
  40.9 1.0 copy-start.4
  42.7 5.2 %collective-permute-start = (f32[128,8,128]{2,1,0:T(8,128)}, f32[128,8,128]{2,1,0:T(8,128)}, u32[]{:S(2)}, u32[]{:S(2)}) collective-permute-start(f32[128,8,128]{2,1,0:T(8,128)} %constant_dynamic-slice_fusion.2), channel_id=1, source_target_pairs={{0,32},{32,0},{64,96},{96,64},{1,33},{33,1},{65,97},{97,65},{2,34}... | collective-permute-start | bytes 1572872 | tf_op jit(solution)/shard_map/ppermute | solution.py:277
  49.2 26.6 %copy-start.5 = (f32[3,3,9]{2,1,0:T(4,128)S(1)}, f32[3,3,9]{2,1,0:T(4,128)}, u32[]{:S(2)}) copy-start(f32[3,3,9]{2,1,0:T(4,128)} %param.7) | copy-start | bytes 976
  49.2 13.2 %collective-permute-start.1 = (f32[128,8,128]{2,1,0:T(8,128)S(1)}, f32[128,8,128]{2,1,0:T(8,128)S(1)}, u32[]{:S(2)}, u32[]{:S(2)}) collective-permute-start(f32[128,8,128]{2,1,0:T(8,128)S(1)} %dynamic-slice_add_fusion.2), channel_id=1, source_target_pairs={{0,64},{32,96},{64,0},{96,32},{1,65},{33,97},{65,1},{97,33},{2,66}... | collective-permute-start | bytes 1572872 | tf_op jit(solution)/shard_map/ppermute | solution.py:278
  62.5 0.8 copy-start.2
  64.1 9.6 %collective-permute-start.5 = (f32[128,4,128]{2,1,0:T(4,128)S(1)}, f32[128,4,128]{2,1,0:T(4,128)}, u32[]{:S(2)}, u32[]{:S(2)}) collective-permute-start(f32[128,4,128]{2,1,0:T(4,128)S(1)} %get-tuple-element.21), channel_id=1, source_target_pairs={{1,0},{2,1},{3,2},{4,3},{5,4},{6,5},{7,6},{8,7},{9,8},{10,9},{11,1... | collective-permute-start | bytes 786440 | tf_op jit(solution)/shard_map/ppermute | solution.py:26
  69.3 14.1 %collective-permute-start.3 = (f32[128,4,128]{2,1,0:T(4,128)}, f32[128,4,128]{2,1,0:T(4,128)S(1)}, u32[]{:S(2)}, u32[]{:S(2)}) collective-permute-start(f32[128,4,128]{2,1,0:T(4,128)} %get-tuple-element.22), channel_id=1, source_target_pairs={{0,1},{1,2},{2,3},{3,4},{4,5},{5,6},{6,7},{7,8},{8,9},{9,10},{10,1... | collective-permute-start | bytes 786440 | tf_op jit(solution)/shard_map/ppermute | solution.py:25
  73.7 12.2 %collective-permute-start.6 = (f32[128,4,128]{2,1,0:T(4,128)}, f32[128,4,128]{2,1,0:T(4,128)}, u32[]{:S(2)}, u32[]{:S(2)}) collective-permute-start(f32[128,4,128]{2,1,0:T(4,128)} %collective-permute-done.5), channel_id=1, source_target_pairs={{0,32},{32,0},{64,96},{96,64},{1,33},{33,1},{65,97},{97,65},{2,34}... | collective-permute-start | bytes 786440 | tf_op jit(solution)/shard_map/ppermute | solution.py:285
  76.0 11.3 %collective-permute-start.2 = (f32[128,8,128]{2,1,0:T(8,128)}, f32[128,8,128]{2,1,0:T(8,128)S(1)}, u32[]{:S(2)}, u32[]{:S(2)}) collective-permute-start(f32[128,8,128]{2,1,0:T(8,128)} %copy-done.2), channel_id=1, source_target_pairs={{0,32},{32,0},{64,96},{96,64},{1,33},{33,1},{65,97},{97,65},{2,34}... | collective-permute-start | bytes 1572872 | tf_op jit(solution)/shard_map/ppermute | solution.py:280
  83.5 3.6 %collective-permute-start.4 = (f32[128,4,128]{2,1,0:T(4,128)S(1)}, f32[128,4,128]{2,1,0:T(4,128)S(1)}, u32[]{:S(2)}, u32[]{:S(2)}) collective-permute-start(f32[128,4,128]{2,1,0:T(4,128)S(1)} %collective-permute-done.3), channel_id=1, source_target_pairs={{0,32},{32,0},{64,96},{96,64},{1,33},{33,1},{65,97},{97,65},{2,34}... | collective-permute-start | bytes 786440 | tf_op jit(solution)/shard_map/ppermute | solution.py:284
  86.9 1.0 copy-start.3
  137.8 2.4 collective-permute-start.7
  140.3 13.4 %collective-permute-start.8 = (f32[128,8,128]{2,1,0:T(8,128)S(1)}, f32[128,8,128]{2,1,0:T(8,128)S(1)}, u32[]{:S(2)}, u32[]{:S(2)}) collective-permute-start(f32[128,8,128]{2,1,0:T(8,128)S(1)} %dynamic-slice_add_fusion.1), channel_id=1, source_target_pairs={{0,64},{32,96},{64,0},{96,32},{1,65},{33,97},{65,1},{97,33},{2,66}... | collective-permute-start | bytes 1572872 | tf_op jit(solution)/shard_map/ppermute | solution.py:278
  154.0 19.7 %collective-permute-start.9 = (f32[128,8,128]{2,1,0:T(8,128)S(1)}, f32[128,8,128]{2,1,0:T(8,128)S(1)}, u32[]{:S(2)}, u32[]{:S(2)}) collective-permute-start(f32[128,8,128]{2,1,0:T(8,128)S(1)} %fusion.38), channel_id=1, source_target_pairs={{0,32},{32,0},{64,96},{96,64},{1,33},{33,1},{65,97},{97,65},{2,34}... | collective-permute-start | bytes 1572872 | tf_op jit(solution)/shard_map/ppermute | solution.py:280
  155.4 9.8 %collective-permute-start.12 = (f32[128,4,128]{2,1,0:T(4,128)S(1)}, f32[128,4,128]{2,1,0:T(4,128)S(1)}, u32[]{:S(2)}, u32[]{:S(2)}) collective-permute-start(f32[128,4,128]{2,1,0:T(4,128)S(1)} %get-tuple-element.15), channel_id=1, source_target_pairs={{1,0},{2,1},{3,2},{4,3},{5,4},{6,5},{7,6},{8,7},{9,8},{10,9},{11,1... | collective-permute-start | bytes 786440 | tf_op jit(solution)/shard_map/ppermute | solution.py:26
  157.3 15.2 %collective-permute-start.10 = (f32[128,4,128]{2,1,0:T(4,128)S(1)}, f32[128,4,128]{2,1,0:T(4,128)S(1)}, u32[]{:S(2)}, u32[]{:S(2)}) collective-permute-start(f32[128,4,128]{2,1,0:T(4,128)S(1)} %get-tuple-element.16), channel_id=1, source_target_pairs={{0,1},{1,2},{2,3},{3,4},{4,5},{5,6},{6,7},{7,8},{8,9},{9,10},{10,1... | collective-permute-start | bytes 786440 | tf_op jit(solution)/shard_map/ppermute | solution.py:25
  165.2 8.6 %collective-permute-start.13 = (f32[128,4,128]{2,1,0:T(4,128)S(1)}, f32[128,4,128]{2,1,0:T(4,128)S(1)}, u32[]{:S(2)}, u32[]{:S(2)}) collective-permute-start(f32[128,4,128]{2,1,0:T(4,128)S(1)} %collective-permute-done.12), channel_id=1, source_target_pairs={{0,32},{32,0},{64,96},{96,64},{1,33},{33,1},{65,97},{97,65},{2,34}... | collective-permute-start | bytes 786440 | tf_op jit(solution)/shard_map/ppermute | solution.py:285
  172.5 2.3 collective-permute-start.11
  224.2 2.8 %collective-permute-start.14 = (f32[128,8,128]{2,1,0:T(8,128)S(1)}, f32[128,8,128]{2,1,0:T(8,128)S(1)}, u32[]{:S(2)}, u32[]{:S(2)}) collective-permute-start(f32[128,8,128]{2,1,0:T(8,128)S(1)} %constant_dynamic-slice_fusion), channel_id=1, source_target_pairs={{0,32},{32,0},{64,96},{96,64},{1,33},{33,1},{65,97},{97,65},{2,34}... | collective-permute-start | bytes 1572872 | tf_op jit(solution)/shard_map/ppermute | solution.py:277
  227.1 13.2 %collective-permute-start.15 = (f32[128,8,128]{2,1,0:T(8,128)S(1)}, f32[128,8,128]{2,1,0:T(8,128)S(1)}, u32[]{:S(2)}, u32[]{:S(2)}) collective-permute-start(f32[128,8,128]{2,1,0:T(8,128)S(1)} %dynamic-slice_add_fusion), channel_id=1, source_target_pairs={{0,64},{32,96},{64,0},{96,32},{1,65},{33,97},{65,1},{97,33},{2,66}... | collective-permute-start | bytes 1572872 | tf_op jit(solution)/shard_map/ppermute | solution.py:278
  240.7 2.8 %collective-permute-start.16 = (f32[128,8,128]{2,1,0:T(8,128)S(1)}, f32[128,8,128]{2,1,0:T(8,128)S(1)}, u32[]{:S(2)}, u32[]{:S(2)}) collective-permute-start(f32[128,8,128]{2,1,0:T(8,128)S(1)} %fusion.36), channel_id=1, source_target_pairs={{0,32},{32,0},{64,96},{96,64},{1,33},{33,1},{65,97},{97,65},{2,34}... | collective-permute-start | bytes 1572872 | tf_op jit(solution)/shard_map/ppermute | solution.py:280

commit v11 on v10

--- a/solution.py
+++ b/solution.py
@@ -114,7 +114,8 @@
     def _():
         recv_ref[:, 1] = jnp.zeros(recv_ref.shape[:1] + recv_ref.shape[2:], jnp.float32)
 
-    rows = nz // 4
+    pieces = 4
+    rows = nz // 2 // pieces
 
     def copies(v, h):
         rows_h = pl.ds(h * rows, rows)
@@ -144,7 +145,7 @@
     tb = [[taps_ref[v * 27 + 9 + t] for t in range(9)] for v in range(count)]
 
     def finish(v):
-        for h in range(2):
+        for h in range(pieces):
             up, down = copies(v, h)
 
             @pl.when(has_hi)
@@ -226,12 +227,11 @@
             return carry
 
         chunks = nz // CZ
-        lax.fori_loop(0, chunks // 2 + 1, middle, 0)
-        lax.fori_loop(0, chunks // 2, along_z_back, 0)
-        launch(v, 0)
-        lax.fori_loop(chunks // 2 + 1, chunks, middle, 0)
-        lax.fori_loop(chunks // 2, chunks, along_z_back, 0)
-        launch(v, 1)
+        step = chunks // pieces
+        for h in range(pieces):
+            lax.fori_loop(0 if h == 0 else h * step + 1, min((h + 1) * step + 1, chunks), middle, 0)
+            lax.fori_loop(h * step, (h + 1) * step, along_z_back, 0)
+            launch(v, h)
 
     for v in range(count):
         finish(v)
@@ -251,8 +251,8 @@
             pltpu.VMEM((count, nz, width, ny), jnp.float32),
             pltpu.VMEM((count, 2, nz // 2, width, ny), jnp.float32),
             pltpu.VMEM((count, 2, nz // 2, width, ny), jnp.float32),
-            pltpu.SemaphoreType.DMA((count, 2, 2)),
-            pltpu.SemaphoreType.DMA((count, 2, 2)),
+            pltpu.SemaphoreType.DMA((count, 2, 4)),
+            pltpu.SemaphoreType.DMA((count, 2, 4)),
         ],
         compiler_params=pltpu.CompilerParams(
             collective_id=0, has_side_effects=True, vmem_limit_bytes=48 * 1024 * 1024

time: 245 us -> 242 us (0.988)
  Pallas kernels: 98.8 us -> 96.1 us
    pallas_call x2, Pallas kernels: 98.8 us -> 96.1 us  [iteration_logs(): pl.pallas_call(_iteration_kernel, in_specs=[pl.BlockSpec(memory_space=plt...]
where the time goes in v11:
time: 242 us
  Pallas kernels  96.1 us (40%)
  waiting for transfers between devices  85 us (35%)
  starting transfers between devices  40.5 us (17%)
  local copies, waits for them, and re-layouts  9.62 us (4%)
  other arithmetic  7.05 us (3%)
  matrix products  3.32 us (1%)
    pallas_call x2, Pallas kernels, iteration_logs(): pl.pallas_call(_iteration_kernel, in_specs=[pl.BlockSpec(memory_space=plt...  96.1 us
    ppermute x3, waiting for transfers between devices, view_sum_update(): own = own + lax.ppermute(own, 'view', chip_swap)  36.6 us
    all_to_all x1, waiting for transfers between devices, per_device(): lax.all_to_all(local_views, 'vol', split_axis=2, concat_axis=1, tiled=True)  19.8 us
    ppermute x2, waiting for transfers between devices, swap_rims(): before = lax.ppermute(last, axis, up)  14.2 us
    all_to_all x1, starting transfers between devices, per_device(): lax.all_to_all(local_views, 'vol', split_axis=2, concat_axis=1, tiled=True)  10.5 us
    ppermute x2, starting transfers between devices, swap_rims(): after = lax.ppermute(first, axis, down)  7.36 us
    ppermute x2, waiting for transfers between devices, swap_rims(): after = lax.ppermute(first, axis, down)  6.96 us
    ppermute x3, starting transfers between devices, view_sum_update(): own = own + lax.ppermute(give, 'view', core_swap)  5.48 us
  transfers between devices with their start and end apart: 18, of which 13 were waited for; matrix products, arithmetic and copies ran while one was open for 1% of the time, Pallas kernels for 0%

profile of v11, /device:TPU:5, one launch (start us, length us, event | category | flops | bytes accessed | tf_op | source)
XLA Modules:
  0.0 241.9 jit_solution(12385168854799368131)
XLA Ops:
  0.0 0.9 reduce_sum.18
  0.9 0.7 broadcast_divide_fusion
  1.7 3.3 %fusion.1 = bf16[3,8,256,128]{3,2,1,0:T(8,128)(2,1)S(1)} fusion(bf16[3,8,256,128]{3,2,1,0:T(8,128)(2,1)S(1)} %copy-done, f32[3,256]{1,0:T(4,128)S(1)} %get-tuple-element.33, f32[3,256]{1,0:T(4,128)S(1)} %get-tuple-element.34, f32[3,256]{1,0:T(4,128)S(1)} %get-tuple-element.35, f32[3,256]{1,0:T(4,128)S(1)} %get-tuple-element.36, ...), kind=kOutput, calls=%fused_computation.2 | convolution fusion | flops 2421424128 | bytes 3173376 | tf_op jit(solution)/shard_map/vxr,vzry->vzxy/dot_general | solution.py:45
  5.0 2.2 copy.7
  7.2 10.5 %all-to-all-start = ((bf16[3,8,256,128]{3,1,0,2:T(8,128)(2,1)}), bf16[3,8,256,128]{3,1,0,2:T(8,128)(2,1)S(1)}, u32[]{:S(2)}, u32[]{:S(2)}) async-start(bf16[3,8,256,128]{3,1,0,2:T(8,128)(2,1)} %copy.7), calls=%async_computation | async-start | bytes 3145728 | tf_op jit(solution)/shard_map/all_to_all | solution.py:297
  17.8 19.8 %all-to-all-done = bf16[3,8,256,128]{3,1,0,2:T(8,128)(2,1)S(1)} async-done(((bf16[3,8,256,128]{3,1,0,2:T(8,128)(2,1)}), bf16[3,8,256,128]{3,1,0,2:T(8,128)(2,1)S(1)}, u32[]{:S(2)}, u32[]{:S(2)}) %all-to-all-start) | async-done | bytes 1572896 | tf_op jit(solution)/shard_map/all_to_all | solution.py:297
  37.6 1.2 copy-done.1
  38.8 1.9 copy.28
  41.0 1.0 copy-done.4
  41.9 0.8 constant_dynamic-slice_fusion.2
  42.7 3.3 %collective-permute-start = (f32[128,8,128]{2,1,0:T(8,128)}, f32[128,8,128]{2,1,0:T(8,128)}, u32[]{:S(2)}, u32[]{:S(2)}) collective-permute-start(f32[128,8,128]{2,1,0:T(8,128)} %constant_dynamic-slice_fusion.2), channel_id=1, source_target_pairs={{0,32},{32,0},{64,96},{96,64},{1,33},{33,1},{65,97},{97,65},{2,34}... | collective-permute-start | bytes 1572872 | tf_op jit(solution)/shard_map/ppermute | solution.py:277
  46.1 1.9 collective-permute-done
  48.0 1.3 dynamic-slice_add_fusion.2
  49.2 1.0 collective-permute-start.1
  50.2 12.2 %collective-permute-done.1 = f32[128,8,128]{2,1,0:T(8,128)S(1)} collective-permute-done((f32[128,8,128]{2,1,0:T(8,128)S(1)}, f32[128,8,128]{2,1,0:T(8,128)S(1)}, u32[]{:S(2)}, u32[]{:S(2)}) %collective-permute-start.1) | collective-permute-done | bytes 524320 | tf_op jit(solution)/shard_map/ppermute | solution.py:278
  62.5 0.8 copy-done.2
  63.3 0.8 fusion.68
  64.1 5.2 %collective-permute-start.5 = (f32[128,4,128]{2,1,0:T(4,128)S(1)}, f32[128,4,128]{2,1,0:T(4,128)}, u32[]{:S(2)}, u32[]{:S(2)}) collective-permute-start(f32[128,4,128]{2,1,0:T(4,128)S(1)} %get-tuple-element.21), channel_id=1, source_target_pairs={{1,0},{2,1},{3,2},{4,3},{5,4},{6,5},{7,6},{8,7},{9,8},{10,9},{11,1... | collective-permute-start | bytes 786440 | tf_op jit(solution)/shard_map/ppermute | solution.py:26
  69.3 1.9 collective-permute-start.3
  71.2 2.4 %collective-permute-done.5 = f32[128,4,128]{2,1,0:T(4,128)} collective-permute-done((f32[128,4,128]{2,1,0:T(4,128)S(1)}, f32[128,4,128]{2,1,0:T(4,128)}, u32[]{:S(2)}, u32[]{:S(2)}) %collective-permute-start.5) | collective-permute-done | bytes 262176 | tf_op jit(solution)/shard_map/ppermute | solution.py:26
  73.7 2.1 collective-permute-start.6
  76.0 7.4 %collective-permute-done.3 = f32[128,4,128]{2,1,0:T(4,128)S(1)} collective-permute-done((f32[128,4,128]{2,1,0:T(4,128)}, f32[128,4,128]{2,1,0:T(4,128)S(1)}, u32[]{:S(2)}, u32[]{:S(2)}) %collective-permute-start.3) | collective-permute-done | bytes 262176 | tf_op jit(solution)/shard_map/ppermute | solution.py:25
  83.5 2.4 collective-permute-start.4
  85.9 1.1 broadcast_select_fusion.11
  87.3 0.7 copy-done.3
  88.1 48.3 %shard_map.46 = f32[256,8,128]{2,1,0:T(8,128)S(1)} custom-call(f32[81]{0:T(128)S(1)} %reshape.17.taps_ref, f32[256,4,128]{2,1,0:T(4,128)S(1)} %pad_maximum_fusion.3.before_ref, f32[256,8,128]{2,1,0:T(8,128)S(1)} %pad_maximum_fusion.mid_ref, f32[256,4,128]{2,1,0:T(4,128)S(1)} %pad_maximum_fusion.4.after_ref, bf16[3,256,8,128]{3,2,1,0:T(8,128)(2,1)S(1)} %bitcast.48), custom_call_target="tpu_custom_call" | custom-call | tf_op jit(solution)/shard_map/pallas_call | solution.py:242
  136.5 0.9 collective-permute-start.7
  137.3 1.5 collective-permute-done.7
  138.9 1.0 collective-permute-start.8
  139.9 12.2 %collective-permute-done.8 = f32[128,8,128]{2,1,0:T(8,128)S(1)} collective-permute-done((f32[128,8,128]{2,1,0:T(8,128)S(1)}, f32[128,8,128]{2,1,0:T(8,128)S(1)}, u32[]{:S(2)}, u32[]{:S(2)}) %collective-permute-start.8) | collective-permute-done | bytes 524320 | tf_op jit(solution)/shard_map/ppermute | solution.py:278
  152.1 0.3 fusion.38
  152.5 1.3 collective-permute-start.9
  153.8 2.1 collective-permute-start.12
  156.0 3.2 %collective-permute-start.10 = (f32[128,4,128]{2,1,0:T(4,128)S(1)}, f32[128,4,128]{2,1,0:T(4,128)S(1)}, u32[]{:S(2)}, u32[]{:S(2)}) collective-permute-start(f32[128,4,128]{2,1,0:T(4,128)S(1)} %get-tuple-element.16), channel_id=1, source_target_pairs={{0,1},{1,2},{2,3},{3,4},{4,5},{5,6},{6,7},{7,8},{8,9},{9,10},{10,1... | collective-permute-start | bytes 786440 | tf_op jit(solution)/shard_map/ppermute | solution.py:25
  159.1 4.5 %collective-permute-done.12 = f32[128,4,128]{2,1,0:T(4,128)S(1)} collective-permute-done((f32[128,4,128]{2,1,0:T(4,128)S(1)}, f32[128,4,128]{2,1,0:T(4,128)S(1)}, u32[]{:S(2)}, u32[]{:S(2)}) %collective-permute-start.12) | collective-permute-done | bytes 262176 | tf_op jit(solution)/shard_map/ppermute | solution.py:26
  163.6 0.8 collective-permute-start.13
  164.4 6.7 %collective-permute-done.10 = f32[128,4,128]{2,1,0:T(4,128)S(1)} collective-permute-done((f32[128,4,128]{2,1,0:T(4,128)S(1)}, f32[128,4,128]{2,1,0:T(4,128)S(1)}, u32[]{:S(2)}, u32[]{:S(2)}) %collective-permute-start.10) | collective-permute-done | bytes 262176 | tf_op jit(solution)/shard_map/ppermute | solution.py:25
  171.2 1.1 collective-permute-start.11
  172.6 0.8 collective-permute-done.11
  173.6 47.9 %shard_map.47 = f32[256,8,128]{2,1,0:T(8,128)S(1)} custom-call(f32[81]{0:T(128)S(1)} %reshape.17.taps_ref, f32[256,4,128]{2,1,0:T(4,128)S(1)} %pad_maximum_fusion.5.before_ref, f32[256,8,128]{2,1,0:T(8,128)S(1)} %pad_maximum_fusion.1.mid_ref, f32[256,4,128]{2,1,0:T(4,128)S(1)} %pad_maximum_fusion.6.after_ref, bf16[3,256,8,128]{3,2,1,0:T(8,128)(2,1)S(1)} %bitcast.49), custom_call_target="tpu_custom_call" | custom-call | tf_op jit(solution)/shard_map/pallas_call | solution.py:242
  221.5 1.3 collective-permute-start.14
  222.8 1.5 collective-permute-done.14
  224.4 1.0 collective-permute-start.15
  225.4 12.2 %collective-permute-done.15 = f32[128,8,128]{2,1,0:T(8,128)S(1)} collective-permute-done((f32[128,8,128]{2,1,0:T(8,128)S(1)}, f32[128,8,128]{2,1,0:T(8,128)S(1)}, u32[]{:S(2)}, u32[]{:S(2)}) %collective-permute-start.15) | collective-permute-done | bytes 524320 | tf_op jit(solution)/shard_map/ppermute | solution.py:278
  237.6 0.3 fusion.36
  237.9 1.3 collective-permute-start.16
  239.2 1.5 collective-permute-done.16
  240.8 1.0 pad_maximum_fusion.2
  (40 shorter events, 1.8 us)
Async XLA Ops:
  0.0 1.7 copy-start
  7.2 30.4 %all-to-all-start = ((bf16[3,8,256,128]{3,1,0,2:T(8,128)(2,1)}), bf16[3,8,256,128]{3,1,0,2:T(8,128)(2,1)S(1)}, u32[]{:S(2)}, u32[]{:S(2)}) async-start(bf16[3,8,256,128]{3,1,0,2:T(8,128)(2,1)} %copy.7), calls=%async_computation | async-start | bytes 3145728 | tf_op jit(solution)/shard_map/all_to_all | solution.py:297
  37.6 1.2 copy-start.1
  40.9 1.0 copy-start.4
  42.7 5.2 %collective-permute-start = (f32[128,8,128]{2,1,0:T(8,128)}, f32[128,8,128]{2,1,0:T(8,128)}, u32[]{:S(2)}, u32[]{:S(2)}) collective-permute-start(f32[128,8,128]{2,1,0:T(8,128)} %constant_dynamic-slice_fusion.2), channel_id=1, source_target_pairs={{0,32},{32,0},{64,96},{96,64},{1,33},{33,1},{65,97},{97,65},{2,34}... | collective-permute-start | bytes 1572872 | tf_op jit(solution)/shard_map/ppermute | solution.py:277
  49.2 26.6 %copy-start.5 = (f32[3,3,9]{2,1,0:T(4,128)S(1)}, f32[3,3,9]{2,1,0:T(4,128)}, u32[]{:S(2)}) copy-start(f32[3,3,9]{2,1,0:T(4,128)} %param.7) | copy-start | bytes 976
  49.2 13.2 %collective-permute-start.1 = (f32[128,8,128]{2,1,0:T(8,128)S(1)}, f32[128,8,128]{2,1,0:T(8,128)S(1)}, u32[]{:S(2)}, u32[]{:S(2)}) collective-permute-start(f32[128,8,128]{2,1,0:T(8,128)S(1)} %dynamic-slice_add_fusion.2), channel_id=1, source_target_pairs={{0,64},{32,96},{64,0},{96,32},{1,65},{33,97},{65,1},{97,33},{2,66}... | collective-permute-start | bytes 1572872 | tf_op jit(solution)/shard_map/ppermute | solution.py:278
  62.5 0.8 copy-start.2
  64.1 9.6 %collective-permute-start.5 = (f32[128,4,128]{2,1,0:T(4,128)S(1)}, f32[128,4,128]{2,1,0:T(4,128)}, u32[]{:S(2)}, u32[]{:S(2)}) collective-permute-start(f32[128,4,128]{2,1,0:T(4,128)S(1)} %get-tuple-element.21), channel_id=1, source_target_pairs={{1,0},{2,1},{3,2},{4,3},{5,4},{6,5},{7,6},{8,7},{9,8},{10,9},{11,1... | collective-permute-start | bytes 786440 | tf_op jit(solution)/shard_map/ppermute | solution.py:26
  69.3 14.1 %collective-permute-start.3 = (f32[128,4,128]{2,1,0:T(4,128)}, f32[128,4,128]{2,1,0:T(4,128)S(1)}, u32[]{:S(2)}, u32[]{:S(2)}) collective-permute-start(f32[128,4,128]{2,1,0:T(4,128)} %get-tuple-element.22), channel_id=1, source_target_pairs={{0,1},{1,2},{2,3},{3,4},{4,5},{5,6},{6,7},{7,8},{8,9},{9,10},{10,1... | collective-permute-start | bytes 786440 | tf_op jit(solution)/shard_map/ppermute | solution.py:25
  73.7 12.2 %collective-permute-start.6 = (f32[128,4,128]{2,1,0:T(4,128)}, f32[128,4,128]{2,1,0:T(4,128)}, u32[]{:S(2)}, u32[]{:S(2)}) collective-permute-start(f32[128,4,128]{2,1,0:T(4,128)} %collective-permute-done.5), channel_id=1, source_target_pairs={{0,32},{32,0},{64,96},{96,64},{1,33},{33,1},{65,97},{97,65},{2,34}... | collective-permute-start | bytes 786440 | tf_op jit(solution)/shard_map/ppermute | solution.py:285
  76.0 11.3 %collective-permute-start.2 = (f32[128,8,128]{2,1,0:T(8,128)}, f32[128,8,128]{2,1,0:T(8,128)S(1)}, u32[]{:S(2)}, u32[]{:S(2)}) collective-permute-start(f32[128,8,128]{2,1,0:T(8,128)} %copy-done.2), channel_id=1, source_target_pairs={{0,32},{32,0},{64,96},{96,64},{1,33},{33,1},{65,97},{97,65},{2,34}... | collective-permute-start | bytes 1572872 | tf_op jit(solution)/shard_map/ppermute | solution.py:280
  83.5 3.6 %collective-permute-start.4 = (f32[128,4,128]{2,1,0:T(4,128)S(1)}, f32[128,4,128]{2,1,0:T(4,128)S(1)}, u32[]{:S(2)}, u32[]{:S(2)}) collective-permute-start(f32[128,4,128]{2,1,0:T(4,128)S(1)} %collective-permute-done.3), channel_id=1, source_target_pairs={{0,32},{32,0},{64,96},{96,64},{1,33},{33,1},{65,97},{97,65},{2,34}... | collective-permute-start | bytes 786440 | tf_op jit(solution)/shard_map/ppermute | solution.py:284
  86.9 1.0 copy-start.3
  136.5 2.4 collective-permute-start.7
  138.9 13.2 %collective-permute-start.8 = (f32[128,8,128]{2,1,0:T(8,128)S(1)}, f32[128,8,128]{2,1,0:T(8,128)S(1)}, u32[]{:S(2)}, u32[]{:S(2)}) collective-permute-start(f32[128,8,128]{2,1,0:T(8,128)S(1)} %dynamic-slice_add_fusion.1), channel_id=1, source_target_pairs={{0,64},{32,96},{64,0},{96,32},{1,65},{33,97},{65,1},{97,33},{2,66}... | collective-permute-start | bytes 1572872 | tf_op jit(solution)/shard_map/ppermute | solution.py:278
  152.5 19.8 %collective-permute-start.9 = (f32[128,8,128]{2,1,0:T(8,128)S(1)}, f32[128,8,128]{2,1,0:T(8,128)S(1)}, u32[]{:S(2)}, u32[]{:S(2)}) collective-permute-start(f32[128,8,128]{2,1,0:T(8,128)S(1)} %fusion.38), channel_id=1, source_target_pairs={{0,32},{32,0},{64,96},{96,64},{1,33},{33,1},{65,97},{97,65},{2,34}... | collective-permute-start | bytes 1572872 | tf_op jit(solution)/shard_map/ppermute | solution.py:280
  153.8 9.8 %collective-permute-start.12 = (f32[128,4,128]{2,1,0:T(4,128)S(1)}, f32[128,4,128]{2,1,0:T(4,128)S(1)}, u32[]{:S(2)}, u32[]{:S(2)}) collective-permute-start(f32[128,4,128]{2,1,0:T(4,128)S(1)} %get-tuple-element.15), channel_id=1, source_target_pairs={{1,0},{2,1},{3,2},{4,3},{5,4},{6,5},{7,6},{8,7},{9,8},{10,9},{11,1... | collective-permute-start | bytes 786440 | tf_op jit(solution)/shard_map/ppermute | solution.py:26
  156.0 15.2 %collective-permute-start.10 = (f32[128,4,128]{2,1,0:T(4,128)S(1)}, f32[128,4,128]{2,1,0:T(4,128)S(1)}, u32[]{:S(2)}, u32[]{:S(2)}) collective-permute-start(f32[128,4,128]{2,1,0:T(4,128)S(1)} %get-tuple-element.16), channel_id=1, source_target_pairs={{0,1},{1,2},{2,3},{3,4},{4,5},{5,6},{6,7},{7,8},{8,9},{9,10},{10,1... | collective-permute-start | bytes 786440 | tf_op jit(solution)/shard_map/ppermute | solution.py:25
  163.6 8.8 %collective-permute-start.13 = (f32[128,4,128]{2,1,0:T(4,128)S(1)}, f32[128,4,128]{2,1,0:T(4,128)S(1)}, u32[]{:S(2)}, u32[]{:S(2)}) collective-permute-start(f32[128,4,128]{2,1,0:T(4,128)S(1)} %collective-permute-done.12), channel_id=1, source_target_pairs={{0,32},{32,0},{64,96},{96,64},{1,33},{33,1},{65,97},{97,65},{2,34}... | collective-permute-start | bytes 786440 | tf_op jit(solution)/shard_map/ppermute | solution.py:285
  171.2 2.3 collective-permute-start.11
  221.5 2.8 %collective-permute-start.14 = (f32[128,8,128]{2,1,0:T(8,128)S(1)}, f32[128,8,128]{2,1,0:T(8,128)S(1)}, u32[]{:S(2)}, u32[]{:S(2)}) collective-permute-start(f32[128,8,128]{2,1,0:T(8,128)S(1)} %constant_dynamic-slice_fusion), channel_id=1, source_target_pairs={{0,32},{32,0},{64,96},{96,64},{1,33},{33,1},{65,97},{97,65},{2,34}... | collective-permute-start | bytes 1572872 | tf_op jit(solution)/shard_map/ppermute | solution.py:277
  224.4 13.2 %collective-permute-start.15 = (f32[128,8,128]{2,1,0:T(8,128)S(1)}, f32[128,8,128]{2,1,0:T(8,128)S(1)}, u32[]{:S(2)}, u32[]{:S(2)}) collective-permute-start(f32[128,8,128]{2,1,0:T(8,128)S(1)} %dynamic-slice_add_fusion), channel_id=1, source_target_pairs={{0,64},{32,96},{64,0},{96,32},{1,65},{33,97},{65,1},{97,33},{2,66}... | collective-permute-start | bytes 1572872 | tf_op jit(solution)/shard_map/ppermute | solution.py:278
  237.9 2.8 %collective-permute-start.16 = (f32[128,8,128]{2,1,0:T(8,128)S(1)}, f32[128,8,128]{2,1,0:T(8,128)S(1)}, u32[]{:S(2)}, u32[]{:S(2)}) collective-permute-start(f32[128,8,128]{2,1,0:T(8,128)S(1)} %fusion.36), channel_id=1, source_target_pairs={{0,32},{32,0},{64,96},{96,64},{1,33},{33,1},{65,97},{97,65},{2,34}... | collective-permute-start | bytes 1572872 | tf_op jit(solution)/shard_map/ppermute | solution.py:280

commit v12 on v11

--- a/solution.py
+++ b/solution.py
@@ -293,8 +293,13 @@
     weight_norm = weights / jnp.sum(weights, axis=-1, keepdims=True)
     taps_norm = psf_taps / jnp.sum(psf_taps, axis=-1, keepdims=True)
     taps_flat = taps_norm.reshape(-1)
-    local_views = resample_views(raw_views, weight_norm, offsets)
-    bricks = lax.all_to_all(local_views, "vol", split_axis=2, concat_axis=1, tiled=True)
+    moved = []
+    for index in range(count):
+        one_view = resample_views(
+            raw_views[index : index + 1], weight_norm[index : index + 1], offsets[index : index + 1]
+        )
+        moved.append(lax.all_to_all(one_view, "vol", split_axis=2, concat_axis=1, tiled=True))
+    bricks = jnp.concatenate(moved, axis=0)
     local_sum = bricks[0].astype(jnp.float32)
     for index in range(1, count):
         local_sum = local_sum + bricks[index].astype(jnp.float32)

time: 242 us -> 254 us (1.050)
  starting transfers between devices: 40.5 us -> 56.3 us
  local copies, waits for them, and re-layouts: 9.62 us -> 5.77 us
    all_to_all x1 -> x3, starting transfers between devices: 10.5 us -> 23.5 us  [per_device(): lax.all_to_all(one_view, 'vol', split_axis=2, concat_axis=1, tiled=True)]
    unnamed x16 -> x4, local copies, waits for them, and re-layouts: 3.69 us -> 0.01 us
    all_to_all x1 -> x3, waiting for transfers between devices: 19.8 us -> 23.2 us  [per_device(): lax.all_to_all(one_view, 'vol', split_axis=2, concat_axis=1, tiled=True)]
  transfers between devices with their start and end apart: 18 -> 20, of which waited for: 13 -> 17; matrix products, arithmetic and copies ran while one was open for 1% -> 2% of each run, Pallas kernels for 0% -> 0%
where the time goes in v12:
time: 254 us; the launch traced here: 253 us
  Pallas kernels  95.7 us (38%)
  waiting for transfers between devices  86.5 us (34%)
  starting transfers between devices  56.3 us (22%)
  local copies, waits for them, and re-layouts  5.77 us (2%)
  other arithmetic  4.83 us (2%)
  matrix products  3.59 us (1%)
    pallas_call x2, Pallas kernels, iteration_logs(): pl.pallas_call(_iteration_kernel, in_specs=[pl.BlockSpec(memory_space=plt...  95.7 us
    ppermute x3, waiting for transfers between devices, view_sum_update(): own = own + lax.ppermute(own, 'view', chip_swap)  36.7 us
    all_to_all x3, starting transfers between devices, per_device(): lax.all_to_all(one_view, 'vol', split_axis=2, concat_axis=1, tiled=True)  23.5 us
    all_to_all x3, waiting for transfers between devices, per_device(): lax.all_to_all(one_view, 'vol', split_axis=2, concat_axis=1, tiled=True)  23.2 us
    ppermute x2, waiting for transfers between devices, swap_rims(): before = lax.ppermute(last, axis, up)  12.1 us
    ppermute x2, starting transfers between devices, swap_rims(): after = lax.ppermute(first, axis, down)  8.16 us
    ppermute x3, starting transfers between devices, view_sum_update(): own = own + lax.ppermute(give, 'view', core_swap)  6.06 us
    ppermute x2, waiting for transfers between devices, swap_rims(): after = lax.ppermute(first, axis, down)  5.64 us
  transfers between devices with their start and end apart: 20, of which 17 were waited for; matrix products, arithmetic and copies ran while one was open for 2% of the time, Pallas kernels for 0%

profile of v12, /device:TPU:5, one launch (start us, length us, event | category | flops | bytes accessed | tf_op | source)
XLA Modules:
  0.0 253.0 jit_solution(16634720018279647043)
XLA Ops:
  0.0 0.8 reduce_sum.18
  0.8 0.7 broadcast_divide_fusion
  1.5 0.8 fusion.196
  2.3 1.9 fusion.1
  4.3 1.2 copy.8
  5.4 10.5 %all-to-all-start = ((bf16[1,8,256,128]{3,1,0,2:T(8,128)(2,1)}), bf16[1,8,256,128]{3,1,0,2:T(8,128)(2,1)S(1)}, u32[]{:S(2)}, u32[]{:S(2)}) async-start(bf16[1,8,256,128]{3,1,0,2:T(8,128)(2,1)} %copy.8), calls=%async_computation | async-start | bytes 1048576 | tf_op jit(solution)/shard_map/all_to_all | solution.py:301
  16.0 0.8 fusion.3
  16.8 1.1 copy.12
  17.9 7.7 %all-to-all-done = bf16[1,8,256,128]{3,1,0,2:T(8,128)(2,1)S(1)} async-done(((bf16[1,8,256,128]{3,1,0,2:T(8,128)(2,1)}), bf16[1,8,256,128]{3,1,0,2:T(8,128)(2,1)S(1)}, u32[]{:S(2)}, u32[]{:S(2)}) %all-to-all-start) | async-done | bytes 524320 | tf_op jit(solution)/shard_map/all_to_all | solution.py:301
  25.7 6.5 %all-to-all-start.2 = ((bf16[1,8,256,128]{3,1,0,2:T(8,128)(2,1)}), bf16[1,8,256,128]{3,1,0,2:T(8,128)(2,1)S(1)}, u32[]{:S(2)}, u32[]{:S(2)}) async-start(bf16[1,8,256,128]{3,1,0,2:T(8,128)(2,1)} %copy.12), calls=%async_computation.2 | async-start | bytes 1048576 | tf_op jit(solution)/shard_map/all_to_all | solution.py:301
  32.1 0.8 fusion.2
  33.0 1.2 copy.10
  34.2 6.8 %all-to-all-done.2 = bf16[1,8,256,128]{3,1,0,2:T(8,128)(2,1)S(1)} async-done(((bf16[1,8,256,128]{3,1,0,2:T(8,128)(2,1)}), bf16[1,8,256,128]{3,1,0,2:T(8,128)(2,1)S(1)}, u32[]{:S(2)}, u32[]{:S(2)}) %all-to-all-start.2) | async-done | bytes 524320 | tf_op jit(solution)/shard_map/all_to_all | solution.py:301
  40.9 6.6 %all-to-all-start.1 = ((bf16[1,8,256,128]{3,1,0,2:T(8,128)(2,1)}), bf16[1,8,256,128]{3,1,0,2:T(8,128)(2,1)S(1)}, u32[]{:S(2)}, u32[]{:S(2)}) async-start(bf16[1,8,256,128]{3,1,0,2:T(8,128)(2,1)} %copy.10), calls=%async_computation.1 | async-start | bytes 1048576 | tf_op jit(solution)/shard_map/all_to_all | solution.py:301
  47.5 8.7 %all-to-all-done.1 = bf16[1,8,256,128]{3,1,0,2:T(8,128)(2,1)S(1)} async-done(((bf16[1,8,256,128]{3,1,0,2:T(8,128)(2,1)}), bf16[1,8,256,128]{3,1,0,2:T(8,128)(2,1)S(1)}, u32[]{:S(2)}, u32[]{:S(2)}) %all-to-all-start.1) | async-done | bytes 524320 | tf_op jit(solution)/shard_map/all_to_all | solution.py:301
  56.4 0.8 constant_dynamic-slice_fusion.2
  57.3 3.5 %collective-permute-start = (f32[128,8,128]{2,1,0:T(8,128)}, f32[128,8,128]{2,1,0:T(8,128)S(1)}, u32[]{:S(2)}, u32[]{:S(2)}) collective-permute-start(f32[128,8,128]{2,1,0:T(8,128)} %constant_dynamic-slice_fusion.2), channel_id=1, source_target_pairs={{0,32},{32,0},{64,96},{96,64},{1,33},{33,1},{65,97},{97,65},{2,34}... | collective-permute-start | bytes 1572872 | tf_op jit(solution)/shard_map/ppermute | solution.py:277
  60.8 1.7 collective-permute-done
  62.6 1.0 collective-permute-start.1
  63.6 12.2 %collective-permute-done.1 = f32[128,8,128]{2,1,0:T(8,128)S(1)} collective-permute-done((f32[128,8,128]{2,1,0:T(8,128)S(1)}, f32[128,8,128]{2,1,0:T(8,128)S(1)}, u32[]{:S(2)}, u32[]{:S(2)}) %collective-permute-start.1) | collective-permute-done | bytes 524320 | tf_op jit(solution)/shard_map/ppermute | solution.py:278
  75.9 6.0 %collective-permute-start.5 = (f32[128,4,128]{2,1,0:T(4,128)S(1)}, f32[128,4,128]{2,1,0:T(4,128)S(1)}, u32[]{:S(2)}, u32[]{:S(2)}) collective-permute-start(f32[128,4,128]{2,1,0:T(4,128)S(1)} %get-tuple-element.19), channel_id=1, source_target_pairs={{1,0},{2,1},{3,2},{4,3},{5,4},{6,5},{7,6},{8,7},{9,8},{10,9},{11,1... | collective-permute-start | bytes 786440 | tf_op jit(solution)/shard_map/ppermute | solution.py:26
  82.0 1.9 collective-permute-start.3
  83.9 2.4 collective-permute-done.5
  86.4 2.1 collective-permute-start.6
  89.2 6.7 %collective-permute-done.3 = f32[128,4,128]{2,1,0:T(4,128)S(1)} collective-permute-done((f32[128,4,128]{2,1,0:T(4,128)S(1)}, f32[128,4,128]{2,1,0:T(4,128)S(1)}, u32[]{:S(2)}, u32[]{:S(2)}) %collective-permute-start.3) | collective-permute-done | bytes 262176 | tf_op jit(solution)/shard_map/ppermute | solution.py:25
  95.9 2.4 collective-permute-start.4
  98.5 1.0 collective-permute-done.4
  99.8 47.9 %shard_map.46 = f32[256,8,128]{2,1,0:T(8,128)S(1)} custom-call(f32[81]{0:T(128)S(1)} %reshape.1098.taps_ref, f32[256,4,128]{2,1,0:T(4,128)S(1)} %pad_maximum_fusion.4.before_ref, f32[256,8,128]{2,1,0:T(8,128)S(1)} %pad_maximum_fusion.1.mid_ref, f32[256,4,128]{2,1,0:T(4,128)S(1)} %pad_maximum_fusion.5.after_ref, ...), custom_call_target="tpu_custom_call" | custom-call | tf_op jit(solution)/shard_map/pallas_call | solution.py:242
  147.7 1.3 collective-permute-start.7
  149.0 1.5 collective-permute-done.7
  150.6 1.0 collective-permute-start.8
  151.6 12.2 %collective-permute-done.8 = f32[128,8,128]{2,1,0:T(8,128)S(1)} collective-permute-done((f32[128,8,128]{2,1,0:T(8,128)S(1)}, f32[128,8,128]{2,1,0:T(8,128)S(1)}, u32[]{:S(2)}, u32[]{:S(2)}) %collective-permute-start.8) | collective-permute-done | bytes 524320 | tf_op jit(solution)/shard_map/ppermute | solution.py:278
  164.2 2.1 collective-permute-start.12
  166.4 3.2 %collective-permute-start.10 = (f32[128,4,128]{2,1,0:T(4,128)S(1)}, f32[128,4,128]{2,1,0:T(4,128)S(1)}, u32[]{:S(2)}, u32[]{:S(2)}) collective-permute-start(f32[128,4,128]{2,1,0:T(4,128)S(1)} %get-tuple-element.14), channel_id=1, source_target_pairs={{0,1},{1,2},{2,3},{3,4},{4,5},{5,6},{6,7},{7,8},{8,9},{9,10},{10,1... | collective-permute-start | bytes 786440 | tf_op jit(solution)/shard_map/ppermute | solution.py:25
  169.5 3.2 %collective-permute-done.12 = f32[128,4,128]{2,1,0:T(4,128)S(1)} collective-permute-done((f32[128,4,128]{2,1,0:T(4,128)S(1)}, f32[128,4,128]{2,1,0:T(4,128)S(1)}, u32[]{:S(2)}, u32[]{:S(2)}) %collective-permute-start.12) | collective-permute-done | bytes 262176 | tf_op jit(solution)/shard_map/ppermute | solution.py:26
  172.7 2.1 collective-permute-start.13
  174.9 5.4 %collective-permute-done.10 = f32[128,4,128]{2,1,0:T(4,128)S(1)} collective-permute-done((f32[128,4,128]{2,1,0:T(4,128)S(1)}, f32[128,4,128]{2,1,0:T(4,128)S(1)}, u32[]{:S(2)}, u32[]{:S(2)}) %collective-permute-start.10) | collective-permute-done | bytes 262176 | tf_op jit(solution)/shard_map/ppermute | solution.py:25
  180.3 2.4 collective-permute-start.11
  182.7 1.2 collective-permute-done.11
  184.2 0.4 collective-permute-done.9
  184.8 47.9 %shard_map.47 = f32[256,8,128]{2,1,0:T(8,128)S(1)} custom-call(f32[81]{0:T(128)S(1)} %reshape.1098.taps_ref, f32[256,4,128]{2,1,0:T(4,128)S(1)} %pad_maximum_fusion.6.before_ref, f32[256,8,128]{2,1,0:T(8,128)S(1)} %pad_maximum_fusion.2.mid_ref, f32[256,4,128]{2,1,0:T(4,128)S(1)} %pad_maximum_fusion.7.after_ref, ...), custom_call_target="tpu_custom_call" | custom-call | tf_op jit(solution)/shard_map/pallas_call | solution.py:242
  232.7 1.3 collective-permute-start.14
  234.0 1.5 collective-permute-done.14
  235.6 1.0 collective-permute-start.15
  236.6 12.2 %collective-permute-done.15 = f32[128,8,128]{2,1,0:T(8,128)S(1)} collective-permute-done((f32[128,8,128]{2,1,0:T(8,128)S(1)}, f32[128,8,128]{2,1,0:T(8,128)S(1)}, u32[]{:S(2)}, u32[]{:S(2)}) %collective-permute-start.15) | collective-permute-done | bytes 524320 | tf_op jit(solution)/shard_map/ppermute | solution.py:278
  249.1 1.3 collective-permute-start.16
  250.4 1.5 collective-permute-done.16
  252.0 1.0 pad_maximum_fusion.3
  (40 shorter events, 3.1 us)
Async XLA Ops:
  4.2 11.7 %copy-start = (bf16[3,8,256,128]{3,2,1,0:T(8,128)(2,1)S(1)}, bf16[3,8,256,128]{3,2,1,0:T(8,128)(2,1)}, u32[]{:S(2)}) copy-start(bf16[3,8,256,128]{3,2,1,0:T(8,128)(2,1)} %param.4) | copy-start | bytes 4718596
  5.4 20.3 %all-to-all-start = ((bf16[1,8,256,128]{3,1,0,2:T(8,128)(2,1)}), bf16[1,8,256,128]{3,1,0,2:T(8,128)(2,1)S(1)}, u32[]{:S(2)}, u32[]{:S(2)}) async-start(bf16[1,8,256,128]{3,1,0,2:T(8,128)(2,1)} %copy.8), calls=%async_computation | async-start | bytes 1048576 | tf_op jit(solution)/shard_map/all_to_all | solution.py:301
  25.7 15.3 %all-to-all-start.2 = ((bf16[1,8,256,128]{3,1,0,2:T(8,128)(2,1)}), bf16[1,8,256,128]{3,1,0,2:T(8,128)(2,1)S(1)}, u32[]{:S(2)}, u32[]{:S(2)}) async-start(bf16[1,8,256,128]{3,1,0,2:T(8,128)(2,1)} %copy.12), calls=%async_computation.2 | async-start | bytes 1048576 | tf_op jit(solution)/shard_map/all_to_all | solution.py:301
  40.9 15.2 %all-to-all-start.1 = ((bf16[1,8,256,128]{3,1,0,2:T(8,128)(2,1)}), bf16[1,8,256,128]{3,1,0,2:T(8,128)(2,1)S(1)}, u32[]{:S(2)}, u32[]{:S(2)}) async-start(bf16[1,8,256,128]{3,1,0,2:T(8,128)(2,1)} %copy.10), calls=%async_computation.1 | async-start | bytes 1048576 | tf_op jit(solution)/shard_map/all_to_all | solution.py:301
  57.3 5.2 %collective-permute-start = (f32[128,8,128]{2,1,0:T(8,128)}, f32[128,8,128]{2,1,0:T(8,128)S(1)}, u32[]{:S(2)}, u32[]{:S(2)}) collective-permute-start(f32[128,8,128]{2,1,0:T(8,128)} %constant_dynamic-slice_fusion.2), channel_id=1, source_target_pairs={{0,32},{32,0},{64,96},{96,64},{1,33},{33,1},{65,97},{97,65},{2,34}... | collective-permute-start | bytes 1572872 | tf_op jit(solution)/shard_map/ppermute | solution.py:277
  62.6 25.9 %copy-start.1 = (f32[3,3,9]{2,1,0:T(4,128)S(1)}, f32[3,3,9]{2,1,0:T(4,128)}, u32[]{:S(2)}) copy-start(f32[3,3,9]{2,1,0:T(4,128)} %param.7) | copy-start | bytes 976
  62.6 13.2 %collective-permute-start.1 = (f32[128,8,128]{2,1,0:T(8,128)S(1)}, f32[128,8,128]{2,1,0:T(8,128)S(1)}, u32[]{:S(2)}, u32[]{:S(2)}) collective-permute-start(f32[128,8,128]{2,1,0:T(8,128)S(1)} %dynamic-slice_add_fusion.2), channel_id=1, source_target_pairs={{0,64},{32,96},{64,0},{96,32},{1,65},{33,97},{65,1},{97,33},{2,66}... | collective-permute-start | bytes 1572872 | tf_op jit(solution)/shard_map/ppermute | solution.py:278
  75.9 10.4 %collective-permute-start.5 = (f32[128,4,128]{2,1,0:T(4,128)S(1)}, f32[128,4,128]{2,1,0:T(4,128)S(1)}, u32[]{:S(2)}, u32[]{:S(2)}) collective-permute-start(f32[128,4,128]{2,1,0:T(4,128)S(1)} %get-tuple-element.19), channel_id=1, source_target_pairs={{1,0},{2,1},{3,2},{4,3},{5,4},{6,5},{7,6},{8,7},{9,8},{10,9},{11,1... | collective-permute-start | bytes 786440 | tf_op jit(solution)/shard_map/ppermute | solution.py:26
  82.0 13.9 %collective-permute-start.3 = (f32[128,4,128]{2,1,0:T(4,128)S(1)}, f32[128,4,128]{2,1,0:T(4,128)S(1)}, u32[]{:S(2)}, u32[]{:S(2)}) collective-permute-start(f32[128,4,128]{2,1,0:T(4,128)S(1)} %get-tuple-element.20), channel_id=1, source_target_pairs={{0,1},{1,2},{2,3},{3,4},{4,5},{5,6},{6,7},{7,8},{8,9},{9,10},{10,1... | collective-permute-start | bytes 786440 | tf_op jit(solution)/shard_map/ppermute | solution.py:25
  86.4 12.0 %collective-permute-start.6 = (f32[128,4,128]{2,1,0:T(4,128)S(1)}, f32[128,4,128]{2,1,0:T(4,128)S(1)}, u32[]{:S(2)}, u32[]{:S(2)}) collective-permute-start(f32[128,4,128]{2,1,0:T(4,128)S(1)} %collective-permute-done.5), channel_id=1, source_target_pairs={{0,32},{32,0},{64,96},{96,64},{1,33},{33,1},{65,97},{97,65},{2,34}... | collective-permute-start | bytes 786440 | tf_op jit(solution)/shard_map/ppermute | solution.py:285
  89.2 10.5 %collective-permute-start.2 = (f32[128,8,128]{2,1,0:T(8,128)S(1)}, f32[128,8,128]{2,1,0:T(8,128)S(1)}, u32[]{:S(2)}, u32[]{:S(2)}) collective-permute-start(f32[128,8,128]{2,1,0:T(8,128)S(1)} %add_multiply_fusion), channel_id=1, source_target_pairs={{0,32},{32,0},{64,96},{96,64},{1,33},{33,1},{65,97},{97,65},{2,34}... | collective-permute-start | bytes 1572872 | tf_op jit(solution)/shard_map/ppermute | solution.py:280
  95.9 3.6 %collective-permute-start.4 = (f32[128,4,128]{2,1,0:T(4,128)S(1)}, f32[128,4,128]{2,1,0:T(4,128)S(1)}, u32[]{:S(2)}, u32[]{:S(2)}) collective-permute-start(f32[128,4,128]{2,1,0:T(4,128)S(1)} %collective-permute-done.3), channel_id=1, source_target_pairs={{0,32},{32,0},{64,96},{96,64},{1,33},{33,1},{65,97},{97,65},{2,34}... | collective-permute-start | bytes 786440 | tf_op jit(solution)/shard_map/ppermute | solution.py:284
  147.7 2.8 %collective-permute-start.7 = (f32[128,8,128]{2,1,0:T(8,128)S(1)}, f32[128,8,128]{2,1,0:T(8,128)S(1)}, u32[]{:S(2)}, u32[]{:S(2)}) collective-permute-start(f32[128,8,128]{2,1,0:T(8,128)S(1)} %constant_dynamic-slice_fusion.1), channel_id=1, source_target_pairs={{0,32},{32,0},{64,96},{96,64},{1,33},{33,1},{65,97},{97,65},{2,34}... | collective-permute-start | bytes 1572872 | tf_op jit(solution)/shard_map/ppermute | solution.py:277
  150.6 13.2 %collective-permute-start.8 = (f32[128,8,128]{2,1,0:T(8,128)S(1)}, f32[128,8,128]{2,1,0:T(8,128)S(1)}, u32[]{:S(2)}, u32[]{:S(2)}) collective-permute-start(f32[128,8,128]{2,1,0:T(8,128)S(1)} %dynamic-slice_add_fusion.1), channel_id=1, source_target_pairs={{0,64},{32,96},{64,0},{96,32},{1,65},{33,97},{65,1},{97,33},{2,66}... | collective-permute-start | bytes 1572872 | tf_op jit(solution)/shard_map/ppermute | solution.py:278
  164.2 8.5 %collective-permute-start.12 = (f32[128,4,128]{2,1,0:T(4,128)S(1)}, f32[128,4,128]{2,1,0:T(4,128)S(1)}, u32[]{:S(2)}, u32[]{:S(2)}) collective-permute-start(f32[128,4,128]{2,1,0:T(4,128)S(1)} %get-tuple-element.13), channel_id=1, source_target_pairs={{1,0},{2,1},{3,2},{4,3},{5,4},{6,5},{7,6},{8,7},{9,8},{10,9},{11,1... | collective-permute-start | bytes 786440 | tf_op jit(solution)/shard_map/ppermute | solution.py:26
  166.4 13.9 %collective-permute-start.10 = (f32[128,4,128]{2,1,0:T(4,128)S(1)}, f32[128,4,128]{2,1,0:T(4,128)S(1)}, u32[]{:S(2)}, u32[]{:S(2)}) collective-permute-start(f32[128,4,128]{2,1,0:T(4,128)S(1)} %get-tuple-element.14), channel_id=1, source_target_pairs={{0,1},{1,2},{2,3},{3,4},{4,5},{5,6},{6,7},{7,8},{8,9},{9,10},{10,1... | collective-permute-start | bytes 786440 | tf_op jit(solution)/shard_map/ppermute | solution.py:25
  172.7 10.0 %collective-permute-start.13 = (f32[128,4,128]{2,1,0:T(4,128)S(1)}, f32[128,4,128]{2,1,0:T(4,128)S(1)}, u32[]{:S(2)}, u32[]{:S(2)}) collective-permute-start(f32[128,4,128]{2,1,0:T(4,128)S(1)} %collective-permute-done.12), channel_id=1, source_target_pairs={{0,32},{32,0},{64,96},{96,64},{1,33},{33,1},{65,97},{97,65},{2,34}... | collective-permute-start | bytes 786440 | tf_op jit(solution)/shard_map/ppermute | solution.py:285
  180.3 3.6 %collective-permute-start.11 = (f32[128,4,128]{2,1,0:T(4,128)S(1)}, f32[128,4,128]{2,1,0:T(4,128)S(1)}, u32[]{:S(2)}, u32[]{:S(2)}) collective-permute-start(f32[128,4,128]{2,1,0:T(4,128)S(1)} %collective-permute-done.10), channel_id=1, source_target_pairs={{0,32},{32,0},{64,96},{96,64},{1,33},{33,1},{65,97},{97,65},{2,34}... | collective-permute-start | bytes 786440 | tf_op jit(solution)/shard_map/ppermute | solution.py:284
  182.7 1.9 collective-permute-start.9
  232.7 2.8 %collective-permute-start.14 = (f32[128,8,128]{2,1,0:T(8,128)S(1)}, f32[128,8,128]{2,1,0:T(8,128)S(1)}, u32[]{:S(2)}, u32[]{:S(2)}) collective-permute-start(f32[128,8,128]{2,1,0:T(8,128)S(1)} %constant_dynamic-slice_fusion), channel_id=1, source_target_pairs={{0,32},{32,0},{64,96},{96,64},{1,33},{33,1},{65,97},{97,65},{2,34}... | collective-permute-start | bytes 1572872 | tf_op jit(solution)/shard_map/ppermute | solution.py:277
  235.6 13.2 %collective-permute-start.15 = (f32[128,8,128]{2,1,0:T(8,128)S(1)}, f32[128,8,128]{2,1,0:T(8,128)S(1)}, u32[]{:S(2)}, u32[]{:S(2)}) collective-permute-start(f32[128,8,128]{2,1,0:T(8,128)S(1)} %dynamic-slice_add_fusion), channel_id=1, source_target_pairs={{0,64},{32,96},{64,0},{96,32},{1,65},{33,97},{65,1},{97,33},{2,66}... | collective-permute-start | bytes 1572872 | tf_op jit(solution)/shard_map/ppermute | solution.py:278
  249.1 2.8 %collective-permute-start.16 = (f32[128,8,128]{2,1,0:T(8,128)S(1)}, f32[128,8,128]{2,1,0:T(8,128)S(1)}, u32[]{:S(2)}, u32[]{:S(2)}) collective-permute-start(f32[128,8,128]{2,1,0:T(8,128)S(1)} %fusion.6), channel_id=1, source_target_pairs={{0,32},{32,0},{64,96},{96,64},{1,33},{33,1},{65,97},{97,65},{2,34}... | collective-permute-start | bytes 1572872 | tf_op jit(solution)/shard_map/ppermute | solution.py:280

commit v13 on v11

--- a/solution.py
+++ b/solution.py
@@ -9,6 +9,7 @@
 
 ITERS = 2
 CZ = 32
+SUB = 16
 
 
 def halos(shard, axis, dim, width):
@@ -207,13 +208,14 @@
         wy_rev = _lane_weights(ty, ny, True)
 
         def middle(c, carry):
-            z0 = pl.multiple_of(c * CZ, CZ)
-            acc = tz[0] * a_ref[v, pl.ds(z0, CZ)]
-            for t in range(1, 9):
-                acc = acc + tz[t] * a_ref[v, pl.ds(z0 + t, CZ)]
-            blurred = _lane_correlate(acc, wy)
-            ratio = brick_ref[v, pl.ds(z0, CZ)].astype(jnp.float32) / blurred
-            c_ref[pl.ds(z0 + 4, CZ)] = _lane_correlate(ratio, wy_rev)
+            for sub in range(0, CZ, SUB):
+                z0 = pl.multiple_of(c * CZ + sub, SUB)
+                acc = tz[0] * a_ref[v, pl.ds(z0, SUB)]
+                for t in range(1, 9):
+                    acc = acc + tz[t] * a_ref[v, pl.ds(z0 + t, SUB)]
+                blurred = _lane_correlate(acc, wy)
+                ratio = brick_ref[v, pl.ds(z0, SUB)].astype(jnp.float32) / blurred
+                c_ref[pl.ds(z0 + 4, SUB)] = _lane_correlate(ratio, wy_rev)
             return carry
 
 

time: 242 us -> 243 us (level)
  no operation moved by 1% of the time
where the time goes in v13:
time: 243 us; the launch traced here: 242 us
  Pallas kernels  96.4 us (40%)
  waiting for transfers between devices  85 us (35%)
  starting transfers between devices  40.5 us (17%)
  local copies, waits for them, and re-layouts  9.62 us (4%)
  other arithmetic  7.05 us (3%)
  matrix products  3.32 us (1%)
    pallas_call x2, Pallas kernels, iteration_logs(): pl.pallas_call(_iteration_kernel, in_specs=[pl.BlockSpec(memory_space=plt...  96.4 us
    ppermute x3, waiting for transfers between devices, view_sum_update(): own = own + lax.ppermute(own, 'view', chip_swap)  36.6 us
    all_to_all x1, waiting for transfers between devices, per_device(): lax.all_to_all(local_views, 'vol', split_axis=2, concat_axis=1, tiled=True)  19.8 us
    ppermute x2, waiting for transfers between devices, swap_rims(): before = lax.ppermute(last, axis, up)  14.2 us
    all_to_all x1, starting transfers between devices, per_device(): lax.all_to_all(local_views, 'vol', split_axis=2, concat_axis=1, tiled=True)  10.5 us
    ppermute x2, starting transfers between devices, swap_rims(): after = lax.ppermute(first, axis, down)  7.36 us
    ppermute x2, waiting for transfers between devices, swap_rims(): after = lax.ppermute(first, axis, down)  6.96 us
    ppermute x3, starting transfers between devices, view_sum_update(): own = own + lax.ppermute(give, 'view', core_swap)  5.48 us
  transfers between devices with their start and end apart: 18, of which 13 were waited for; matrix products, arithmetic and copies ran while one was open for 1% of the time, Pallas kernels for 0%

profile of v13, /device:TPU:5, one launch (start us, length us, event | category | flops | bytes accessed | tf_op | source)
XLA Modules:
  0.0 242.2 jit_solution(14483145261800109412)
XLA Ops:
  0.0 0.9 reduce_sum.18
  0.9 0.7 broadcast_divide_fusion
  1.7 3.3 %fusion.1 = bf16[3,8,256,128]{3,2,1,0:T(8,128)(2,1)S(1)} fusion(bf16[3,8,256,128]{3,2,1,0:T(8,128)(2,1)S(1)} %copy-done, f32[3,256]{1,0:T(4,128)S(1)} %get-tuple-element.33, f32[3,256]{1,0:T(4,128)S(1)} %get-tuple-element.34, f32[3,256]{1,0:T(4,128)S(1)} %get-tuple-element.35, f32[3,256]{1,0:T(4,128)S(1)} %get-tuple-element.36, ...), kind=kOutput, calls=%fused_computation.2 | convolution fusion | flops 2421424128 | bytes 3173376 | tf_op jit(solution)/shard_map/vxr,vzry->vzxy/dot_general | solution.py:46
  5.0 2.2 copy.7
  7.2 10.5 %all-to-all-start = ((bf16[3,8,256,128]{3,1,0,2:T(8,128)(2,1)}), bf16[3,8,256,128]{3,1,0,2:T(8,128)(2,1)S(1)}, u32[]{:S(2)}, u32[]{:S(2)}) async-start(bf16[3,8,256,128]{3,1,0,2:T(8,128)(2,1)} %copy.7), calls=%async_computation | async-start | bytes 3145728 | tf_op jit(solution)/shard_map/all_to_all | solution.py:299
  17.8 19.8 %all-to-all-done = bf16[3,8,256,128]{3,1,0,2:T(8,128)(2,1)S(1)} async-done(((bf16[3,8,256,128]{3,1,0,2:T(8,128)(2,1)}), bf16[3,8,256,128]{3,1,0,2:T(8,128)(2,1)S(1)}, u32[]{:S(2)}, u32[]{:S(2)}) %all-to-all-start) | async-done | bytes 1572896 | tf_op jit(solution)/shard_map/all_to_all | solution.py:299
  37.6 1.2 copy-done.1
  38.8 1.9 copy.28
  41.0 1.0 copy-done.4
  41.9 0.8 constant_dynamic-slice_fusion.2
  42.7 3.3 %collective-permute-start = (f32[128,8,128]{2,1,0:T(8,128)}, f32[128,8,128]{2,1,0:T(8,128)}, u32[]{:S(2)}, u32[]{:S(2)}) collective-permute-start(f32[128,8,128]{2,1,0:T(8,128)} %constant_dynamic-slice_fusion.2), channel_id=1, source_target_pairs={{0,32},{32,0},{64,96},{96,64},{1,33},{33,1},{65,97},{97,65},{2,34}... | collective-permute-start | bytes 1572872 | tf_op jit(solution)/shard_map/ppermute | solution.py:279
  46.1 1.9 collective-permute-done
  48.0 1.3 dynamic-slice_add_fusion.2
  49.2 1.0 collective-permute-start.1
  50.2 12.2 %collective-permute-done.1 = f32[128,8,128]{2,1,0:T(8,128)S(1)} collective-permute-done((f32[128,8,128]{2,1,0:T(8,128)S(1)}, f32[128,8,128]{2,1,0:T(8,128)S(1)}, u32[]{:S(2)}, u32[]{:S(2)}) %collective-permute-start.1) | collective-permute-done | bytes 524320 | tf_op jit(solution)/shard_map/ppermute | solution.py:280
  62.5 0.8 copy-done.2
  63.3 0.8 fusion.68
  64.1 5.2 %collective-permute-start.5 = (f32[128,4,128]{2,1,0:T(4,128)S(1)}, f32[128,4,128]{2,1,0:T(4,128)}, u32[]{:S(2)}, u32[]{:S(2)}) collective-permute-start(f32[128,4,128]{2,1,0:T(4,128)S(1)} %get-tuple-element.21), channel_id=1, source_target_pairs={{1,0},{2,1},{3,2},{4,3},{5,4},{6,5},{7,6},{8,7},{9,8},{10,9},{11,1... | collective-permute-start | bytes 786440 | tf_op jit(solution)/shard_map/ppermute | solution.py:27
  69.3 1.9 collective-permute-start.3
  71.2 2.4 %collective-permute-done.5 = f32[128,4,128]{2,1,0:T(4,128)} collective-permute-done((f32[128,4,128]{2,1,0:T(4,128)S(1)}, f32[128,4,128]{2,1,0:T(4,128)}, u32[]{:S(2)}, u32[]{:S(2)}) %collective-permute-start.5) | collective-permute-done | bytes 262176 | tf_op jit(solution)/shard_map/ppermute | solution.py:27
  73.7 2.1 collective-permute-start.6
  76.0 7.4 %collective-permute-done.3 = f32[128,4,128]{2,1,0:T(4,128)S(1)} collective-permute-done((f32[128,4,128]{2,1,0:T(4,128)}, f32[128,4,128]{2,1,0:T(4,128)S(1)}, u32[]{:S(2)}, u32[]{:S(2)}) %collective-permute-start.3) | collective-permute-done | bytes 262176 | tf_op jit(solution)/shard_map/ppermute | solution.py:26
  83.5 2.4 collective-permute-start.4
  85.9 1.1 broadcast_select_fusion.11
  87.3 0.7 copy-done.3
  88.1 48.4 %shard_map.46 = f32[256,8,128]{2,1,0:T(8,128)S(1)} custom-call(f32[81]{0:T(128)S(1)} %reshape.17.taps_ref, f32[256,4,128]{2,1,0:T(4,128)S(1)} %pad_maximum_fusion.3.before_ref, f32[256,8,128]{2,1,0:T(8,128)S(1)} %pad_maximum_fusion.mid_ref, f32[256,4,128]{2,1,0:T(4,128)S(1)} %pad_maximum_fusion.4.after_ref, bf16[3,256,8,128]{3,2,1,0:T(8,128)(2,1)S(1)} %bitcast.48), custom_call_target="tpu_custom_call" | custom-call | tf_op jit(solution)/shard_map/pallas_call | solution.py:244
  136.6 0.9 collective-permute-start.7
  137.5 1.5 collective-permute-done.7
  139.1 1.0 collective-permute-start.8
  140.1 12.2 %collective-permute-done.8 = f32[128,8,128]{2,1,0:T(8,128)S(1)} collective-permute-done((f32[128,8,128]{2,1,0:T(8,128)S(1)}, f32[128,8,128]{2,1,0:T(8,128)S(1)}, u32[]{:S(2)}, u32[]{:S(2)}) %collective-permute-start.8) | collective-permute-done | bytes 524320 | tf_op jit(solution)/shard_map/ppermute | solution.py:280
  152.3 0.3 fusion.38
  152.6 1.3 collective-permute-start.9
  154.0 2.1 collective-permute-start.12
  156.1 3.2 %collective-permute-start.10 = (f32[128,4,128]{2,1,0:T(4,128)S(1)}, f32[128,4,128]{2,1,0:T(4,128)S(1)}, u32[]{:S(2)}, u32[]{:S(2)}) collective-permute-start(f32[128,4,128]{2,1,0:T(4,128)S(1)} %get-tuple-element.16), channel_id=1, source_target_pairs={{0,1},{1,2},{2,3},{3,4},{4,5},{5,6},{6,7},{7,8},{8,9},{9,10},{10,1... | collective-permute-start | bytes 786440 | tf_op jit(solution)/shard_map/ppermute | solution.py:26
  159.3 4.5 %collective-permute-done.12 = f32[128,4,128]{2,1,0:T(4,128)S(1)} collective-permute-done((f32[128,4,128]{2,1,0:T(4,128)S(1)}, f32[128,4,128]{2,1,0:T(4,128)S(1)}, u32[]{:S(2)}, u32[]{:S(2)}) %collective-permute-start.12) | collective-permute-done | bytes 262176 | tf_op jit(solution)/shard_map/ppermute | solution.py:27
  163.8 0.8 collective-permute-start.13
  164.6 6.7 %collective-permute-done.10 = f32[128,4,128]{2,1,0:T(4,128)S(1)} collective-permute-done((f32[128,4,128]{2,1,0:T(4,128)S(1)}, f32[128,4,128]{2,1,0:T(4,128)S(1)}, u32[]{:S(2)}, u32[]{:S(2)}) %collective-permute-start.10) | collective-permute-done | bytes 262176 | tf_op jit(solution)/shard_map/ppermute | solution.py:26
  171.3 1.1 collective-permute-start.11
  172.8 0.8 collective-permute-done.11
  173.8 48.0 %shard_map.47 = f32[256,8,128]{2,1,0:T(8,128)S(1)} custom-call(f32[81]{0:T(128)S(1)} %reshape.17.taps_ref, f32[256,4,128]{2,1,0:T(4,128)S(1)} %pad_maximum_fusion.5.before_ref, f32[256,8,128]{2,1,0:T(8,128)S(1)} %pad_maximum_fusion.1.mid_ref, f32[256,4,128]{2,1,0:T(4,128)S(1)} %pad_maximum_fusion.6.after_ref, bf16[3,256,8,128]{3,2,1,0:T(8,128)(2,1)S(1)} %bitcast.49), custom_call_target="tpu_custom_call" | custom-call | tf_op jit(solution)/shard_map/pallas_call | solution.py:244
  221.8 1.3 collective-permute-start.14
  223.1 1.5 collective-permute-done.14
  224.7 1.0 collective-permute-start.15
  225.7 12.2 %collective-permute-done.15 = f32[128,8,128]{2,1,0:T(8,128)S(1)} collective-permute-done((f32[128,8,128]{2,1,0:T(8,128)S(1)}, f32[128,8,128]{2,1,0:T(8,128)S(1)}, u32[]{:S(2)}, u32[]{:S(2)}) %collective-permute-start.15) | collective-permute-done | bytes 524320 | tf_op jit(solution)/shard_map/ppermute | solution.py:280
  237.9 0.3 fusion.36
  238.3 1.3 collective-permute-start.16
  239.5 1.5 collective-permute-done.16
  241.1 1.0 pad_maximum_fusion.2
  (40 shorter events, 1.8 us)
Async XLA Ops:
  0.0 1.7 copy-start
  7.2 30.4 %all-to-all-start = ((bf16[3,8,256,128]{3,1,0,2:T(8,128)(2,1)}), bf16[3,8,256,128]{3,1,0,2:T(8,128)(2,1)S(1)}, u32[]{:S(2)}, u32[]{:S(2)}) async-start(bf16[3,8,256,128]{3,1,0,2:T(8,128)(2,1)} %copy.7), calls=%async_computation | async-start | bytes 3145728 | tf_op jit(solution)/shard_map/all_to_all | solution.py:299
  37.6 1.2 copy-start.1
  40.9 1.0 copy-start.4
  42.7 5.2 %collective-permute-start = (f32[128,8,128]{2,1,0:T(8,128)}, f32[128,8,128]{2,1,0:T(8,128)}, u32[]{:S(2)}, u32[]{:S(2)}) collective-permute-start(f32[128,8,128]{2,1,0:T(8,128)} %constant_dynamic-slice_fusion.2), channel_id=1, source_target_pairs={{0,32},{32,0},{64,96},{96,64},{1,33},{33,1},{65,97},{97,65},{2,34}... | collective-permute-start | bytes 1572872 | tf_op jit(solution)/shard_map/ppermute | solution.py:279
  49.2 26.6 %copy-start.5 = (f32[3,3,9]{2,1,0:T(4,128)S(1)}, f32[3,3,9]{2,1,0:T(4,128)}, u32[]{:S(2)}) copy-start(f32[3,3,9]{2,1,0:T(4,128)} %param.7) | copy-start | bytes 976
  49.2 13.2 %collective-permute-start.1 = (f32[128,8,128]{2,1,0:T(8,128)S(1)}, f32[128,8,128]{2,1,0:T(8,128)S(1)}, u32[]{:S(2)}, u32[]{:S(2)}) collective-permute-start(f32[128,8,128]{2,1,0:T(8,128)S(1)} %dynamic-slice_add_fusion.2), channel_id=1, source_target_pairs={{0,64},{32,96},{64,0},{96,32},{1,65},{33,97},{65,1},{97,33},{2,66}... | collective-permute-start | bytes 1572872 | tf_op jit(solution)/shard_map/ppermute | solution.py:280
  62.5 0.8 copy-start.2
  64.1 9.6 %collective-permute-start.5 = (f32[128,4,128]{2,1,0:T(4,128)S(1)}, f32[128,4,128]{2,1,0:T(4,128)}, u32[]{:S(2)}, u32[]{:S(2)}) collective-permute-start(f32[128,4,128]{2,1,0:T(4,128)S(1)} %get-tuple-element.21), channel_id=1, source_target_pairs={{1,0},{2,1},{3,2},{4,3},{5,4},{6,5},{7,6},{8,7},{9,8},{10,9},{11,1... | collective-permute-start | bytes 786440 | tf_op jit(solution)/shard_map/ppermute | solution.py:27
  69.3 14.1 %collective-permute-start.3 = (f32[128,4,128]{2,1,0:T(4,128)}, f32[128,4,128]{2,1,0:T(4,128)S(1)}, u32[]{:S(2)}, u32[]{:S(2)}) collective-permute-start(f32[128,4,128]{2,1,0:T(4,128)} %get-tuple-element.22), channel_id=1, source_target_pairs={{0,1},{1,2},{2,3},{3,4},{4,5},{5,6},{6,7},{7,8},{8,9},{9,10},{10,1... | collective-permute-start | bytes 786440 | tf_op jit(solution)/shard_map/ppermute | solution.py:26
  73.7 12.2 %collective-permute-start.6 = (f32[128,4,128]{2,1,0:T(4,128)}, f32[128,4,128]{2,1,0:T(4,128)}, u32[]{:S(2)}, u32[]{:S(2)}) collective-permute-start(f32[128,4,128]{2,1,0:T(4,128)} %collective-permute-done.5), channel_id=1, source_target_pairs={{0,32},{32,0},{64,96},{96,64},{1,33},{33,1},{65,97},{97,65},{2,34}... | collective-permute-start | bytes 786440 | tf_op jit(solution)/shard_map/ppermute | solution.py:287
  76.0 11.3 %collective-permute-start.2 = (f32[128,8,128]{2,1,0:T(8,128)}, f32[128,8,128]{2,1,0:T(8,128)S(1)}, u32[]{:S(2)}, u32[]{:S(2)}) collective-permute-start(f32[128,8,128]{2,1,0:T(8,128)} %copy-done.2), channel_id=1, source_target_pairs={{0,32},{32,0},{64,96},{96,64},{1,33},{33,1},{65,97},{97,65},{2,34}... | collective-permute-start | bytes 1572872 | tf_op jit(solution)/shard_map/ppermute | solution.py:282
  83.5 3.6 %collective-permute-start.4 = (f32[128,4,128]{2,1,0:T(4,128)S(1)}, f32[128,4,128]{2,1,0:T(4,128)S(1)}, u32[]{:S(2)}, u32[]{:S(2)}) collective-permute-start(f32[128,4,128]{2,1,0:T(4,128)S(1)} %collective-permute-done.3), channel_id=1, source_target_pairs={{0,32},{32,0},{64,96},{96,64},{1,33},{33,1},{65,97},{97,65},{2,34}... | collective-permute-start | bytes 786440 | tf_op jit(solution)/shard_map/ppermute | solution.py:286
  86.9 1.0 copy-start.3
  136.6 2.4 collective-permute-start.7
  139.1 13.2 %collective-permute-start.8 = (f32[128,8,128]{2,1,0:T(8,128)S(1)}, f32[128,8,128]{2,1,0:T(8,128)S(1)}, u32[]{:S(2)}, u32[]{:S(2)}) collective-permute-start(f32[128,8,128]{2,1,0:T(8,128)S(1)} %dynamic-slice_add_fusion.1), channel_id=1, source_target_pairs={{0,64},{32,96},{64,0},{96,32},{1,65},{33,97},{65,1},{97,33},{2,66}... | collective-permute-start | bytes 1572872 | tf_op jit(solution)/shard_map/ppermute | solution.py:280
  152.6 19.8 %collective-permute-start.9 = (f32[128,8,128]{2,1,0:T(8,128)S(1)}, f32[128,8,128]{2,1,0:T(8,128)S(1)}, u32[]{:S(2)}, u32[]{:S(2)}) collective-permute-start(f32[128,8,128]{2,1,0:T(8,128)S(1)} %fusion.38), channel_id=1, source_target_pairs={{0,32},{32,0},{64,96},{96,64},{1,33},{33,1},{65,97},{97,65},{2,34}... | collective-permute-start | bytes 1572872 | tf_op jit(solution)/shard_map/ppermute | solution.py:282
  154.0 9.8 %collective-permute-start.12 = (f32[128,4,128]{2,1,0:T(4,128)S(1)}, f32[128,4,128]{2,1,0:T(4,128)S(1)}, u32[]{:S(2)}, u32[]{:S(2)}) collective-permute-start(f32[128,4,128]{2,1,0:T(4,128)S(1)} %get-tuple-element.15), channel_id=1, source_target_pairs={{1,0},{2,1},{3,2},{4,3},{5,4},{6,5},{7,6},{8,7},{9,8},{10,9},{11,1... | collective-permute-start | bytes 786440 | tf_op jit(solution)/shard_map/ppermute | solution.py:27
  156.1 15.2 %collective-permute-start.10 = (f32[128,4,128]{2,1,0:T(4,128)S(1)}, f32[128,4,128]{2,1,0:T(4,128)S(1)}, u32[]{:S(2)}, u32[]{:S(2)}) collective-permute-start(f32[128,4,128]{2,1,0:T(4,128)S(1)} %get-tuple-element.16), channel_id=1, source_target_pairs={{0,1},{1,2},{2,3},{3,4},{4,5},{5,6},{6,7},{7,8},{8,9},{9,10},{10,1... | collective-permute-start | bytes 786440 | tf_op jit(solution)/shard_map/ppermute | solution.py:26
  163.8 8.8 %collective-permute-start.13 = (f32[128,4,128]{2,1,0:T(4,128)S(1)}, f32[128,4,128]{2,1,0:T(4,128)S(1)}, u32[]{:S(2)}, u32[]{:S(2)}) collective-permute-start(f32[128,4,128]{2,1,0:T(4,128)S(1)} %collective-permute-done.12), channel_id=1, source_target_pairs={{0,32},{32,0},{64,96},{96,64},{1,33},{33,1},{65,97},{97,65},{2,34}... | collective-permute-start | bytes 786440 | tf_op jit(solution)/shard_map/ppermute | solution.py:287
  171.3 2.3 collective-permute-start.11
  221.8 2.8 %collective-permute-start.14 = (f32[128,8,128]{2,1,0:T(8,128)S(1)}, f32[128,8,128]{2,1,0:T(8,128)S(1)}, u32[]{:S(2)}, u32[]{:S(2)}) collective-permute-start(f32[128,8,128]{2,1,0:T(8,128)S(1)} %constant_dynamic-slice_fusion), channel_id=1, source_target_pairs={{0,32},{32,0},{64,96},{96,64},{1,33},{33,1},{65,97},{97,65},{2,34}... | collective-permute-start | bytes 1572872 | tf_op jit(solution)/shard_map/ppermute | solution.py:279
  224.7 13.2 %collective-permute-start.15 = (f32[128,8,128]{2,1,0:T(8,128)S(1)}, f32[128,8,128]{2,1,0:T(8,128)S(1)}, u32[]{:S(2)}, u32[]{:S(2)}) collective-permute-start(f32[128,8,128]{2,1,0:T(8,128)S(1)} %dynamic-slice_add_fusion), channel_id=1, source_target_pairs={{0,64},{32,96},{64,0},{96,32},{1,65},{33,97},{65,1},{97,33},{2,66}... | collective-permute-start | bytes 1572872 | tf_op jit(solution)/shard_map/ppermute | solution.py:280
  238.3 2.8 %collective-permute-start.16 = (f32[128,8,128]{2,1,0:T(8,128)S(1)}, f32[128,8,128]{2,1,0:T(8,128)S(1)}, u32[]{:S(2)}, u32[]{:S(2)}) collective-permute-start(f32[128,8,128]{2,1,0:T(8,128)S(1)} %fusion.36), channel_id=1, source_target_pairs={{0,32},{32,0},{64,96},{96,64},{1,33},{33,1},{65,97},{97,65},{2,34}... | collective-permute-start | bytes 1572872 | tf_op jit(solution)/shard_map/ppermute | solution.py:282

commit v14 on v11

--- a/solution.py
+++ b/solution.py
@@ -275,12 +275,25 @@
     own = lax.dynamic_slice_in_dim(part, core * half, half, axis=0)
     give = lax.dynamic_slice_in_dim(part, (1 - core) * half, half, axis=0)
     own = own + lax.ppermute(give, "view", core_swap)
-    own = own + lax.ppermute(own, "view", chip_swap)
-    fresh = update(own, core * half, half)
+    if rim_width is None:
+        own = own + lax.ppermute(own, "view", chip_swap)
+        fresh = update(own, core * half, half)
+        return _by_core(core, fresh, lax.ppermute(fresh, "view", core_swap))
+    splits = 2
+    quarter = half // splits
+    fresh_parts, before_parts, after_parts = [], [], []
+    for index in range(splits):
+        piece = own[index * quarter : (index + 1) * quarter]
+        piece = piece + lax.ppermute(piece, "view", chip_swap)
+        fresh_piece = update(piece, core * half + index * quarter, quarter)
+        low, high = halos(fresh_piece, "vol", 1, rim_width)
+        fresh_parts.append(fresh_piece)
+        before_parts.append(low)
+        after_parts.append(high)
+    fresh = jnp.concatenate(fresh_parts, axis=0)
     whole = _by_core(core, fresh, lax.ppermute(fresh, "view", core_swap))
-    if rim_width is None:
-        return whole
-    before, after = halos(fresh, "vol", 1, rim_width)
+    before = jnp.concatenate(before_parts, axis=0)
+    after = jnp.concatenate(after_parts, axis=0)
     before = _by_core(core, before, lax.ppermute(before, "view", core_swap))
     after = _by_core(core, after, lax.ppermute(after, "view", core_swap))
     return whole, before, after

time: 242 us -> 250 us (1.033)
  starting transfers between devices: 40.5 us -> 64.5 us
  waiting for transfers between devices: 85 us -> 65 us
  local copies, waits for them, and re-layouts: 9.62 us -> 12.4 us
    ppermute x0 -> x5, waiting for transfers between devices: none -> 25.2 us  [the longest x4 23.7 us: view_sum_update(): piece = piece + lax.ppermute(piece, 'view', chip_swap)]
    ppermute x3 -> x1, waiting for transfers between devices: 36.6 us -> 12.2 us  [view_sum_update(): own = own + lax.ppermute(own, 'view', chip_swap)]
    ppermute x2 -> x4, starting transfers between devices: 7.36 us -> 22.4 us  [swap_rims(): after = lax.ppermute(first, axis, down)]
    ppermute x2 -> x4, waiting for transfers between devices: 14.2 us -> 0.01 us  [swap_rims(): before = lax.ppermute(last, axis, up)]
    ppermute x2 -> x4, waiting for transfers between devices: 6.96 us -> 0.75 us  [swap_rims(): after = lax.ppermute(first, axis, down)]
    ppermute x2 -> x4, starting transfers between devices: 5.08 us -> 10.1 us  [swap_rims(): before = lax.ppermute(last, axis, up)]
    ppermute x0 -> x5, starting transfers between devices: none -> 4.29 us  [the longest x4 3.01 us: view_sum_update(): piece = piece + lax.ppermute(piece, 'view', chip_swap)]
  transfers between devices with their start and end apart: 18 -> 24, of which waited for: 13 -> 13; matrix products, arithmetic and copies ran while one was open for 1% -> 1% of each run, Pallas kernels for 0% -> 0%
where the time goes in v14:
time: 250 us
  Pallas kernels  95.6 us (38%)
  waiting for transfers between devices  65 us (26%)
  starting transfers between devices  64.5 us (26%)
  local copies, waits for them, and re-layouts  12.4 us (5%)
  other arithmetic  8.2 us (3%)
  matrix products  3.32 us (1%)
    pallas_call x2, Pallas kernels, iteration_logs(): pl.pallas_call(_iteration_kernel, in_specs=[pl.BlockSpec(memory_space=plt...  95.6 us
    ppermute x4, waiting for transfers between devices, view_sum_update(): piece = piece + lax.ppermute(piece, 'view', chip_swap)  23.7 us
    ppermute x4, starting transfers between devices, swap_rims(): after = lax.ppermute(first, axis, down)  22.4 us
    all_to_all x1, waiting for transfers between devices, per_device(): lax.all_to_all(local_views, 'vol', split_axis=2, concat_axis=1, tiled=True)  19.8 us
    ppermute x1, waiting for transfers between devices, view_sum_update(): own = own + lax.ppermute(own, 'view', chip_swap)  12.2 us
    all_to_all x1, starting transfers between devices, per_device(): lax.all_to_all(local_views, 'vol', split_axis=2, concat_axis=1, tiled=True)  10.5 us
    ppermute x4, starting transfers between devices, swap_rims(): before = lax.ppermute(last, axis, up)  10.1 us
    ppermute x3, starting transfers between devices, view_sum_update(): own = own + lax.ppermute(give, 'view', core_swap)  5.9 us
  transfers between devices with their start and end apart: 24, of which 13 were waited for; matrix products, arithmetic and copies ran while one was open for 1% of the time, Pallas kernels for 0%

profile of v14, /device:TPU:5, one launch (start us, length us, event | category | flops | bytes accessed | tf_op | source)
XLA Modules:
  0.0 249.6 jit_solution(8618109544460921010)
XLA Ops:
  0.0 0.9 reduce_sum.18
  1.7 3.3 %fusion.1 = bf16[3,8,256,128]{3,2,1,0:T(8,128)(2,1)S(1)} fusion(bf16[3,8,256,128]{3,2,1,0:T(8,128)(2,1)S(1)} %copy-done, f32[3,256]{1,0:T(4,128)S(1)} %get-tuple-element.45, f32[3,256]{1,0:T(4,128)S(1)} %get-tuple-element.46, f32[3,256]{1,0:T(4,128)S(1)} %get-tuple-element.47, f32[3,256]{1,0:T(4,128)S(1)} %get-tuple-element.48, ...), kind=kOutput, calls=%fused_computation.2 | convolution fusion | flops 2421424128 | bytes 3173376 | tf_op jit(solution)/shard_map/vxr,vzry->vzxy/dot_general | solution.py:45
  5.0 2.2 copy.7
  7.2 10.5 %all-to-all-start = ((bf16[3,8,256,128]{3,1,0,2:T(8,128)(2,1)}), bf16[3,8,256,128]{3,1,0,2:T(8,128)(2,1)S(1)}, u32[]{:S(2)}, u32[]{:S(2)}) async-start(bf16[3,8,256,128]{3,1,0,2:T(8,128)(2,1)} %copy.7), calls=%async_computation | async-start | bytes 3145728 | tf_op jit(solution)/shard_map/all_to_all | solution.py:310
  17.8 19.8 %all-to-all-done = bf16[3,8,256,128]{3,1,0,2:T(8,128)(2,1)S(1)} async-done(((bf16[3,8,256,128]{3,1,0,2:T(8,128)(2,1)}), bf16[3,8,256,128]{3,1,0,2:T(8,128)(2,1)S(1)}, u32[]{:S(2)}, u32[]{:S(2)}) %all-to-all-start) | async-done | bytes 1572896 | tf_op jit(solution)/shard_map/all_to_all | solution.py:310
  37.6 1.2 copy-done.1
  38.8 1.9 copy.28
  40.9 1.0 copy-done.5
  41.9 0.8 constant_dynamic-slice_fusion.2
  42.7 3.3 %collective-permute-start = (f32[128,8,128]{2,1,0:T(8,128)}, f32[128,8,128]{2,1,0:T(8,128)}, u32[]{:S(2)}, u32[]{:S(2)}) collective-permute-start(f32[128,8,128]{2,1,0:T(8,128)} %constant_dynamic-slice_fusion.2), channel_id=1, source_target_pairs={{0,32},{32,0},{64,96},{96,64},{1,33},{33,1},{65,97},{97,65},{2,34}... | collective-permute-start | bytes 1572872 | tf_op jit(solution)/shard_map/ppermute | solution.py:277
  46.1 1.9 collective-permute-done
  48.0 1.3 dynamic-slice_add_fusion.2
  49.3 1.0 collective-permute-start.1
  50.8 6.1 %collective-permute-done.1 = f32[64,8,128]{2,1,0:T(8,128)S(1)} collective-permute-done((f32[64,8,128]{2,1,0:T(8,128)S(1)}, f32[64,8,128]{2,1,0:T(8,128)S(1)}, u32[]{:S(2)}, u32[]{:S(2)}) %collective-permute-start.1) | collective-permute-done | bytes 262176 | tf_op jit(solution)/shard_map/ppermute | solution.py:287
  56.9 5.6 %collective-permute-done.2 = f32[64,8,128]{2,1,0:T(8,128)S(1)} collective-permute-done((f32[64,8,128]{2,1,0:T(8,128)S(1)}, f32[64,8,128]{2,1,0:T(8,128)S(1)}, u32[]{:S(2)}, u32[]{:S(2)}) %collective-permute-start.2) | collective-permute-done | bytes 262176 | tf_op jit(solution)/shard_map/ppermute | solution.py:287
  63.3 2.3 collective-permute-start.4
  66.4 2.9 %collective-permute-start.5 = (f32[64,4,128]{2,1,0:T(4,128)}, f32[64,4,128]{2,1,0:T(4,128)}, u32[]{:S(2)}, u32[]{:S(2)}) collective-permute-start(f32[64,4,128]{2,1,0:T(4,128)} %get-tuple-element.34), channel_id=1, source_target_pairs={{0,1},{1,2},{2,3},{3,4},{4,5},{5,6},{6,7},{7,8},{8,9},{9,10},{10,1... | collective-permute-start | bytes 393224 | tf_op jit(solution)/shard_map/ppermute | solution.py:25
  69.5 8.1 %collective-permute-start.7 = (f32[64,4,128]{2,1,0:T(4,128)}, f32[64,4,128]{2,1,0:T(4,128)S(1)}, u32[]{:S(2)}, u32[]{:S(2)}) collective-permute-start(f32[64,4,128]{2,1,0:T(4,128)} %get-tuple-element.35), channel_id=1, source_target_pairs={{1,0},{2,1},{3,2},{4,3},{5,4},{6,5},{7,6},{8,7},{9,8},{10,9},{11,1... | collective-permute-start | bytes 393224 | tf_op jit(solution)/shard_map/ppermute | solution.py:26
  77.6 2.9 %collective-permute-start.8 = (f32[64,4,128]{2,1,0:T(4,128)}, f32[64,4,128]{2,1,0:T(4,128)S(1)}, u32[]{:S(2)}, u32[]{:S(2)}) collective-permute-start(f32[64,4,128]{2,1,0:T(4,128)} %get-tuple-element.33), channel_id=1, source_target_pairs={{1,0},{2,1},{3,2},{4,3},{5,4},{6,5},{7,6},{8,7},{9,8},{10,9},{11,1... | collective-permute-start | bytes 393224 | tf_op jit(solution)/shard_map/ppermute | solution.py:26
  80.6 0.9 constant_dynamic-update-slice_fusion
  81.5 2.4 collective-permute-start.6
  83.9 1.0 pad_maximum_fusion.3
  85.1 1.7 collective-permute-start.9
  87.0 1.0 collective-permute-done.9
  89.2 47.8 %shard_map.46 = f32[256,8,128]{2,1,0:T(8,128)S(1)} custom-call(f32[81]{0:T(128)S(1)} %reshape.17.taps_ref, f32[256,4,128]{2,1,0:T(4,128)S(1)} %pad_maximum_fusion.4.before_ref, f32[256,8,128]{2,1,0:T(8,128)S(1)} %pad_maximum_fusion.mid_ref, f32[256,4,128]{2,1,0:T(4,128)S(1)} %pad_maximum_fusion.5.after_ref, bf16[3,256,8,128]{3,2,1,0:T(8,128)(2,1)S(1)} %bitcast.48), custom_call_target="tpu_custom_call" | custom-call | tf_op jit(solution)/shard_map/pallas_call | solution.py:242
  137.1 1.3 collective-permute-start.10
  138.3 1.5 collective-permute-done.10
  140.0 0.8 copy-done.4
  140.8 0.8 fusion.69
  141.6 0.9 collective-permute-start.11
  143.1 6.3 %collective-permute-done.11 = f32[64,8,128]{2,1,0:T(8,128)S(1)} collective-permute-done((f32[64,8,128]{2,1,0:T(8,128)}, f32[64,8,128]{2,1,0:T(8,128)S(1)}, u32[]{:S(2)}, u32[]{:S(2)}) %collective-permute-start.11) | collective-permute-done | bytes 262176 | tf_op jit(solution)/shard_map/ppermute | solution.py:287
  149.3 5.7 %collective-permute-done.12 = f32[64,8,128]{2,1,0:T(8,128)} collective-permute-done((f32[64,8,128]{2,1,0:T(8,128)}, f32[64,8,128]{2,1,0:T(8,128)}, u32[]{:S(2)}, u32[]{:S(2)}) %collective-permute-start.12) | collective-permute-done | bytes 262176 | tf_op jit(solution)/shard_map/ppermute | solution.py:287
  155.1 1.5 fusion.56
  156.6 3.0 %collective-permute-start.14 = (f32[64,4,128]{2,1,0:T(4,128)S(1)}, f32[64,4,128]{2,1,0:T(4,128)S(1)}, u32[]{:S(2)}, u32[]{:S(2)}) collective-permute-start(f32[64,4,128]{2,1,0:T(4,128)S(1)} %get-tuple-element.32), channel_id=1, source_target_pairs={{0,1},{1,2},{2,3},{3,4},{4,5},{5,6},{6,7},{7,8},{8,9},{9,10},{10,1... | collective-permute-start | bytes 393224 | tf_op jit(solution)/shard_map/ppermute | solution.py:25
  159.6 1.9 collective-permute-start.15
  161.5 9.1 %collective-permute-start.17 = (f32[64,4,128]{2,1,0:T(4,128)S(1)}, f32[64,4,128]{2,1,0:T(4,128)S(1)}, u32[]{:S(2)}, u32[]{:S(2)}) collective-permute-start(f32[64,4,128]{2,1,0:T(4,128)S(1)} %get-tuple-element.31), channel_id=1, source_target_pairs={{1,0},{2,1},{3,2},{4,3},{5,4},{6,5},{7,6},{8,7},{9,8},{10,9},{11,1... | collective-permute-start | bytes 393224 | tf_op jit(solution)/shard_map/ppermute | solution.py:26
  170.6 2.3 collective-permute-start.18
  173.0 2.4 collective-permute-start.16
  176.3 3.5 %collective-permute-start.19 = (f32[128,4,128]{2,1,0:T(4,128)S(1)}, f32[128,4,128]{2,1,0:T(4,128)S(1)}, u32[]{:S(2)}, u32[]{:S(2)}) collective-permute-start(f32[128,4,128]{2,1,0:T(4,128)S(1)} %constant_dynamic-update-slice_fusion.6), channel_id=1, source_target_pairs={{0,32},{32,0},{64,96},{96,64},{1,33},{33,1},{65,97},{97,65},{2,34}... | collective-permute-start | bytes 786440 | tf_op jit(solution)/shard_map/ppermute | solution.py:298
  180.0 1.0 collective-permute-done.19
  181.3 47.9 %shard_map.47 = f32[256,8,128]{2,1,0:T(8,128)S(1)} custom-call(f32[81]{0:T(128)S(1)} %reshape.17.taps_ref, f32[256,4,128]{2,1,0:T(4,128)S(1)} %pad_maximum_fusion.7.before_ref, f32[256,8,128]{2,1,0:T(8,128)S(1)} %pad_maximum_fusion.1.mid_ref, f32[256,4,128]{2,1,0:T(4,128)S(1)} %pad_maximum_fusion.8.after_ref, bf16[3,256,8,128]{3,2,1,0:T(8,128)(2,1)S(1)} %bitcast.49), custom_call_target="tpu_custom_call" | custom-call | tf_op jit(solution)/shard_map/pallas_call | solution.py:242
  229.2 1.3 collective-permute-start.20
  230.5 1.5 collective-permute-done.20
  232.1 1.0 collective-permute-start.21
  233.1 12.2 %collective-permute-done.21 = f32[128,8,128]{2,1,0:T(8,128)S(1)} collective-permute-done((f32[128,8,128]{2,1,0:T(8,128)S(1)}, f32[128,8,128]{2,1,0:T(8,128)S(1)}, u32[]{:S(2)}, u32[]{:S(2)}) %collective-permute-start.21) | collective-permute-done | bytes 524320 | tf_op jit(solution)/shard_map/ppermute | solution.py:279
  245.7 1.3 collective-permute-start.22
  246.9 1.5 collective-permute-done.22
  248.5 1.0 pad_maximum_fusion.2
  (72 shorter events, 7.5 us)
Async XLA Ops:
  0.0 1.7 copy-start
  7.2 30.4 %all-to-all-start = ((bf16[3,8,256,128]{3,1,0,2:T(8,128)(2,1)}), bf16[3,8,256,128]{3,1,0,2:T(8,128)(2,1)S(1)}, u32[]{:S(2)}, u32[]{:S(2)}) async-start(bf16[3,8,256,128]{3,1,0,2:T(8,128)(2,1)} %copy.7), calls=%async_computation | async-start | bytes 3145728 | tf_op jit(solution)/shard_map/all_to_all | solution.py:310
  37.6 1.2 copy-start.1
  40.9 1.0 copy-start.5
  42.7 5.2 %collective-permute-start = (f32[128,8,128]{2,1,0:T(8,128)}, f32[128,8,128]{2,1,0:T(8,128)}, u32[]{:S(2)}, u32[]{:S(2)}) collective-permute-start(f32[128,8,128]{2,1,0:T(8,128)} %constant_dynamic-slice_fusion.2), channel_id=1, source_target_pairs={{0,32},{32,0},{64,96},{96,64},{1,33},{33,1},{65,97},{97,65},{2,34}... | collective-permute-start | bytes 1572872 | tf_op jit(solution)/shard_map/ppermute | solution.py:277
  49.3 20.1 %copy-start.8 = (f32[3,3,9]{2,1,0:T(4,128)S(1)}, f32[3,3,9]{2,1,0:T(4,128)}, u32[]{:S(2)}) copy-start(f32[3,3,9]{2,1,0:T(4,128)} %param.7) | copy-start | bytes 976
  49.3 7.6 %collective-permute-start.1 = (f32[64,8,128]{2,1,0:T(8,128)S(1)}, f32[64,8,128]{2,1,0:T(8,128)S(1)}, u32[]{:S(2)}, u32[]{:S(2)}) collective-permute-start(f32[64,8,128]{2,1,0:T(8,128)S(1)} %get-tuple-element.27), channel_id=1, source_target_pairs={{0,64},{32,96},{64,0},{96,32},{1,65},{33,97},{65,1},{97,33},{2,66}... | collective-permute-start | bytes 786440 | tf_op jit(solution)/shard_map/ppermute | solution.py:287
  50.3 12.2 %collective-permute-start.2 = (f32[64,8,128]{2,1,0:T(8,128)S(1)}, f32[64,8,128]{2,1,0:T(8,128)S(1)}, u32[]{:S(2)}, u32[]{:S(2)}) collective-permute-start(f32[64,8,128]{2,1,0:T(8,128)S(1)} %get-tuple-element.28), channel_id=1, source_target_pairs={{0,64},{32,96},{64,0},{96,32},{1,65},{33,97},{65,1},{97,33},{2,66}... | collective-permute-start | bytes 786440 | tf_op jit(solution)/shard_map/ppermute | solution.py:287
  62.5 3.1 %copy-start.6 = (f32[64,8,128]{2,1,0:T(8,128)}, f32[64,8,128]{2,1,0:T(8,128)S(1)}, u32[]{:S(2)}) copy-start(f32[64,8,128]{2,1,0:T(8,128)S(1)} %get-tuple-element.26) | copy-start | bytes 786436
  63.3 17.2 %collective-permute-start.4 = (f32[64,4,128]{2,1,0:T(4,128)}, f32[64,4,128]{2,1,0:T(4,128)S(1)}, u32[]{:S(2)}, u32[]{:S(2)}) collective-permute-start(f32[64,4,128]{2,1,0:T(4,128)} %get-tuple-element.36), channel_id=1, source_target_pairs={{0,1},{1,2},{2,3},{3,4},{4,5},{5,6},{6,7},{7,8},{8,9},{9,10},{10,1... | collective-permute-start | bytes 393224 | tf_op jit(solution)/shard_map/ppermute | solution.py:25
  66.4 14.2 %collective-permute-start.5 = (f32[64,4,128]{2,1,0:T(4,128)}, f32[64,4,128]{2,1,0:T(4,128)}, u32[]{:S(2)}, u32[]{:S(2)}) collective-permute-start(f32[64,4,128]{2,1,0:T(4,128)} %get-tuple-element.34), channel_id=1, source_target_pairs={{0,1},{1,2},{2,3},{3,4},{4,5},{5,6},{6,7},{7,8},{8,9},{9,10},{10,1... | collective-permute-start | bytes 393224 | tf_op jit(solution)/shard_map/ppermute | solution.py:25
  69.5 15.5 %collective-permute-start.7 = (f32[64,4,128]{2,1,0:T(4,128)}, f32[64,4,128]{2,1,0:T(4,128)S(1)}, u32[]{:S(2)}, u32[]{:S(2)}) collective-permute-start(f32[64,4,128]{2,1,0:T(4,128)} %get-tuple-element.35), channel_id=1, source_target_pairs={{1,0},{2,1},{3,2},{4,3},{5,4},{6,5},{7,6},{8,7},{9,8},{10,9},{11,1... | collective-permute-start | bytes 393224 | tf_op jit(solution)/shard_map/ppermute | solution.py:26
  77.6 7.4 %collective-permute-start.8 = (f32[64,4,128]{2,1,0:T(4,128)}, f32[64,4,128]{2,1,0:T(4,128)S(1)}, u32[]{:S(2)}, u32[]{:S(2)}) collective-permute-start(f32[64,4,128]{2,1,0:T(4,128)} %get-tuple-element.33), channel_id=1, source_target_pairs={{1,0},{2,1},{3,2},{4,3},{5,4},{6,5},{7,6},{8,7},{9,8},{10,9},{11,1... | collective-permute-start | bytes 393224 | tf_op jit(solution)/shard_map/ppermute | solution.py:26
  81.5 5.3 %collective-permute-start.6 = (f32[128,4,128]{2,1,0:T(4,128)S(1)}, f32[128,4,128]{2,1,0:T(4,128)S(1)}, u32[]{:S(2)}, u32[]{:S(2)}) collective-permute-start(f32[128,4,128]{2,1,0:T(4,128)S(1)} %constant_dynamic-update-slice_fusion), channel_id=1, source_target_pairs={{0,32},{32,0},{64,96},{96,64},{1,33},{33,1},{65,97},{97,65},{2,34}... | collective-permute-start | bytes 786440 | tf_op jit(solution)/shard_map/ppermute | solution.py:297
  84.9 3.2 %collective-permute-start.3 = (f32[128,8,128]{2,1,0:T(8,128)S(1)}, f32[128,8,128]{2,1,0:T(8,128)S(1)}, u32[]{:S(2)}, u32[]{:S(2)}) collective-permute-start(f32[128,8,128]{2,1,0:T(8,128)S(1)} %pad_maximum_fusion.3), channel_id=1, source_target_pairs={{0,32},{32,0},{64,96},{96,64},{1,33},{33,1},{65,97},{97,65},{2,34}... | collective-permute-start | bytes 1572872 | tf_op jit(solution)/shard_map/ppermute | solution.py:294
  85.1 2.9 %collective-permute-start.9 = (f32[128,4,128]{2,1,0:T(4,128)S(1)}, f32[128,4,128]{2,1,0:T(4,128)S(1)}, u32[]{:S(2)}, u32[]{:S(2)}) collective-permute-start(f32[128,4,128]{2,1,0:T(4,128)S(1)} %constant_dynamic-update-slice_fusion.2), channel_id=1, source_target_pairs={{0,32},{32,0},{64,96},{96,64},{1,33},{33,1},{65,97},{97,65},{2,34}... | collective-permute-start | bytes 786440 | tf_op jit(solution)/shard_map/ppermute | solution.py:298
  86.9 1.3 copy-start.7
  88.3 0.8 copy-start.2
  88.3 1.0 copy-start.3
  137.1 2.8 %collective-permute-start.10 = (f32[128,8,128]{2,1,0:T(8,128)S(1)}, f32[128,8,128]{2,1,0:T(8,128)S(1)}, u32[]{:S(2)}, u32[]{:S(2)}) collective-permute-start(f32[128,8,128]{2,1,0:T(8,128)S(1)} %constant_dynamic-slice_fusion.1), channel_id=1, source_target_pairs={{0,32},{32,0},{64,96},{96,64},{1,33},{33,1},{65,97},{97,65},{2,34}... | collective-permute-start | bytes 1572872 | tf_op jit(solution)/shard_map/ppermute | solution.py:277
  139.9 0.8 copy-start.4
  141.6 7.7 %collective-permute-start.11 = (f32[64,8,128]{2,1,0:T(8,128)}, f32[64,8,128]{2,1,0:T(8,128)S(1)}, u32[]{:S(2)}, u32[]{:S(2)}) collective-permute-start(f32[64,8,128]{2,1,0:T(8,128)} %get-tuple-element.19), channel_id=1, source_target_pairs={{0,64},{32,96},{64,0},{96,32},{1,65},{33,97},{65,1},{97,33},{2,66}... | collective-permute-start | bytes 786440 | tf_op jit(solution)/shard_map/ppermute | solution.py:287
  142.5 12.5 %collective-permute-start.12 = (f32[64,8,128]{2,1,0:T(8,128)}, f32[64,8,128]{2,1,0:T(8,128)}, u32[]{:S(2)}, u32[]{:S(2)}) collective-permute-start(f32[64,8,128]{2,1,0:T(8,128)} %get-tuple-element.20), channel_id=1, source_target_pairs={{0,64},{32,96},{64,0},{96,32},{1,65},{33,97},{65,1},{97,33},{2,66}... | collective-permute-start | bytes 786440 | tf_op jit(solution)/shard_map/ppermute | solution.py:287
  156.6 16.4 %collective-permute-start.14 = (f32[64,4,128]{2,1,0:T(4,128)S(1)}, f32[64,4,128]{2,1,0:T(4,128)S(1)}, u32[]{:S(2)}, u32[]{:S(2)}) collective-permute-start(f32[64,4,128]{2,1,0:T(4,128)S(1)} %get-tuple-element.32), channel_id=1, source_target_pairs={{0,1},{1,2},{2,3},{3,4},{4,5},{5,6},{6,7},{7,8},{8,9},{9,10},{10,1... | collective-permute-start | bytes 393224 | tf_op jit(solution)/shard_map/ppermute | solution.py:25
  159.6 13.4 %collective-permute-start.15 = (f32[64,4,128]{2,1,0:T(4,128)S(1)}, f32[64,4,128]{2,1,0:T(4,128)S(1)}, u32[]{:S(2)}, u32[]{:S(2)}) collective-permute-start(f32[64,4,128]{2,1,0:T(4,128)S(1)} %get-tuple-element.30), channel_id=1, source_target_pairs={{0,1},{1,2},{2,3},{3,4},{4,5},{5,6},{6,7},{7,8},{8,9},{9,10},{10,1... | collective-permute-start | bytes 393224 | tf_op jit(solution)/shard_map/ppermute | solution.py:25
  161.5 14.0 %collective-permute-start.17 = (f32[64,4,128]{2,1,0:T(4,128)S(1)}, f32[64,4,128]{2,1,0:T(4,128)S(1)}, u32[]{:S(2)}, u32[]{:S(2)}) collective-permute-start(f32[64,4,128]{2,1,0:T(4,128)S(1)} %get-tuple-element.31), channel_id=1, source_target_pairs={{1,0},{2,1},{3,2},{4,3},{5,4},{6,5},{7,6},{8,7},{9,8},{10,9},{11,1... | collective-permute-start | bytes 393224 | tf_op jit(solution)/shard_map/ppermute | solution.py:26
  170.6 5.7 %collective-permute-start.18 = (f32[64,4,128]{2,1,0:T(4,128)S(1)}, f32[64,4,128]{2,1,0:T(4,128)S(1)}, u32[]{:S(2)}, u32[]{:S(2)}) collective-permute-start(f32[64,4,128]{2,1,0:T(4,128)S(1)} %get-tuple-element.29), channel_id=1, source_target_pairs={{1,0},{2,1},{3,2},{4,3},{5,4},{6,5},{7,6},{8,7},{9,8},{10,9},{11,1... | collective-permute-start | bytes 393224 | tf_op jit(solution)/shard_map/ppermute | solution.py:26
  173.0 6.8 %collective-permute-start.16 = (f32[128,4,128]{2,1,0:T(4,128)S(1)}, f32[128,4,128]{2,1,0:T(4,128)S(1)}, u32[]{:S(2)}, u32[]{:S(2)}) collective-permute-start(f32[128,4,128]{2,1,0:T(4,128)S(1)} %constant_dynamic-update-slice_fusion.4), channel_id=1, source_target_pairs={{0,32},{32,0},{64,96},{96,64},{1,33},{33,1},{65,97},{97,65},{2,34}... | collective-permute-start | bytes 786440 | tf_op jit(solution)/shard_map/ppermute | solution.py:297
  175.5 5.7 %collective-permute-start.13 = (f32[128,8,128]{2,1,0:T(8,128)S(1)}, f32[128,8,128]{2,1,0:T(8,128)S(1)}, u32[]{:S(2)}, u32[]{:S(2)}) collective-permute-start(f32[128,8,128]{2,1,0:T(8,128)S(1)} %pad_maximum_fusion.6), channel_id=1, source_target_pairs={{0,32},{32,0},{64,96},{96,64},{1,33},{33,1},{65,97},{97,65},{2,34}... | collective-permute-start | bytes 1572872 | tf_op jit(solution)/shard_map/ppermute | solution.py:294
  176.3 4.7 %collective-permute-start.19 = (f32[128,4,128]{2,1,0:T(4,128)S(1)}, f32[128,4,128]{2,1,0:T(4,128)S(1)}, u32[]{:S(2)}, u32[]{:S(2)}) collective-permute-start(f32[128,4,128]{2,1,0:T(4,128)S(1)} %constant_dynamic-update-slice_fusion.6), channel_id=1, source_target_pairs={{0,32},{32,0},{64,96},{96,64},{1,33},{33,1},{65,97},{97,65},{2,34}... | collective-permute-start | bytes 786440 | tf_op jit(solution)/shard_map/ppermute | solution.py:298
  229.2 2.8 %collective-permute-start.20 = (f32[128,8,128]{2,1,0:T(8,128)S(1)}, f32[128,8,128]{2,1,0:T(8,128)S(1)}, u32[]{:S(2)}, u32[]{:S(2)}) collective-permute-start(f32[128,8,128]{2,1,0:T(8,128)S(1)} %constant_dynamic-slice_fusion), channel_id=1, source_target_pairs={{0,32},{32,0},{64,96},{96,64},{1,33},{33,1},{65,97},{97,65},{2,34}... | collective-permute-start | bytes 1572872 | tf_op jit(solution)/shard_map/ppermute | solution.py:277
  232.1 13.2 %collective-permute-start.21 = (f32[128,8,128]{2,1,0:T(8,128)S(1)}, f32[128,8,128]{2,1,0:T(8,128)S(1)}, u32[]{:S(2)}, u32[]{:S(2)}) collective-permute-start(f32[128,8,128]{2,1,0:T(8,128)S(1)} %dynamic-slice_add_fusion), channel_id=1, source_target_pairs={{0,64},{32,96},{64,0},{96,32},{1,65},{33,97},{65,1},{97,33},{2,66}... | collective-permute-start | bytes 1572872 | tf_op jit(solution)/shard_map/ppermute | solution.py:279
  245.7 2.8 %collective-permute-start.22 = (f32[128,8,128]{2,1,0:T(8,128)S(1)}, f32[128,8,128]{2,1,0:T(8,128)S(1)}, u32[]{:S(2)}, u32[]{:S(2)}) collective-permute-start(f32[128,8,128]{2,1,0:T(8,128)S(1)} %fusion.36), channel_id=1, source_target_pairs={{0,32},{32,0},{64,96},{96,64},{1,33},{33,1},{65,97},{97,65},{2,34}... | collective-permute-start | bytes 1572872 | tf_op jit(solution)/shard_map/ppermute | solution.py:281

commit v15 on v11

--- a/solution.py
+++ b/solution.py
@@ -35,13 +35,14 @@
     wide_ref[:, rim + width :, :] = after_ref[pl.ds(z0, CZ)]
 
 
-def resample_views(raw_views, weight_norm, offsets):
+def resample_views(raw_views, band_weights, offsets):
     rows = raw_views.shape[2]
-    band = weight_norm.shape[2]
+    band = band_weights.shape[2]
     lag = jnp.arange(rows, dtype=jnp.int32)[None, None, :] - offsets[:, :, None]
     matrix = jnp.zeros(lag.shape, jnp.float32)
     for k in range(band):
-        matrix = matrix + jnp.where(lag == k, weight_norm[:, :, k : k + 1], 0.0)
+        matrix = matrix + jnp.where(lag == k, band_weights[:, :, k : k + 1], 0.0)
+    matrix = matrix / jnp.sum(band_weights, axis=-1, keepdims=True)
     result = jnp.einsum(
         "vxr,vzry->vzxy",
         matrix,
@@ -290,10 +291,9 @@
     count = raw_views.shape[0]
     total_views = count * lax.axis_size("view")
     rim_width = (psf_taps.shape[2] - 1) // 2
-    weight_norm = weights / jnp.sum(weights, axis=-1, keepdims=True)
     taps_norm = psf_taps / jnp.sum(psf_taps, axis=-1, keepdims=True)
     taps_flat = taps_norm.reshape(-1)
-    local_views = resample_views(raw_views, weight_norm, offsets)
+    local_views = resample_views(raw_views, weights, offsets)
     bricks = lax.all_to_all(local_views, "vol", split_axis=2, concat_axis=1, tiled=True)
     local_sum = bricks[0].astype(jnp.float32)
     for index in range(1, count):

time: 242 us -> 243 us (level)
  no operation moved by 1% of the time
where the time goes in v15:
time: 243 us; the launch traced here: 242 us
  Pallas kernels  96.1 us (40%)
  waiting for transfers between devices  84.9 us (35%)
  starting transfers between devices  40.5 us (17%)
  local copies, waits for them, and re-layouts  10.6 us (4%)
  other arithmetic  6.19 us (3%)
  matrix products  3.44 us (1%)
    pallas_call x2, Pallas kernels, iteration_logs(): pl.pallas_call(_iteration_kernel, in_specs=[pl.BlockSpec(memory_space=plt...  96.1 us
    ppermute x3, waiting for transfers between devices, view_sum_update(): own = own + lax.ppermute(own, 'view', chip_swap)  36.6 us
    all_to_all x1, waiting for transfers between devices, per_device(): lax.all_to_all(local_views, 'vol', split_axis=2, concat_axis=1, tiled=True)  19.8 us
    ppermute x2, waiting for transfers between devices, swap_rims(): before = lax.ppermute(last, axis, up)  14.2 us
    all_to_all x1, starting transfers between devices, per_device(): lax.all_to_all(local_views, 'vol', split_axis=2, concat_axis=1, tiled=True)  10.5 us
    ppermute x2, starting transfers between devices, swap_rims(): after = lax.ppermute(first, axis, down)  7.32 us
    ppermute x2, waiting for transfers between devices, swap_rims(): after = lax.ppermute(first, axis, down)  6.96 us
    ppermute x3, starting transfers between devices, view_sum_update(): own = own + lax.ppermute(give, 'view', core_swap)  5.52 us
  transfers between devices with their start and end apart: 18, of which 13 were waited for; matrix products, arithmetic and copies ran while one was open for 1% of the time, Pallas kernels for 0%

profile of v15, /device:TPU:5, one launch (start us, length us, event | category | flops | bytes accessed | tf_op | source)
XLA Modules:
  0.0 242.2 jit_solution(14436866096293591478)
XLA Ops:
  0.0 1.0 fusion.71
  1.1 0.8 reduce_sum.18
  1.9 3.4 %fusion.1 = bf16[3,8,256,128]{3,2,1,0:T(8,128)(2,1)S(1)} fusion(bf16[3,8,256,128]{3,2,1,0:T(8,128)(2,1)S(1)} %copy-done, f32[3,256]{1,0:T(4,128)S(1)} %reduce_sum.18, f32[3,256]{1,0:T(4,128)S(1)} %get-tuple-element.33, f32[3,256]{1,0:T(4,128)S(1)} %get-tuple-element.34, f32[3,256]{1,0:T(4,128)S(1)} %get-tuple-element.35, ...), kind=kOutput, calls=%fused_computation.2 | convolution fusion | flops 2421620736 | bytes 3176448 | tf_op jit(solution)/shard_map/vxr,vzry->vzxy/dot_general | solution.py:46
  5.3 2.2 copy.7
  7.5 10.5 %all-to-all-start = ((bf16[3,8,256,128]{3,1,0,2:T(8,128)(2,1)}), bf16[3,8,256,128]{3,1,0,2:T(8,128)(2,1)S(1)}, u32[]{:S(2)}, u32[]{:S(2)}) async-start(bf16[3,8,256,128]{3,1,0,2:T(8,128)(2,1)} %copy.7), calls=%async_computation | async-start | bytes 3145728 | tf_op jit(solution)/shard_map/all_to_all | solution.py:297
  18.1 19.8 %all-to-all-done = bf16[3,8,256,128]{3,1,0,2:T(8,128)(2,1)S(1)} async-done(((bf16[3,8,256,128]{3,1,0,2:T(8,128)(2,1)}), bf16[3,8,256,128]{3,1,0,2:T(8,128)(2,1)S(1)}, u32[]{:S(2)}, u32[]{:S(2)}) %all-to-all-start) | async-done | bytes 1572896 | tf_op jit(solution)/shard_map/all_to_all | solution.py:297
  37.9 1.2 copy-done.1
  39.1 1.9 copy.28
  41.2 1.0 copy-done.4
  42.2 0.8 constant_dynamic-slice_fusion.2
  43.0 3.4 %collective-permute-start = (f32[128,8,128]{2,1,0:T(8,128)}, f32[128,8,128]{2,1,0:T(8,128)}, u32[]{:S(2)}, u32[]{:S(2)}) collective-permute-start(f32[128,8,128]{2,1,0:T(8,128)} %constant_dynamic-slice_fusion.2), channel_id=1, source_target_pairs={{0,32},{32,0},{64,96},{96,64},{1,33},{33,1},{65,97},{97,65},{2,34}... | collective-permute-start | bytes 1572872 | tf_op jit(solution)/shard_map/ppermute | solution.py:278
  46.4 1.9 collective-permute-done
  48.3 1.3 dynamic-slice_add_fusion.2
  49.5 1.0 collective-permute-start.1
  50.5 12.2 %collective-permute-done.1 = f32[128,8,128]{2,1,0:T(8,128)S(1)} collective-permute-done((f32[128,8,128]{2,1,0:T(8,128)S(1)}, f32[128,8,128]{2,1,0:T(8,128)S(1)}, u32[]{:S(2)}, u32[]{:S(2)}) %collective-permute-start.1) | collective-permute-done | bytes 524320 | tf_op jit(solution)/shard_map/ppermute | solution.py:279
  62.8 0.8 copy-done.2
  63.6 0.8 fusion.70
  64.4 5.2 %collective-permute-start.5 = (f32[128,4,128]{2,1,0:T(4,128)S(1)}, f32[128,4,128]{2,1,0:T(4,128)}, u32[]{:S(2)}, u32[]{:S(2)}) collective-permute-start(f32[128,4,128]{2,1,0:T(4,128)S(1)} %get-tuple-element.21), channel_id=1, source_target_pairs={{1,0},{2,1},{3,2},{4,3},{5,4},{6,5},{7,6},{8,7},{9,8},{10,9},{11,1... | collective-permute-start | bytes 786440 | tf_op jit(solution)/shard_map/ppermute | solution.py:26
  69.6 1.9 collective-permute-start.3
  71.5 2.4 %collective-permute-done.5 = f32[128,4,128]{2,1,0:T(4,128)} collective-permute-done((f32[128,4,128]{2,1,0:T(4,128)S(1)}, f32[128,4,128]{2,1,0:T(4,128)}, u32[]{:S(2)}, u32[]{:S(2)}) %collective-permute-start.5) | collective-permute-done | bytes 262176 | tf_op jit(solution)/shard_map/ppermute | solution.py:26
  74.0 2.1 collective-permute-start.6
  76.3 7.4 %collective-permute-done.3 = f32[128,4,128]{2,1,0:T(4,128)S(1)} collective-permute-done((f32[128,4,128]{2,1,0:T(4,128)}, f32[128,4,128]{2,1,0:T(4,128)S(1)}, u32[]{:S(2)}, u32[]{:S(2)}) %collective-permute-start.3) | collective-permute-done | bytes 262176 | tf_op jit(solution)/shard_map/ppermute | solution.py:25
  83.7 2.4 collective-permute-start.4
  86.2 1.1 broadcast_select_fusion.11
  87.5 0.7 copy-done.3
  88.4 48.3 %shard_map.46 = f32[256,8,128]{2,1,0:T(8,128)S(1)} custom-call(f32[81]{0:T(128)S(1)} %reshape.17.taps_ref, f32[256,4,128]{2,1,0:T(4,128)S(1)} %pad_maximum_fusion.3.before_ref, f32[256,8,128]{2,1,0:T(8,128)S(1)} %pad_maximum_fusion.mid_ref, f32[256,4,128]{2,1,0:T(4,128)S(1)} %pad_maximum_fusion.4.after_ref, bf16[3,256,8,128]{3,2,1,0:T(8,128)(2,1)S(1)} %bitcast.48), custom_call_target="tpu_custom_call" | custom-call | tf_op jit(solution)/shard_map/pallas_call | solution.py:243
  136.7 0.9 collective-permute-start.7
  137.6 1.5 collective-permute-done.7
  139.2 1.0 collective-permute-start.8
  140.2 12.2 %collective-permute-done.8 = f32[128,8,128]{2,1,0:T(8,128)S(1)} collective-permute-done((f32[128,8,128]{2,1,0:T(8,128)S(1)}, f32[128,8,128]{2,1,0:T(8,128)S(1)}, u32[]{:S(2)}, u32[]{:S(2)}) %collective-permute-start.8) | collective-permute-done | bytes 524320 | tf_op jit(solution)/shard_map/ppermute | solution.py:279
  152.4 0.3 fusion.39
  152.7 1.3 collective-permute-start.9
  154.1 2.1 collective-permute-start.12
  156.2 3.2 %collective-permute-start.10 = (f32[128,4,128]{2,1,0:T(4,128)S(1)}, f32[128,4,128]{2,1,0:T(4,128)S(1)}, u32[]{:S(2)}, u32[]{:S(2)}) collective-permute-start(f32[128,4,128]{2,1,0:T(4,128)S(1)} %get-tuple-element.16), channel_id=1, source_target_pairs={{0,1},{1,2},{2,3},{3,4},{4,5},{5,6},{6,7},{7,8},{8,9},{9,10},{10,1... | collective-permute-start | bytes 786440 | tf_op jit(solution)/shard_map/ppermute | solution.py:25
  159.4 4.5 %collective-permute-done.12 = f32[128,4,128]{2,1,0:T(4,128)S(1)} collective-permute-done((f32[128,4,128]{2,1,0:T(4,128)S(1)}, f32[128,4,128]{2,1,0:T(4,128)S(1)}, u32[]{:S(2)}, u32[]{:S(2)}) %collective-permute-start.12) | collective-permute-done | bytes 262176 | tf_op jit(solution)/shard_map/ppermute | solution.py:26
  163.9 0.8 collective-permute-start.13
  164.7 6.7 %collective-permute-done.10 = f32[128,4,128]{2,1,0:T(4,128)S(1)} collective-permute-done((f32[128,4,128]{2,1,0:T(4,128)S(1)}, f32[128,4,128]{2,1,0:T(4,128)S(1)}, u32[]{:S(2)}, u32[]{:S(2)}) %collective-permute-start.10) | collective-permute-done | bytes 262176 | tf_op jit(solution)/shard_map/ppermute | solution.py:25
  171.5 1.1 collective-permute-start.11
  172.9 0.8 collective-permute-done.11
  173.9 47.9 %shard_map.47 = f32[256,8,128]{2,1,0:T(8,128)S(1)} custom-call(f32[81]{0:T(128)S(1)} %reshape.17.taps_ref, f32[256,4,128]{2,1,0:T(4,128)S(1)} %pad_maximum_fusion.5.before_ref, f32[256,8,128]{2,1,0:T(8,128)S(1)} %pad_maximum_fusion.1.mid_ref, f32[256,4,128]{2,1,0:T(4,128)S(1)} %pad_maximum_fusion.6.after_ref, bf16[3,256,8,128]{3,2,1,0:T(8,128)(2,1)S(1)} %bitcast.49), custom_call_target="tpu_custom_call" | custom-call | tf_op jit(solution)/shard_map/pallas_call | solution.py:243
  221.8 1.3 collective-permute-start.14
  223.1 1.5 collective-permute-done.14
  224.7 1.0 collective-permute-start.15
  225.7 12.2 %collective-permute-done.15 = f32[128,8,128]{2,1,0:T(8,128)S(1)} collective-permute-done((f32[128,8,128]{2,1,0:T(8,128)S(1)}, f32[128,8,128]{2,1,0:T(8,128)S(1)}, u32[]{:S(2)}, u32[]{:S(2)}) %collective-permute-start.15) | collective-permute-done | bytes 524320 | tf_op jit(solution)/shard_map/ppermute | solution.py:279
  237.9 0.3 fusion.37
  238.2 1.3 collective-permute-start.16
  239.5 1.5 collective-permute-done.16
  241.1 1.0 pad_maximum_fusion.2
  (39 shorter events, 1.8 us)
Async XLA Ops:
  0.0 1.9 copy-start
  7.5 30.4 %all-to-all-start = ((bf16[3,8,256,128]{3,1,0,2:T(8,128)(2,1)}), bf16[3,8,256,128]{3,1,0,2:T(8,128)(2,1)S(1)}, u32[]{:S(2)}, u32[]{:S(2)}) async-start(bf16[3,8,256,128]{3,1,0,2:T(8,128)(2,1)} %copy.7), calls=%async_computation | async-start | bytes 3145728 | tf_op jit(solution)/shard_map/all_to_all | solution.py:297
  37.9 1.2 copy-start.1
  41.2 1.0 copy-start.4
  43.0 5.3 %collective-permute-start = (f32[128,8,128]{2,1,0:T(8,128)}, f32[128,8,128]{2,1,0:T(8,128)}, u32[]{:S(2)}, u32[]{:S(2)}) collective-permute-start(f32[128,8,128]{2,1,0:T(8,128)} %constant_dynamic-slice_fusion.2), channel_id=1, source_target_pairs={{0,32},{32,0},{64,96},{96,64},{1,33},{33,1},{65,97},{97,65},{2,34}... | collective-permute-start | bytes 1572872 | tf_op jit(solution)/shard_map/ppermute | solution.py:278
  49.5 26.6 %copy-start.5 = (f32[3,3,9]{2,1,0:T(4,128)S(1)}, f32[3,3,9]{2,1,0:T(4,128)}, u32[]{:S(2)}) copy-start(f32[3,3,9]{2,1,0:T(4,128)} %param.7) | copy-start | bytes 976
  49.5 13.2 %collective-permute-start.1 = (f32[128,8,128]{2,1,0:T(8,128)S(1)}, f32[128,8,128]{2,1,0:T(8,128)S(1)}, u32[]{:S(2)}, u32[]{:S(2)}) collective-permute-start(f32[128,8,128]{2,1,0:T(8,128)S(1)} %dynamic-slice_add_fusion.2), channel_id=1, source_target_pairs={{0,64},{32,96},{64,0},{96,32},{1,65},{33,97},{65,1},{97,33},{2,66}... | collective-permute-start | bytes 1572872 | tf_op jit(solution)/shard_map/ppermute | solution.py:279
  62.8 0.8 copy-start.2
  64.4 9.6 %collective-permute-start.5 = (f32[128,4,128]{2,1,0:T(4,128)S(1)}, f32[128,4,128]{2,1,0:T(4,128)}, u32[]{:S(2)}, u32[]{:S(2)}) collective-permute-start(f32[128,4,128]{2,1,0:T(4,128)S(1)} %get-tuple-element.21), channel_id=1, source_target_pairs={{1,0},{2,1},{3,2},{4,3},{5,4},{6,5},{7,6},{8,7},{9,8},{10,9},{11,1... | collective-permute-start | bytes 786440 | tf_op jit(solution)/shard_map/ppermute | solution.py:26
  69.6 14.1 %collective-permute-start.3 = (f32[128,4,128]{2,1,0:T(4,128)}, f32[128,4,128]{2,1,0:T(4,128)S(1)}, u32[]{:S(2)}, u32[]{:S(2)}) collective-permute-start(f32[128,4,128]{2,1,0:T(4,128)} %get-tuple-element.22), channel_id=1, source_target_pairs={{0,1},{1,2},{2,3},{3,4},{4,5},{5,6},{6,7},{7,8},{8,9},{9,10},{10,1... | collective-permute-start | bytes 786440 | tf_op jit(solution)/shard_map/ppermute | solution.py:25
  74.0 12.2 %collective-permute-start.6 = (f32[128,4,128]{2,1,0:T(4,128)}, f32[128,4,128]{2,1,0:T(4,128)}, u32[]{:S(2)}, u32[]{:S(2)}) collective-permute-start(f32[128,4,128]{2,1,0:T(4,128)} %collective-permute-done.5), channel_id=1, source_target_pairs={{0,32},{32,0},{64,96},{96,64},{1,33},{33,1},{65,97},{97,65},{2,34}... | collective-permute-start | bytes 786440 | tf_op jit(solution)/shard_map/ppermute | solution.py:286
  76.3 11.3 %collective-permute-start.2 = (f32[128,8,128]{2,1,0:T(8,128)}, f32[128,8,128]{2,1,0:T(8,128)S(1)}, u32[]{:S(2)}, u32[]{:S(2)}) collective-permute-start(f32[128,8,128]{2,1,0:T(8,128)} %copy-done.2), channel_id=1, source_target_pairs={{0,32},{32,0},{64,96},{96,64},{1,33},{33,1},{65,97},{97,65},{2,34}... | collective-permute-start | bytes 1572872 | tf_op jit(solution)/shard_map/ppermute | solution.py:281
  83.7 3.6 %collective-permute-start.4 = (f32[128,4,128]{2,1,0:T(4,128)S(1)}, f32[128,4,128]{2,1,0:T(4,128)S(1)}, u32[]{:S(2)}, u32[]{:S(2)}) collective-permute-start(f32[128,4,128]{2,1,0:T(4,128)S(1)} %collective-permute-done.3), channel_id=1, source_target_pairs={{0,32},{32,0},{64,96},{96,64},{1,33},{33,1},{65,97},{97,65},{2,34}... | collective-permute-start | bytes 786440 | tf_op jit(solution)/shard_map/ppermute | solution.py:285
  87.2 1.0 copy-start.3
  136.7 2.4 collective-permute-start.7
  139.2 13.2 %collective-permute-start.8 = (f32[128,8,128]{2,1,0:T(8,128)S(1)}, f32[128,8,128]{2,1,0:T(8,128)S(1)}, u32[]{:S(2)}, u32[]{:S(2)}) collective-permute-start(f32[128,8,128]{2,1,0:T(8,128)S(1)} %dynamic-slice_add_fusion.1), channel_id=1, source_target_pairs={{0,64},{32,96},{64,0},{96,32},{1,65},{33,97},{65,1},{97,33},{2,66}... | collective-permute-start | bytes 1572872 | tf_op jit(solution)/shard_map/ppermute | solution.py:279
  152.7 19.8 %collective-permute-start.9 = (f32[128,8,128]{2,1,0:T(8,128)S(1)}, f32[128,8,128]{2,1,0:T(8,128)S(1)}, u32[]{:S(2)}, u32[]{:S(2)}) collective-permute-start(f32[128,8,128]{2,1,0:T(8,128)S(1)} %fusion.39), channel_id=1, source_target_pairs={{0,32},{32,0},{64,96},{96,64},{1,33},{33,1},{65,97},{97,65},{2,34}... | collective-permute-start | bytes 1572872 | tf_op jit(solution)/shard_map/ppermute | solution.py:281
  154.1 9.8 %collective-permute-start.12 = (f32[128,4,128]{2,1,0:T(4,128)S(1)}, f32[128,4,128]{2,1,0:T(4,128)S(1)}, u32[]{:S(2)}, u32[]{:S(2)}) collective-permute-start(f32[128,4,128]{2,1,0:T(4,128)S(1)} %get-tuple-element.15), channel_id=1, source_target_pairs={{1,0},{2,1},{3,2},{4,3},{5,4},{6,5},{7,6},{8,7},{9,8},{10,9},{11,1... | collective-permute-start | bytes 786440 | tf_op jit(solution)/shard_map/ppermute | solution.py:26
  156.2 15.2 %collective-permute-start.10 = (f32[128,4,128]{2,1,0:T(4,128)S(1)}, f32[128,4,128]{2,1,0:T(4,128)S(1)}, u32[]{:S(2)}, u32[]{:S(2)}) collective-permute-start(f32[128,4,128]{2,1,0:T(4,128)S(1)} %get-tuple-element.16), channel_id=1, source_target_pairs={{0,1},{1,2},{2,3},{3,4},{4,5},{5,6},{6,7},{7,8},{8,9},{9,10},{10,1... | collective-permute-start | bytes 786440 | tf_op jit(solution)/shard_map/ppermute | solution.py:25
  163.9 8.8 %collective-permute-start.13 = (f32[128,4,128]{2,1,0:T(4,128)S(1)}, f32[128,4,128]{2,1,0:T(4,128)S(1)}, u32[]{:S(2)}, u32[]{:S(2)}) collective-permute-start(f32[128,4,128]{2,1,0:T(4,128)S(1)} %collective-permute-done.12), channel_id=1, source_target_pairs={{0,32},{32,0},{64,96},{96,64},{1,33},{33,1},{65,97},{97,65},{2,34}... | collective-permute-start | bytes 786440 | tf_op jit(solution)/shard_map/ppermute | solution.py:286
  171.5 2.3 collective-permute-start.11
  221.8 2.8 %collective-permute-start.14 = (f32[128,8,128]{2,1,0:T(8,128)S(1)}, f32[128,8,128]{2,1,0:T(8,128)S(1)}, u32[]{:S(2)}, u32[]{:S(2)}) collective-permute-start(f32[128,8,128]{2,1,0:T(8,128)S(1)} %constant_dynamic-slice_fusion), channel_id=1, source_target_pairs={{0,32},{32,0},{64,96},{96,64},{1,33},{33,1},{65,97},{97,65},{2,34}... | collective-permute-start | bytes 1572872 | tf_op jit(solution)/shard_map/ppermute | solution.py:278
  224.7 13.2 %collective-permute-start.15 = (f32[128,8,128]{2,1,0:T(8,128)S(1)}, f32[128,8,128]{2,1,0:T(8,128)S(1)}, u32[]{:S(2)}, u32[]{:S(2)}) collective-permute-start(f32[128,8,128]{2,1,0:T(8,128)S(1)} %dynamic-slice_add_fusion), channel_id=1, source_target_pairs={{0,64},{32,96},{64,0},{96,32},{1,65},{33,97},{65,1},{97,33},{2,66}... | collective-permute-start | bytes 1572872 | tf_op jit(solution)/shard_map/ppermute | solution.py:279
  238.2 2.8 %collective-permute-start.16 = (f32[128,8,128]{2,1,0:T(8,128)S(1)}, f32[128,8,128]{2,1,0:T(8,128)S(1)}, u32[]{:S(2)}, u32[]{:S(2)}) collective-permute-start(f32[128,8,128]{2,1,0:T(8,128)S(1)} %fusion.37), channel_id=1, source_target_pairs={{0,32},{32,0},{64,96},{96,64},{1,33},{33,1},{65,97},{97,65},{2,34}... | collective-permute-start | bytes 1572872 | tf_op jit(solution)/shard_map/ppermute | solution.py:281
